TPU v7x, 32 devices: a whole 2x2x4 slice. The times are simulated.
32 devices in a mesh: dp: 4 (over y, x), seq: 4 (over z), tensor: 2 (over core).
Axes of the slice: x: 2, y: 2, z: 4, core: 2. Of those that a mesh axis runs over, the one named last changes fastest.
Arguments:
- tokens: bfloat16 [8, 1024, 2048], P('dp', 'seq'), may hold values from -6 to 6
- doc_starts: int32 [8, 1024], P('dp', 'seq'), may hold values 0 or 1
- attn_gain: bfloat16 [2048], P(('dp', 'seq')), may hold values from 0.5 to 1.5
- mlp_gain: bfloat16 [2048], P(('dp', 'seq')), may hold values from 0.5 to 1.5
- query_weight: bfloat16 [2048, 256], P(('dp', 'seq'), 'tensor'), may hold values from -0.125 to 0.125
- key_weight: bfloat16 [2048, 256], P(('dp', 'seq'), 'tensor'), may hold values from -0.125 to 0.125
- value_weight: bfloat16 [2048, 2048], P(('dp', 'seq'), 'tensor'), may hold values from -0.125 to 0.125
- output_weight: bfloat16 [2048, 2048], P('tensor', ('dp', 'seq')), may hold values from -2 to 2
- gate_weight: bfloat16 [2048, 5504], P(('dp', 'seq'), 'tensor'), may hold values from -0.125 to 0.125
- up_weight: bfloat16 [2048, 5504], P(('dp', 'seq'), 'tensor'), may hold values from -0.125 to 0.125
- down_weight: bfloat16 [5504, 2048], P('tensor', ('dp', 'seq')), may hold values from -0.078125 to 0.078125
- cotangent: bfloat16 [8, 1024, 2048], P('dp', 'seq'), may hold values from -6 to 6
Outputs:
- block_out: bfloat16 [8, 1024, 2048], P('dp', 'seq')
- grad_tokens: float32 [8, 1024, 2048], P('dp', 'seq')
- grad_attn_gain: float32 [2048], P(('dp', 'seq'))
- grad_mlp_gain: float32 [2048], P(('dp', 'seq'))
- grad_query: float32 [2048, 256], P(('dp', 'seq'), 'tensor')
- grad_key: float32 [2048, 256], P(('dp', 'seq'), 'tensor')
- grad_value: float32 [2048, 2048], P(('dp', 'seq'), 'tensor')
- grad_output: float32 [2048, 2048], P('tensor', ('dp', 'seq'))
- grad_gate: float32 [2048, 5504], P(('dp', 'seq'), 'tensor')
- grad_up: float32 [2048, 5504], P(('dp', 'seq'), 'tensor')
- grad_down: float32 [5504, 2048], P('tensor', ('dp', 'seq'))
All inputs are finite; a program needn't handle non-finite values. No bound on the sum of `doc_starts` on one device may be relied on, other than what follows from the above.
Results may differ from a plain program's by a relative error of at most 0.013.
Values may be sent and summed in bfloat16 or wider, within the bound.
A program may use at most 256 MiB of HBM per device.

v0:
```python
from functools import partial

import jax
import jax.numpy as jnp
from jax import lax
from jax.sharding import PartitionSpec as P

FDIM = 16
VHEAD = 128
MICRO = 2


norm_epsilon = 1e-05
highest = lax.Precision.HIGHEST
outer_scale = 0.17677669529663687


def prefix(x, axis, combine, identity, reverse):
    size, index = (lax.axis_size(axis), lax.axis_index(axis))
    everything = jax.tree.map(lambda part: lax.all_gather(part, axis), x)
    start = jax.tree.map(
        lambda part, zero: jnp.broadcast_to(jnp.asarray(zero, part.dtype), part.shape), x, identity
    )

    def turn(k, before):
        at = size - 1 - k if reverse else k
        reached = at > index if reverse else at < index
        new = combine(before, jax.tree.map(lambda part: part[at], everything))
        return jax.tree.map(lambda a, b: jnp.where(reached, a, b), new, before)

    return lax.fori_loop(0, size, turn, start)


def features(vectors):
    ones_col = jnp.ones(vectors.shape[:-1] + (1,), jnp.float32)
    outer_terms = vectors[..., :, None] * vectors[..., None, :] * outer_scale
    outer_terms = outer_terms.reshape(vectors.shape[:-1] + (vectors.shape[-1] * vectors.shape[-1],))
    return jnp.concatenate([ones_col, 0.5 * vectors, outer_terms], axis=-1)


def mix_span(queries, key_rows, values, state_in, norm_in, segments):
    length = queries.shape[1]
    scores = jnp.einsum("rthf,rshf->rhts", queries, key_rows, precision=highest) / 4.0
    kernel = 1.0 + scores + 0.5 * scores * scores
    position = jnp.arange(length)
    causal = position[None, :] <= position[:, None]
    allowed = causal[None] & (segments[:, :, None] == segments[:, None, :])
    kernel = jnp.where(allowed[:, None], kernel, 0.0)
    numerator = jnp.einsum("rhts,rshe->rthe", kernel, values, precision=highest)
    denominator = jnp.transpose(jnp.sum(kernel, axis=-1), (0, 2, 1))
    head_part = (segments == 0).astype(jnp.float32)[:, :, None]
    lifted = features(queries)
    numerator = numerator + head_part[..., None] * jnp.einsum(
        "rthf,rhfe->rthe", lifted, state_in, precision=highest
    )
    denominator = denominator + head_part * jnp.einsum(
        "rthf,rhf->rth", lifted, norm_in, precision=highest
    )
    return numerator / denominator[..., None]


def tail_span(key_rows, values, segments):
    tail_mask = (segments == segments[:, -1:]).astype(jnp.float32)
    lifted = features(key_rows) * tail_mask[:, :, None, None]
    tail_state = jnp.einsum("rshf,rshe->rhfe", lifted, values, precision=highest)
    return (tail_state, jnp.sum(lifted, axis=1))


def combine_carry(earlier_part, later_part):
    keep_rate = 1.0 - later_part[2]
    return (
        later_part[0] + keep_rate[:, None, None, None] * earlier_part[0],
        later_part[1] + keep_rate[:, None, None] * earlier_part[1],
        jnp.maximum(earlier_part[2], later_part[2]),
    )


def inverse_rms(inputs):
    return lax.rsqrt(jnp.mean(inputs * inputs, axis=-1, keepdims=True) + norm_epsilon)


def norm_backward(inputs, scale_row, gain_vec, grad_normed):
    scaled_grad = grad_normed * gain_vec
    grad_gain = jnp.sum(grad_normed * inputs * scale_row, axis=0)
    grad_inputs = scale_row * scaled_grad - inputs * scale_row * scale_row * scale_row * jnp.mean(
        scaled_grad * inputs, axis=-1, keepdims=True
    )
    return (grad_inputs, grad_gain)


def inner_rows(left_mat, right_mat):
    return lax.dot_general(
        left_mat, right_mat, (((0,), (0,)), ((), ())), preferred_element_type=jnp.float32
    )


def by_transpose(left_mat, right_mat):
    return lax.dot_general(
        left_mat, right_mat, (((1,), (1,)), ((), ())), preferred_element_type=jnp.float32
    )


def local(
    tokens,
    doc_starts,
    attn_gain,
    mlp_gain,
    query_weight,
    key_weight,
    value_weight,
    output_weight,
    gate_weight,
    up_weight,
    down_weight,
    cotangent,
):
    micro_rows = tokens.shape[0] // MICRO
    span_len = tokens.shape[1]
    model_width = tokens.shape[2]
    head_count = query_weight.shape[1] // FDIM
    outputs_main = []
    outputs_grad = []
    totals = None
    for micro_index in range(MICRO):
        row_start = micro_index * micro_rows
        rows_in = tokens[row_start : row_start + micro_rows]
        starts_in = doc_starts[row_start : row_start + micro_rows]
        cot_in = cotangent[row_start : row_start + micro_rows].reshape(-1, model_width)
        (
            full_query,
            full_key,
            full_value,
            full_gate,
            full_up,
            full_output,
            full_down,
            gain_one,
            gain_two,
        ) = (
            lax.all_gather(query_weight, ("dp", "seq"), axis=0, tiled=True),
            lax.all_gather(key_weight, ("dp", "seq"), axis=0, tiled=True),
            lax.all_gather(value_weight, ("dp", "seq"), axis=0, tiled=True),
            lax.all_gather(gate_weight, ("dp", "seq"), axis=0, tiled=True),
            lax.all_gather(up_weight, ("dp", "seq"), axis=0, tiled=True),
            lax.all_gather(output_weight, ("dp", "seq"), axis=1, tiled=True),
            lax.all_gather(down_weight, ("dp", "seq"), axis=1, tiled=True),
            lax.all_gather(attn_gain, ("dp", "seq"), axis=0, tiled=True),
            lax.all_gather(mlp_gain, ("dp", "seq"), axis=0, tiled=True),
        )
        gain_one_f = gain_one.astype(jnp.float32)
        gain_two_f = gain_two.astype(jnp.float32)
        flat_rows = rows_in.reshape(-1, model_width).astype(jnp.float32)
        scale_one = inverse_rms(flat_rows)
        normed_one = (flat_rows * scale_one * gain_one_f).astype(jnp.bfloat16)
        query_low = jnp.dot(normed_one, full_query, preferred_element_type=jnp.float32).astype(
            jnp.bfloat16
        )
        key_low = jnp.dot(normed_one, full_key, preferred_element_type=jnp.float32).astype(
            jnp.bfloat16
        )
        value_low = jnp.dot(normed_one, full_value, preferred_element_type=jnp.float32).astype(
            jnp.bfloat16
        )
        queries = query_low.astype(jnp.float32).reshape(micro_rows, span_len, head_count, FDIM)
        key_rows = key_low.astype(jnp.float32).reshape(micro_rows, span_len, head_count, FDIM)
        values = value_low.astype(jnp.float32).reshape(micro_rows, span_len, head_count, VHEAD)
        segments = jnp.cumsum(starts_in, axis=1)
        reset_flag = (segments[:, -1] > 0).astype(jnp.float32)
        (tail_state, tail_norm), tail_pull = jax.vjp(
            partial(tail_span, segments=segments), key_rows, values
        )
        state_in, norm_in, reset_in = prefix(
            (tail_state, tail_norm, reset_flag),
            "seq",
            combine_carry,
            (jnp.zeros_like(tail_state), jnp.zeros_like(tail_norm), jnp.zeros_like(reset_flag)),
            False,
        )
        mixed_heads, mix_pull = jax.vjp(
            partial(mix_span, segments=segments), queries, key_rows, values, state_in, norm_in
        )
        mixed_low = mixed_heads.reshape(-1, head_count * VHEAD).astype(jnp.bfloat16)
        branch_one = jnp.dot(mixed_low, full_output, preferred_element_type=jnp.float32)
        residual = flat_rows + lax.psum(branch_one, "tensor")
        scale_two = inverse_rms(residual)
        normed_two = (residual * scale_two * gain_two_f).astype(jnp.bfloat16)
        gate_proj = jnp.dot(normed_two, full_gate, preferred_element_type=jnp.float32)
        up_proj = jnp.dot(normed_two, full_up, preferred_element_type=jnp.float32)
        sigmoid_gate = jax.nn.sigmoid(gate_proj)
        hidden = (gate_proj * sigmoid_gate * up_proj).astype(jnp.bfloat16)
        branch_two = jnp.dot(hidden, full_down, preferred_element_type=jnp.float32)
        block_low = (
            residual + lax.psum(branch_two.astype(jnp.bfloat16), "tensor").astype(jnp.float32)
        ).astype(jnp.bfloat16)
        outputs_main.append(block_low.reshape(micro_rows, span_len, model_width))
        grad_down = inner_rows(hidden, cot_in)
        grad_hidden = by_transpose(cot_in, full_down)
        grad_gate_low = (
            grad_hidden * up_proj * sigmoid_gate * (1.0 + gate_proj * (1.0 - sigmoid_gate))
        ).astype(jnp.bfloat16)
        grad_up_low = (grad_hidden * gate_proj * sigmoid_gate).astype(jnp.bfloat16)
        grad_gate = inner_rows(normed_two, grad_gate_low)
        grad_up = inner_rows(normed_two, grad_up_low)
        grad_normed_two = by_transpose(grad_gate_low, full_gate) + by_transpose(
            grad_up_low, full_up
        )
        grad_normed_two = lax.psum(grad_normed_two, "tensor")
        grad_resid, grad_gain_two = norm_backward(residual, scale_two, gain_two_f, grad_normed_two)
        grad_resid = grad_resid + cot_in.astype(jnp.float32)
        grad_resid_low = grad_resid.astype(jnp.bfloat16)
        grad_output = inner_rows(mixed_low, grad_resid_low)
        grad_mixed = by_transpose(grad_resid_low, full_output).astype(jnp.bfloat16)
        grad_mixed = (
            lax.optimization_barrier(grad_mixed)
            .astype(jnp.float32)
            .reshape(micro_rows, span_len, head_count, VHEAD)
        )
        grad_queries, grad_keys, grad_values, grad_state, grad_norm = mix_pull(grad_mixed)
        carried_state, carried_norm, reset_out = prefix(
            (grad_state, grad_norm, reset_flag),
            "seq",
            combine_carry,
            (jnp.zeros_like(grad_state), jnp.zeros_like(grad_norm), jnp.zeros_like(reset_flag)),
            True,
        )
        more_keys, more_values = tail_pull((carried_state, carried_norm))
        grad_query_low = grad_queries.reshape(-1, head_count * FDIM).astype(jnp.bfloat16)
        grad_key_low = (grad_keys + more_keys).reshape(-1, head_count * FDIM).astype(jnp.bfloat16)
        grad_value_low = (
            (grad_values + more_values).reshape(-1, head_count * VHEAD).astype(jnp.bfloat16)
        )
        grad_query = inner_rows(normed_one, grad_query_low)
        grad_key = inner_rows(normed_one, grad_key_low)
        grad_value = inner_rows(normed_one, grad_value_low)
        grad_normed_one = (
            by_transpose(grad_query_low, full_query)
            + by_transpose(grad_key_low, full_key)
            + by_transpose(grad_value_low, full_value)
        )
        grad_normed_one = lax.psum(grad_normed_one, "tensor")
        grad_inputs, grad_gain_one = norm_backward(
            flat_rows, scale_one, gain_one_f, grad_normed_one
        )
        outputs_grad.append((grad_resid + grad_inputs).reshape(micro_rows, span_len, model_width))
        shares = (
            grad_query,
            grad_key,
            grad_value,
            grad_gate,
            grad_up,
            grad_output,
            grad_down,
            grad_gain_one,
            grad_gain_two,
        )
        if totals is None:
            totals = shares
        else:
            totals = jax.tree.map(jnp.add, totals, shares)
    totals = (
        lax.psum_scatter(totals[0], ("dp", "seq"), scatter_dimension=0, tiled=True),
        lax.psum_scatter(totals[1], ("dp", "seq"), scatter_dimension=0, tiled=True),
        lax.psum_scatter(totals[2], ("dp", "seq"), scatter_dimension=0, tiled=True),
        lax.psum_scatter(totals[3], ("dp", "seq"), scatter_dimension=0, tiled=True),
        lax.psum_scatter(totals[4], ("dp", "seq"), scatter_dimension=0, tiled=True),
        lax.psum_scatter(totals[5], ("dp", "seq"), scatter_dimension=1, tiled=True),
        lax.psum_scatter(totals[6], ("dp", "seq"), scatter_dimension=1, tiled=True),
        lax.psum_scatter(totals[7], ("dp", "seq"), scatter_dimension=0, tiled=True),
        lax.psum_scatter(totals[8], ("dp", "seq"), scatter_dimension=0, tiled=True),
    )
    return (
        jnp.concatenate(outputs_main, axis=0),
        jnp.concatenate(outputs_grad, axis=0),
        totals[7],
        totals[8],
        totals[0],
        totals[1],
        totals[2],
        totals[5],
        totals[3],
        totals[4],
        totals[6],
    )


def solution(mesh):
    return jax.shard_map(
        local,
        mesh=mesh,
        in_specs=(
            P("dp", "seq", None),
            P("dp", "seq"),
            P(("dp", "seq")),
            P(("dp", "seq")),
            P(("dp", "seq"), "tensor"),
            P(("dp", "seq"), "tensor"),
            P(("dp", "seq"), "tensor"),
            P("tensor", ("dp", "seq")),
            P(("dp", "seq"), "tensor"),
            P(("dp", "seq"), "tensor"),
            P("tensor", ("dp", "seq")),
            P("dp", "seq", None),
        ),
        out_specs=(
            P("dp", "seq", None),
            P("dp", "seq", None),
            P(("dp", "seq")),
            P(("dp", "seq")),
            P(("dp", "seq"), "tensor"),
            P(("dp", "seq"), "tensor"),
            P(("dp", "seq"), "tensor"),
            P("tensor", ("dp", "seq")),
            P(("dp", "seq"), "tensor"),
            P(("dp", "seq"), "tensor"),
            P("tensor", ("dp", "seq")),
        ),
        check_vma=False,
    )
```

profile of v0, /device:TPU:0, one launch (start us, length us, event | category | flops | bytes accessed | tf_op | source)
XLA Modules:
  0.0 3251.2 jit_solution(12867327998906486753)
XLA Ops:
  8.0 42.4 %all-gather.8 = bf16[16,1,128]{2,1,0:T(2,128)(2,1)S(1)} all-gather(bf16[1,1,128]{2,1,0:T(2,128)(2,1)} %bitcast.757), channel_id=1, replica_groups=mesh['dp'=4,'seq'=4,'tensor'=2] {'dp','seq'}, dimensions={0}, use_global_device_ids=true | all-gather | bytes 4352 | tf_op jit(solution)/shard_map/all_gather | solution.py:147
  61.0 46.7 %all_gather.99 = bf16[2048,128]{1,0:T(8,128)(2,1)S(1)} all-gather(bf16[128,128]{1,0:T(8,128)(2,1)S(1)} %copy-done.112), channel_id=1, replica_groups=mesh['dp'=4,'seq'=4,'tensor'=2] {'dp','seq'}, dimensions={0}, use_global_device_ids=true | all-gather | bytes 557056 | tf_op jit(solution)/shard_map/all_gather | solution.py:141
  110.7 3.7 fusion.77
  124.4 70.8 %all_gather.98 = bf16[2048,128]{1,0:T(8,128)(2,1)S(1)} all-gather(bf16[128,128]{1,0:T(8,128)(2,1)S(1)} %copy-done.113), channel_id=1, replica_groups=mesh['dp'=4,'seq'=4,'tensor'=2] {'dp','seq'}, dimensions={0}, use_global_device_ids=true | all-gather | bytes 557056 | tf_op jit(solution)/shard_map/all_gather | solution.py:140
  201.6 16.8 all-gather.3
  220.8 25.9 all-gather.1
  250.5 9.7 all-reduce.5
  267.9 24.9 while.75
  275.1 3.2 fusion.336
  281.6 3.2 fusion.336
  295.9 24.9 while.74
  320.9 3.3 fusion.172
  325.5 5.8 divide_convert_fusion
  331.3 4.0 divide_convert_fusion.1
  335.3 51.5 %all-gather.22.cloned.1.call-done = bf16[1024,2048]{1,0:T(8,128)(2,1)} async-done(((bf16[1024,128]{1,0:T(8,128)(2,1)}), bf16[1024,2048]{1,0:T(8,128)(2,1)}) %all-gather.22.cloned.1.call-update) | async-done | bytes 4194320 | tf_op jit(solution)/shard_map/all_gather | solution.py:145
  386.8 4.9 fusion.233
  396.5 37.8 %all-gather.9 = bf16[16,1,128]{2,1,0:T(2,128)(2,1)S(1)} all-gather(bf16[1,1,128]{2,1,0:T(2,128)(2,1)S(1)} %bitcast.758), channel_id=1, replica_groups=mesh['dp'=4,'seq'=4,'tensor'=2] {'dp','seq'}, dimensions={0}, use_global_device_ids=true | all-gather | bytes 4352 | tf_op jit(solution)/shard_map/all_gather | solution.py:148
  439.9 164.7 %all-gather.24.cloned.1.call-done = bf16[2048,2752]{0,1:T(8,128)(2,1)} async-done(((bf16[128,2752]{0,1:T(8,128)(2,1)}), bf16[2048,2752]{0,1:T(8,128)(2,1)}) %all-gather.24.cloned.1.call-update) | async-done | bytes 11272208 | tf_op jit(solution)/shard_map/all_gather | solution.py:143
  604.6 8.9 fusion.234
  613.5 171.6 %all-gather.26.cloned.1.call-done = bf16[2048,2752]{0,1:T(8,128)(2,1)} async-done(((bf16[128,2752]{0,1:T(8,128)(2,1)}), bf16[2048,2752]{0,1:T(8,128)(2,1)}) %all-gather.26.cloned.1.call-update) | async-done | bytes 11272208 | tf_op jit(solution)/shard_map/all_gather | solution.py:144
  785.1 9.0 fusion.235
  794.1 4.9 fusion.231
  799.1 5.0 fusion.232
  804.1 161.5 %all-gather.28.cloned.1.call-done = bf16[2752,2048]{1,0:T(8,128)(2,1)} async-done(((bf16[2752,128]{1,0:T(8,128)(2,1)}), bf16[2752,2048]{1,0:T(8,128)(2,1)}) %all-gather.28.cloned.1.call-update) | async-done | bytes 11272208 | tf_op jit(solution)/shard_map/all_gather | solution.py:146
  965.6 11.7 multiply_convert_fusion
  978.4 8.8 fusion.239
  987.2 8.2 multiply_convert_fusion.2
  998.7 9.0 convolution_add_fusion.7
  1007.7 4.5 convolution_add_fusion.8
  1012.5 9.6 convolution_convert_fusion
  1022.9 4.2 convolution_convert_fusion.1
  1027.1 12.1 all-reduce.17.cloned.1.call-done
  1039.1 4.6 multiply_reduce_fusion.1
  1043.8 20.1 all-reduce.21.cloned.1.call-done
  1063.9 6.5 convert_add_fusion.1
  1080.7 3.6 add_bitcast_fusion
  1092.0 4.2 convolution_bitcast_fusion.1
  1099.3 3.5 add_bitcast_fusion.1
  1115.2 15.8 all-gather.7
  1131.0 14.2 all-gather.5
  1158.6 3.7 fusion.106
  1162.3 3.6 fusion.114
  1166.7 18.3 while.77
  1190.8 3.9 fusion.74
  1194.7 57.5 %all-gather.34.cloned.1.call-done = f32[4,8,273,128]{3,1,2,0:T(8,128)} async-done(((f32[1,8,273,128]{3,1,2,0:T(8,128)}), f32[4,8,273,128]{3,1,2,0:T(8,128)}) %all-gather.34.cloned.1.call-update) | async-done | bytes 4472848 | tf_op jit(solution)/shard_map/all_gather | solution.py:20
  1252.2 18.1 while.76
  1270.3 5.0 fusion.75
  1296.5 4.0 fusion.147
  1300.5 4.7 convolution_add_fusion.3
  1306.7 5.1 convolution_add_fusion.4
  1312.3 12.6 fusion.242
  1324.9 14.6 convolution_add_fusion.1
  1339.7 12.4 fusion.243
  1352.0 14.6 convolution_add_fusion
  1366.9 12.4 fusion.119
  1379.3 14.7 convolution_add_fusion.2
  1398.7 3.5 fusion.49
  1402.2 74.9 %all-reduce.4 = (f32[2048]{0:T(1024)S(1)}, f32[2048]{0:T(1024)S(1)}) all-reduce(f32[2048]{0:T(1024)S(1)} %add.419, f32[2048]{0:T(1024)S(1)} %add.420), channel_id=10, replica_groups=mesh['dp'=4,'seq'=4,'tensor'=2] {'dp','seq'}, use_global_device_ids=true, to_apply=%region_44.45.clone | all-reduce | flops 4096 | bytes 32768
  1478.3 4.2 fusion.45
  1484.8 175.5 %reduce-scatter.14.cloned.1.call-done = f32[1024,128]{1,0:T(8,128)} async-done(((f32[1024,2048]{1,0:T(8,128)}), f32[1024,128]{1,0:T(8,128)}) %reduce-scatter.14.cloned.1.call-update) | async-done | bytes 524304 | tf_op jit(solution)/shard_map/reduce_scatter | solution.py:266
  1660.2 182.6 %reduce-scatter.12.cloned.1.call-done = f32[128,1024]{1,0:T(8,128)} async-done(((f32[2048,1024]{1,0:T(8,128)}), f32[128,1024]{1,0:T(8,128)}) %reduce-scatter.12.cloned.1.call-update) | async-done | bytes 524304 | tf_op jit(solution)/shard_map/reduce_scatter | solution.py:263
  1842.8 465.5 %reduce-scatter.16.cloned.1.call-done = f32[128,2752]{0,1:T(8,128)} async-done(((f32[2048,2752]{0,1:T(8,128)}), f32[128,2752]{0,1:T(8,128)}) %reduce-scatter.16.cloned.1.call-update) | async-done | bytes 1409040 | tf_op jit(solution)/shard_map/reduce_scatter | solution.py:264
  2308.3 468.0 %reduce-scatter.18.cloned.1.call-done = f32[128,2752]{0,1:T(8,128)} async-done(((f32[2048,2752]{0,1:T(8,128)}), f32[128,2752]{0,1:T(8,128)}) %reduce-scatter.18.cloned.1.call-update) | async-done | bytes 1409040 | tf_op jit(solution)/shard_map/reduce_scatter | solution.py:265
  2776.3 467.9 %reduce-scatter.20.cloned.1.call-done = f32[2752,128]{1,0:T(8,128)} async-done(((f32[2752,2048]{1,0:T(8,128)}), f32[2752,128]{1,0:T(8,128)}) %reduce-scatter.20.cloned.1.call-update) | async-done | bytes 1409040 | tf_op jit(solution)/shard_map/reduce_scatter | solution.py:267
  (569 shorter events, 224.3 us)
Async XLA Ops:
  7.2 100.6 %copy-start.1 = (bf16[2,256,2048]{2,1,0:T(8,128)(2,1)S(1)}, bf16[2,256,2048]{2,1,0:T(8,128)(2,1)}, u32[]{:S(2)}) copy-start(bf16[2,256,2048]{2,1,0:T(8,128)(2,1)} %param.20) | copy-start | bytes 6291460
  7.2 53.8 %copy-start.112 = (bf16[128,128]{1,0:T(8,128)(2,1)S(1)}, bf16[128,128]{1,0:T(8,128)(2,1)}, u32[]{:S(2)}) copy-start(bf16[128,128]{1,0:T(8,128)(2,1)} %param.25) | copy-start | bytes 98308
  7.2 103.5 %all-gather.20.cloned.1.call-start = ((), (), s32[]{:S(2)}) async-start(), calls=%async_computation.7 | async-start | bytes 4456448 | tf_op jit(solution)/shard_map/all_gather | solution.py:142
  7.9 259.9 %all-gather.32.cloned.1.call-start = ((), (), s32[]{:S(2)}) async-start(), calls=%async_computation.20 | async-start | bytes 5591040 | tf_op jit(solution)/shard_map/all_gather | solution.py:20
  50.4 146.0 %copy-start.58 = (f32[16,1,128]{2,1,0:T(1,128)}, f32[16,1,128]{2,1,0:T(1,128)S(1)}, u32[]{:S(2)}) copy-start(f32[16,1,128]{2,1,0:T(1,128)S(1)} %convert_element_type.332) | copy-start | bytes 24580
  55.0 143.4 %copy-start.97 = (f32[273]{0:T(512)}, f32[273]{0:T(512)S(1)}, u32[]{:S(2)}) copy-start(f32[273]{0:T(512)S(1)} %pad.19.clone) | copy-start | bytes 3280
  61.0 134.2 %copy-start.106 = (f32[256]{0:T(256)}, f32[256]{0:T(256)S(1)}, u32[]{:S(2)}) copy-start(f32[256]{0:T(256)S(1)} %get-tuple-element.951) | copy-start | bytes 3076
  61.0 135.4 %copy-start.114 = (f32[256]{0:T(256)}, f32[256]{0:T(256)S(1)}, u32[]{:S(2)}) copy-start(f32[256]{0:T(256)S(1)} %get-tuple-element.952) | copy-start | bytes 3076
  61.0 137.4 %copy-start.116 = (f32[256]{0:T(256)}, f32[256]{0:T(256)S(1)}, u32[]{:S(2)}) copy-start(f32[256]{0:T(256)S(1)} %get-tuple-element.954) | copy-start | bytes 3076
  61.0 137.4 %copy-start.118 = (f32[256]{0:T(256)}, f32[256]{0:T(256)S(1)}, u32[]{:S(2)}) copy-start(f32[256]{0:T(256)S(1)} %get-tuple-element.953) | copy-start | bytes 3076
  108.3 151.9 %copy-start.60 = (bf16[256,128]{0,1:T(8,128)(2,1)}, bf16[256,128]{0,1:T(8,128)(2,1)S(1)}, u32[]{:S(2)}) copy-start(bf16[256,128]{0,1:T(8,128)(2,1)S(1)} %convolution_convert_fusion.6) | copy-start | bytes 196612
  117.1 178.8 %all-gather.30.cloned.1.call-start = ((), (), s32[]{:S(2)}) async-start(), calls=%async_computation.19 | async-start | bytes 5591040 | tf_op jit(solution)/shard_map/all_gather | solution.py:20
  117.8 143.9 %copy-start.62 = (bf16[256,128]{0,1:T(8,128)(2,1)}, bf16[256,128]{0,1:T(8,128)(2,1)S(1)}, u32[]{:S(2)}) copy-start(bf16[256,128]{0,1:T(8,128)(2,1)S(1)} %convolution_convert_fusion.8) | copy-start | bytes 196612
  120.8 144.6 %copy-start.72 = (bf16[32,8,8,128]{3,2,1,0:T(8,128)(2,1)}, bf16[32,8,8,128]{3,2,1,0:T(8,128)(2,1)S(1)}, u32[]{:S(2)}) copy-start(bf16[32,8,8,128]{3,2,1,0:T(8,128)(2,1)S(1)} %fusion.76) | copy-start | bytes 1572868
  123.6 263.2 %all-gather.22.cloned.1.call-start = ((), (), s32[]{:S(2)}) async-start(), calls=%async_computation.8 | async-start | bytes 4456448 | tf_op jit(solution)/shard_map/all_gather | solution.py:145
  124.2 310.2 %all-reduce.19.cloned.1.call-start = ((), (), s32[]{:S(2)}) async-start(), calls=%async_computation.25 | async-start | bytes 8388608 | tf_op jit(solution)/shard_map/psum | solution.py:184
  124.4 135.9 %copy-start.101 = (pred[256,256]{0,1:T(8,128)(4,1)}, pred[256,256]{0,1:T(8,128)(4,1)S(1)}, u32[]{:S(2)}) copy-start(pred[256,256]{0,1:T(8,128)(4,1)S(1)} %fusion.158) | copy-start | bytes 196612
  196.4 63.8 %copy-start.87 = (bf16[256,128]{0,1:T(8,128)(2,1)}, bf16[256,128]{0,1:T(8,128)(2,1)S(1)}, u32[]{:S(2)}) copy-start(bf16[256,128]{0,1:T(8,128)(2,1)S(1)} %get-tuple-element.940) | copy-start | bytes 196612
  197.7 49.0 %copy-start.84 = (bf16[256,128]{0,1:T(8,128)(2,1)}, bf16[256,128]{0,1:T(8,128)(2,1)S(1)}, u32[]{:S(2)}) copy-start(bf16[256,128]{0,1:T(8,128)(2,1)S(1)} %get-tuple-element.946) | copy-start | bytes 196612
  219.1 29.2 copy-start.142
  267.9 24.9 copy-start.93
  267.9 24.9 copy-start.98
  295.9 25.0 copy-start.91
  324.8 750.2 %copy-start.124 = (f32[256,8]{0,1:T(8,128)}, f32[256,8]{0,1:T(8,128)S(1)}, u32[]{:S(2)}) copy-start(f32[256,8]{0,1:T(8,128)S(1)} %get-tuple-element.900) | copy-start | bytes 24580
  331.3 55.5 %copy-start.64 = (bf16[1,256,8,128]{1,3,2,0:T(8,128)(2,1)}, bf16[1,256,8,128]{1,3,2,0:T(8,128)(2,1)S(1)}, u32[]{:S(2)}) copy-start(bf16[1,256,8,128]{1,3,2,0:T(8,128)(2,1)S(1)} %get-tuple-element.943) | copy-start | bytes 1572868
  335.3 56.4 %copy-start.57 = (bf16[1,256,8,128]{1,3,2,0:T(8,128)(2,1)}, bf16[1,256,8,128]{1,3,2,0:T(8,128)(2,1)S(1)}, u32[]{:S(2)}) copy-start(bf16[1,256,8,128]{1,3,2,0:T(8,128)(2,1)S(1)} %get-tuple-element.949) | copy-start | bytes 1572868
  394.4 210.2 %all-gather.24.cloned.1.call-start = ((), (), s32[]{:S(2)}) async-start(), calls=%async_computation.9 | async-start | bytes 11976704 | tf_op jit(solution)/shard_map/all_gather | solution.py:143
  395.0 390.1 %all-gather.26.cloned.1.call-start = ((), (), s32[]{:S(2)}) async-start(), calls=%async_computation.10 | async-start | bytes 11976704 | tf_op jit(solution)/shard_map/all_gather | solution.py:144
  395.7 569.8 %all-gather.28.cloned.1.call-start = ((), (), s32[]{:S(2)}) async-start(), calls=%async_computation.11 | async-start | bytes 11976704 | tf_op jit(solution)/shard_map/all_gather | solution.py:146
  396.5 642.7 %all-reduce.17.cloned.1.call-start = ((), (), s32[]{:S(2)}) async-start(), calls=%async_computation.24 | async-start | bytes 8388608 | tf_op jit(solution)/shard_map/psum | solution.py:207
  439.9 345.2 %copy-start.22 = (bf16[256,2048]{1,0:T(8,128)(2,1)}, bf16[256,2048]{1,0:T(8,128)(2,1)S(1)}, u32[]{:S(2)}) copy-start(bf16[256,2048]{1,0:T(8,128)(2,1)S(1)} %get-tuple-element.936) | copy-start | bytes 3145732
  439.9 359.2 %copy-start.25 = (bf16[256,2048]{1,0:T(8,128)(2,1)}, bf16[256,2048]{1,0:T(8,128)(2,1)S(1)}, u32[]{:S(2)}) copy-start(bf16[256,2048]{1,0:T(8,128)(2,1)S(1)} %get-tuple-element.935) | copy-start | bytes 3145732
  785.1 14.0 slice-start.9
  785.1 14.0 slice-start.10
  965.5 21.7 slice-start.3
  965.6 21.7 slice-start.4
  977.3 21.4 copy-start.17
  978.4 17.0 slice-start
  978.4 17.0 slice-start.1
  995.4 12.2 slice-start.12
  1012.2 51.6 %all-reduce.21.cloned.1.call-start = ((), (), s32[]{:S(2)}) async-start(), calls=%async_computation.26 | async-start | bytes 4194304 | tf_op jit(solution)/shard_map/psum | solution.py:193
  1027.0 139.7 %all-gather.36.cloned.1.call-start = ((), (), s32[]{:S(2)}) async-start(), calls=%async_computation.22 | async-start | bytes 5591040 | tf_op jit(solution)/shard_map/all_gather | solution.py:20
  1078.7 173.5 %all-gather.34.cloned.1.call-start = ((), (), s32[]{:S(2)}) async-start(), calls=%async_computation.21 | async-start | bytes 5591040 | tf_op jit(solution)/shard_map/all_gather | solution.py:20
  1112.7 286.0 %all-reduce.15.cloned.1.call-start = ((), (), s32[]{:S(2)}) async-start(), calls=%async_computation.23 | async-start | bytes 8388608 | tf_op jit(solution)/shard_map/psum | solution.py:240
  1112.7 32.6 %copy-start.77 = (bf16[32,8,8,128]{3,2,1,0:T(8,128)(2,1)S(1)}, bf16[32,8,8,128]{3,2,1,0:T(8,128)(2,1)}, u32[]{:S(2)}) copy-start(bf16[32,8,8,128]{3,2,1,0:T(8,128)(2,1)} %copy-done.75) | copy-start | bytes 1572868
  1112.7 32.5 %copy-start.103 = (pred[256,256]{0,1:T(8,128)(4,1)S(1)}, pred[256,256]{0,1:T(8,128)(4,1)}, u32[]{:S(2)}) copy-start(pred[256,256]{0,1:T(8,128)(4,1)} %copy-done.101) | copy-start | bytes 196612
  1112.7 32.5 %copy-start.146 = (f32[8,256,256]{1,2,0:T(8,128)S(1)}, f32[8,256,256]{1,2,0:T(8,128)}, u32[]{:S(2)}) copy-start(f32[8,256,256]{1,2,0:T(8,128)} %copy-done.145) | copy-start | bytes 6291460
  1166.7 18.4 copy-start.119
  1190.8 61.4 %copy-start.139 = (f32[4]{0:T(128)S(1)}, f32[4]{0:T(128)}, u32[]{:S(2)}) copy-start(f32[4]{0:T(128)} %get-tuple-element.884) | copy-start | bytes 52
  1252.2 18.1 copy-start.67
  1252.2 18.1 copy-start.117
  1290.4 194.4 %reduce-scatter.8.cloned.1.call-start = ((), (), s32[]{:S(2)}) async-start(), calls=%async_computation.12 | async-start | bytes 1114112 | tf_op jit(solution)/shard_map/reduce_scatter | solution.py:261
  1294.2 190.6 %reduce-scatter.10.cloned.1.call-start = ((), (), s32[]{:S(2)}) async-start(), calls=%async_computation.13 | async-start | bytes 1114112 | tf_op jit(solution)/shard_map/reduce_scatter | solution.py:262
  1296.4 363.8 %reduce-scatter.14.cloned.1.call-start = ((), (), s32[]{:S(2)}) async-start(), calls=%async_computation.15 | async-start | bytes 8912896 | tf_op jit(solution)/shard_map/reduce_scatter | solution.py:266
  1305.2 537.6 %reduce-scatter.12.cloned.1.call-start = ((), (), s32[]{:S(2)}) async-start(), calls=%async_computation.14 | async-start | bytes 8912896 | tf_op jit(solution)/shard_map/reduce_scatter | solution.py:263
  1311.8 13.1 copy-start.16
  1311.8 996.5 %reduce-scatter.16.cloned.1.call-start = ((), (), s32[]{:S(2)}) async-start(), calls=%async_computation.16 | async-start | bytes 23953408 | tf_op jit(solution)/shard_map/reduce_scatter | solution.py:264
  1312.3 12.6 copy-start.23
  1339.6 12.5 copy-start.18
  1339.6 1436.7 %reduce-scatter.18.cloned.1.call-start = ((), (), s32[]{:S(2)}) async-start(), calls=%async_computation.17 | async-start | bytes 23953408 | tf_op jit(solution)/shard_map/reduce_scatter | solution.py:265
  1339.6 12.4 copy-start.24
  1366.7 12.6 copy-start.14
  1366.7 1877.5 %reduce-scatter.20.cloned.1.call-start = ((), (), s32[]{:S(2)}) async-start(), calls=%async_computation.18 | async-start | bytes 23953408 | tf_op jit(solution)/shard_map/reduce_scatter | solution.py:267
  1366.9 12.4 copy-start.27
  (120 other events, 443.2 us)
Sparse Core Ops, SparseCore 0:
  10.8 84.3 all-gather.19
  117.2 89.9 all-gather.31
  209.4 85.4 all-gather.29
  297.5 89.2 all-gather.21
  394.5 26.7 all-reduce.18
  424.2 180.3 all-gather.23
  607.7 177.3 all-gather.25
  788.1 177.3 all-gather.27
  1012.4 26.7 all-reduce.16
  1041.4 22.4 all-reduce.20
  1078.8 87.8 all-gather.35
  1168.2 83.9 all-gather.33
  1290.5 27.0 all-reduce.14
  1320.3 79.8 reduce-scatter.7
  1403.0 75.7 reduce-scatter.9
  1481.5 178.7 reduce-scatter.13
  1662.9 179.8 reduce-scatter.11
  1845.5 462.6 reduce-scatter.15
  2311.2 465.0 reduce-scatter.17
  2779.0 465.0 reduce-scatter.19
where the time goes:
time: 3260 us; the launch traced here: 3250 us
  waiting for transfers between devices  2400 us (74%)
  blocking collectives  355 us (11%)
  matrix products  294 us (9%)
  other arithmetic  117 us (4%)
  local copies, waits for them, and re-layouts  60.8 us (2%)
    reduce_scatter x1, waiting for transfers between devices, local(): lax.psum_scatter(totals[4], ('dp', 'seq'), scatter_dimension=0, tiled=True)  468 us
    reduce_scatter x1, waiting for transfers between devices, local(): lax.psum_scatter(totals[6], ('dp', 'seq'), scatter_dimension=1, tiled=True)  468 us
    reduce_scatter x1, waiting for transfers between devices, local(): lax.psum_scatter(totals[3], ('dp', 'seq'), scatter_dimension=0, tiled=True)  465 us
    reduce_scatter x1, waiting for transfers between devices, local(): lax.psum_scatter(totals[2], ('dp', 'seq'), scatter_dimension=0, tiled=True)  183 us
    reduce_scatter x1, waiting for transfers between devices, local(): lax.psum_scatter(totals[5], ('dp', 'seq'), scatter_dimension=1, tiled=True)  175 us
    all_gather x1, waiting for transfers between devices, local(): lax.all_gather(up_weight, ('dp', 'seq'), axis=0, tiled=True)  172 us
    all_gather x1, waiting for transfers between devices, local(): lax.all_gather(gate_weight, ('dp', 'seq'), axis=0, tiled=True)  165 us
    all_gather x1, waiting for transfers between devices, local(): lax.all_gather(down_weight, ('dp', 'seq'), axis=1, tiled=True)  161 us
  transfers between devices with their start and end apart: 20, of which 13 were waited for; matrix products, arithmetic and copies ran while one was open for 11% of the time, Pallas kernels for 0%

commit v1 on v0

--- a/solution.py
+++ b/solution.py
@@ -283,9 +283,264 @@
     )
 
 
+def nt_dot(a, b):
+    return lax.dot_general(a, b, (((1,), (1,)), ((), ())), preferred_element_type=jnp.float32)
+
+
+def tn_dot(a, b):
+    return lax.dot_general(a, b, (((0,), (0,)), ((), ())), preferred_element_type=jnp.float32)
+
+
+def nn_dot(a, b):
+    return lax.dot_general(a, b, (((1,), (0,)), ((), ())), preferred_element_type=jnp.float32)
+
+
+def gather_rows(own):
+    return lax.all_gather(own, ("dp", "tensor"), axis=0, tiled=True)
+
+
+def scatter_rows(partial_sum):
+    return lax.psum_scatter(
+        partial_sum.astype(jnp.bfloat16), ("dp", "tensor"), scatter_dimension=0, tiled=True
+    ).astype(jnp.float32)
+
+
+def swap_rows(x):
+    return lax.all_to_all(x, "seq", split_axis=0, concat_axis=0, tiled=True)
+
+
+def to_whole_rows(x, rows, length):
+    span = lax.axis_size("seq")
+    width = x.shape[-1]
+    x = swap_rows(x.reshape(span * rows, length, width))
+    return x.reshape(span, rows, length, width).transpose(1, 0, 2, 3).reshape(
+        rows, span * length, width
+    )
+
+
+def from_whole_rows(x, rows, length):
+    span = lax.axis_size("seq")
+    width = x.shape[-1]
+    x = x.reshape(rows, span, length, width).transpose(1, 0, 2, 3)
+    x = swap_rows(x.reshape(span * rows, length, width))
+    return x.reshape(span * rows * length, width)
+
+
+def attention_forward(queries, keys, values, segments):
+    length = queries.shape[1]
+    scores = jnp.einsum("rthf,rshf->rhts", queries, keys, preferred_element_type=jnp.float32) / 4.0
+    position = jnp.arange(length)
+    allowed = (position[None, :] <= position[:, None])[None] & (
+        segments[:, :, None] == segments[:, None, :]
+    )
+    weight = jnp.where(allowed[:, None], 1.0 + scores + 0.5 * scores * scores, 0.0)
+    den = jnp.sum(weight, axis=-1)
+    num = jnp.einsum(
+        "rhts,rshe->rhte", weight.astype(jnp.bfloat16), values, preferred_element_type=jnp.float32
+    )
+    return num / den[..., None], den, weight, scores, allowed
+
+
+def attention_backward(queries, keys, values, mixed, den, weight, scores, allowed, dmixed):
+    dn = jnp.transpose(dmixed, (0, 2, 1, 3)).astype(jnp.float32) / den[..., None]
+    dd = -jnp.sum(dn * mixed, axis=-1)
+    dn_low = dn.astype(jnp.bfloat16)
+    dw = jnp.einsum("rhte,rshe->rhts", dn_low, values, preferred_element_type=jnp.float32)
+    dw = jnp.where(allowed[:, None], dw + dd[..., None], 0.0)
+    dvalues = jnp.einsum(
+        "rhts,rhte->rshe", weight.astype(jnp.bfloat16), dn_low, preferred_element_type=jnp.float32
+    )
+    da = (dw * (1.0 + scores) * 0.25).astype(jnp.bfloat16)
+    dqueries = jnp.einsum("rhts,rshf->rthf", da, keys, preferred_element_type=jnp.float32)
+    dkeys = jnp.einsum("rhts,rthf->rshf", da, queries, preferred_element_type=jnp.float32)
+    return dqueries, dkeys, dvalues
+
+
+def plane_local(
+    tokens,
+    doc_starts,
+    attn_gain,
+    mlp_gain,
+    query_weight,
+    key_weight,
+    value_weight,
+    output_weight,
+    gate_weight,
+    up_weight,
+    down_weight,
+    cotangent,
+):
+    plane, span, cores = (lax.axis_size("dp"), lax.axis_size("seq"), lax.axis_size("tensor"))
+    rows, length, width = tokens.shape
+    chunk = width // (plane * span)
+    own = rows * length // cores
+    heads = query_weight.shape[1] // FDIM // plane
+    hidden_part = gate_weight.shape[1] // plane
+    vcols, qcols = heads * VHEAD, heads * FDIM
+    all_rows = rows * plane // span
+
+    def seq_major(a):
+        return (
+            a.reshape(a.shape[:-1] + (plane, span, chunk)).swapaxes(-3, -2).reshape(a.shape)
+        )
+
+    def plane_major(a):
+        return (
+            a.reshape(a.shape[:-1] + (span, plane, chunk)).swapaxes(-3, -2).reshape(a.shape)
+        )
+
+    core = lax.axis_index("tensor")
+    small = jnp.concatenate(
+        [
+            attn_gain.astype(jnp.float32)[None],
+            mlp_gain.astype(jnp.float32)[None],
+            doc_starts.astype(jnp.float32).reshape(-1, chunk),
+        ]
+    )
+    small = lax.all_gather(small, ("seq", "dp"), axis=0, tiled=False)
+    gain_one = small[:, 0].reshape(width)
+    gain_two = small[:, 1].reshape(width)
+    starts = small[:, 2:].reshape(span, plane * rows, length)
+    starts = lax.dynamic_slice_in_dim(starts, lax.axis_index("seq") * all_rows, all_rows, 1)
+    segments = jnp.cumsum(starts.transpose(1, 0, 2).reshape(all_rows, span * length), axis=1)
+
+    def spread(pack):
+        pack = lax.all_to_all(pack, "dp", split_axis=0, concat_axis=0, tiled=True)
+        pack = lax.all_gather(pack, "seq", axis=0, tiled=False)
+        return pack.transpose(2, 0, 1, 3).reshape(pack.shape[2], width)
+
+    def collect(grads):
+        part = lax.psum_scatter(
+            grads.astype(jnp.bfloat16), "seq", scatter_dimension=1, tiled=True
+        )
+        part = part.reshape(part.shape[0], plane, chunk).transpose(1, 0, 2)
+        return lax.all_to_all(part, "dp", split_axis=0, concat_axis=0, tiled=True).astype(
+            jnp.float32
+        )
+
+    def split(w):
+        return w.reshape(plane, -1, chunk)
+
+    attn_pack = spread(
+        jnp.concatenate(
+            [split(value_weight.T), split(query_weight.T), split(key_weight.T), split(output_weight)],
+            axis=1,
+        )
+    )
+    ffn_pack = spread(
+        jnp.concatenate([split(gate_weight.T), split(up_weight.T), split(down_weight)], axis=1)
+    )
+    qkv_rows = vcols + 2 * qcols
+    w_qkv, w_out = attn_pack[:qkv_rows], attn_pack[qkv_rows:]
+    w_gate_up, w_down = ffn_pack[: 2 * hidden_part], ffn_pack[2 * hidden_part :]
+
+    def mine(a):
+        a = lax.dynamic_slice_in_dim(a.reshape(rows * length, width), core * own, own, 0)
+        return seq_major(a)
+
+    x = mine(tokens).astype(jnp.float32)
+    cot_own = mine(cotangent)
+    scale_one = inverse_rms(x)
+    normed_one = gather_rows((x * scale_one * gain_one).astype(jnp.bfloat16))
+    cot = gather_rows(cot_own)
+    qkv = nt_dot(normed_one, w_qkv).astype(jnp.bfloat16)
+    qkv = to_whole_rows(qkv, all_rows, length)
+    values = qkv[..., :vcols].reshape(all_rows, -1, heads, VHEAD)
+    queries = qkv[..., vcols : vcols + qcols].reshape(all_rows, -1, heads, FDIM)
+    keys = qkv[..., vcols + qcols :].reshape(all_rows, -1, heads, FDIM)
+    mixed, den, weight, scores, allowed = attention_forward(queries, keys, values, segments)
+    mixed_low = mixed.transpose(0, 2, 1, 3).reshape(all_rows, -1, vcols).astype(jnp.bfloat16)
+    mixed_low = from_whole_rows(mixed_low, all_rows, length)
+    residual = x + scatter_rows(nn_dot(mixed_low, w_out))
+    scale_two = inverse_rms(residual)
+    normed_two = gather_rows((residual * scale_two * gain_two).astype(jnp.bfloat16))
+    gate_up = nt_dot(normed_two, w_gate_up)
+    gate, up = gate_up[:, :hidden_part], gate_up[:, hidden_part:]
+    sig = jax.nn.sigmoid(gate)
+    hidden = (gate * sig * up).astype(jnp.bfloat16)
+    block_own = (residual + scatter_rows(nn_dot(hidden, w_down))).astype(jnp.bfloat16)
+
+    dhidden = nt_dot(cot, w_down)
+    dgate = (dhidden * up * sig * (1.0 + gate * (1.0 - sig))).astype(jnp.bfloat16)
+    dup = (dhidden * gate * sig).astype(jnp.bfloat16)
+    dgate_up = jnp.concatenate([dgate, dup], axis=1)
+    dnormed_two = scatter_rows(nn_dot(dgate_up, w_gate_up))
+    ffn_grads = collect(
+        jnp.concatenate([tn_dot(dgate_up, normed_two), tn_dot(hidden, cot)], axis=0)
+    )
+    dresid, gain_two_grad = norm_backward(residual, scale_two, gain_two, dnormed_two)
+    dresid = dresid + cot_own.astype(jnp.float32)
+    dresid_low = gather_rows(dresid.astype(jnp.bfloat16))
+    dmixed = nt_dot(dresid_low, w_out).astype(jnp.bfloat16)
+    dmixed = to_whole_rows(dmixed, all_rows, length).reshape(all_rows, -1, heads, VHEAD)
+    dqueries, dkeys, dvalues = attention_backward(
+        queries, keys, values, mixed, den, weight, scores, allowed, dmixed
+    )
+    dqkv = jnp.concatenate(
+        [
+            d.reshape(all_rows, span * length, -1).astype(jnp.bfloat16)
+            for d in (dvalues, dqueries, dkeys)
+        ],
+        axis=-1,
+    )
+    dqkv = from_whole_rows(dqkv, all_rows, length)
+    dnormed_one = scatter_rows(nn_dot(dqkv, w_qkv))
+    attn_grads = collect(
+        jnp.concatenate([tn_dot(dqkv, normed_one), tn_dot(mixed_low, dresid_low)], axis=0)
+    )
+    dtokens, gain_one_grad = norm_backward(x, scale_one, gain_one, dnormed_one)
+    dtokens = dresid + dtokens
+    gain_grads = lax.psum(jnp.stack([gain_one_grad, gain_two_grad]), "tensor")
+    gain_grads = lax.psum_scatter(
+        gain_grads, ("seq", "dp"), scatter_dimension=1, tiled=True
+    )
+
+    def whole(a):
+        a = lax.all_gather(plane_major(a), "tensor", axis=0, tiled=True)
+        return a.reshape(rows, length, width)
+
+    def stacked(a, start, size):
+        return a[:, start : start + size].reshape(plane * size, chunk)
+
+    h = hidden_part
+    return (
+        whole(block_own),
+        whole(dtokens),
+        gain_grads[0],
+        gain_grads[1],
+        stacked(attn_grads, vcols, qcols).T,
+        stacked(attn_grads, vcols + qcols, qcols).T,
+        stacked(attn_grads, 0, vcols).T,
+        stacked(attn_grads, qkv_rows, vcols),
+        stacked(ffn_grads, 0, h).T,
+        stacked(ffn_grads, h, h).T,
+        stacked(ffn_grads, 2 * h, h),
+    )
+
+
+def fits_plane(mesh, tokens, query_weight, gate_weight):
+    plane, span, cores = (mesh.shape[a] for a in ("dp", "seq", "tensor"))
+    heads = query_weight.shape[1] // FDIM // cores
+    return (
+        plane == 4
+        and cores == 2
+        and heads % plane == 0
+        and (gate_weight.shape[1] // cores) % (16 * plane) == 0
+        and tokens.shape[0] % span == 0
+    )
+
+
 def solution(mesh):
+    def step(*args):
+        use = fits_plane(mesh, args[0], args[4], args[8])
+        return sharded(mesh, plane_local if use else local)(*args)
+
+    return step
+
+
+def sharded(mesh, body):
     return jax.shard_map(
-        local,
+        body,
         mesh=mesh,
         in_specs=(
             P("dp", "seq", None),

time: 3260 us -> 1320 us (0.40)
  waiting for transfers between devices: 2400 us -> 785 us
  blocking collectives: 355 us -> 157 us
  matrix products: 294 us -> 171 us
  other arithmetic: 117 us -> 33.5 us
  local copies, waits for them, and re-layouts: 60.8 us -> 132 us
    reduce_scatter x7 -> x6, waiting for transfers between devices: 1760 us -> 362 us  [the longest x4 184 us: scatter_rows(): lax.psum_scatter(partial_sum.astype(jnp.bfloat16), ('dp', 'tensor'), scat...]
    all_gather x9 -> x8, waiting for transfers between devices: 608 us -> 305 us  [the longest x4 146 us: gather_rows(): return lax.all_gather(own, ('dp', 'tensor'), axis=0, tiled=True)]
    all_gather x8 -> x1, blocking collectives: 270 us -> 40.6 us  [plane_local(): small = lax.all_gather(small, ('seq', 'dp'), axis=0, tiled=False)]
    dot_general x70 -> x18, matrix products: 294 us -> 171 us  [the longest x4 48.3 us: nt_dot(): lax.dot_general(a, b, (((1,), (1,)), ((), ())), preferred_element_type=jn...]
    all_to_all x0 -> x4, blocking collectives: none -> 114 us  [the longest x2 64.4 us: swap_rows(): return lax.all_to_all(x, 'seq', split_axis=0, concat_axis=0, tiled=True)]
    unnamed x2 -> x0, blocking collectives: 84.6 us -> none
    all_to_all x0 -> x4, waiting for transfers between devices: none -> 57.9 us  [the longest x2 50.1 us: swap_rows(): return lax.all_to_all(x, 'seq', split_axis=0, concat_axis=0, tiled=True)]
    unnamed x20 -> x16, waiting for transfers between devices: 3.38 us -> 59.6 us
  transfers between devices with their start and end apart: 20 -> 19, of which waited for: 13 -> 18; matrix products, arithmetic and copies ran while one was open for 11% -> 15% of each run, Pallas kernels for 0% -> 0%
where the time goes in v1:
time: 1320 us; the launch traced here: 1310 us
  waiting for transfers between devices  785 us (59%)
  matrix products  171 us (13%)
  blocking collectives  157 us (12%)
  local copies, waits for them, and re-layouts  132 us (10%)
  other arithmetic  33.5 us (3%)
  starting transfers between devices  18.2 us (1%)
  between operations  14.8 us (1%)
    reduce_scatter x4, waiting for transfers between devices, scatter_rows(): lax.psum_scatter(partial_sum.astype(jnp.bfloat16), ('dp', 'tensor'), scat...  184 us
    reduce_scatter x2, waiting for transfers between devices, collect(): lax.psum_scatter(grads.astype(jnp.bfloat16), 'seq', scatter_dimension=1,...  178 us
    all_gather x4, waiting for transfers between devices, gather_rows(): return lax.all_gather(own, ('dp', 'tensor'), axis=0, tiled=True)  146 us
    all_gather x2, waiting for transfers between devices, spread(): pack = lax.all_gather(pack, 'seq', axis=0, tiled=False)  142 us
    all_to_all x2, blocking collectives, swap_rows(): return lax.all_to_all(x, 'seq', split_axis=0, concat_axis=0, tiled=True)  64.4 us
    unnamed x16, waiting for transfers between devices  59.6 us
    all_to_all x2, waiting for transfers between devices, swap_rows(): return lax.all_to_all(x, 'seq', split_axis=0, concat_axis=0, tiled=True)  50.1 us
    all_to_all x2, blocking collectives, spread(): pack = lax.all_to_all(pack, 'dp', split_axis=0, concat_axis=0, tiled=True)  49.6 us
  transfers between devices with their start and end apart: 19, of which 18 were waited for; matrix products, arithmetic and copies ran while one was open for 15% of the time, Pallas kernels for 0%

profile of v1, /device:TPU:0, one launch (start us, length us, event | category | flops | bytes accessed | tf_op | source)
XLA Modules:
  0.0 1311.2 jit_solution(396383917929149709)
XLA Ops:
  11.1 14.5 %all_to_all.40 = bf16[4,576,128]{2,1,0:T(8,128)(2,1)} all-to-all(bf16[4,576,128]{2,1,0:T(8,128)(2,1)S(1)} %pad_maximum_fusion.7), channel_id=1, replica_groups=mesh['dp'=4,'seq'=4,'tensor'=2] {'dp'}, dimensions={0} | all-to-all | bytes 1179648 | tf_op jit(solution)/shard_map/all_to_all | solution.py:408
  25.7 2.8 constant_dynamic-slice_fusion
  33.4 40.6 %all-gather.3 = f32[16,6,128]{2,1,0:T(8,128)S(1)} all-gather(f32[1,6,128]{2,1,0:T(8,128)S(1)} %maximum_bitcast_fusion), channel_id=2, replica_groups=mesh['dp'=4,'seq'=4,'tensor'=2] {'seq','dp'}, dimensions={0}, use_global_device_ids=true | all-gather | bytes 52224 | tf_op jit(solution)/shard_map/all_gather | solution.py:400
  76.2 4.3 copy.125
  80.5 2.9 slice.109
  83.4 48.6 %all-gather.13.cloned.1.call-done = bf16[2048,2048]{1,0:T(8,128)(2,1)} async-done(((bf16[256,2048]{1,0:T(8,128)(2,1)}), bf16[2048,2048]{1,0:T(8,128)(2,1)}) %all-gather.13.cloned.1.call-update) | async-done | bytes 8388624 | tf_op jit(solution)/shard_map/all_gather | solution.py:299
  131.9 6.7 convolution_convert_fusion.7
  139.8 5.1 all-to-all-start.1
  146.3 2.6 compare_and_fusion
  148.9 27.7 %all-to-all-done.1 = bf16[8,256,320]{1,2,0:T(8,128)(2,1)S(1)} async-done(((bf16[8,256,320]{1,2,0:T(8,128)(2,1)}), bf16[8,256,320]{1,2,0:T(8,128)(2,1)S(1)}, u32[]{:S(2)}, u32[]{:S(2)}) %all-to-all-start.1) | async-done | bytes 1310752 | tf_op jit(solution)/shard_map/all_to_all | solution.py:309
  178.7 8.9 fusion
  187.7 3.5 fusion.16
  195.2 3.5 all-to-all-start.2
  198.7 2.8 slice.115
  201.6 22.4 %all-to-all-done.2 = bf16[8,256,256]{2,1,0:T(8,128)(2,1)S(1)} async-done(((bf16[8,256,256]{2,1,0:T(8,128)(2,1)}), bf16[8,256,256]{2,1,0:T(8,128)(2,1)S(1)}, u32[]{:S(2)}, u32[]{:S(2)}) %all-to-all-start.2) | async-done | bytes 1048608 | tf_op jit(solution)/shard_map/all_to_all | solution.py:309
  224.0 7.2 convolution_convert_fusion.4
  233.7 35.1 %all_to_all.41 = bf16[4,2064,128]{2,1,0:T(8,128)(2,1)} all-to-all(bf16[4,2064,128]{2,1,0:T(8,128)(2,1)S(1)} %pad_maximum_fusion.5), channel_id=1, replica_groups=mesh['dp'=4,'seq'=4,'tensor'=2] {'dp'}, dimensions={0} | all-to-all | bytes 4227072 | tf_op jit(solution)/shard_map/all_to_all | solution.py:408
  268.9 33.9 %reduce-scatter.10.cloned.1.call-done = bf16[256,2048]{1,0:T(8,128)(2,1)} async-done(((bf16[2048,2048]{1,0:T(8,128)(2,1)}), bf16[256,2048]{1,0:T(8,128)(2,1)}) %reduce-scatter.10.cloned.1.call-update) | async-done | bytes 1048592 | tf_op jit(solution)/shard_map/reduce_scatter | solution.py:303
  310.8 2.7 reshape.278
  313.7 141.3 %all-gather.27.cloned.1.call-done = bf16[16,2064,128]{2,1,0:T(8,128)(2,1)} async-done(((bf16[4,2064,128]{2,1,0:T(8,128)(2,1)}), bf16[16,2064,128]{2,1,0:T(8,128)(2,1)}) %all-gather.27.cloned.1.call-update) | async-done | bytes 8454160 | tf_op jit(solution)/shard_map/all_gather | solution.py:409
  455.0 26.4 %copy.182 = bf16[4,4,2064,128]{3,1,0,2:T(4,128)(2,1)S(1)} copy(bf16[4,4,2064,128]{3,2,1,0:T(8,128)(2,1)} %bitcast.199) | data formatting | bytes 16908288 | tf_op jit(solution)/shard_map/all_gather | solution.py:409
  481.5 2.8 slice.120
  484.3 4.2 slice.117
  488.6 5.7 slice.98
  494.3 10.6 copy.132
  504.9 4.7 all-gather.15.cloned.1.call-done
  509.6 18.4 %fusion.31 = f32[2048,1376]{0,1:T(8,128)} fusion(bf16[2048,2048]{1,0:T(8,128)(2,1)} %all-gather.15.cloned.1.call-done, bf16[1376,2048]{0,1:T(8,128)(2,1)} %bitcast.202), kind=kOutput, calls=%fused_computation.90 | convolution fusion | flops 11542724608 | bytes 25296896 | tf_op jit(solution)/shard_map/dot_general | solution.py:287
  528.0 38.5 %all-gather.19.cloned.1.call-done = bf16[2048,2048]{1,0:T(8,128)(2,1)} async-done(((bf16[256,2048]{1,0:T(8,128)(2,1)}), bf16[2048,2048]{1,0:T(8,128)(2,1)}) %all-gather.19.cloned.1.call-update) | async-done | bytes 8388624 | tf_op jit(solution)/shard_map/all_gather | solution.py:299
  566.5 17.2 %multiply_convert_fusion.2 = (bf16[2048,688]{0,1:T(8,128)(2,1)}, bf16[2048,688]{0,1:T(8,128)(2,1)}, bf16[2048,688]{0,1:T(8,128)(2,1)}) fusion(f32[2048,1376]{0,1:T(8,128)} %fusion.31, bf16[2048,2048]{1,0:T(8,128)(2,1)} %all-gather.19.cloned.1.call-done, bf16[688,2048]{1,0:T(8,128)(2,1)} %slice.98), kind=kOutput, calls=%fused_computation.14 | convolution fusion | flops 5793906688 | bytes 30932992 | tf_op jit(solution)/shard_map/dot_general | solution.py:287
  583.7 17.4 %convolution_convert_fusion.3 = bf16[2048,2048]{1,0:T(8,128)(2,1)} fusion(bf16[1376,2048]{0,1:T(8,128)(2,1)S(1)} %bitcast.203, bf16[2048,688]{0,1:T(8,128)(2,1)} %get-tuple-element.51, bf16[2048,688]{0,1:T(8,128)(2,1)} %get-tuple-element.50), kind=kOutput, calls=%fused_computation.10 | convolution fusion | flops 11558191104 | bytes 19660800 | tf_op jit(solution)/shard_map/dot_general | solution.py:295
  601.2 71.4 %reduce-scatter.14.cloned.1.call-done = bf16[256,2048]{1,0:T(8,128)(2,1)} async-done(((bf16[2048,2048]{1,0:T(8,128)(2,1)}), bf16[256,2048]{1,0:T(8,128)(2,1)}) %reduce-scatter.14.cloned.1.call-update) | async-done | bytes 1048592 | tf_op jit(solution)/shard_map/reduce_scatter | solution.py:303
  677.3 54.0 %all-gather.21.cloned.1.call-done = bf16[2048,2048]{1,0:T(8,128)(2,1)} async-done(((bf16[256,2048]{1,0:T(8,128)(2,1)}), bf16[2048,2048]{1,0:T(8,128)(2,1)}) %all-gather.21.cloned.1.call-update) | async-done | bytes 8388624 | tf_op jit(solution)/shard_map/all_gather | solution.py:299
  731.3 6.0 convolution_convert_fusion.9
  737.2 30.6 %all_to_all.42 = bf16[8,256,256]{2,1,0:T(8,128)(2,1)S(1)} all-to-all(bf16[8,256,256]{2,1,0:T(8,128)(2,1)S(1)} %bitcast.230), channel_id=1, replica_groups=mesh['dp'=4,'seq'=4,'tensor'=2] {'seq'}, dimensions={0} | all-to-all | bytes 2097152 | tf_op jit(solution)/shard_map/all_to_all | solution.py:309
  769.4 2.9 copy.136
  772.3 3.3 reshape.297
  775.6 8.0 fusion.17
  785.2 11.4 multiply_convert_fusion
  796.6 5.8 fusion.19
  803.9 2.6 convert_element_type.179
  808.0 33.8 %all_to_all.43 = bf16[8,256,320]{1,2,0:T(8,128)(2,1)S(1)} all-to-all(bf16[8,256,320]{1,2,0:T(8,128)(2,1)S(1)} %bitcast.208), channel_id=1, replica_groups=mesh['dp'=4,'seq'=4,'tensor'=2] {'seq'}, dimensions={0} | all-to-all | bytes 2621440 | tf_op jit(solution)/shard_map/all_to_all | solution.py:309
  843.0 6.9 convolution_convert_fusion.2
  850.0 11.6 convolution_convert_fusion
  861.6 11.2 convolution_convert_fusion.5
  872.8 16.3 %convolution_convert_fusion.1 = bf16[1376,2048]{1,0:T(8,128)(2,1)} fusion(bf16[2048,2048]{1,0:T(8,128)(2,1)} %all-gather.15.cloned.1.call-done, bf16[2048,688]{0,1:T(8,128)(2,1)S(1)} %copy-done.34, bf16[2048,688]{0,1:T(8,128)(2,1)S(1)} %copy-done.33), kind=kOutput, calls=%fused_computation.8 | convolution fusion | flops 11556814848 | bytes 19660800 | tf_op jit(solution)/shard_map/dot_general | solution.py:291
  889.2 8.5 pad_maximum_fusion
  897.8 6.2 convolution_convert_fusion.8
  904.1 6.7 convolution_convert_fusion.6
  912.7 6.8 reduce-scatter.16.cloned.1.call-done
  922.8 71.6 %reduce-scatter.12.cloned.1.call-done = bf16[256,2048]{1,0:T(8,128)(2,1)} async-done(((bf16[2048,2048]{1,0:T(8,128)(2,1)}), bf16[256,2048]{1,0:T(8,128)(2,1)}) %reduce-scatter.12.cloned.1.call-update) | async-done | bytes 1048592 | tf_op jit(solution)/shard_map/reduce_scatter | solution.py:303
  994.5 4.5 fusion.7
  1005.0 2.9 copy.147
  1007.9 134.4 %reduce-scatter.20.cloned.1.call-done = bf16[2064,512]{1,0:T(8,128)(2,1)} async-done(((bf16[2064,2048]{1,0:T(8,128)(2,1)}), bf16[2064,512]{1,0:T(8,128)(2,1)}) %reduce-scatter.20.cloned.1.call-update) | async-done | bytes 2113552 | tf_op jit(solution)/shard_map/reduce_scatter | solution.py:413
  1142.4 3.3 bitcast_bitcast_fusion
  1145.7 4.5 all-to-all-start.7
  1150.1 43.8 %reduce-scatter.18.cloned.1.call-done = bf16[576,512]{1,0:T(8,128)(2,1)} async-done(((bf16[576,2048]{1,0:T(8,128)(2,1)}), bf16[576,512]{1,0:T(8,128)(2,1)}) %reduce-scatter.18.cloned.1.call-update) | async-done | bytes 589840 | tf_op jit(solution)/shard_map/reduce_scatter | solution.py:413
  1195.9 3.6 all-to-all-start.6
  1199.6 3.6 fusion.26
  1203.2 7.8 all-to-all-done.6
  1214.4 59.4 %reduce-scatter.22.cloned.1.call-done = f32[128,2]{1,0:T(8,128)} async-done(((f32[2048,2]{1,0:T(8,128)}), f32[128,2]{1,0:T(8,128)}) %reduce-scatter.22.cloned.1.call-update) | async-done | bytes 1040
  1277.6 5.1 all-gather.17.cloned.1.call-done
  1282.7 3.9 copy.164
  1286.6 12.5 all-gather.23.cloned.1.call-done
  1299.1 5.3 copy.166
  (172 shorter events, 62.9 us)
Async XLA Ops:
  7.2 18.5 %copy-start.29 = (s32[2,256]{1,0:T(2,128)S(1)}, s32[2,256]{1,0:T(2,128)}, u32[]{:S(2)}) copy-start(s32[2,256]{1,0:T(2,128)} %param.13) | copy-start | bytes 6148
  7.2 69.0 %all-gather.25.cloned.1.call-start = ((), (), s32[]{:S(2)}) async-start(), calls=%async_computation.27 | async-start | bytes 2949120 | tf_op jit(solution)/shard_map/all_gather | solution.py:409
  25.6 106.3 %all-gather.13.cloned.1.call-start = ((), (), s32[]{:S(2)}) async-start(), calls=%async_computation.15 | async-start | bytes 9437184 | tf_op jit(solution)/shard_map/all_gather | solution.py:299
  31.1 2.2 copy-start.30
  31.1 2.2 copy-start.31
  74.3 6.2 copy-start.25
  74.3 6.2 copy-start.21
  139.8 36.8 %all-to-all-start.1 = ((bf16[8,256,320]{1,2,0:T(8,128)(2,1)}), bf16[8,256,320]{1,2,0:T(8,128)(2,1)S(1)}, u32[]{:S(2)}, u32[]{:S(2)}) async-start(bf16[8,256,320]{1,2,0:T(8,128)(2,1)} %bitcast.205), calls=%async_computation.1 | async-start | bytes 2621440 | tf_op jit(solution)/shard_map/all_to_all | solution.py:309
  176.6 2.1 copy-start.8
  176.8 10.8 copy-start.17
  176.8 10.8 copy-start.19
  176.9 10.7 copy-start.14
  187.6 4.2 copy-start.32
  195.2 28.8 %all-to-all-start.2 = ((bf16[8,256,256]{2,1,0:T(8,128)(2,1)}), bf16[8,256,256]{2,1,0:T(8,128)(2,1)S(1)}, u32[]{:S(2)}, u32[]{:S(2)}) async-start(bf16[8,256,256]{2,1,0:T(8,128)(2,1)} %bitcast.214), calls=%async_computation.2 | async-start | bytes 2097152 | tf_op jit(solution)/shard_map/all_to_all | solution.py:309
  198.7 104.1 %reduce-scatter.10.cloned.1.call-start = ((), (), s32[]{:S(2)}) async-start(), calls=%async_computation.16 | async-start | bytes 9437184 | tf_op jit(solution)/shard_map/reduce_scatter | solution.py:303
  224.0 7.2 copy-start.3
  231.2 1.1 copy-start.15
  231.2 1.3 copy-start.16
  231.2 223.9 %all-gather.27.cloned.1.call-start = ((), (), s32[]{:S(2)}) async-start(), calls=%async_computation.28 | async-start | bytes 10567680 | tf_op jit(solution)/shard_map/all_gather | solution.py:409
  268.8 240.7 %all-gather.15.cloned.1.call-start = ((), (), s32[]{:S(2)}) async-start(), calls=%async_computation.17 | async-start | bytes 9437184 | tf_op jit(solution)/shard_map/all_gather | solution.py:299
  302.8 1.7 copy-start.1
  304.5 370.2 %copy-start.23 = (f32[256]{0:T(256)}, f32[256]{0:T(256)S(1)}, u32[]{:S(2)}) copy-start(f32[256]{0:T(256)S(1)} %add_rsqrt_fusion) | copy-start | bytes 3076
  305.8 260.6 %all-gather.19.cloned.1.call-start = ((), (), s32[]{:S(2)}) async-start(), calls=%async_computation.20 | async-start | bytes 9437184 | tf_op jit(solution)/shard_map/all_gather | solution.py:299
  313.5 359.1 %reduce-scatter.14.cloned.1.call-start = ((), (), s32[]{:S(2)}) async-start(), calls=%async_computation.21 | async-start | bytes 9437184 | tf_op jit(solution)/shard_map/reduce_scatter | solution.py:303
  566.5 17.2 %copy-start.7 = (bf16[1376,4,4,128]{0,3,2,1:T(8,128)(2,1)S(1)}, bf16[1376,4,4,128]{0,3,2,1:T(8,128)(2,1)}, u32[]{:S(2)}) copy-start(bf16[1376,4,4,128]{0,3,2,1:T(8,128)(2,1)} %copy.132) | copy-start | bytes 16908292
  601.1 130.1 %all-gather.21.cloned.1.call-start = ((), (), s32[]{:S(2)}) async-start(), calls=%async_computation.22 | async-start | bytes 9437184 | tf_op jit(solution)/shard_map/all_gather | solution.py:299
  672.6 2.0 copy-start.2
  672.6 2.1 copy-start.4
  674.7 2.1 copy-start.27
  676.8 242.7 %reduce-scatter.16.cloned.1.call-start = ((), (), s32[]{:S(2)}) async-start(), calls=%async_computation.23 | async-start | bytes 9437184 | tf_op jit(solution)/shard_map/reduce_scatter | solution.py:303
  775.6 8.0 copy-start.6
  775.6 8.0 copy-start.10
  783.6 1.6 copy-start.9
  785.2 11.4 copy-start.20
  796.6 5.8 copy-start
  796.6 5.8 copy-start.18
  808.0 35.0 %copy-start.11 = (bf16[320,4,4,128]{0,3,2,1:T(8,128)(2,1)S(1)}, bf16[320,4,4,128]{0,3,2,1:T(8,128)(2,1)}, u32[]{:S(2)}) copy-start(bf16[320,4,4,128]{0,3,2,1:T(8,128)(2,1)} %slice.109) | copy-start | bytes 3932164
  841.9 1.1 copy-start.12
  849.9 144.6 %reduce-scatter.12.cloned.1.call-start = ((), (), s32[]{:S(2)}) async-start(), calls=%async_computation.18 | async-start | bytes 9437184 | tf_op jit(solution)/shard_map/reduce_scatter | solution.py:303
  861.5 280.8 %reduce-scatter.20.cloned.1.call-start = ((), (), s32[]{:S(2)}) async-start(), calls=%async_computation.26 | async-start | bytes 10567680 | tf_op jit(solution)/shard_map/reduce_scatter | solution.py:413
  861.6 11.2 copy-start.33
  861.6 11.2 copy-start.34
  897.7 296.2 %reduce-scatter.18.cloned.1.call-start = ((), (), s32[]{:S(2)}) async-start(), calls=%async_computation.25 | async-start | bytes 2949120 | tf_op jit(solution)/shard_map/reduce_scatter | solution.py:413
  897.8 6.3 copy-start.13
  910.8 8.7 copy-start.22
  910.8 8.7 copy-start.26
  912.4 82.1 %copy-start.24 = (f32[256]{0:T(256)S(1)}, f32[256]{0:T(256)}, u32[]{:S(2)}) copy-start(f32[256]{0:T(256)} %copy-done.23) | copy-start | bytes 3076
  912.4 82.1 %copy-start.28 = (f32[256]{0:T(256)S(1)}, f32[256]{0:T(256)}, u32[]{:S(2)}) copy-start(f32[256]{0:T(256)} %copy-done.27) | copy-start | bytes 3076
  912.4 361.3 %reduce-scatter.22.cloned.1.call-start = ((), (), s32[]{:S(2)}) async-start(), calls=%async_computation.29 | async-start | bytes 1114112
  922.8 359.9 %all-gather.17.cloned.1.call-start = ((), (), s32[]{:S(2)}) async-start(), calls=%async_computation.19 | async-start | bytes 3145728 | tf_op jit(solution)/shard_map/all_gather | solution.py:499
  999.0 3.6 copy-start.5
  1002.5 296.5 %all-gather.23.cloned.1.call-start = ((), (), s32[]{:S(2)}) async-start(), calls=%async_computation.24 | async-start | bytes 6291456 | tf_op jit(solution)/shard_map/all_gather | solution.py:499
  1145.7 50.3 %all-to-all-start.7 = ((bf16[4,2064,128]{2,1,0:T(8,128)(2,1)}), bf16[4,2064,128]{2,1,0:T(8,128)(2,1)}, u32[]{:S(2)}, u32[]{:S(2)}) async-start(bf16[4,2064,128]{2,1,0:T(8,128)(2,1)} %bitcast_bitcast_fusion), calls=%async_computation.13 | async-start | bytes 4227072 | tf_op jit(solution)/shard_map/all_to_all | solution.py:417
  1195.9 15.1 %all-to-all-start.6 = ((bf16[4,576,128]{2,1,0:T(8,128)(2,1)}), bf16[4,576,128]{2,1,0:T(8,128)(2,1)S(1)}, u32[]{:S(2)}, u32[]{:S(2)}) async-start(bf16[4,576,128]{2,1,0:T(8,128)(2,1)} %bitcast_bitcast_fusion.1), calls=%async_computation.11 | async-start | bytes 1179648 | tf_op jit(solution)/shard_map/all_to_all | solution.py:417
Sparse Core Ops, SparseCore 0:
  25.7 50.4 all-gather.24
  78.6 53.2 all-gather.12
  231.3 71.4 reduce-scatter.9
  304.3 150.6 all-gather.26
  456.9 52.6 all-gather.14
  512.1 54.3 all-gather.18
  601.3 71.3 reduce-scatter.13
  676.9 54.3 all-gather.20
  850.0 69.3 reduce-scatter.15
  923.2 71.2 reduce-scatter.11
  996.8 145.4 reduce-scatter.19
  1145.1 48.8 reduce-scatter.17
  1196.2 77.4 reduce-scatter.21
  1275.2 7.4 all-gather.16
  1284.2 14.8 all-gather.22

commit v2 on v1

--- a/solution.py
+++ b/solution.py
@@ -3,6 +3,8 @@
 import jax
 import jax.numpy as jnp
 from jax import lax
+from jax.experimental import pallas as pl
+from jax.experimental.pallas import tpu as pltpu
 from jax.sharding import PartitionSpec as P
 
 FDIM = 16
@@ -283,6 +285,10 @@
     )
 
 
+MESH_ID = pl.DeviceIdType.MESH
+VMEM_LIMIT = 52 << 20
+
+
 def nt_dot(a, b):
     return lax.dot_general(a, b, (((1,), (1,)), ((), ())), preferred_element_type=jnp.float32)
 
@@ -295,34 +301,373 @@
     return lax.dot_general(a, b, (((1,), (0,)), ((), ())), preferred_element_type=jnp.float32)
 
 
-def gather_rows(own):
-    return lax.all_gather(own, ("dp", "tensor"), axis=0, tiled=True)
-
-
-def scatter_rows(partial_sum):
-    return lax.psum_scatter(
-        partial_sum.astype(jnp.bfloat16), ("dp", "tensor"), scatter_dimension=0, tiled=True
-    ).astype(jnp.float32)
-
-
-def swap_rows(x):
-    return lax.all_to_all(x, "seq", split_axis=0, concat_axis=0, tiled=True)
-
-
-def to_whole_rows(x, rows, length):
+def plane_places():
+    at, core = lax.axis_index("dp"), lax.axis_index("tensor")
+    x_bit, y_bit = lax.rem(at, 2), at // 2
+    return (
+        at,
+        y_bit * 2 + (1 - x_bit),
+        (1 - y_bit) * 2 + x_bit,
+        (1 - y_bit) * 2 + (1 - x_bit),
+        core,
+    )
+
+
+def greet(places):
+    barrier = pltpu.get_barrier_semaphore()
+    for place in places:
+        pl.semaphore_signal(barrier, inc=1, device_id=place, device_id_type=MESH_ID)
+    pl.semaphore_wait(barrier, len(places))
+
+
+class Sender:
+    def __init__(self, sems):
+        self.sems, self.used = sems, 0
+
+    def __call__(self, src, dst, place):
+        index = self.used
+        self.used += 1
+        return pltpu.make_async_remote_copy(
+            src_ref=src,
+            dst_ref=dst,
+            send_sem=self.sems.at[0, index],
+            recv_sem=self.sems.at[1, index],
+            device_id=place,
+            device_id_type=MESH_ID,
+        )
+
+
+def greet_plane():
+    at, x_at, y_at, _, core = plane_places()
+    greet([{"dp": x_at}, {"dp": y_at}, {"tensor": 1 - core}])
+
+
+def add_rows(dst, *srcs, step=64):
+    def body(i, carry):
+        r = pl.ds(pl.multiple_of(i * step, step), step)
+        total = srcs[0][r].astype(jnp.float32)
+        for s in srcs[1:]:
+            total = total + s[r].astype(jnp.float32)
+        dst[r] = total.astype(dst.dtype)
+        return carry
+
+    lax.fori_loop(0, srcs[0].shape[0] // step, body, 0)
+
+
+GATHER_COPIES = 13
+SCATTER_COPIES = 10
+
+
+def gather_steps(own_ref, out_ref, copy, local_sem):
+    at, x_at, y_at, d_at, core = plane_places()
+    half = own_ref.shape[0] // 2
+    xp, yp, sp = {"dp": x_at}, {"dp": y_at}, {"tensor": 1 - core}
+    lo, hi = pl.ds(0, half), pl.ds(half, half)
+    mine = out_ref.at[at, core]
+    x_lo = copy(own_ref.at[lo], mine.at[lo], xp)
+    y_hi = copy(own_ref.at[hi], mine.at[hi], yp)
+    x_hi = copy(own_ref.at[hi], mine.at[hi], xp)
+    y_lo = copy(own_ref.at[lo], mine.at[lo], yp)
+    pair = copy(own_ref, mine, sp)
+    for c in (x_lo, y_hi, x_hi, y_lo, pair):
+        c.start()
+    local_copy = pltpu.make_async_copy(own_ref, mine, local_sem)
+    local_copy.start()
+    from_x, from_y, from_d = out_ref.at[x_at, core], out_ref.at[y_at, core], out_ref.at[d_at, core]
+    on_y = copy(from_x.at[lo], from_x.at[lo], yp)
+    on_x = copy(from_y.at[hi], from_y.at[hi], xp)
+    late = [pair]
+
+    def hand(block, rows):
+        c = copy(block.at[rows], block.at[rows], sp)
+        c.start()
+        late.append(c)
+
+    x_lo.wait_recv()
+    on_y.start()
+    hand(from_x, lo)
+    y_hi.wait_recv()
+    on_x.start()
+    hand(from_y, hi)
+    x_hi.wait_recv()
+    hand(from_x, hi)
+    y_lo.wait_recv()
+    hand(from_y, lo)
+    on_y.wait_recv()
+    hand(from_d, lo)
+    on_x.wait_recv()
+    hand(from_d, hi)
+    for c in late:
+        c.wait_recv()
+    for c in [x_lo, y_hi, x_hi, y_lo, on_y, on_x] + late:
+        c.wait_send()
+    local_copy.wait()
+
+
+def gather_kernel(own_ref, out_ref, sems, local_sem):
+    greet_plane()
+    gather_steps(own_ref, out_ref, Sender(sems), local_sem)
+
+
+def plane_gather(own, cid):
+    m, width = own.shape
+    out = pl.pallas_call(
+        gather_kernel,
+        name="plane_gather",
+        out_shape=jax.ShapeDtypeStruct((4, 2, m, width), own.dtype),
+        in_specs=[pl.BlockSpec(memory_space=pltpu.VMEM)],
+        out_specs=pl.BlockSpec(memory_space=pl.ANY),
+        scratch_shapes=[pltpu.SemaphoreType.DMA((2, GATHER_COPIES)), pltpu.SemaphoreType.DMA],
+        compiler_params=pltpu.CompilerParams(collective_id=cid, has_side_effects=True),
+        cost_estimate=pl.CostEstimate(flops=0, bytes_accessed=own.size * 80, transcendentals=0),
+    )(own)
+    return out.reshape(8 * m, width)
+
+
+def scatter_steps(part_ref, out_ref, pair_ref, sum_ref, got_ref, copy):
+    at, x_at, y_at, d_at, core = plane_places()
+    half = part_ref.shape[2] // 2
+    xp, yp, sp = {"dp": x_at}, {"dp": y_at}, {"tensor": 1 - core}
+    lo, hi = pl.ds(0, half), pl.ds(half, half)
+    order = (d_at, x_at, y_at, at)
+    pairs = [copy(part_ref.at[to, 1 - core], pair_ref.at[j], sp) for j, to in enumerate(order)]
+    for c in pairs:
+        c.start()
+
+    def total(j, rows, *more):
+        add_rows(
+            sum_ref.at[j, rows], part_ref.at[order[j], core, rows], pair_ref.at[j, rows], *more
+        )
+
+    def sent(j, rows, place):
+        return copy(sum_ref.at[j, rows], got_ref.at[j, rows], place)
+
+    d_lo, d_hi = sent(0, lo, xp), sent(0, hi, yp)
+    x_lo, y_hi, x_hi, y_lo = sent(1, lo, xp), sent(2, hi, yp), sent(1, hi, xp), sent(2, lo, yp)
+    pairs[0].wait_recv()
+    total(0, lo)
+    d_lo.start()
+    total(0, hi)
+    d_hi.start()
+    pairs[1].wait_recv()
+    total(1, lo)
+    x_lo.start()
+    pairs[2].wait_recv()
+    total(2, hi)
+    y_hi.start()
+    d_lo.wait_recv()
+    total(2, lo, got_ref.at[0, lo])
+    y_lo.start()
+    d_hi.wait_recv()
+    total(1, hi, got_ref.at[0, hi])
+    x_hi.start()
+    pairs[3].wait_recv()
+    for c in (x_lo, y_hi, y_lo, x_hi):
+        c.wait_recv()
+    add_rows(out_ref, part_ref.at[at, core], pair_ref.at[3], got_ref.at[1], got_ref.at[2])
+    for c in pairs + [d_lo, d_hi, x_lo, y_hi, x_hi, y_lo]:
+        c.wait_send()
+
+
+def scatter_kernel(part_ref, out_ref, pair_ref, sum_ref, got_ref, sems):
+    greet_plane()
+    scatter_steps(part_ref, out_ref, pair_ref, sum_ref, got_ref, Sender(sems))
+
+
+def plane_scatter(part, cid):
+    rows, width = part.shape
+    m = rows // 8
+    return pl.pallas_call(
+        scatter_kernel,
+        name="plane_scatter",
+        out_shape=jax.ShapeDtypeStruct((m, width), jnp.float32),
+        in_specs=[pl.BlockSpec(memory_space=pltpu.VMEM)],
+        out_specs=pl.BlockSpec(memory_space=pltpu.VMEM),
+        scratch_shapes=[
+            pltpu.VMEM((4, m, width), part.dtype),
+            pltpu.VMEM((3, m, width), part.dtype),
+            pltpu.VMEM((3, m, width), part.dtype),
+            pltpu.SemaphoreType.DMA((2, SCATTER_COPIES)),
+        ],
+        compiler_params=pltpu.CompilerParams(
+            collective_id=cid, has_side_effects=True, vmem_limit_bytes=VMEM_LIMIT
+        ),
+        cost_estimate=pl.CostEstimate(flops=0, bytes_accessed=part.size * 10, transcendentals=0),
+    )(part.reshape(4, 2, m, width))
+
+
+def exchange_kernel(axis, take, put, count, *refs):
+    ins, outs, sems, local_sems = refs[:count], refs[count : 2 * count], refs[-2], refs[-1]
+    size, me = lax.axis_size(axis), lax.axis_index(axis)
+    peers = [lax.rem(me + k, size) for k in range(1, size)]
+    greet([{axis: p} for p in peers])
+    copy = Sender(sems)
+    copies = [copy(take(i, p), put(o, me), {axis: p}) for i, o in zip(ins, outs) for p in peers]
+    copies += [
+        pltpu.make_async_copy(take(i, me), put(o, me), local_sems.at[n])
+        for n, (i, o) in enumerate(zip(ins, outs))
+    ]
+    for c in copies:
+        c.start()
+    for c in copies:
+        c.wait()
+
+
+def block_of(ref, index):
+    return ref.at[index]
+
+
+def columns_of(ref, index):
+    width = ref.shape[1] // lax.axis_size("dp")
+    return ref.at[:, pl.ds(pl.multiple_of(index * width, width), width)]
+
+
+def exchange(arrays, axis, cid, shapes, take=block_of, put=block_of):
+    count, peers = len(arrays), lax.axis_size(axis) - 1
+    anywhere = [pl.BlockSpec(memory_space=pl.ANY)] * count
+    return pl.pallas_call(
+        partial(exchange_kernel, axis, take, put, count),
+        name="exchange_" + axis,
+        out_shape=[jax.ShapeDtypeStruct(s, x.dtype) for s, x in zip(shapes, arrays)],
+        in_specs=anywhere,
+        out_specs=anywhere,
+        scratch_shapes=[
+            pltpu.SemaphoreType.DMA((2, count * peers)),
+            pltpu.SemaphoreType.DMA((count,)),
+        ],
+        compiler_params=pltpu.CompilerParams(collective_id=cid, has_side_effects=True),
+        cost_estimate=pl.CostEstimate(
+            flops=0, bytes_accessed=60 * sum(x.size for x in arrays), transcendentals=0
+        ),
+    )(*arrays)
+
+
+def first_kernel(pack_ref, small_ref, out_ref, all_ref, sems, small_sems, local_sems):
+    plane, span = lax.axis_size("dp"), lax.axis_size("seq")
+    at, z = lax.axis_index("dp"), lax.axis_index("seq")
+    places = [
+        {"dp": lax.rem(at + i, plane), "seq": lax.rem(z + k, span)}
+        for k in range(span)
+        for i in range(plane)
+        if i or k
+    ]
+    greet(places)
+    copy, copy_small = Sender(sems), Sender(small_sems)
+    block = all_ref.at[z * plane + at]
+    copies = [copy_small(small_ref, block, p) for p in places]
+    for i in range(1, plane):
+        to = lax.rem(at + i, plane)
+        copies.append(copy(pack_ref.at[to], columns_of(out_ref, at), {"dp": to}))
+    copies.append(pltpu.make_async_copy(small_ref, block, local_sems.at[0]))
+    copies.append(
+        pltpu.make_async_copy(pack_ref.at[at], columns_of(out_ref, at), local_sems.at[1])
+    )
+    for c in copies:
+        c.start()
+    for c in copies:
+        c.wait()
+
+
+def first_exchange(pack, small, cid):
+    plane, span = lax.axis_size("dp"), lax.axis_size("seq")
+    _, size, chunk = pack.shape
+    anywhere = pl.BlockSpec(memory_space=pl.ANY)
+    whole = pl.BlockSpec(memory_space=pltpu.VMEM)
+    return pl.pallas_call(
+        first_kernel,
+        name="first_exchange",
+        out_shape=[
+            jax.ShapeDtypeStruct((size, plane * chunk), pack.dtype),
+            jax.ShapeDtypeStruct((span * plane,) + small.shape, small.dtype),
+        ],
+        in_specs=[anywhere, whole],
+        out_specs=[anywhere, whole],
+        scratch_shapes=[
+            pltpu.SemaphoreType.DMA((2, plane - 1)),
+            pltpu.SemaphoreType.DMA((2, plane * span - 1)),
+            pltpu.SemaphoreType.DMA((2,)),
+        ],
+        compiler_params=pltpu.CompilerParams(collective_id=cid, has_side_effects=True),
+        cost_estimate=pl.CostEstimate(
+            flops=0, bytes_accessed=60 * pack.size, transcendentals=0
+        ),
+    )(pack, small)
+
+
+def ffn_kernel(normed_ref, cot_ref, w_ref, out_ref, dnormed_ref, dgate_ref, dup_ref, hidden_ref):
+    parts, units, depth = w_ref.shape
+    units //= 3
+
+    def rows(k):
+        return pl.ds(k * units, units)
+
+    def cols(s):
+        return pl.ds(s * depth, depth)
+
+    def project(x_ref, k):
+        total = nt_dot(x_ref[:, cols(0)], w_ref[0, rows(k)])
+        for s in range(1, parts):
+            total += nt_dot(x_ref[:, cols(s)], w_ref[s, rows(k)])
+        return total
+
+    gate, up, dhidden = project(normed_ref, 0), project(normed_ref, 1), project(cot_ref, 2)
+    sig = jax.nn.sigmoid(gate)
+    silu = gate * sig
+    hidden = (silu * up).astype(jnp.bfloat16)
+    dgate = (dhidden * up * sig * (1.0 + gate * (1.0 - sig))).astype(jnp.bfloat16)
+    dup = (dhidden * silu).astype(jnp.bfloat16)
+    hidden_ref[...], dgate_ref[...], dup_ref[...] = hidden, dgate, dup
+    for s in range(parts):
+        dnormed_ref[:, cols(s)] = (
+            nn_dot(dgate, w_ref[s, rows(0)]) + nn_dot(dup, w_ref[s, rows(1)])
+        ).astype(jnp.bfloat16)
+        out_ref[:, cols(s)] = nn_dot(hidden, w_ref[s, rows(2)]).astype(jnp.bfloat16)
+
+
+def ffn(normed, cot, weights, block=256):
+    tokens, width = normed.shape
+    units = weights.shape[1] // 3
+    wide = pl.BlockSpec((block, width), lambda i: (i, 0))
+    thin = pl.BlockSpec((block, units), lambda i: (i, 0))
+    return pl.pallas_call(
+        ffn_kernel,
+        name="ffn",
+        grid=(tokens // block,),
+        out_shape=[jax.ShapeDtypeStruct((tokens, width), jnp.bfloat16)] * 2
+        + [jax.ShapeDtypeStruct((tokens, units), jnp.bfloat16)] * 3,
+        in_specs=[
+            wide,
+            wide,
+            pl.BlockSpec(weights.shape, lambda i: (0, 0, 0), pipeline_mode=pl.Buffered(1)),
+        ],
+        out_specs=[wide, wide, thin, thin, thin],
+        compiler_params=pltpu.CompilerParams(vmem_limit_bytes=VMEM_LIMIT),
+        cost_estimate=pl.CostEstimate(
+            flops=12 * tokens * width * units,
+            bytes_accessed=2 * (4 * tokens * width + weights.size + 3 * tokens * units),
+            transcendentals=tokens * units,
+        ),
+    )(normed, cot, weights)
+
+
+def to_whole_rows(x, rows, length, cid):
     span = lax.axis_size("seq")
     width = x.shape[-1]
-    x = swap_rows(x.reshape(span * rows, length, width))
+    [x] = exchange(
+        [x.reshape(span, rows * length, width)], "seq", cid, [(span, rows * length, width)]
+    )
     return x.reshape(span, rows, length, width).transpose(1, 0, 2, 3).reshape(
         rows, span * length, width
     )
 
 
-def from_whole_rows(x, rows, length):
+def from_whole_rows(x, rows, length, cid):
     span = lax.axis_size("seq")
     width = x.shape[-1]
     x = x.reshape(rows, span, length, width).transpose(1, 0, 2, 3)
-    x = swap_rows(x.reshape(span * rows, length, width))
+    [x] = exchange(
+        [x.reshape(span, rows * length, width)], "seq", cid, [(span, rows * length, width)]
+    )
     return x.reshape(span * rows * length, width)
 
 
@@ -390,49 +735,52 @@
         )
 
     core = lax.axis_index("tensor")
+    def over_seq(pack):
+        return lax.all_gather(pack, "seq", axis=0, tiled=False)
+
+    def flat(pack):
+        return pack.transpose(1, 0, 2).reshape(-1, width)
+
+    def summed(grads):
+        return lax.psum_scatter(
+            grads.astype(jnp.bfloat16), "seq", scatter_dimension=1, tiled=True
+        )
+
+    def collect(parts, cid):
+        return exchange(
+            parts, "dp", cid, [(plane, p.shape[0], chunk) for p in parts], take=columns_of
+        )
+
+    def split(w):
+        return w.reshape(plane, -1, chunk)
+
     small = jnp.concatenate(
         [
             attn_gain.astype(jnp.float32)[None],
             mlp_gain.astype(jnp.float32)[None],
             doc_starts.astype(jnp.float32).reshape(-1, chunk),
+            jnp.zeros((2, chunk), jnp.float32),
         ]
     )
-    small = lax.all_gather(small, ("seq", "dp"), axis=0, tiled=False)
+    attn_pack = jnp.concatenate(
+        [split(value_weight.T), split(query_weight.T), split(key_weight.T), split(output_weight)],
+        axis=1,
+    )
+    attn_pack, small = first_exchange(attn_pack, small, 1)
+    ffn_pack = jnp.concatenate([split(gate_weight.T), split(up_weight.T), split(down_weight)], axis=1)
+    ffn_pack, _ = lax.optimization_barrier((ffn_pack, attn_pack))
+    [ffn_pack] = exchange(
+        [ffn_pack], "dp", 2, [(ffn_pack.shape[1], plane * chunk)], put=columns_of
+    )
+    attn_pack, ffn_pack = over_seq(attn_pack), over_seq(ffn_pack)
     gain_one = small[:, 0].reshape(width)
     gain_two = small[:, 1].reshape(width)
-    starts = small[:, 2:].reshape(span, plane * rows, length)
+    starts = small[:, 2:-2].reshape(span, plane * rows, length)
     starts = lax.dynamic_slice_in_dim(starts, lax.axis_index("seq") * all_rows, all_rows, 1)
     segments = jnp.cumsum(starts.transpose(1, 0, 2).reshape(all_rows, span * length), axis=1)
 
-    def spread(pack):
-        pack = lax.all_to_all(pack, "dp", split_axis=0, concat_axis=0, tiled=True)
-        pack = lax.all_gather(pack, "seq", axis=0, tiled=False)
-        return pack.transpose(2, 0, 1, 3).reshape(pack.shape[2], width)
-
-    def collect(grads):
-        part = lax.psum_scatter(
-            grads.astype(jnp.bfloat16), "seq", scatter_dimension=1, tiled=True
-        )
-        part = part.reshape(part.shape[0], plane, chunk).transpose(1, 0, 2)
-        return lax.all_to_all(part, "dp", split_axis=0, concat_axis=0, tiled=True).astype(
-            jnp.float32
-        )
-
-    def split(w):
-        return w.reshape(plane, -1, chunk)
-
-    attn_pack = spread(
-        jnp.concatenate(
-            [split(value_weight.T), split(query_weight.T), split(key_weight.T), split(output_weight)],
-            axis=1,
-        )
-    )
-    ffn_pack = spread(
-        jnp.concatenate([split(gate_weight.T), split(up_weight.T), split(down_weight)], axis=1)
-    )
     qkv_rows = vcols + 2 * qcols
-    w_qkv, w_out = attn_pack[:qkv_rows], attn_pack[qkv_rows:]
-    w_gate_up, w_down = ffn_pack[: 2 * hidden_part], ffn_pack[2 * hidden_part :]
+    w_qkv, w_out = flat(attn_pack[:, :qkv_rows]), flat(attn_pack[:, qkv_rows:])
 
     def mine(a):
         a = lax.dynamic_slice_in_dim(a.reshape(rows * length, width), core * own, own, 0)
@@ -441,38 +789,34 @@
     x = mine(tokens).astype(jnp.float32)
     cot_own = mine(cotangent)
     scale_one = inverse_rms(x)
-    normed_one = gather_rows((x * scale_one * gain_one).astype(jnp.bfloat16))
-    cot = gather_rows(cot_own)
+    normed_one = plane_gather((x * scale_one * gain_one).astype(jnp.bfloat16), 3)
+    cot = plane_gather(cot_own, 4)
     qkv = nt_dot(normed_one, w_qkv).astype(jnp.bfloat16)
-    qkv = to_whole_rows(qkv, all_rows, length)
+    qkv = to_whole_rows(qkv, all_rows, length, 5)
     values = qkv[..., :vcols].reshape(all_rows, -1, heads, VHEAD)
     queries = qkv[..., vcols : vcols + qcols].reshape(all_rows, -1, heads, FDIM)
     keys = qkv[..., vcols + qcols :].reshape(all_rows, -1, heads, FDIM)
     mixed, den, weight, scores, allowed = attention_forward(queries, keys, values, segments)
     mixed_low = mixed.transpose(0, 2, 1, 3).reshape(all_rows, -1, vcols).astype(jnp.bfloat16)
-    mixed_low = from_whole_rows(mixed_low, all_rows, length)
-    residual = x + scatter_rows(nn_dot(mixed_low, w_out))
+    mixed_low = from_whole_rows(mixed_low, all_rows, length, 6)
+    residual = x + plane_scatter(nn_dot(mixed_low, w_out).astype(jnp.bfloat16), 7)
     scale_two = inverse_rms(residual)
-    normed_two = gather_rows((residual * scale_two * gain_two).astype(jnp.bfloat16))
-    gate_up = nt_dot(normed_two, w_gate_up)
-    gate, up = gate_up[:, :hidden_part], gate_up[:, hidden_part:]
-    sig = jax.nn.sigmoid(gate)
-    hidden = (gate * sig * up).astype(jnp.bfloat16)
-    block_own = (residual + scatter_rows(nn_dot(hidden, w_down))).astype(jnp.bfloat16)
-
-    dhidden = nt_dot(cot, w_down)
-    dgate = (dhidden * up * sig * (1.0 + gate * (1.0 - sig))).astype(jnp.bfloat16)
-    dup = (dhidden * gate * sig).astype(jnp.bfloat16)
-    dgate_up = jnp.concatenate([dgate, dup], axis=1)
-    dnormed_two = scatter_rows(nn_dot(dgate_up, w_gate_up))
-    ffn_grads = collect(
-        jnp.concatenate([tn_dot(dgate_up, normed_two), tn_dot(hidden, cot)], axis=0)
-    )
+    normed_two = plane_gather((residual * scale_two * gain_two).astype(jnp.bfloat16), 11)
+    out_part, dnormed_part, dgate, dup, hidden = ffn(normed_two, cot, ffn_pack)
+    down_grad = tn_dot(hidden, cot).astype(jnp.bfloat16)
+    gate_grad = tn_dot(dgate, normed_two).astype(jnp.bfloat16)
+    up_grad = tn_dot(dup, normed_two).astype(jnp.bfloat16)
+    dnormed_part, gate_grad, up_grad, down_grad = lax.optimization_barrier(
+        (dnormed_part, gate_grad, up_grad, down_grad)
+    )
+    down_grad, gate_grad, up_grad = summed(down_grad), summed(gate_grad), summed(up_grad)
+    dnormed_two = plane_scatter(dnormed_part, 9)
     dresid, gain_two_grad = norm_backward(residual, scale_two, gain_two, dnormed_two)
     dresid = dresid + cot_own.astype(jnp.float32)
-    dresid_low = gather_rows(dresid.astype(jnp.bfloat16))
+    dresid_low = plane_gather(dresid.astype(jnp.bfloat16), 12)
+    block_own = (residual + plane_scatter(out_part, 8)).astype(jnp.bfloat16)
     dmixed = nt_dot(dresid_low, w_out).astype(jnp.bfloat16)
-    dmixed = to_whole_rows(dmixed, all_rows, length).reshape(all_rows, -1, heads, VHEAD)
+    dmixed = to_whole_rows(dmixed, all_rows, length, 13).reshape(all_rows, -1, heads, VHEAD)
     dqueries, dkeys, dvalues = attention_backward(
         queries, keys, values, mixed, den, weight, scores, allowed, dmixed
     )
@@ -483,24 +827,30 @@
         ],
         axis=-1,
     )
-    dqkv = from_whole_rows(dqkv, all_rows, length)
-    dnormed_one = scatter_rows(nn_dot(dqkv, w_qkv))
-    attn_grads = collect(
-        jnp.concatenate([tn_dot(dqkv, normed_one), tn_dot(mixed_low, dresid_low)], axis=0)
-    )
+    dqkv = from_whole_rows(dqkv, all_rows, length, 14)
+    dnormed_one = plane_scatter(nn_dot(dqkv, w_qkv).astype(jnp.bfloat16), 10)
+    out_grad = summed(tn_dot(mixed_low, dresid_low))
+    qkv_grad = tn_dot(dqkv, normed_one)
     dtokens, gain_one_grad = norm_backward(x, scale_one, gain_one, dnormed_one)
     dtokens = dresid + dtokens
-    gain_grads = lax.psum(jnp.stack([gain_one_grad, gain_two_grad]), "tensor")
-    gain_grads = lax.psum_scatter(
-        gain_grads, ("seq", "dp"), scatter_dimension=1, tiled=True
-    )
+    gain_grads = jnp.stack([gain_one_grad, gain_two_grad])
+    qkv_grad = summed(
+        jnp.concatenate([qkv_grad, jnp.pad(gain_grads, ((0, 14), (0, 0)))], axis=0)
+    )
+    down_grad, gate_grad, up_grad, dtokens = lax.optimization_barrier(
+        (down_grad, gate_grad, up_grad, dtokens)
+    )
+    down_grad, gate_grad, up_grad = collect([down_grad, gate_grad, up_grad], 15)
+    out_grad, qkv_grad = collect([out_grad, qkv_grad], 16)
+    gain_grads = qkv_grad[:, qkv_rows : qkv_rows + 2].astype(jnp.float32).sum(axis=0)
+    gain_grads = lax.psum(gain_grads, "tensor")
 
     def whole(a):
         a = lax.all_gather(plane_major(a), "tensor", axis=0, tiled=True)
         return a.reshape(rows, length, width)
 
     def stacked(a, start, size):
-        return a[:, start : start + size].reshape(plane * size, chunk)
+        return a[:, start : start + size].reshape(plane * size, chunk).astype(jnp.float32)
 
     h = hidden_part
     return (
@@ -508,13 +858,13 @@
         whole(dtokens),
         gain_grads[0],
         gain_grads[1],
-        stacked(attn_grads, vcols, qcols).T,
-        stacked(attn_grads, vcols + qcols, qcols).T,
-        stacked(attn_grads, 0, vcols).T,
-        stacked(attn_grads, qkv_rows, vcols),
-        stacked(ffn_grads, 0, h).T,
-        stacked(ffn_grads, h, h).T,
-        stacked(ffn_grads, 2 * h, h),
+        stacked(qkv_grad, vcols, qcols).T,
+        stacked(qkv_grad, vcols + qcols, qcols).T,
+        stacked(qkv_grad, 0, vcols).T,
+        stacked(out_grad, 0, vcols),
+        stacked(gate_grad, 0, h).T,
+        stacked(up_grad, 0, h).T,
+        stacked(down_grad, 0, h),
     )
 
 

time: 1320 us -> 962 us (0.73)
  waiting for transfers between devices: 785 us -> 58.4 us
  Pallas kernels: 0 us -> 644 us
  blocking collectives: 157 us -> 2.44 us
  local copies, waits for them, and re-layouts: 132 us -> 73.6 us
  matrix products: 171 us -> 116 us
  starting transfers between devices: 18.2 us -> 0.79 us
    pallas_call x0 -> x17, Pallas kernels: none -> 644 us  [the longest x7 235 us: exchange(): pl.pallas_call(partial(exchange_kernel, axis, take, put, count), name='ex...]
    reduce_scatter x6 -> x5, waiting for transfers between devices: 362 us -> 57.9 us  [summed(): lax.psum_scatter(grads.astype(jnp.bfloat16), 'seq', scatter_dimension=1,...]
    all_gather x6 -> x2, waiting for transfers between devices: 288 us -> 0.02 us  [over_seq(): return lax.all_gather(pack, 'seq', axis=0, tiled=False)]
    all_to_all x4 -> x0, blocking collectives: 114 us -> none  [the longest x2 64.4 us: swap_rows(): return lax.all_to_all(x, 'seq', split_axis=0, concat_axis=0, tiled=True)]
    unnamed x16 -> x9, waiting for transfers between devices: 59.6 us -> 0.48 us
    all_to_all x4 -> x0, waiting for transfers between devices: 57.9 us -> none  [the longest x2 50.1 us: swap_rows(): return lax.all_to_all(x, 'seq', split_axis=0, concat_axis=0, tiled=True)]
    all_gather x1 -> x0, blocking collectives: 40.6 us -> none  [plane_local(): small = lax.all_gather(small, ('seq', 'dp'), axis=0, tiled=False)]
    dot_general x4 -> x2, matrix products: 48.3 us -> 13.7 us  [nt_dot(): lax.dot_general(a, b, (((1,), (1,)), ((), ())), preferred_element_type=jn...]
  transfers between devices with their start and end apart: 19 -> 9, of which waited for: 18 -> 2; matrix products, arithmetic and copies ran while one was open for 15% -> 19% of each run, Pallas kernels for 0% -> 61%
where the time goes in v2:
time: 962 us; the launch traced here: 951 us
  Pallas kernels  644 us (67%)
  matrix products  116 us (12%)
  local copies, waits for them, and re-layouts  73.6 us (8%)
  waiting for transfers between devices  58.4 us (6%)
  other arithmetic  41.2 us (4%)
  between operations  15.1 us (2%)
    pallas_call x7, Pallas kernels, exchange(): pl.pallas_call(partial(exchange_kernel, axis, take, put, count), name='ex...  235 us
    pallas_call x4, Pallas kernels, plane_scatter(): pl.pallas_call(scatter_kernel, name='plane_scatter', out_shape=jax.ShapeD...  179 us
    pallas_call x4, Pallas kernels, plane_gather(): pl.pallas_call(gather_kernel, name='plane_gather', out_shape=jax.ShapeDty...  163 us
    reduce_scatter x5, waiting for transfers between devices, summed(): lax.psum_scatter(grads.astype(jnp.bfloat16), 'seq', scatter_dimension=1,...  57.9 us
    pallas_call x1, Pallas kernels, ffn(): pl.pallas_call(ffn_kernel, name='ffn', grid=(tokens // block,), out_shape...  50 us
    dot_general x5, matrix products, tn_dot(): lax.dot_general(a, b, (((0,), (0,)), ((), ())), preferred_element_type=jn...  44.7 us
    unnamed x74, local copies, waits for them, and re-layouts  20.6 us
  transfers between devices with their start and end apart: 9, of which 2 were waited for; matrix products, arithmetic and copies ran while one was open for 19% of the time, Pallas kernels for 61%

profile of v2, /device:TPU:0, one launch (start us, length us, event | category | flops | bytes accessed | tf_op | source)
XLA Modules:
  0.0 951.4 jit_solution(10703467512542639460)
XLA Ops:
  12.4 1.8 pad_maximum_fusion.3.pack_ref
  14.2 16.7 %first_exchange.1 = (bf16[576,512]{1,0:T(8,128)(2,1)}, f32[16,8,128]{2,1,0:T(8,128)}) custom-call(bf16[4,576,128]{2,1,0:T(8,128)(2,1)} %pad_maximum_fusion.3.pack_ref, f32[8,128]{1,0:T(8,128)} %maximum_maximum_fusion.small_ref), custom_call_target="tpu_custom_call" | custom-call | bytes 17694720 | tf_op jit(solution)/shard_map/first_exchange/pallas_call | solution.py:576
  32.5 26.6 %exchange_dp.3 = bf16[2064,512]{1,0:T(8,128)(2,1)} custom-call(bf16[4,2064,128]{2,1,0:T(8,128)(2,1)} %pad_maximum_fusion.refs_0_), custom_call_target="tpu_custom_call" | custom-call | bytes 63406080 | tf_op jit(solution)/shard_map/exchange_dp/pallas_call | solution.py:528
  61.0 1.7 constant_dynamic-slice_fusion
  64.3 1.6 reshape.295.own_ref
  66.6 2.0 copy.44
  68.6 2.1 reshape.313
  72.3 40.0 %plane_gather.4 = bf16[4,2,256,2048]{3,2,1,0:T(8,128)(2,1)} custom-call(bf16[256,2048]{1,0:T(8,128)(2,1)} %multiply_convert_fusion.2.own_ref), custom_call_target="tpu_custom_call" | custom-call | bytes 41943040 | tf_op jit(solution)/shard_map/plane_gather/pallas_call | solution.py:414
  112.2 40.9 %plane_gather.6 = bf16[4,2,256,2048]{3,2,1,0:T(8,128)(2,1)} custom-call(bf16[256,2048]{1,0:T(8,128)(2,1)} %reshape.295.own_ref), custom_call_target="tpu_custom_call" | custom-call | bytes 41943040 | tf_op jit(solution)/shard_map/plane_gather/pallas_call | solution.py:414
  153.5 2.6 compare_and_fusion
  162.7 6.7 convolution_convert_fusion.6
  170.9 52.4 %exchange_seq.4 = bf16[4,512,320]{2,1,0:T(8,128)(2,1)} custom-call(bf16[4,512,320]{2,1,0:T(8,128)(2,1)} %bitcast.198), custom_call_target="tpu_custom_call" | custom-call | bytes 39321600 | tf_op jit(solution)/shard_map/exchange_seq/pallas_call | solution.py:528
  223.4 3.7 copy.51
  227.0 2.8 reshape.284
  229.9 1.9 copy-done.11
  231.8 9.1 fusion
  240.9 3.4 fusion.2
  245.1 1.9 convert_element_type.171
  248.4 50.4 %exchange_seq.5 = bf16[4,512,256]{2,1,0:T(8,128)(2,1)} custom-call(bf16[4,512,256]{2,1,0:T(8,128)(2,1)} %bitcast.206), custom_call_target="tpu_custom_call" | custom-call | bytes 31457280 | tf_op jit(solution)/shard_map/exchange_seq/pallas_call | solution.py:528
  298.8 6.8 convolution_convert_fusion.1
  305.7 44.3 %plane_scatter.4 = f32[256,2048]{1,0:T(8,128)} custom-call(bf16[4,2,256,2048]{3,2,1,0:T(8,128)(2,1)} %bitcast.182), custom_call_target="tpu_custom_call" | custom-call | bytes 41943040 | tf_op jit(solution)/shard_map/plane_scatter/pallas_call | solution.py:480
  349.9 1.9 multiply_reduce_fusion.5
  354.4 41.2 %plane_gather.5 = bf16[4,2,256,2048]{3,2,1,0:T(8,128)(2,1)} custom-call(bf16[256,2048]{1,0:T(8,128)(2,1)} %multiply_convert_fusion.1.own_ref), custom_call_target="tpu_custom_call" | custom-call | bytes 41943040 | tf_op jit(solution)/shard_map/plane_gather/pallas_call | solution.py:414
  395.7 50.0 %ffn.1 = (bf16[2048,2048]{1,0:T(8,128)(2,1)}, bf16[2048,2048]{1,0:T(8,128)(2,1)}, bf16[2048,688]{1,0:T(8,128)(2,1)}, bf16[2048,688]{1,0:T(8,128)(2,1)}, bf16[2048,688]{1,0:T(8,128)(2,1)}) custom-call(bf16[2048,2048]{1,0:T(8,128)(2,1)} %bitcast.192, bf16[2048,2048]{1,0:T(8,128)(2,1)} %bitcast.190, bf16[4,2064,512]{2,1,0:T(8,128)(2,1)} %bitcast.248), custom_call_target="tpu_custom_call" | custom-call | flops 34628173824 | bytes 50462720 | tf_op jit(solution)/shard_map/ffn/pallas_call | solution.py:632
  445.7 10.6 %convolution_convert_fusion.2 = bf16[688,2048]{1,0:T(8,128)(2,1)} fusion(bf16[2048,688]{1,0:T(8,128)(2,1)} %get-tuple-element.39, bf16[2048,2048]{1,0:T(8,128)(2,1)} %bitcast.191), kind=kOutput, calls=%fused_computation.8 | convolution fusion | flops 5772771328 | bytes 14024704 | tf_op jit(solution)/shard_map/dot_general | solution.py:297
  456.3 10.6 %convolution_convert_fusion.4 = bf16[688,2048]{1,0:T(8,128)(2,1)} fusion(bf16[2048,688]{1,0:T(8,128)(2,1)} %get-tuple-element.37, bf16[2048,2048]{1,0:T(8,128)(2,1)} %bitcast.193), kind=kOutput, calls=%fused_computation.10 | convolution fusion | flops 5772771328 | bytes 14024704 | tf_op jit(solution)/shard_map/dot_general | solution.py:297
  466.8 10.5 %convolution_convert_fusion.3 = bf16[688,2048]{1,0:T(8,128)(2,1)} fusion(bf16[2048,688]{1,0:T(8,128)(2,1)} %get-tuple-element.38, bf16[2048,2048]{1,0:T(8,128)(2,1)} %bitcast.194), kind=kOutput, calls=%fused_computation.9 | convolution fusion | flops 5772771328 | bytes 14024704 | tf_op jit(solution)/shard_map/dot_general | solution.py:297
  478.0 45.2 %plane_scatter.6 = f32[256,2048]{1,0:T(8,128)} custom-call(bf16[4,2,256,2048]{3,2,1,0:T(8,128)(2,1)} %bitcast.186), custom_call_target="tpu_custom_call" | custom-call | bytes 41943040 | tf_op jit(solution)/shard_map/plane_scatter/pallas_call | solution.py:480
  523.2 2.4 multiply_reduce_fusion
  525.7 1.7 fusion.10.own_ref
  527.5 40.5 %plane_gather.7 = bf16[4,2,256,2048]{3,2,1,0:T(8,128)(2,1)} custom-call(bf16[256,2048]{1,0:T(8,128)(2,1)} %fusion.10.own_ref), custom_call_target="tpu_custom_call" | custom-call | bytes 41943040 | tf_op jit(solution)/shard_map/plane_gather/pallas_call | solution.py:414
  568.0 7.0 convolution_convert_fusion.8
  575.0 34.0 %exchange_seq.6 = bf16[4,512,256]{2,1,0:T(8,128)(2,1)} custom-call(bf16[4,512,256]{2,1,0:T(8,128)(2,1)} %bitcast.218), custom_call_target="tpu_custom_call" | custom-call | bytes 31457280 | tf_op jit(solution)/shard_map/exchange_seq/pallas_call | solution.py:528
  609.0 2.8 convert_bitcast_fusion
  611.8 3.0 copy.58
  614.7 3.3 reshape.318
  618.1 2.7 multiply_reduce_fusion.3
  620.9 46.0 %plane_scatter.5 = f32[256,2048]{1,0:T(8,128)} custom-call(bf16[4,2,256,2048]{3,2,1,0:T(8,128)(2,1)} %bitcast.185), custom_call_target="tpu_custom_call" | custom-call | bytes 41943040 | tf_op jit(solution)/shard_map/plane_scatter/pallas_call | solution.py:480
  667.0 10.7 %multiply_convert_fusion = bf16[2,2,1024,1024]{2,3,1,0:T(8,128)(2,1)} fusion(f32[2,2,1024,1024]{2,3,1,0:T(8,128)} %get-tuple-element.82, f32[2,2,1024]{2,1,0:T(2,128)S(1)} %neg.7, pred[2,1024,1024]{1,2,0:T(8,128)(4,1)S(1)} %copy-done.12, bf16[2,1024,2,128]{1,3,2,0:T(8,128)(2,1)S(1)} %bitcast.217, f32[2,2,1024]{2,1,0:T(2,128)S(1)} %get-tuple-element.70, ...), kind=kOutput, calls=%fused_computation | convolution fusion | flops 1104150528 | bytes 30441472 | tf_op jit(solution)/shard_map/rhte,rshe->rhts/dot_general | solution.py:693
  677.7 4.6 fusion.4
  682.4 5.7 fusion.5
  688.1 7.9 fusion.3
  696.1 2.6 convert_element_type.189
  698.7 2.6 copy.65
  703.4 3.0 pad_maximum_fusion.1
  706.4 34.9 %exchange_seq.7 = bf16[4,512,320]{2,1,0:T(8,128)(2,1)} custom-call(bf16[4,512,320]{2,1,0:T(8,128)(2,1)} %bitcast.197), custom_call_target="tpu_custom_call" | custom-call | bytes 39321600 | tf_op jit(solution)/shard_map/exchange_seq/pallas_call | solution.py:528
  741.3 9.6 %convolution_convert_fusion = bf16[2048,2048]{1,0:T(8,128)(2,1)} fusion(bf16[2048,320]{1,0:T(8,128)(2,1)} %bitcast.212, bf16[320,2048]{1,0:T(8,128)(2,1)} %bitcast.215), kind=kOutput, calls=%fused_computation.5 | convolution fusion | flops 2688548864 | bytes 11010048 | tf_op jit(solution)/shard_map/dot_general | solution.py:301
  750.9 43.5 %plane_scatter.7 = f32[256,2048]{1,0:T(8,128)} custom-call(bf16[4,2,256,2048]{3,2,1,0:T(8,128)(2,1)} %bitcast.187), custom_call_target="tpu_custom_call" | custom-call | bytes 41943040 | tf_op jit(solution)/shard_map/plane_scatter/pallas_call | solution.py:480
  794.5 2.3 multiply_reduce_fusion.1
  797.3 4.6 subtract_add_fusion
  801.9 1.8 reshape.301
  803.7 1.6 copy.57
  805.3 6.8 convolution_convert_fusion.7
  812.5 6.3 convolution_convert_fusion.5
  821.1 2.4 reshape.310
  823.5 2.9 copy.68
  826.5 3.9 copy.83
  830.4 24.0 %reduce-scatter.12.cloned.1.call-done.refs_0_ = bf16[256,512]{1,0:T(8,128)(2,1)} async-done(((bf16[256,2048]{1,0:T(8,128)(2,1)}), bf16[256,512]{1,0:T(8,128)(2,1)}) %reduce-scatter.12.cloned.1.call-update) | async-done | bytes 262160 | tf_op jit(solution)/shard_map/reduce_scatter | solution.py:745
  854.4 33.8 %reduce-scatter.14.cloned.1.call-done.refs_1_ = bf16[336,512]{1,0:T(8,128)(2,1)} async-done(((bf16[336,2048]{1,0:T(8,128)(2,1)}), bf16[336,512]{1,0:T(8,128)(2,1)}) %reduce-scatter.14.cloned.1.call-update) | async-done | bytes 344080 | tf_op jit(solution)/shard_map/reduce_scatter | solution.py:745
  888.2 10.2 %exchange_dp.4 = (bf16[4,256,128]{2,1,0:T(8,128)(2,1)}, bf16[4,336,128]{2,1,0:T(8,128)(2,1)}) custom-call(bf16[256,512]{1,0:T(8,128)(2,1)} %reduce-scatter.12.cloned.1.call-done.refs_0_, bf16[336,512]{1,0:T(8,128)(2,1)} %reduce-scatter.14.cloned.1.call-done.refs_1_), custom_call_target="tpu_custom_call" | custom-call | bytes 18186240 | tf_op jit(solution)/shard_map/exchange_dp/pallas_call | solution.py:528
  903.5 2.4 psum.7
  907.3 26.8 %exchange_dp.5 = (bf16[4,688,128]{2,1,0:T(8,128)(2,1)}, bf16[4,688,128]{2,1,0:T(8,128)(2,1)}, bf16[4,688,128]{2,1,0:T(8,128)(2,1)}) custom-call(bf16[688,512]{1,0:T(8,128)(2,1)} %reduce-scatter.6.cloned.1.call-done.refs_0_, bf16[688,512]{1,0:T(8,128)(2,1)} %reduce-scatter.8.cloned.1.call-done.refs_1_, bf16[688,512]{1,0:T(8,128)(2,1)} %reduce-scatter.10.cloned.1.call-done.refs_2_), custom_call_target="tpu_custom_call" | custom-call | bytes 63406080 | tf_op jit(solution)/shard_map/exchange_dp/pallas_call | solution.py:528
  934.2 2.4 convert_bitcast_fusion.2
  939.0 5.3 copy.84
  (154 shorter events, 41.0 us)
Async XLA Ops:
  7.2 23.8 %copy-start.18 = (bf16[2752,128]{1,0:T(8,128)(2,1)S(1)}, bf16[2752,128]{1,0:T(8,128)(2,1)}, u32[]{:S(2)}) copy-start(bf16[2752,128]{1,0:T(8,128)(2,1)} %param.22) | copy-start | bytes 2113540
  7.2 23.8 %copy-start.19 = (bf16[128,2752]{0,1:T(8,128)(2,1)S(1)}, bf16[128,2752]{0,1:T(8,128)(2,1)}, u32[]{:S(2)}) copy-start(bf16[128,2752]{0,1:T(8,128)(2,1)} %param.21) | copy-start | bytes 2113540
  7.2 23.8 %copy-start.20 = (bf16[128,2752]{0,1:T(8,128)(2,1)S(1)}, bf16[128,2752]{0,1:T(8,128)(2,1)}, u32[]{:S(2)}) copy-start(bf16[128,2752]{0,1:T(8,128)(2,1)} %param.20) | copy-start | bytes 2113540
  7.2 148.9 %all-gather.11.cloned.1.call-start = ((), (), s32[]{:S(2)}) async-start(), calls=%async_computation.12 | async-start | bytes 2949120 | tf_op jit(solution)/shard_map/all_gather | solution.py:739
  30.9 364.7 %all-gather.13.cloned.1.call-start = ((), (), s32[]{:S(2)}) async-start(), calls=%async_computation.13 | async-start | bytes 10567680 | tf_op jit(solution)/shard_map/all_gather | solution.py:739
  59.1 0.8 copy-start.26
  59.1 761.0 %reduce-scatter.6.cloned.1.call-start = ((), (), s32[]{:S(2)}) async-start(), calls=%async_computation.6 | async-start | bytes 3522560 | tf_op jit(solution)/shard_map/reduce_scatter | solution.py:745
  71.0 41.2 %copy-start.28 = (f32[256]{0:T(256)}, f32[256]{0:T(256)S(1)}, u32[]{:S(2)}) copy-start(f32[256]{0:T(256)S(1)} %add_rsqrt_fusion.1) | copy-start | bytes 3076
  71.0 41.2 %copy-start.24 = (f32[16,1,128]{2,1,0:T(1,128)}, f32[16,1,128]{2,1,0:T(1,128)S(1)}, u32[]{:S(2)}) copy-start(f32[16,1,128]{2,1,0:T(1,128)S(1)} %get-tuple-element.79) | copy-start | bytes 24580
  229.8 2.0 copy-start.11
  229.9 11.1 %copy-start.14 = (bf16[2,1024,256]{1,2,0:T(8,128)(2,1)}, bf16[2,1024,256]{1,2,0:T(8,128)(2,1)S(1)}, u32[]{:S(2)}) copy-start(bf16[2,1024,256]{1,2,0:T(8,128)(2,1)S(1)} %slice.65) | copy-start | bytes 3145732
  229.9 11.0 %copy-start.21 = (bf16[2,1024,32]{1,2,0:T(8,128)(2,1)}, bf16[2,1024,32]{1,2,0:T(8,128)(2,1)S(1)}, u32[]{:S(2)}) copy-start(bf16[2,1024,32]{1,2,0:T(8,128)(2,1)S(1)} %get-tuple-element.74) | copy-start | bytes 393220
  240.9 4.2 copy-start.32
  240.9 426.0 %copy-start.27 = (f32[2,2,1024]{2,1,0:T(2,128)}, f32[2,2,1024]{2,1,0:T(2,128)S(1)}, u32[]{:S(2)}) copy-start(f32[2,2,1024]{2,1,0:T(2,128)S(1)} %get-tuple-element.70) | copy-start | bytes 49156
  248.4 50.4 %copy-start.10 = (bf16[4,256,512]{1,2,0:T(8,128)(2,1)S(1)}, bf16[4,256,512]{1,2,0:T(8,128)(2,1)}, u32[]{:S(2)}) copy-start(bf16[4,256,512]{1,2,0:T(8,128)(2,1)} %copy.87) | copy-start | bytes 3145732
  351.8 1.4 copy-start
  477.4 342.8 %reduce-scatter.8.cloned.1.call-start = ((), (), s32[]{:S(2)}) async-start(), calls=%async_computation.7 | async-start | bytes 3522560 | tf_op jit(solution)/shard_map/reduce_scatter | solution.py:745
  477.9 342.2 %reduce-scatter.10.cloned.1.call-start = ((), (), s32[]{:S(2)}) async-start(), calls=%async_computation.8 | async-start | bytes 3522560 | tf_op jit(solution)/shard_map/reduce_scatter | solution.py:745
  478.0 45.2 %copy-start.1 = (f32[256,2048]{1,0:T(8,128)S(1)}, f32[256,2048]{1,0:T(8,128)}, u32[]{:S(2)}) copy-start(f32[256,2048]{1,0:T(8,128)} %copy-done) | copy-start | bytes 6291460
  523.2 2.4 copy-start.3
  523.2 2.5 copy-start.5
  525.7 1.7 copy-start.30
  618.0 208.4 %all-gather.7.cloned.1.call-start = ((), (), s32[]{:S(2)}) async-start(), calls=%async_computation.5 | async-start | bytes 3145728 | tf_op jit(solution)/shard_map/all_gather | solution.py:849
  620.8 46.1 %copy-start.9 = (f32[2,1024,2,128]{1,3,2,0:T(8,128)S(1)}, f32[2,1024,2,128]{1,3,2,0:T(8,128)}, u32[]{:S(2)}) copy-start(f32[2,1024,2,128]{1,3,2,0:T(8,128)} %reshape.318) | copy-start | bytes 6291460
  620.8 46.1 %copy-start.12 = (pred[2,1024,1024]{1,2,0:T(8,128)(4,1)S(1)}, pred[2,1024,1024]{1,2,0:T(8,128)(4,1)}, u32[]{:S(2)}) copy-start(pred[2,1024,1024]{1,2,0:T(8,128)(4,1)} %compare_and_fusion) | copy-start | bytes 6291460
  620.9 46.1 %copy-start.15 = (bf16[2,1024,256]{1,2,0:T(8,128)(2,1)S(1)}, bf16[2,1024,256]{1,2,0:T(8,128)(2,1)}, u32[]{:S(2)}) copy-start(bf16[2,1024,256]{1,2,0:T(8,128)(2,1)} %copy-done.14) | copy-start | bytes 3145732
  667.0 10.8 %copy-start.22 = (bf16[2,1024,32]{1,2,0:T(8,128)(2,1)S(1)}, bf16[2,1024,32]{1,2,0:T(8,128)(2,1)}, u32[]{:S(2)}) copy-start(bf16[2,1024,32]{1,2,0:T(8,128)(2,1)} %copy-done.21) | copy-start | bytes 393220
  750.9 43.5 %copy-start.25 = (f32[16,1,128]{2,1,0:T(1,128)S(1)}, f32[16,1,128]{2,1,0:T(1,128)}, u32[]{:S(2)}) copy-start(f32[16,1,128]{2,1,0:T(1,128)} %copy-done.24) | copy-start | bytes 24580
  750.9 43.5 %copy-start.29 = (f32[256]{0:T(256)S(1)}, f32[256]{0:T(256)}, u32[]{:S(2)}) copy-start(f32[256]{0:T(256)} %copy-done.28) | copy-start | bytes 3076
  750.9 45.8 %copy-start.7 = (f32[256,2048]{1,0:T(8,128)S(1)}, f32[256,2048]{1,0:T(8,128)}, u32[]{:S(2)}) copy-start(f32[256,2048]{1,0:T(8,128)} %plane_scatter.5) | copy-start | bytes 6291460
  794.4 2.3 copy-start.2
  794.4 2.8 copy-start.4
  794.4 2.8 copy-start.31
  803.7 1.7 copy-start.6
  805.3 7.3 copy-start.13
  805.3 49.1 %reduce-scatter.12.cloned.1.call-start = ((), (), s32[]{:S(2)}) async-start(), calls=%async_computation.10 | async-start | bytes 1310720 | tf_op jit(solution)/shard_map/reduce_scatter | solution.py:745
  812.2 76.0 %reduce-scatter.14.cloned.1.call-start = ((), (), s32[]{:S(2)}) async-start(), calls=%async_computation.11 | async-start | bytes 1720320 | tf_op jit(solution)/shard_map/reduce_scatter | solution.py:745
  818.8 2.3 copy-start.8
  820.0 119.0 %all-gather.9.cloned.1.call-start = ((), (), s32[]{:S(2)}) async-start(), calls=%async_computation.9 | async-start | bytes 6291456 | tf_op jit(solution)/shard_map/all_gather | solution.py:849
  898.4 8.1 copy-start.23
  934.2 2.4 copy-start.17
  934.2 3.6 copy-start.16
Sparse Core Ops, SparseCore 0:
  31.1 48.6 all-gather.10
  81.4 183.0 all-gather.12
  477.5 58.1 reduce-scatter.5
  537.9 65.9 reduce-scatter.7
  618.2 59.7 reduce-scatter.9
  805.4 17.6 all-gather.6
  826.0 28.3 reduce-scatter.11
  857.3 30.8 reduce-scatter.13
  890.4 12.5 all-gather.8

commit v3 on v2

--- a/solution.py
+++ b/solution.py
@@ -286,7 +286,9 @@
 
 
 MESH_ID = pl.DeviceIdType.MESH
-VMEM_LIMIT = 52 << 20
+VMEM_LIMIT = 58 << 20
+LANES = 128
+ROW_STEP = 32
 
 
 def nt_dot(a, b):
@@ -373,6 +375,7 @@
         c.start()
     local_copy = pltpu.make_async_copy(own_ref, mine, local_sem)
     local_copy.start()
+    yield
     from_x, from_y, from_d = out_ref.at[x_at, core], out_ref.at[y_at, core], out_ref.at[d_at, core]
     on_y = copy(from_x.at[lo], from_x.at[lo], yp)
     on_x = copy(from_y.at[hi], from_y.at[hi], xp)
@@ -404,26 +407,6 @@
     local_copy.wait()
 
 
-def gather_kernel(own_ref, out_ref, sems, local_sem):
-    greet_plane()
-    gather_steps(own_ref, out_ref, Sender(sems), local_sem)
-
-
-def plane_gather(own, cid):
-    m, width = own.shape
-    out = pl.pallas_call(
-        gather_kernel,
-        name="plane_gather",
-        out_shape=jax.ShapeDtypeStruct((4, 2, m, width), own.dtype),
-        in_specs=[pl.BlockSpec(memory_space=pltpu.VMEM)],
-        out_specs=pl.BlockSpec(memory_space=pl.ANY),
-        scratch_shapes=[pltpu.SemaphoreType.DMA((2, GATHER_COPIES)), pltpu.SemaphoreType.DMA],
-        compiler_params=pltpu.CompilerParams(collective_id=cid, has_side_effects=True),
-        cost_estimate=pl.CostEstimate(flops=0, bytes_accessed=own.size * 80, transcendentals=0),
-    )(own)
-    return out.reshape(8 * m, width)
-
-
 def scatter_steps(part_ref, out_ref, pair_ref, sum_ref, got_ref, copy):
     at, x_at, y_at, d_at, core = plane_places()
     half = part_ref.shape[2] // 2
@@ -433,6 +416,7 @@
     pairs = [copy(part_ref.at[to, 1 - core], pair_ref.at[j], sp) for j, to in enumerate(order)]
     for c in pairs:
         c.start()
+    yield
 
     def total(j, rows, *more):
         add_rows(
@@ -469,33 +453,6 @@
         c.wait_send()
 
 
-def scatter_kernel(part_ref, out_ref, pair_ref, sum_ref, got_ref, sems):
-    greet_plane()
-    scatter_steps(part_ref, out_ref, pair_ref, sum_ref, got_ref, Sender(sems))
-
-
-def plane_scatter(part, cid):
-    rows, width = part.shape
-    m = rows // 8
-    return pl.pallas_call(
-        scatter_kernel,
-        name="plane_scatter",
-        out_shape=jax.ShapeDtypeStruct((m, width), jnp.float32),
-        in_specs=[pl.BlockSpec(memory_space=pltpu.VMEM)],
-        out_specs=pl.BlockSpec(memory_space=pltpu.VMEM),
-        scratch_shapes=[
-            pltpu.VMEM((4, m, width), part.dtype),
-            pltpu.VMEM((3, m, width), part.dtype),
-            pltpu.VMEM((3, m, width), part.dtype),
-            pltpu.SemaphoreType.DMA((2, SCATTER_COPIES)),
-        ],
-        compiler_params=pltpu.CompilerParams(
-            collective_id=cid, has_side_effects=True, vmem_limit_bytes=VMEM_LIMIT
-        ),
-        cost_estimate=pl.CostEstimate(flops=0, bytes_accessed=part.size * 10, transcendentals=0),
-    )(part.reshape(4, 2, m, width))
-
-
 def exchange_kernel(axis, take, put, count, *refs):
     ins, outs, sems, local_sems = refs[:count], refs[count : 2 * count], refs[-2], refs[-1]
     size, me = lax.axis_size(axis), lax.axis_index(axis)
@@ -650,55 +607,712 @@
     )(normed, cot, weights)
 
 
-def to_whole_rows(x, rows, length, cid):
+def run(*steps):
+    for g in steps:
+        for _ in g:
+            pass
+
+
+def row_blocks(rows, step, body):
+    def inner(i, carry):
+        return body(pl.ds(pl.multiple_of(i * step, step), step), carry)
+
+    return lambda init: lax.fori_loop(0, rows // step, inner, init)
+
+
+def lanes(k):
+    return pl.ds(k * LANES, LANES)
+
+
+def seq_major_block(k):
+    plane, span = lax.axis_size("dp"), lax.axis_size("seq")
+    s, g = divmod(k, plane)
+    return g * span + s
+
+
+def mean_of(acc, width):
+    return jnp.sum(acc, axis=1, keepdims=True) * (1.0 / width)
+
+
+def kernel_call(body, name, cid, outs, ins, scratch, flops=0, moved=0):
+    params = dict(has_side_effects=True, vmem_limit_bytes=VMEM_LIMIT)
+    return pl.pallas_call(
+        body,
+        name=name,
+        out_shape=[jax.ShapeDtypeStruct(s, d) for s, d, _ in outs],
+        in_specs=[pl.BlockSpec(memory_space=m) for _, m in ins],
+        out_specs=[pl.BlockSpec(memory_space=m) for _, _, m in outs],
+        scratch_shapes=scratch,
+        compiler_params=pltpu.CompilerParams(collective_id=cid, **params),
+        cost_estimate=pl.CostEstimate(flops=flops, bytes_accessed=moved, transcendentals=0),
+    )(*[a for a, _ in ins])
+
+
+def copies(count):
+    return pltpu.SemaphoreType.DMA((2, count))
+
+
+def entry_kernel(
+    tokens_ref, cot_ref, small_ref, all_ref, x_ref, cot_own_ref, normed_ref, sems, local_sem
+):
+    greet_plane()
+    core = lax.axis_index("tensor")
+    m, width = x_ref.shape
+    blocks = width // LANES
+
+    def body(r, carry):
+        acc = jnp.zeros((ROW_STEP, LANES), jnp.float32)
+        for k in range(blocks):
+            source = lanes(seq_major_block(k))
+            v = tokens_ref[core, r, source]
+            x_ref[r, lanes(k)] = v
+            cot_own_ref[r, lanes(k)] = cot_ref[core, r, source]
+            v = v.astype(jnp.float32)
+            acc += v * v
+        scale = lax.rsqrt(mean_of(acc, width) + norm_epsilon)
+        for k in range(blocks):
+            v = x_ref[r, lanes(k)].astype(jnp.float32)
+            normed_ref[r, lanes(k)] = (v * scale * small_ref[k, 0:1, :]).astype(jnp.bfloat16)
+        return carry
+
+    row_blocks(m, ROW_STEP, body)(0)
+    run(gather_steps(normed_ref, all_ref, Sender(sems), local_sem))
+
+
+def entry(tokens, cot, small, cid):
+    cores, m, width = tokens.shape
+    whole = pltpu.VMEM
+    gathered, x, cot_own = kernel_call(
+        entry_kernel,
+        "entry",
+        cid,
+        [
+            ((4, cores, m, width), jnp.bfloat16, pl.ANY),
+            ((m, width), jnp.bfloat16, whole),
+            ((m, width), jnp.bfloat16, whole),
+        ],
+        [(tokens, whole), (cot, whole), (small, whole)],
+        [pltpu.VMEM((m, width), jnp.bfloat16), copies(GATHER_COPIES), pltpu.SemaphoreType.DMA],
+        moved=tokens.size * 40,
+    )
+    return gathered.reshape(-1, width), x, cot_own
+
+
+def head_mask(rows, head):
+    lane = lax.broadcasted_iota(jnp.int32, (rows, LANES), 1)
+    return (lane >= head * FDIM) & (lane < (head + 1) * FDIM)
+
+
+def keys_in_place(qkv_ref, keys_ref, vcols, qcols):
+    for j in range(qkv_ref.shape[0]):
+        tile = qkv_ref[j, :, pl.ds(vcols, LANES)].astype(jnp.float32)
+        keys_ref[j] = pltpu.roll(tile, LANES - qcols, axis=1).astype(jnp.bfloat16)
+
+
+def masked_weights(query, key, col_ref, row_ref, r, i, j, length):
+    a = nt_dot(query, key) * 0.25
+    t = lax.broadcasted_iota(jnp.int32, (length, length), 0) + i * length
+    s = lax.broadcasted_iota(jnp.int32, (length, length), 1) + j * length
+    keep = (s <= t) & (col_ref[r, i] == row_ref[r, j])
+    return a, jnp.where(keep, 1.0 + a + 0.5 * a * a, 0.0), keep
+
+
+def mix_kernel(
+    heads,
+    normed_ref,
+    pack_ref,
+    col_ref,
+    row_ref,
+    cot_ref,
+    qkv_ref,
+    mixed_ref,
+    exact_ref,
+    den_ref,
+    cot_all_ref,
+    out_qkv,
+    out_mixed,
+    keys_ref,
+    sems,
+    cot_sems,
+    local_sem,
+):
+    span, z = lax.axis_size("seq"), lax.axis_index("seq")
+    parts, _, depth = pack_ref.shape
+    tokens = qkv_ref.shape[1]
+    rows, length = col_ref.shape[0], col_ref.shape[2]
+    vcols, qcols = heads * VHEAD, heads * FDIM
+    at, x_at, y_at, _, core = plane_places()
+    peers = [lax.rem(z + k, span) for k in range(1, span)]
+    greet([{"dp": x_at}, {"dp": y_at}, {"tensor": 1 - core}] + [{"seq": p} for p in peers])
+    gather = gather_steps(cot_ref, cot_all_ref, Sender(cot_sems), local_sem)
+    next(gather)
+    copy = Sender(sems)
+
+    def project(dest, out):
+        x = pl.ds(pl.multiple_of(dest * tokens, tokens), tokens)
+        value = jnp.zeros((tokens, vcols), jnp.float32)
+        tile = jnp.zeros((tokens, LANES), jnp.float32)
+        for s in range(parts):
+            piece = normed_ref[x, pl.ds(s * depth, depth)]
+            value += nt_dot(piece, pack_ref[s, pl.ds(0, vcols)])
+            tile += nt_dot(piece, pack_ref[s, pl.ds(vcols, LANES)])
+        lane = lax.broadcasted_iota(jnp.int32, (tokens, LANES), 1)
+        out[:, pl.ds(0, vcols)] = value.astype(jnp.bfloat16)
+        out[:, pl.ds(vcols, LANES)] = jnp.where(lane < 2 * qcols, tile, 0.0).astype(jnp.bfloat16)
+
+    there = []
+    for k, p in enumerate(peers):
+        project(p, out_qkv.at[k])
+        there.append(copy(out_qkv.at[k], qkv_ref.at[z], {"seq": p}))
+        there[-1].start()
+    project(z, qkv_ref.at[z])
+    run(gather)
+    for c in there:
+        c.wait()
+    keys_in_place(qkv_ref, keys_ref, vcols, qcols)
+
+    def mixer(i, out):
+        def one_row(r, carry):
+            t = pl.ds(pl.multiple_of(r * length, length), length)
+            tile = qkv_ref[i, t, pl.ds(vcols, LANES)]
+            queries = [
+                jnp.where(head_mask(length, h), tile, jnp.zeros_like(tile)) for h in range(heads)
+            ]
+
+            def block(j, carry):
+                new = []
+                for h in range(heads):
+                    num, den = carry[h]
+                    _, w, _ = masked_weights(
+                        queries[h], keys_ref[j, t], col_ref, row_ref, r, i, j, length
+                    )
+                    value = qkv_ref[j, t, pl.ds(h * VHEAD, VHEAD)]
+                    new.append(
+                        (
+                            num + nn_dot(w.astype(jnp.bfloat16), value),
+                            den + jnp.sum(w, axis=1, keepdims=True),
+                        )
+                    )
+                return tuple(new)
+
+            zero = (
+                jnp.zeros((length, VHEAD), jnp.float32),
+                jnp.zeros((length, 1), jnp.float32),
+            )
+            done = lax.fori_loop(0, i + 1, block, (zero,) * heads)
+            lane = lax.broadcasted_iota(jnp.int32, (length, LANES), 1)
+            dens = jnp.zeros((length, LANES), jnp.float32)
+            for h, (num, den) in enumerate(done):
+                v = num / den
+                exact_ref[i, t, pl.ds(h * VHEAD, VHEAD)] = v
+                out[t, pl.ds(h * VHEAD, VHEAD)] = v.astype(jnp.bfloat16)
+                dens = jnp.where(lane == h, den, dens)
+            den_ref[i, t] = dens
+            return carry
+
+        lax.fori_loop(0, rows, one_row, 0)
+
+    back = []
+    for k, p in enumerate(peers):
+        mixer(p, out_mixed.at[k])
+        back.append(copy(out_mixed.at[k], mixed_ref.at[z], {"seq": p}))
+        back[-1].start()
+    mixer(z, mixed_ref.at[z])
+    for c in back:
+        c.wait()
+
+
+def mix(normed, pack, seg_col, seg_row, cot_own, heads, cid):
     span = lax.axis_size("seq")
-    width = x.shape[-1]
-    [x] = exchange(
-        [x.reshape(span, rows * length, width)], "seq", cid, [(span, rows * length, width)]
-    )
-    return x.reshape(span, rows, length, width).transpose(1, 0, 2, 3).reshape(
-        rows, span * length, width
-    )
-
-
-def from_whole_rows(x, rows, length, cid):
-    span = lax.axis_size("seq")
-    width = x.shape[-1]
-    x = x.reshape(rows, span, length, width).transpose(1, 0, 2, 3)
-    [x] = exchange(
-        [x.reshape(span, rows * length, width)], "seq", cid, [(span, rows * length, width)]
-    )
-    return x.reshape(span * rows * length, width)
-
-
-def attention_forward(queries, keys, values, segments):
-    length = queries.shape[1]
-    scores = jnp.einsum("rthf,rshf->rhts", queries, keys, preferred_element_type=jnp.float32) / 4.0
-    position = jnp.arange(length)
-    allowed = (position[None, :] <= position[:, None])[None] & (
-        segments[:, :, None] == segments[:, None, :]
-    )
-    weight = jnp.where(allowed[:, None], 1.0 + scores + 0.5 * scores * scores, 0.0)
-    den = jnp.sum(weight, axis=-1)
-    num = jnp.einsum(
-        "rhts,rshe->rhte", weight.astype(jnp.bfloat16), values, preferred_element_type=jnp.float32
-    )
-    return num / den[..., None], den, weight, scores, allowed
-
-
-def attention_backward(queries, keys, values, mixed, den, weight, scores, allowed, dmixed):
-    dn = jnp.transpose(dmixed, (0, 2, 1, 3)).astype(jnp.float32) / den[..., None]
-    dd = -jnp.sum(dn * mixed, axis=-1)
-    dn_low = dn.astype(jnp.bfloat16)
-    dw = jnp.einsum("rhte,rshe->rhts", dn_low, values, preferred_element_type=jnp.float32)
-    dw = jnp.where(allowed[:, None], dw + dd[..., None], 0.0)
-    dvalues = jnp.einsum(
-        "rhts,rhte->rshe", weight.astype(jnp.bfloat16), dn_low, preferred_element_type=jnp.float32
-    )
-    da = (dw * (1.0 + scores) * 0.25).astype(jnp.bfloat16)
-    dqueries = jnp.einsum("rhts,rshf->rthf", da, keys, preferred_element_type=jnp.float32)
-    dkeys = jnp.einsum("rhts,rthf->rshf", da, queries, preferred_element_type=jnp.float32)
-    return dqueries, dkeys, dvalues
+    tokens = normed.shape[0] // span
+    vcols = heads * VHEAD
+    m, width = cot_own.shape
+    whole = pltpu.VMEM
+    qkv, mixed, exact, den, cot = kernel_call(
+        partial(mix_kernel, heads),
+        "mix",
+        cid,
+        [
+            ((span, tokens, vcols + LANES), jnp.bfloat16, whole),
+            ((span, tokens, vcols), jnp.bfloat16, whole),
+            ((span, tokens, vcols), jnp.float32, whole),
+            ((span, tokens, LANES), jnp.float32, whole),
+            ((4, 2, m, width), jnp.bfloat16, pl.ANY),
+        ],
+        [(normed, whole), (pack, whole), (seg_col, whole), (seg_row, whole), (cot_own, whole)],
+        [
+            pltpu.VMEM((span - 1, tokens, vcols + LANES), jnp.bfloat16),
+            pltpu.VMEM((span - 1, tokens, vcols), jnp.bfloat16),
+            pltpu.VMEM((span, tokens, LANES), jnp.bfloat16),
+            copies(2 * (span - 1)),
+            copies(GATHER_COPIES),
+            pltpu.SemaphoreType.DMA,
+        ],
+        moved=normed.size * 40,
+    )
+    return qkv, mixed.reshape(-1, vcols), exact, den, cot.reshape(-1, width)
+
+
+def branch_kernel(
+    mixed_ref,
+    pack_ref,
+    x_ref,
+    small_ref,
+    residual_ref,
+    all_ref,
+    part_ref,
+    pair_ref,
+    sum_ref,
+    got_ref,
+    normed_ref,
+    sems,
+    gather_sems,
+    local_sem,
+):
+    greet_plane()
+    parts, _, depth = pack_ref.shape
+    m, width = x_ref.shape
+    vcols = mixed_ref.shape[1]
+    first = pack_ref.shape[1] - vcols
+
+    def project(b, carry):
+        left = mixed_ref[pl.ds(pl.multiple_of(b * m, m), m)]
+        for s in range(parts):
+            part_ref[b // 2, lax.rem(b, 2), :, pl.ds(s * depth, depth)] = nn_dot(
+                left, pack_ref[s, pl.ds(first, vcols)]
+            ).astype(jnp.bfloat16)
+        return carry
+
+    lax.fori_loop(0, 8, project, 0)
+    run(scatter_steps(part_ref, residual_ref, pair_ref, sum_ref, got_ref, Sender(sems)))
+
+    def body(r, carry):
+        acc = jnp.zeros((ROW_STEP, LANES), jnp.float32)
+        for k in range(width // LANES):
+            v = residual_ref[r, lanes(k)] + x_ref[r, lanes(k)].astype(jnp.float32)
+            residual_ref[r, lanes(k)] = v
+            acc += v * v
+        scale = lax.rsqrt(mean_of(acc, width) + norm_epsilon)
+        for k in range(width // LANES):
+            normed_ref[r, lanes(k)] = (
+                residual_ref[r, lanes(k)] * scale * small_ref[k, 1:2, :]
+            ).astype(jnp.bfloat16)
+        return carry
+
+    row_blocks(m, ROW_STEP, body)(0)
+    run(gather_steps(normed_ref, all_ref, Sender(gather_sems), local_sem))
+
+
+def scatter_scratch(m, width):
+    return [
+        pltpu.VMEM((4, m, width), jnp.bfloat16),
+        pltpu.VMEM((3, m, width), jnp.bfloat16),
+        pltpu.VMEM((3, m, width), jnp.bfloat16),
+    ]
+
+
+def branch(mixed, pack, x, small, cid):
+    m, width = x.shape
+    whole = pltpu.VMEM
+    residual, gathered = kernel_call(
+        branch_kernel,
+        "branch",
+        cid,
+        [((m, width), jnp.float32, whole), ((4, 2, m, width), jnp.bfloat16, pl.ANY)],
+        [(mixed, whole), (pack, whole), (x, whole), (small, whole)],
+        [pltpu.VMEM((4, 2, m, width), jnp.bfloat16)]
+        + scatter_scratch(m, width)
+        + [
+            pltpu.VMEM((m, width), jnp.bfloat16),
+            copies(SCATTER_COPIES),
+            copies(GATHER_COPIES),
+            pltpu.SemaphoreType.DMA,
+        ],
+        moved=x.size * 120,
+    )
+    return residual, gathered.reshape(-1, width)
+
+
+def norm_gradient(r, value_at, grad_ref, gain_at, gain_grad, finish, width):
+    squares = jnp.zeros((ROW_STEP, LANES), jnp.float32)
+    cross = jnp.zeros((ROW_STEP, LANES), jnp.float32)
+    for k in range(width // LANES):
+        v = value_at(r, k)
+        squares += v * v
+        cross += v * grad_ref[r, lanes(k)] * gain_at(k)
+    scale = lax.rsqrt(mean_of(squares, width) + norm_epsilon)
+    pull = mean_of(cross, width) * scale * scale * scale
+    for k in range(width // LANES):
+        v, g = value_at(r, k), grad_ref[r, lanes(k)]
+        gain_grad[:, lanes(k)] += jnp.sum(
+            (g * v * scale).reshape(ROW_STEP // 8, 8, LANES), axis=0
+        )
+        finish(r, k, scale * g * gain_at(k) - v * pull)
+
+
+def middle_kernel(
+    part_ref,
+    residual_ref,
+    cot_ref,
+    small_ref,
+    dresid_ref,
+    gain_ref,
+    all_ref,
+    pair_ref,
+    sum_ref,
+    got_ref,
+    low_ref,
+    sems,
+    gather_sems,
+    local_sem,
+):
+    greet_plane()
+    m, width = residual_ref.shape
+    run(scatter_steps(part_ref, dresid_ref, pair_ref, sum_ref, got_ref, Sender(sems)))
+    gain_ref[...] = jnp.zeros_like(gain_ref)
+
+    def finish(r, k, v):
+        v += cot_ref[r, lanes(k)].astype(jnp.float32)
+        dresid_ref[r, lanes(k)] = v
+        low_ref[r, lanes(k)] = v.astype(jnp.bfloat16)
+
+    def body(r, carry):
+        norm_gradient(
+            r,
+            lambda r, k: residual_ref[r, lanes(k)],
+            dresid_ref,
+            lambda k: small_ref[k, 1:2, :],
+            gain_ref,
+            finish,
+            width,
+        )
+        return carry
+
+    row_blocks(m, ROW_STEP, body)(0)
+    run(gather_steps(low_ref, all_ref, Sender(gather_sems), local_sem))
+
+
+def middle(part, residual, cot_own, small, cid):
+    m, width = residual.shape
+    whole = pltpu.VMEM
+    dresid, gain, gathered = kernel_call(
+        middle_kernel,
+        "middle",
+        cid,
+        [
+            ((m, width), jnp.float32, whole),
+            ((8, width), jnp.float32, whole),
+            ((4, 2, m, width), jnp.bfloat16, pl.ANY),
+        ],
+        [
+            (part.reshape(4, 2, m, width), whole),
+            (residual, whole),
+            (cot_own, whole),
+            (small, whole),
+        ],
+        scatter_scratch(m, width)
+        + [
+            pltpu.VMEM((m, width), jnp.bfloat16),
+            copies(SCATTER_COPIES),
+            copies(GATHER_COPIES),
+            pltpu.SemaphoreType.DMA,
+        ],
+        moved=residual.size * 120,
+    )
+    return dresid, gain, gathered.reshape(-1, width)
+
+
+def unmix_kernel(
+    heads,
+    dresid_ref,
+    pack_ref,
+    col_ref,
+    row_ref,
+    qkv_ref,
+    exact_ref,
+    den_ref,
+    part_ref,
+    residual_ref,
+    dqkv_ref,
+    block_ref,
+    out_dmixed,
+    dmixed_ref,
+    out_dqkv,
+    keys_ref,
+    dtile_ref,
+    dkey_ref,
+    dvalue_ref,
+    total_ref,
+    pair_ref,
+    sum_ref,
+    got_ref,
+    sems,
+    scatter_sems,
+):
+    span, z = lax.axis_size("seq"), lax.axis_index("seq")
+    parts, _, depth = pack_ref.shape
+    tokens = qkv_ref.shape[1]
+    rows, length = col_ref.shape[0], col_ref.shape[2]
+    vcols, qcols = heads * VHEAD, heads * FDIM
+    first = pack_ref.shape[1] - vcols
+    at, x_at, y_at, _, core = plane_places()
+    peers = [lax.rem(z + k, span) for k in range(1, span)]
+    greet([{"dp": x_at}, {"dp": y_at}, {"tensor": 1 - core}] + [{"seq": p} for p in peers])
+    scatter = scatter_steps(part_ref, total_ref, pair_ref, sum_ref, got_ref, Sender(scatter_sems))
+    next(scatter)
+    copy = Sender(sems)
+
+    def project(dest, out):
+        x = pl.ds(pl.multiple_of(dest * tokens, tokens), tokens)
+        total = jnp.zeros((tokens, vcols), jnp.float32)
+        for s in range(parts):
+            total += nt_dot(
+                dresid_ref[x, pl.ds(s * depth, depth)], pack_ref[s, pl.ds(first, vcols)]
+            )
+        out[...] = total.astype(jnp.bfloat16)
+
+    there = []
+    for k, p in enumerate(peers):
+        project(p, out_dmixed.at[k])
+        there.append(copy(out_dmixed.at[k], dmixed_ref.at[z], {"seq": p}))
+        there[-1].start()
+    project(z, dmixed_ref.at[z])
+    keys_in_place(qkv_ref, keys_ref, vcols, qcols)
+    dkey_ref[...] = jnp.zeros_like(dkey_ref)
+    dvalue_ref[...] = jnp.zeros_like(dvalue_ref)
+    run(scatter)
+
+    def finish(r, carry):
+        block_ref[r] = (residual_ref[r] + total_ref[r]).astype(jnp.bfloat16)
+        return carry
+
+    row_blocks(block_ref.shape[0], ROW_STEP, finish)(0)
+    for c in there:
+        c.wait()
+
+    def one_block(step, carry):
+        r, i = step // span, lax.rem(step, span)
+        t = pl.ds(pl.multiple_of(r * length, length), length)
+        tile = qkv_ref[i, t, pl.ds(vcols, LANES)]
+        dtile = jnp.zeros((length, LANES), jnp.float32)
+        for h in range(heads):
+            inside = head_mask(length, h)
+            v = pl.ds(h * VHEAD, VHEAD)
+            query = jnp.where(inside, tile, jnp.zeros_like(tile))
+            dn = dmixed_ref[i, t, v].astype(jnp.float32) / den_ref[i, t, pl.ds(h, 1)]
+            dd = -jnp.sum(dn * exact_ref[i, t, v], axis=1, keepdims=True)
+            dn_low = dn.astype(jnp.bfloat16)
+
+            def block(j, dquery, query=query, v=v, dn_low=dn_low, dd=dd, inside=inside):
+                key = keys_ref[j, t]
+                a, w, keep = masked_weights(query, key, col_ref, row_ref, r, i, j, length)
+                dw = jnp.where(keep, nt_dot(dn_low, qkv_ref[j, t, v]) + dd, 0.0)
+                da = (dw * (1.0 + a) * 0.25).astype(jnp.bfloat16)
+                dvalue_ref[j, t, v] += tn_dot(w.astype(jnp.bfloat16), dn_low)
+                dkey_ref[j, t] += jnp.where(inside, tn_dot(da, query), 0.0)
+                return dquery + nn_dot(da, key)
+
+            dquery = lax.fori_loop(0, i + 1, block, jnp.zeros((length, LANES), jnp.float32))
+            dtile += jnp.where(inside, dquery, 0.0)
+        dtile_ref[i, t] = dtile
+        return carry
+
+    lax.fori_loop(0, rows * span, one_block, 0)
+
+    def pack(i, out):
+        out[:, pl.ds(0, vcols)] = dvalue_ref[i].astype(jnp.bfloat16)
+        out[:, pl.ds(vcols, LANES)] = (
+            dtile_ref[i] + pltpu.roll(dkey_ref[i], qcols, axis=1)
+        ).astype(jnp.bfloat16)
+
+    back = []
+    for k, p in enumerate(peers):
+        pack(p, out_dqkv.at[k])
+        back.append(copy(out_dqkv.at[k], dqkv_ref.at[z], {"seq": p}))
+        back[-1].start()
+    pack(z, dqkv_ref.at[z])
+    for c in back:
+        c.wait()
+
+
+def unmix(dresid_low, pack, seg_col, seg_row, qkv, exact, den, part, residual, heads, cid):
+    span, tokens, wide = qkv.shape
+    vcols = heads * VHEAD
+    m, width = residual.shape
+    whole = pltpu.VMEM
+    ins = (dresid_low, pack, seg_col, seg_row, qkv, exact, den, part.reshape(4, 2, m, width), residual)
+    dqkv, block = kernel_call(
+        partial(unmix_kernel, heads),
+        "unmix",
+        cid,
+        [((span, tokens, wide), jnp.bfloat16, whole), ((m, width), jnp.bfloat16, whole)],
+        [(a, whole) for a in ins],
+        [
+            pltpu.VMEM((span - 1, tokens, vcols), jnp.bfloat16),
+            pltpu.VMEM((span, tokens, vcols), jnp.bfloat16),
+            pltpu.VMEM((span - 1, tokens, wide), jnp.bfloat16),
+            pltpu.VMEM((span, tokens, LANES), jnp.bfloat16),
+            pltpu.VMEM((span, tokens, LANES), jnp.float32),
+            pltpu.VMEM((span, tokens, LANES), jnp.float32),
+            pltpu.VMEM((span, tokens, vcols), jnp.float32),
+            pltpu.VMEM((m, width), jnp.float32),
+        ]
+        + scatter_scratch(m, width)
+        + [copies(2 * (span - 1)), copies(SCATTER_COPIES)],
+        moved=residual.size * 160,
+    )
+    return dqkv.reshape(-1, wide), block
+
+
+def everyone():
+    plane, span, cores = (lax.axis_size(a) for a in ("dp", "seq", "tensor"))
+    at, z, core = (lax.axis_index(a) for a in ("dp", "seq", "tensor"))
+    others = [
+        {
+            "dp": lax.rem(at + i, plane),
+            "seq": lax.rem(z + k, span),
+            "tensor": lax.rem(core + c, cores),
+        }
+        for k in range(span)
+        for i in range(plane)
+        for c in range(cores)
+        if i or k or c
+    ]
+    return others, (at * span + z) * cores + core
+
+
+def exit_kernel(
+    dqkv_ref,
+    pack_ref,
+    x_ref,
+    dresid_ref,
+    block_ref,
+    small_ref,
+    gain_two_ref,
+    grad_ref,
+    out_ref,
+    gains_ref,
+    gain_ref,
+    out_gain,
+    got_gain,
+    part_ref,
+    total_ref,
+    ordered_ref,
+    low_ref,
+    pair_ref,
+    sum_ref,
+    got_ref,
+    sems,
+    pair_sems,
+    gain_sems,
+    local_sems,
+):
+    others, me = everyone()
+    greet(others)
+    core = lax.axis_index("tensor")
+    plane, span = lax.axis_size("dp"), lax.axis_size("seq")
+    parts, _, depth = pack_ref.shape
+    m, width = x_ref.shape
+    wide = dqkv_ref.shape[1] - LANES + 2 * FDIM * ((dqkv_ref.shape[1] - LANES) // VHEAD)
+    blocks = width // LANES
+    copy = Sender(pair_sems)
+
+    def project(b, carry):
+        left = dqkv_ref[pl.ds(pl.multiple_of(b * m, m), m), pl.ds(0, wide)]
+        for s in range(parts):
+            part_ref[b // 2, lax.rem(b, 2), :, pl.ds(s * depth, depth)] = nn_dot(
+                left, pack_ref[s, pl.ds(0, wide)]
+            ).astype(jnp.bfloat16)
+        return carry
+
+    lax.fori_loop(0, 8, project, 0)
+    scatter = scatter_steps(part_ref, total_ref, pair_ref, sum_ref, got_ref, Sender(sems))
+    next(scatter)
+
+    def order(r, carry):
+        for k in range(blocks):
+            low_ref[r, lanes(seq_major_block(k))] = block_ref[r, lanes(k)]
+        return carry
+
+    row_blocks(m, ROW_STEP, order)(0)
+    to_pair = [copy(low_ref, out_ref.at[core], {"tensor": 1 - core})]
+    local = [pltpu.make_async_copy(low_ref, out_ref.at[core], local_sems.at[0])]
+    to_pair[0].start()
+    local[0].start()
+    run(scatter)
+    gain_ref[...] = jnp.zeros_like(gain_ref)
+
+    def finish(r, k, v):
+        ordered_ref[r, lanes(seq_major_block(k))] = v + dresid_ref[r, lanes(k)]
+
+    def body(r, carry):
+        norm_gradient(
+            r,
+            lambda r, k: x_ref[r, lanes(k)].astype(jnp.float32),
+            total_ref,
+            lambda k: small_ref[k, 0:1, :],
+            gain_ref,
+            finish,
+            width,
+        )
+        return carry
+
+    row_blocks(m, ROW_STEP, body)(0)
+    to_pair.append(copy(ordered_ref, grad_ref.at[core], {"tensor": 1 - core}))
+    local.append(pltpu.make_async_copy(ordered_ref, grad_ref.at[core], local_sems.at[1]))
+    to_pair[1].start()
+    local[1].start()
+    out_gain[...] = jnp.zeros_like(out_gain)
+    for k in range(blocks):
+        for row, ref in enumerate((gain_ref, gain_two_ref)):
+            out_gain[k, row : row + 1] = jnp.sum(ref[:, lanes(k)], axis=0, keepdims=True)
+    copy_gain = Sender(gain_sems)
+    for p in others:
+        block = out_gain.at[p["seq"] * plane + p["dp"], pl.ds(0, 8)]
+        to_pair.append(copy_gain(block, got_gain.at[me], p))
+        to_pair[-1].start()
+    mine = lax.axis_index("seq") * plane + lax.axis_index("dp")
+    got_gain[me] = out_gain[mine]
+    for c in to_pair + local:
+        c.wait()
+    total = got_gain[0]
+    for k in range(1, len(others) + 1):
+        total += got_gain[k]
+    gains_ref[...] = total
+
+
+def leave(dqkv, pack, x, dresid, block, small, gain_two, cid):
+    m, width = x.shape
+    devices = lax.axis_size(("dp", "seq", "tensor"))
+    whole = pltpu.VMEM
+    return kernel_call(
+        exit_kernel,
+        "leave",
+        cid,
+        [
+            ((2, m, width), jnp.float32, pl.ANY),
+            ((2, m, width), jnp.bfloat16, pl.ANY),
+            ((8, LANES), jnp.float32, whole),
+        ],
+        [(a, whole) for a in (dqkv, pack, x, dresid, block, small, gain_two)],
+        [
+            pltpu.VMEM((8, width), jnp.float32),
+            pltpu.VMEM((width // LANES, 8, LANES), jnp.float32),
+            pltpu.VMEM((devices, 8, LANES), jnp.float32),
+            pltpu.VMEM((4, 2, m, width), jnp.bfloat16),
+            pltpu.VMEM((m, width), jnp.float32),
+            pltpu.VMEM((m, width), jnp.float32),
+            pltpu.VMEM((m, width), jnp.bfloat16),
+        ]
+        + scatter_scratch(m, width)
+        + [
+            copies(SCATTER_COPIES),
+            copies(2),
+            copies(devices - 1),
+            pltpu.SemaphoreType.DMA((2,)),
+        ],
+        moved=x.size * 120,
+    )
 
 
 def plane_local(
@@ -724,22 +1338,8 @@
     vcols, qcols = heads * VHEAD, heads * FDIM
     all_rows = rows * plane // span
 
-    def seq_major(a):
-        return (
-            a.reshape(a.shape[:-1] + (plane, span, chunk)).swapaxes(-3, -2).reshape(a.shape)
-        )
-
-    def plane_major(a):
-        return (
-            a.reshape(a.shape[:-1] + (span, plane, chunk)).swapaxes(-3, -2).reshape(a.shape)
-        )
-
-    core = lax.axis_index("tensor")
     def over_seq(pack):
         return lax.all_gather(pack, "seq", axis=0, tiled=False)
-
-    def flat(pack):
-        return pack.transpose(1, 0, 2).reshape(-1, width)
 
     def summed(grads):
         return lax.psum_scatter(
@@ -773,35 +1373,18 @@
         [ffn_pack], "dp", 2, [(ffn_pack.shape[1], plane * chunk)], put=columns_of
     )
     attn_pack, ffn_pack = over_seq(attn_pack), over_seq(ffn_pack)
-    gain_one = small[:, 0].reshape(width)
-    gain_two = small[:, 1].reshape(width)
     starts = small[:, 2:-2].reshape(span, plane * rows, length)
     starts = lax.dynamic_slice_in_dim(starts, lax.axis_index("seq") * all_rows, all_rows, 1)
     segments = jnp.cumsum(starts.transpose(1, 0, 2).reshape(all_rows, span * length), axis=1)
 
     qkv_rows = vcols + 2 * qcols
-    w_qkv, w_out = flat(attn_pack[:, :qkv_rows]), flat(attn_pack[:, qkv_rows:])
-
-    def mine(a):
-        a = lax.dynamic_slice_in_dim(a.reshape(rows * length, width), core * own, own, 0)
-        return seq_major(a)
-
-    x = mine(tokens).astype(jnp.float32)
-    cot_own = mine(cotangent)
-    scale_one = inverse_rms(x)
-    normed_one = plane_gather((x * scale_one * gain_one).astype(jnp.bfloat16), 3)
-    cot = plane_gather(cot_own, 4)
-    qkv = nt_dot(normed_one, w_qkv).astype(jnp.bfloat16)
-    qkv = to_whole_rows(qkv, all_rows, length, 5)
-    values = qkv[..., :vcols].reshape(all_rows, -1, heads, VHEAD)
-    queries = qkv[..., vcols : vcols + qcols].reshape(all_rows, -1, heads, FDIM)
-    keys = qkv[..., vcols + qcols :].reshape(all_rows, -1, heads, FDIM)
-    mixed, den, weight, scores, allowed = attention_forward(queries, keys, values, segments)
-    mixed_low = mixed.transpose(0, 2, 1, 3).reshape(all_rows, -1, vcols).astype(jnp.bfloat16)
-    mixed_low = from_whole_rows(mixed_low, all_rows, length, 6)
-    residual = x + plane_scatter(nn_dot(mixed_low, w_out).astype(jnp.bfloat16), 7)
-    scale_two = inverse_rms(residual)
-    normed_two = plane_gather((residual * scale_two * gain_two).astype(jnp.bfloat16), 11)
+    seg_col = segments.reshape(all_rows, span, length, 1)
+    seg_row = segments.reshape(all_rows, span, 1, length)
+    normed_one, x, cot_own = entry(
+        tokens.reshape(cores, own, width), cotangent.reshape(cores, own, width), small, 3
+    )
+    qkv, mixed, exact, den, cot = mix(normed_one, attn_pack, seg_col, seg_row, cot_own, heads, 4)
+    residual, normed_two = branch(mixed, attn_pack, x, small, 5)
     out_part, dnormed_part, dgate, dup, hidden = ffn(normed_two, cot, ffn_pack)
     down_grad = tn_dot(hidden, cot).astype(jnp.bfloat16)
     gate_grad = tn_dot(dgate, normed_two).astype(jnp.bfloat16)
@@ -810,52 +1393,33 @@
         (dnormed_part, gate_grad, up_grad, down_grad)
     )
     down_grad, gate_grad, up_grad = summed(down_grad), summed(gate_grad), summed(up_grad)
-    dnormed_two = plane_scatter(dnormed_part, 9)
-    dresid, gain_two_grad = norm_backward(residual, scale_two, gain_two, dnormed_two)
-    dresid = dresid + cot_own.astype(jnp.float32)
-    dresid_low = plane_gather(dresid.astype(jnp.bfloat16), 12)
-    block_own = (residual + plane_scatter(out_part, 8)).astype(jnp.bfloat16)
-    dmixed = nt_dot(dresid_low, w_out).astype(jnp.bfloat16)
-    dmixed = to_whole_rows(dmixed, all_rows, length, 13).reshape(all_rows, -1, heads, VHEAD)
-    dqueries, dkeys, dvalues = attention_backward(
-        queries, keys, values, mixed, den, weight, scores, allowed, dmixed
-    )
-    dqkv = jnp.concatenate(
-        [
-            d.reshape(all_rows, span * length, -1).astype(jnp.bfloat16)
-            for d in (dvalues, dqueries, dkeys)
-        ],
-        axis=-1,
-    )
-    dqkv = from_whole_rows(dqkv, all_rows, length, 14)
-    dnormed_one = plane_scatter(nn_dot(dqkv, w_qkv).astype(jnp.bfloat16), 10)
-    out_grad = summed(tn_dot(mixed_low, dresid_low))
-    qkv_grad = tn_dot(dqkv, normed_one)
-    dtokens, gain_one_grad = norm_backward(x, scale_one, gain_one, dnormed_one)
-    dtokens = dresid + dtokens
-    gain_grads = jnp.stack([gain_one_grad, gain_two_grad])
-    qkv_grad = summed(
-        jnp.concatenate([qkv_grad, jnp.pad(gain_grads, ((0, 14), (0, 0)))], axis=0)
+    dresid, gain_two_grad, dresid_low = middle(dnormed_part, residual, cot_own, small, 6)
+    dresid_low, down_grad = lax.optimization_barrier((dresid_low, down_grad))
+    dqkv, block_own = unmix(
+        dresid_low, attn_pack, seg_col, seg_row, qkv, exact, den, out_part, residual, heads, 7
+    )
+    out_grad = tn_dot(mixed, dresid_low).astype(jnp.bfloat16)
+    qkv_grad = tn_dot(dqkv, normed_one)[:qkv_rows].astype(jnp.bfloat16)
+    dqkv, out_grad, qkv_grad, gate_grad, up_grad = lax.optimization_barrier(
+        (dqkv, out_grad, qkv_grad, gate_grad, up_grad)
+    )
+    out_grad, qkv_grad = summed(out_grad), summed(qkv_grad)
+    dtokens, block_out, gain_grads = leave(
+        dqkv, attn_pack, x, dresid, block_own, small, gain_two_grad, 8
     )
     down_grad, gate_grad, up_grad, dtokens = lax.optimization_barrier(
         (down_grad, gate_grad, up_grad, dtokens)
     )
-    down_grad, gate_grad, up_grad = collect([down_grad, gate_grad, up_grad], 15)
-    out_grad, qkv_grad = collect([out_grad, qkv_grad], 16)
-    gain_grads = qkv_grad[:, qkv_rows : qkv_rows + 2].astype(jnp.float32).sum(axis=0)
-    gain_grads = lax.psum(gain_grads, "tensor")
-
-    def whole(a):
-        a = lax.all_gather(plane_major(a), "tensor", axis=0, tiled=True)
-        return a.reshape(rows, length, width)
+    down_grad, gate_grad, up_grad = collect([down_grad, gate_grad, up_grad], 9)
+    out_grad, qkv_grad = collect([out_grad, qkv_grad], 10)
 
     def stacked(a, start, size):
         return a[:, start : start + size].reshape(plane * size, chunk).astype(jnp.float32)
 
     h = hidden_part
     return (
-        whole(block_own),
-        whole(dtokens),
+        block_out.reshape(rows, length, width),
+        dtokens.reshape(rows, length, width),
         gain_grads[0],
         gain_grads[1],
         stacked(qkv_grad, vcols, qcols).T,

time: 962 us -> 782 us (0.81)
  matrix products: 116 us -> 45 us
  local copies, waits for them, and re-layouts: 73.6 us -> 15.6 us
  waiting for transfers between devices: 58.4 us -> 1.89 us
  Pallas kernels: 644 us -> 683 us
  other arithmetic: 41.2 us -> 14.1 us
    pallas_call x8 -> x6, Pallas kernels: 342 us -> 553 us  [kernel_call(): pl.pallas_call(body, name=name, out_shape=[jax.ShapeDtypeStruct(s, d) for...]
    pallas_call x7 -> x3, Pallas kernels: 235 us -> 63.3 us  [exchange(): pl.pallas_call(partial(exchange_kernel, axis, take, put, count), name='ex...]
    dot_general x10 -> x0, matrix products: 71.4 us -> none  [the longest x2 16.4 us: nn_dot(): lax.dot_general(a, b, (((1,), (0,)), ((), ())), preferred_element_type=jn...]
    reduce_scatter x5, waiting for transfers between devices: 57.9 us -> 0.03 us  [summed(): lax.psum_scatter(grads.astype(jnp.bfloat16), 'seq', scatter_dimension=1,...]
    convert_element_type x13 -> x0, local copies, waits for them, and re-layouts: 22.6 us -> none  [the longest x6 7.48 us: plane_local(): d.reshape(all_rows, span * length, -1).astype(jnp.bfloat16)]
    unnamed x74 -> x22, local copies, waits for them, and re-layouts: 20.6 us -> 3.92 us
    reshape x7 -> x0, local copies, waits for them, and re-layouts: 16.7 us -> none  [the longest x4 8.64 us: plane_major(): a.reshape(a.shape[:-1] + (span, plane, chunk)).swapaxes(-3, -2)]
    reduce_sum x6 -> x0, other arithmetic: 10.3 us -> none  [the longest x2 4.65 us: norm_backward(): grad_gain = jnp.sum(grad_normed * inputs * scale_row, axis=0)]
  transfers between devices with their start and end apart: 9 -> 7, of which waited for: 2 -> 0; matrix products, arithmetic and copies ran while one was open for 19% -> 3% of each run, Pallas kernels for 61% -> 78%
where the time goes in v3:
time: 782 us; the launch traced here: 775 us
  Pallas kernels  683 us (87%)
  matrix products  45 us (6%)
  local copies, waits for them, and re-layouts  15.6 us (2%)
  between operations  14.9 us (2%)
  other arithmetic  14.1 us (2%)
    pallas_call x6, Pallas kernels, kernel_call(): pl.pallas_call(body, name=name, out_shape=[jax.ShapeDtypeStruct(s, d) for...  553 us
    pallas_call x3, Pallas kernels, exchange(): pl.pallas_call(partial(exchange_kernel, axis, take, put, count), name='ex...  63.3 us
    pallas_call x1, Pallas kernels, ffn(): pl.pallas_call(ffn_kernel, name='ffn', grid=(tokens // block,), out_shape...  49.8 us
    dot_general x5, matrix products, tn_dot(): lax.dot_general(a, b, (((0,), (0,)), ((), ())), preferred_element_type=jn...  45 us
    pallas_call x1, Pallas kernels, first_exchange(): pl.pallas_call(first_kernel, name='first_exchange', out_shape=[jax.ShapeD...  16.7 us
  transfers between devices with their start and end apart: 7, of which 0 were waited for; matrix products, arithmetic and copies ran while one was open for 3% of the time, Pallas kernels for 78%

profile of v3, /device:TPU:0, one launch (start us, length us, event | category | flops | bytes accessed | tf_op | source)
XLA Modules:
  0.0 774.5 jit_solution(8758224856404225426)
XLA Ops:
  7.2 0.0 all-gather.5.cloned.1.call-start
  7.3 0.8 convert_element_type.50
  8.1 0.9 copy.31
  9.0 0.9 copy.32
  9.8 1.1 copy.30
  11.0 0.1 pad.6.clone
  11.1 0.7 bitcast_convert_fusion.5
  11.8 0.7 maximum_maximum_fusion.small_ref
  12.4 1.8 pad_maximum_fusion.1.pack_ref
  14.2 16.7 %first_exchange.1 = (bf16[576,512]{1,0:T(8,128)(2,1)}, f32[16,8,128]{2,1,0:T(8,128)}) custom-call(bf16[4,576,128]{2,1,0:T(8,128)(2,1)} %pad_maximum_fusion.1.pack_ref, f32[8,128]{1,0:T(8,128)} %maximum_maximum_fusion.small_ref), custom_call_target="tpu_custom_call" | custom-call | bytes 17694720 | tf_op jit(solution)/shard_map/first_exchange/pallas_call | solution.py:533
  30.9 0.0 all-gather.5.cloned.1.call-update
  31.0 0.0 all-gather.7.cloned.1.call-start
  31.1 1.5 pad_maximum_fusion.refs_0_
  32.5 26.6 %exchange_dp.3 = bf16[2064,512]{1,0:T(8,128)(2,1)} custom-call(bf16[4,2064,128]{2,1,0:T(8,128)(2,1)} %pad_maximum_fusion.refs_0_), custom_call_target="tpu_custom_call" | custom-call | bytes 63406080 | tf_op jit(solution)/shard_map/exchange_dp/pallas_call | solution.py:485
  59.1 0.0 all-gather.7.cloned.1.call-update
  59.1 0.0 reduce-scatter.6.cloned.1.call-start
  59.2 0.0 copy-done.3
  59.3 0.6 reduce-window.6
  59.9 0.2 slice_reduce_fusion
  60.0 0.2 reduce-window.9
  60.2 0.1 broadcast_add_fusion
  60.3 1.9 reduce_window_sum.34.col_ref
  62.1 43.4 %entry.1 = (bf16[4,2,256,2048]{3,2,1,0:T(8,128)(2,1)}, bf16[256,2048]{1,0:T(8,128)(2,1)}, bf16[256,2048]{1,0:T(8,128)(2,1)}) custom-call(bf16[2,256,2048]{2,1,0:T(8,128)(2,1)} %tokens_ref.1, bf16[2,256,2048]{2,1,0:T(8,128)(2,1)} %cot_ref.1, f32[16,8,128]{2,1,0:T(8,128)} %get-tuple-element.57.small_ref), custom_call_target="tpu_custom_call" | custom-call | bytes 41943040 | tf_op jit(solution)/shard_map/entry/pallas_call | solution.py:639
  105.6 0.0 all-gather.5.cloned.1.call-done
  105.6 130.1 %mix.1 = (bf16[4,512,384]{2,1,0:T(8,128)(2,1)}, bf16[4,512,256]{2,1,0:T(8,128)(2,1)}, f32[4,512,256]{2,1,0:T(8,128)}, f32[4,512,128]{2,1,0:T(8,128)}, bf16[4,2,256,2048]{3,2,1,0:T(8,128)(2,1)}) custom-call(bf16[2048,2048]{1,0:T(8,128)(2,1)} %bitcast.82, bf16[4,576,512]{2,1,0:T(8,128)(2,1)} %bitcast.78, f32[2,4,256,1]{3,2,1,0:T(8,128)} %reduce_window_sum.34.col_ref, ...), custom_call_target="tpu_custom_call" | custom-call | bytes 167772160 | tf_op jit(solution)/shard_map/mix/pallas_call | solution.py:639
  235.7 87.5 %branch.1 = (f32[256,2048]{1,0:T(8,128)}, bf16[4,2,256,2048]{3,2,1,0:T(8,128)(2,1)}) custom-call(bf16[2048,256]{1,0:T(8,128)(2,1)} %bitcast.86, bf16[4,576,512]{2,1,0:T(8,128)(2,1)} %bitcast.79, bf16[256,2048]{1,0:T(8,128)(2,1)} %get-tuple-element.62.x_ref, f32[16,8,128]{2,1,0:T(8,128)} %get-tuple-element.57.small_ref), custom_call_target="tpu_custom_call" | custom-call | bytes 62914560 | tf_op jit(solution)/shard_map/branch/pallas_call | solution.py:639
  323.2 0.0 all-gather.7.cloned.1.call-done
  323.2 49.8 %ffn.1 = (bf16[2048,2048]{1,0:T(8,128)(2,1)}, bf16[2048,2048]{1,0:T(8,128)(2,1)}, bf16[2048,688]{1,0:T(8,128)(2,1)}, bf16[2048,688]{1,0:T(8,128)(2,1)}, bf16[2048,688]{1,0:T(8,128)(2,1)}) custom-call(bf16[2048,2048]{1,0:T(8,128)(2,1)} %bitcast.107, bf16[2048,2048]{1,0:T(8,128)(2,1)} %bitcast.110, bf16[4,2064,512]{2,1,0:T(8,128)(2,1)} %bitcast.106), custom_call_target="tpu_custom_call" | custom-call | flops 34628173824 | bytes 50462720 | tf_op jit(solution)/shard_map/ffn/pallas_call | solution.py:589
  373.0 10.6 %convolution_convert_fusion = bf16[688,2048]{1,0:T(8,128)(2,1)} fusion(bf16[2048,688]{1,0:T(8,128)(2,1)} %get-tuple-element.69, bf16[2048,2048]{1,0:T(8,128)(2,1)} %bitcast.111), kind=kOutput, calls=%fused_computation | convolution fusion | flops 5772771328 | bytes 14024704 | tf_op jit(solution)/shard_map/dot_general | solution.py:299
  383.6 10.6 %convolution_convert_fusion.2 = bf16[688,2048]{1,0:T(8,128)(2,1)} fusion(bf16[2048,688]{1,0:T(8,128)(2,1)} %get-tuple-element.67, bf16[2048,2048]{1,0:T(8,128)(2,1)} %bitcast.108), kind=kOutput, calls=%fused_computation.2 | convolution fusion | flops 5772771328 | bytes 14024704 | tf_op jit(solution)/shard_map/dot_general | solution.py:299
  394.2 0.0 copy-done.9
  394.2 9.7 %convolution_convert_fusion.1 = bf16[688,2048]{1,0:T(8,128)(2,1)} fusion(bf16[2048,688]{1,0:T(8,128)(2,1)S(1)} %copy-done.9, bf16[2048,2048]{1,0:T(8,128)(2,1)} %bitcast.109), kind=kOutput, calls=%fused_computation.1 | convolution fusion | flops 5772771328 | bytes 14024704 | tf_op jit(solution)/shard_map/dot_general | solution.py:299
  404.0 0.0 reduce-scatter.6.cloned.1.call-update
  404.0 0.0 reduce-scatter.8.cloned.1.call-start
  404.0 0.5 reduce-scatter.8.cloned.1.call-update
  404.6 0.0 reduce-scatter.10.cloned.1.call-start
  404.6 0.5 reduce-scatter.10.cloned.1.call-update
  405.2 0.0 reduce-scatter.12.cloned.1.call-start
  405.2 86.1 %middle.1 = (f32[256,2048]{1,0:T(8,128)}, f32[8,2048]{1,0:T(8,128)}, bf16[4,2,256,2048]{3,2,1,0:T(8,128)(2,1)}) custom-call(bf16[4,2,256,2048]{3,2,1,0:T(8,128)(2,1)} %bitcast.85, f32[256,2048]{1,0:T(8,128)} %get-tuple-element.71.residual_ref, bf16[256,2048]{1,0:T(8,128)(2,1)} %get-tuple-element.60.cot_ref, f32[16,8,128]{2,1,0:T(8,128)} %get-tuple-element.57.small_ref), custom_call_target="tpu_custom_call" | custom-call | bytes 62914560 | tf_op jit(solution)/shard_map/middle/pallas_call | solution.py:639
  491.3 0.0 reduce-scatter.6.cloned.1.call-done.refs_0_
  491.3 137.2 %unmix.1 = (bf16[4,512,384]{2,1,0:T(8,128)(2,1)}, bf16[256,2048]{1,0:T(8,128)(2,1)}) custom-call(bf16[2048,2048]{1,0:T(8,128)(2,1)} %bitcast.76, bf16[4,576,512]{2,1,0:T(8,128)(2,1)} %bitcast.80, f32[2,4,256,1]{3,2,1,0:T(8,128)} %reduce_window_sum.34.col_ref, f32[2,4,1,256]{3,2,1,0:T(1,128)} %bitcast.100, bf16[4,512,384]{2,1,0:T(8,128)(2,1)} %get-tuple-element.75.qkv_ref, ...), custom_call_target="tpu_custom_call" | custom-call | bytes 83886080 | tf_op jit(solution)/shard_map/unmix/pallas_call | solution.py:639
  628.5 7.3 fusion.1
  635.9 1.1 slice.43
  637.0 0.5 copy-done
  637.6 6.7 convolution_convert_fusion.3
  644.3 0.0 reduce-scatter.12.cloned.1.call-update
  644.3 0.0 reduce-scatter.14.cloned.1.call-start
  644.3 0.7 reduce-scatter.14.cloned.1.call-update
  645.0 68.9 %leave.1 = (f32[2,256,2048]{2,1,0:T(8,128)}, bf16[2,256,2048]{2,1,0:T(8,128)(2,1)}, f32[8,128]{1,0:T(8,128)}) custom-call(bf16[2048,384]{1,0:T(8,128)(2,1)} %bitcast.89, bf16[4,576,512]{2,1,0:T(8,128)(2,1)} %bitcast.81, bf16[256,2048]{1,0:T(8,128)(2,1)} %get-tuple-element.62.x_ref, f32[256,2048]{1,0:T(8,128)} %get-tuple-element.83.dresid_ref, ...), custom_call_target="tpu_custom_call" | custom-call | bytes 62914560 | tf_op jit(solution)/shard_map/leave/pallas_call | solution.py:639
  713.9 27.1 %exchange_dp.5 = (bf16[4,688,128]{2,1,0:T(8,128)(2,1)}, bf16[4,688,128]{2,1,0:T(8,128)(2,1)}, bf16[4,688,128]{2,1,0:T(8,128)(2,1)}) custom-call(bf16[688,512]{1,0:T(8,128)(2,1)} %reduce-scatter.6.cloned.1.call-done.refs_0_, bf16[688,512]{1,0:T(8,128)(2,1)} %reduce-scatter.8.cloned.1.call-done.refs_1_, bf16[688,512]{1,0:T(8,128)(2,1)} %reduce-scatter.10.cloned.1.call-done.refs_2_), custom_call_target="tpu_custom_call" | custom-call | bytes 63406080 | tf_op jit(solution)/shard_map/exchange_dp/pallas_call | solution.py:485
  741.0 1.3 slice_bitcast_fusion
  742.3 2.3 convert_bitcast_fusion.1
  744.5 2.3 convert_bitcast_fusion
  746.8 1.2 bitcast_convert_fusion
  748.1 9.6 %exchange_dp.4 = (bf16[4,256,128]{2,1,0:T(8,128)(2,1)}, bf16[4,320,128]{2,1,0:T(8,128)(2,1)}) custom-call(bf16[256,512]{1,0:T(8,128)(2,1)} %reduce-scatter.12.cloned.1.call-done.refs_0_, bf16[320,512]{1,0:T(8,128)(2,1)} %reduce-scatter.14.cloned.1.call-done.refs_1_), custom_call_target="tpu_custom_call" | custom-call | bytes 17694720 | tf_op jit(solution)/shard_map/exchange_dp/pallas_call | solution.py:485
  757.7 0.8 fusion
  758.5 1.0 slice.36
  759.5 0.7 copy.37
  760.2 0.7 copy.36
  760.9 0.1 bitcast_convert_fusion.2
  761.0 1.0 copy.38
  762.0 1.9 bitcast_convert_fusion.1
  763.9 1.3 copy.41
  765.2 2.0 copy.42
  (30 shorter events, 0.1 us)
Async XLA Ops:
  7.2 23.8 %copy-start.5 = (bf16[2752,128]{1,0:T(8,128)(2,1)S(1)}, bf16[2752,128]{1,0:T(8,128)(2,1)}, u32[]{:S(2)}) copy-start(bf16[2752,128]{1,0:T(8,128)(2,1)} %param.22) | copy-start | bytes 2113540
  7.2 23.8 %copy-start.6 = (bf16[128,2752]{0,1:T(8,128)(2,1)S(1)}, bf16[128,2752]{0,1:T(8,128)(2,1)}, u32[]{:S(2)}) copy-start(bf16[128,2752]{0,1:T(8,128)(2,1)} %param.21) | copy-start | bytes 2113540
  7.2 23.8 %copy-start.7 = (bf16[128,2752]{0,1:T(8,128)(2,1)S(1)}, bf16[128,2752]{0,1:T(8,128)(2,1)}, u32[]{:S(2)}) copy-start(bf16[128,2752]{0,1:T(8,128)(2,1)} %param.20) | copy-start | bytes 2113540
  7.2 98.4 %all-gather.5.cloned.1.call-start = ((), (), s32[]{:S(2)}) async-start(), calls=%async_computation.10 | async-start | bytes 2949120 | tf_op jit(solution)/shard_map/all_gather | solution.py:1342
  31.0 292.2 %all-gather.7.cloned.1.call-start = ((), (), s32[]{:S(2)}) async-start(), calls=%async_computation.11 | async-start | bytes 10567680 | tf_op jit(solution)/shard_map/all_gather | solution.py:1342
  32.5 26.7 %copy-start.3 = (f32[16,8,128]{2,1,0:T(8,128)S(1)}, f32[16,8,128]{2,1,0:T(8,128)}, u32[]{:S(2)}) copy-start(f32[16,8,128]{2,1,0:T(8,128)} %get-tuple-element.57.small_ref) | copy-start | bytes 196612
  59.1 432.1 %reduce-scatter.6.cloned.1.call-start = ((), (), s32[]{:S(2)}) async-start(), calls=%async_computation.5 | async-start | bytes 3522560 | tf_op jit(solution)/shard_map/reduce_scatter | solution.py:1345
  60.3 45.3 %copy-start.8 = (f32[2,8,128]{2,1,0:T(8,128)}, f32[2,8,128]{2,1,0:T(8,128)S(1)}, u32[]{:S(2)}) copy-start(f32[2,8,128]{2,1,0:T(8,128)S(1)} %broadcast_add_fusion) | copy-start | bytes 24580
  383.6 10.7 %copy-start.9 = (bf16[2048,688]{1,0:T(8,128)(2,1)S(1)}, bf16[2048,688]{1,0:T(8,128)(2,1)}, u32[]{:S(2)}) copy-start(bf16[2048,688]{1,0:T(8,128)(2,1)} %get-tuple-element.68) | copy-start | bytes 8454148
  404.0 240.3 %reduce-scatter.8.cloned.1.call-start = ((), (), s32[]{:S(2)}) async-start(), calls=%async_computation.6 | async-start | bytes 3522560 | tf_op jit(solution)/shard_map/reduce_scatter | solution.py:1345
  404.6 239.7 %reduce-scatter.10.cloned.1.call-start = ((), (), s32[]{:S(2)}) async-start(), calls=%async_computation.7 | async-start | bytes 3522560 | tf_op jit(solution)/shard_map/reduce_scatter | solution.py:1345
  405.2 342.9 %reduce-scatter.12.cloned.1.call-start = ((), (), s32[]{:S(2)}) async-start(), calls=%async_computation.8 | async-start | bytes 1310720 | tf_op jit(solution)/shard_map/reduce_scatter | solution.py:1345
  635.9 1.7 copy-start
  644.3 103.8 %reduce-scatter.14.cloned.1.call-start = ((), (), s32[]{:S(2)}) async-start(), calls=%async_computation.9 | async-start | bytes 1638400 | tf_op jit(solution)/shard_map/reduce_scatter | solution.py:1345
  741.0 5.8 copy-start.4
  746.8 17.1 %copy-start.2 = (bf16[2,256,2048]{2,1,0:T(8,128)(2,1)S(1)}, bf16[2,256,2048]{2,1,0:T(8,128)(2,1)}, u32[]{:S(2)}) copy-start(bf16[2,256,2048]{2,1,0:T(8,128)(2,1)} %get-tuple-element.120) | copy-start | bytes 6291460
  762.0 3.3 copy-start.1
Sparse Core Ops, SparseCore 0:
  31.1 48.6 all-gather.4
  81.4 205.3 all-gather.6
  404.1 69.3 reduce-scatter.5
  475.7 63.5 reduce-scatter.7
  542.0 78.1 reduce-scatter.9
  644.4 34.3 reduce-scatter.11
  681.6 31.9 reduce-scatter.13

commit v4 on v3

--- a/solution.py
+++ b/solution.py
@@ -375,39 +375,56 @@
         c.start()
     local_copy = pltpu.make_async_copy(own_ref, mine, local_sem)
     local_copy.start()
-    yield
     from_x, from_y, from_d = out_ref.at[x_at, core], out_ref.at[y_at, core], out_ref.at[d_at, core]
     on_y = copy(from_x.at[lo], from_x.at[lo], yp)
     on_x = copy(from_y.at[hi], from_y.at[hi], xp)
-    late = [pair]
-
-    def hand(block, rows):
-        c = copy(block.at[rows], block.at[rows], sp)
-        c.start()
-        late.append(c)
-
+    handed = [
+        copy(block.at[rows], block.at[rows], sp)
+        for block, rows in (
+            (from_x, lo),
+            (from_y, hi),
+            (from_x, hi),
+            (from_y, lo),
+            (from_d, lo),
+            (from_d, hi),
+        )
+    ]
+    yield
+    local_copy.wait()
+    yield
+    pair.wait_recv()
+    yield
     x_lo.wait_recv()
     on_y.start()
-    hand(from_x, lo)
+    handed[0].start()
     y_hi.wait_recv()
     on_x.start()
-    hand(from_y, hi)
+    handed[1].start()
+    yield
+    handed[0].wait_recv()
+    handed[1].wait_recv()
+    yield
     x_hi.wait_recv()
-    hand(from_x, hi)
+    handed[2].start()
     y_lo.wait_recv()
-    hand(from_y, lo)
+    handed[3].start()
+    yield
+    handed[2].wait_recv()
+    handed[3].wait_recv()
+    yield
     on_y.wait_recv()
-    hand(from_d, lo)
+    handed[4].start()
     on_x.wait_recv()
-    hand(from_d, hi)
-    for c in late:
-        c.wait_recv()
-    for c in [x_lo, y_hi, x_hi, y_lo, on_y, on_x] + late:
+    handed[5].start()
+    yield
+    handed[4].wait_recv()
+    handed[5].wait_recv()
+    yield
+    for c in [x_lo, y_hi, x_hi, y_lo, on_y, on_x, pair] + handed:
         c.wait_send()
-    local_copy.wait()
-
-
-def scatter_steps(part_ref, out_ref, pair_ref, sum_ref, got_ref, copy):
+
+
+def scatter_steps(part_ref, out_ref, pair_ref, sum_ref, got_ref, copy, held=None):
     at, x_at, y_at, d_at, core = plane_places()
     half = part_ref.shape[2] // 2
     xp, yp, sp = {"dp": x_at}, {"dp": y_at}, {"tensor": 1 - core}
@@ -416,57 +433,77 @@
     pairs = [copy(part_ref.at[to, 1 - core], pair_ref.at[j], sp) for j, to in enumerate(order)]
     for c in pairs:
         c.start()
+    own = [part_ref.at[to, core] for to in order]
+    fetched = []
+    if held is not None:
+        buffer, held_sems = held
+        fetched = [
+            pltpu.make_async_copy(o, buffer.at[j], held_sems.at[j]) for j, o in enumerate(own)
+        ]
+        own = [buffer.at[j] for j in range(4)]
+        for c in fetched:
+            c.start()
     yield
 
+    def ready(j):
+        if fetched:
+            fetched[j].wait()
+        pairs[j].wait_recv()
+
     def total(j, rows, *more):
-        add_rows(
-            sum_ref.at[j, rows], part_ref.at[order[j], core, rows], pair_ref.at[j, rows], *more
-        )
+        add_rows(sum_ref.at[j, rows], own[j].at[rows], pair_ref.at[j, rows], *more)
 
     def sent(j, rows, place):
         return copy(sum_ref.at[j, rows], got_ref.at[j, rows], place)
 
     d_lo, d_hi = sent(0, lo, xp), sent(0, hi, yp)
     x_lo, y_hi, x_hi, y_lo = sent(1, lo, xp), sent(2, hi, yp), sent(1, hi, xp), sent(2, lo, yp)
-    pairs[0].wait_recv()
+    ready(0)
     total(0, lo)
     d_lo.start()
     total(0, hi)
     d_hi.start()
-    pairs[1].wait_recv()
+    ready(1)
     total(1, lo)
     x_lo.start()
-    pairs[2].wait_recv()
+    ready(2)
     total(2, hi)
     y_hi.start()
+    yield
     d_lo.wait_recv()
     total(2, lo, got_ref.at[0, lo])
     y_lo.start()
     d_hi.wait_recv()
     total(1, hi, got_ref.at[0, hi])
     x_hi.start()
-    pairs[3].wait_recv()
+    yield
+    ready(3)
     for c in (x_lo, y_hi, y_lo, x_hi):
         c.wait_recv()
-    add_rows(out_ref, part_ref.at[at, core], pair_ref.at[3], got_ref.at[1], got_ref.at[2])
+    add_rows(out_ref, own[3], pair_ref.at[3], got_ref.at[1], got_ref.at[2])
     for c in pairs + [d_lo, d_hi, x_lo, y_hi, x_hi, y_lo]:
         c.wait_send()
 
 
-def exchange_kernel(axis, take, put, count, *refs):
-    ins, outs, sems, local_sems = refs[:count], refs[count : 2 * count], refs[-2], refs[-1]
-    size, me = lax.axis_size(axis), lax.axis_index(axis)
-    peers = [lax.rem(me + k, size) for k in range(1, size)]
-    greet([{axis: p} for p in peers])
-    copy = Sender(sems)
-    copies = [copy(take(i, p), put(o, me), {axis: p}) for i, o in zip(ins, outs) for p in peers]
-    copies += [
+def swap_shards(ins, outs, peers, me, take, put, copy, local_sems):
+    started = [
+        copy(take(i, p), put(o, me), {"dp": p}) for i, o in zip(ins, outs) for p in peers
+    ]
+    started += [
         pltpu.make_async_copy(take(i, me), put(o, me), local_sems.at[n])
         for n, (i, o) in enumerate(zip(ins, outs))
     ]
-    for c in copies:
+    for c in started:
         c.start()
-    for c in copies:
+    return started
+
+
+def exchange_kernel(take, put, count, *refs):
+    ins, outs, sems, local_sems = refs[:count], refs[count : 2 * count], refs[-2], refs[-1]
+    size, me = lax.axis_size("dp"), lax.axis_index("dp")
+    peers = [lax.rem(me + k, size) for k in range(1, size)]
+    greet([{"dp": p} for p in peers])
+    for c in swap_shards(ins, outs, peers, me, take, put, Sender(sems), local_sems):
         c.wait()
 
 
@@ -479,12 +516,12 @@
     return ref.at[:, pl.ds(pl.multiple_of(index * width, width), width)]
 
 
-def exchange(arrays, axis, cid, shapes, take=block_of, put=block_of):
-    count, peers = len(arrays), lax.axis_size(axis) - 1
+def exchange(arrays, cid, shapes, take=block_of, put=block_of):
+    count, peers = len(arrays), lax.axis_size("dp") - 1
     anywhere = [pl.BlockSpec(memory_space=pl.ANY)] * count
     return pl.pallas_call(
-        partial(exchange_kernel, axis, take, put, count),
-        name="exchange_" + axis,
+        partial(exchange_kernel, take, put, count),
+        name="exchange",
         out_shape=[jax.ShapeDtypeStruct(s, x.dtype) for s, x in zip(shapes, arrays)],
         in_specs=anywhere,
         out_specs=anywhere,
@@ -549,62 +586,6 @@
             flops=0, bytes_accessed=60 * pack.size, transcendentals=0
         ),
     )(pack, small)
-
-
-def ffn_kernel(normed_ref, cot_ref, w_ref, out_ref, dnormed_ref, dgate_ref, dup_ref, hidden_ref):
-    parts, units, depth = w_ref.shape
-    units //= 3
-
-    def rows(k):
-        return pl.ds(k * units, units)
-
-    def cols(s):
-        return pl.ds(s * depth, depth)
-
-    def project(x_ref, k):
-        total = nt_dot(x_ref[:, cols(0)], w_ref[0, rows(k)])
-        for s in range(1, parts):
-            total += nt_dot(x_ref[:, cols(s)], w_ref[s, rows(k)])
-        return total
-
-    gate, up, dhidden = project(normed_ref, 0), project(normed_ref, 1), project(cot_ref, 2)
-    sig = jax.nn.sigmoid(gate)
-    silu = gate * sig
-    hidden = (silu * up).astype(jnp.bfloat16)
-    dgate = (dhidden * up * sig * (1.0 + gate * (1.0 - sig))).astype(jnp.bfloat16)
-    dup = (dhidden * silu).astype(jnp.bfloat16)
-    hidden_ref[...], dgate_ref[...], dup_ref[...] = hidden, dgate, dup
-    for s in range(parts):
-        dnormed_ref[:, cols(s)] = (
-            nn_dot(dgate, w_ref[s, rows(0)]) + nn_dot(dup, w_ref[s, rows(1)])
-        ).astype(jnp.bfloat16)
-        out_ref[:, cols(s)] = nn_dot(hidden, w_ref[s, rows(2)]).astype(jnp.bfloat16)
-
-
-def ffn(normed, cot, weights, block=256):
-    tokens, width = normed.shape
-    units = weights.shape[1] // 3
-    wide = pl.BlockSpec((block, width), lambda i: (i, 0))
-    thin = pl.BlockSpec((block, units), lambda i: (i, 0))
-    return pl.pallas_call(
-        ffn_kernel,
-        name="ffn",
-        grid=(tokens // block,),
-        out_shape=[jax.ShapeDtypeStruct((tokens, width), jnp.bfloat16)] * 2
-        + [jax.ShapeDtypeStruct((tokens, units), jnp.bfloat16)] * 3,
-        in_specs=[
-            wide,
-            wide,
-            pl.BlockSpec(weights.shape, lambda i: (0, 0, 0), pipeline_mode=pl.Buffered(1)),
-        ],
-        out_specs=[wide, wide, thin, thin, thin],
-        compiler_params=pltpu.CompilerParams(vmem_limit_bytes=VMEM_LIMIT),
-        cost_estimate=pl.CostEstimate(
-            flops=12 * tokens * width * units,
-            bytes_accessed=2 * (4 * tokens * width + weights.size + 3 * tokens * units),
-            transcendentals=tokens * units,
-        ),
-    )(normed, cot, weights)
 
 
 def run(*steps):
@@ -859,15 +840,12 @@
     x_ref,
     small_ref,
     residual_ref,
-    all_ref,
+    normed_ref,
     part_ref,
     pair_ref,
     sum_ref,
     got_ref,
-    normed_ref,
     sems,
-    gather_sems,
-    local_sem,
 ):
     greet_plane()
     parts, _, depth = pack_ref.shape
@@ -900,7 +878,6 @@
         return carry
 
     row_blocks(m, ROW_STEP, body)(0)
-    run(gather_steps(normed_ref, all_ref, Sender(gather_sems), local_sem))
 
 
 def scatter_scratch(m, width):
@@ -914,23 +891,225 @@
 def branch(mixed, pack, x, small, cid):
     m, width = x.shape
     whole = pltpu.VMEM
-    residual, gathered = kernel_call(
+    return kernel_call(
         branch_kernel,
         "branch",
         cid,
-        [((m, width), jnp.float32, whole), ((4, 2, m, width), jnp.bfloat16, pl.ANY)],
+        [((m, width), jnp.float32, whole), ((m, width), jnp.bfloat16, whole)],
         [(mixed, whole), (pack, whole), (x, whole), (small, whole)],
         [pltpu.VMEM((4, 2, m, width), jnp.bfloat16)]
         + scatter_scratch(m, width)
-        + [
-            pltpu.VMEM((m, width), jnp.bfloat16),
-            copies(SCATTER_COPIES),
+        + [copies(SCATTER_COPIES)],
+        moved=x.size * 80,
+    )
+
+
+def parity(i):
+    return i % 2 if isinstance(i, int) else lax.rem(i, 2)
+
+
+def choose(test, a, b):
+    if isinstance(test, bool):
+        return a if test else b
+    return jnp.where(test, a, b)
+
+
+def ffn_block(x_at, cot_at, w_ref, out_ref, dnormed_ref, dgate_ref, dup_ref, hidden_ref):
+    parts, units, depth = w_ref.shape
+    units //= 3
+
+    def rows(k):
+        return pl.ds(k * units, units)
+
+    def cols(s):
+        return pl.ds(s * depth, depth)
+
+    def project(at, k):
+        total = nt_dot(at(cols(0)), w_ref[0, rows(k)])
+        for s in range(1, parts):
+            total += nt_dot(at(cols(s)), w_ref[s, rows(k)])
+        return total
+
+    gate, up, dhidden = project(x_at, 0), project(x_at, 1), project(cot_at, 2)
+    sig = jax.nn.sigmoid(gate)
+    silu = gate * sig
+    hidden = (silu * up).astype(jnp.bfloat16)
+    dgate = (dhidden * up * sig * (1.0 + gate * (1.0 - sig))).astype(jnp.bfloat16)
+    dup = (dhidden * silu).astype(jnp.bfloat16)
+    for s in range(parts):
+        dnormed_ref[:, cols(s)] = (
+            nn_dot(dgate, w_ref[s, rows(0)]) + nn_dot(dup, w_ref[s, rows(1)])
+        ).astype(jnp.bfloat16)
+        out_ref[:, cols(s)] = nn_dot(hidden, w_ref[s, rows(2)]).astype(jnp.bfloat16)
+    hidden_ref[...], dgate_ref[...], dup_ref[...] = hidden.T, dgate.T, dup.T
+
+
+def expand_kernel(
+    own_ref,
+    cot_hbm,
+    w_hbm,
+    normed_hbm,
+    out_hbm,
+    dnormed_hbm,
+    dgate_hbm,
+    dup_hbm,
+    hidden_hbm,
+    normed_ref,
+    w_ref,
+    cot_ref,
+    out_ref,
+    dnormed_ref,
+    dgate_ref,
+    dup_ref,
+    hidden_ref,
+    sems,
+    local_sem,
+    w_sem,
+    cot_sems,
+    store_sems,
+    keep_sems,
+):
+    greet_plane()
+    at, x_at, y_at, d_at, core = plane_places()
+    m = own_ref.shape[0]
+    half = m // 2
+    gather = gather_steps(own_ref, normed_ref, Sender(sems), local_sem)
+    next(gather)
+    weights = pltpu.make_async_copy(w_hbm, w_ref, w_sem)
+    weights.start()
+
+    def halves(i):
+        k = choose(parity(i) == 0, core, 1 - core)
+        one = choose(i < 2, at, choose(i < 6, x_at, d_at))
+        two = choose(i < 2, at, choose(i < 6, y_at, d_at))
+        late = (i >= 4) & (i < 6)
+        late = int(late) if isinstance(late, bool) else late.astype(jnp.int32)
+        first, second = late * half, (1 - late) * half
+        if not isinstance(i, int):
+            first, second = pl.multiple_of(first, half), pl.multiple_of(second, half)
+        return (one, k, first), (two, k, second)
+
+    def cot_copies(i):
+        slot = parity(i)
+        return [
+            pltpu.make_async_copy(
+                cot_hbm.at[c, k, pl.ds(r, half)],
+                cot_ref.at[slot, pl.ds(n * half, half)],
+                cot_sems.at[slot, n],
+            )
+            for n, (c, k, r) in enumerate(halves(i))
+        ]
+
+    def store_copies(i):
+        slot = parity(i)
+        found = []
+        for n, (c, k, r) in enumerate(halves(i)):
+            rows = pl.ds(n * half, half)
+            column = pl.ds(pl.multiple_of((c * 2 + k) * m + r, half), half)
+            pairs = [
+                (out_ref.at[slot, rows], out_hbm.at[c, k, pl.ds(r, half)]),
+                (dnormed_ref.at[slot, rows], dnormed_hbm.at[c, k, pl.ds(r, half)]),
+                (dgate_ref.at[slot, :, rows], dgate_hbm.at[:, column]),
+                (dup_ref.at[slot, :, rows], dup_hbm.at[:, column]),
+                (hidden_ref.at[slot, :, rows], hidden_hbm.at[:, column]),
+            ]
+            found += [
+                pltpu.make_async_copy(a, b, store_sems.at[slot, n * len(pairs) + q])
+                for q, (a, b) in enumerate(pairs)
+            ]
+        return found
+
+    for c in cot_copies(0):
+        c.start()
+    next(gather)
+    weights.wait()
+
+    def body(i, carry):
+        for step in range(1, 8):
+
+            @pl.when(i == step)
+            def _():
+                next(gather)
+
+        @pl.when(i < 7)
+        def _():
+            for c in cot_copies(i + 1):
+                c.start()
+
+        for c in cot_copies(i):
+            c.wait()
+
+        @pl.when(i >= 2)
+        def _():
+            for c in store_copies(i - 2):
+                c.wait()
+
+        slot = lax.rem(i, 2)
+        pieces = halves(i)
+
+        def x_cols(cols):
+            return jnp.concatenate([normed_ref[c, k, pl.ds(r, half), cols] for c, k, r in pieces])
+
+        def cot_cols(cols):
+            return cot_ref[slot, :, cols]
+
+        ffn_block(
+            x_cols,
+            cot_cols,
+            w_ref,
+            out_ref.at[slot],
+            dnormed_ref.at[slot],
+            dgate_ref.at[slot],
+            dup_ref.at[slot],
+            hidden_ref.at[slot],
+        )
+        for c in store_copies(i):
+            c.start()
+        return carry
+
+    lax.fori_loop(0, 8, body, 0)
+    keep = pltpu.make_async_copy(normed_ref, normed_hbm, keep_sems.at[0])
+    keep.start()
+    for i in (6, 7):
+        for c in store_copies(i):
+            c.wait()
+    keep.wait()
+    run(gather)
+
+
+def expand(own, cot, weights, cid):
+    m, width = own.shape
+    units = weights.shape[1] // 3
+    tokens = 8 * m
+    whole, low = pltpu.VMEM, jnp.bfloat16
+    blocks = ((4, 2, m, width), low, pl.ANY)
+    thin = ((units, tokens), low, pl.ANY)
+    normed, out, dnormed, dgate, dup, hidden = kernel_call(
+        expand_kernel,
+        "expand",
+        cid,
+        [blocks, blocks, blocks, thin, thin, thin],
+        [(own, whole), (cot.reshape(4, 2, m, width), pl.ANY), (weights, pl.ANY)],
+        [
+            pltpu.VMEM((4, 2, m, width), low),
+            pltpu.VMEM(weights.shape, low),
+            pltpu.VMEM((2, m, width), low),
+            pltpu.VMEM((2, m, width), low),
+            pltpu.VMEM((2, m, width), low),
+            pltpu.VMEM((2, units, m), low),
+            pltpu.VMEM((2, units, m), low),
+            pltpu.VMEM((2, units, m), low),
             copies(GATHER_COPIES),
             pltpu.SemaphoreType.DMA,
+            pltpu.SemaphoreType.DMA,
+            pltpu.SemaphoreType.DMA((2, 2)),
+            pltpu.SemaphoreType.DMA((2, 10)),
+            pltpu.SemaphoreType.DMA((1,)),
         ],
-        moved=x.size * 120,
-    )
-    return residual, gathered.reshape(-1, width)
+        flops=12 * tokens * width * units,
+        moved=1 << 28,
+    )
+    return normed.reshape(tokens, width), out, dnormed, dgate, dup, hidden
 
 
 def norm_gradient(r, value_at, grad_ref, gain_at, gain_grad, finish, width):
@@ -951,24 +1130,124 @@
 
 
 def middle_kernel(
-    part_ref,
+    part_hbm,
+    normed_hbm,
+    dgate_hbm,
+    dup_hbm,
+    total_ref,
+    gate_hbm,
+    up_hbm,
+    held_ref,
+    pair_ref,
+    sum_ref,
+    got_ref,
+    normed_ref,
+    left_ref,
+    grad_ref,
+    sems,
+    held_sems,
+    load_sems,
+    store_sems,
+):
+    greet_plane()
+    scatter = scatter_steps(
+        part_hbm, total_ref, pair_ref, sum_ref, got_ref, Sender(sems), (held_ref, held_sems)
+    )
+    next(scatter)
+    loads = [
+        pltpu.make_async_copy(a, b, load_sems.at[n])
+        for n, (a, b) in enumerate(
+            (
+                (dgate_hbm, left_ref.at[0]),
+                (normed_hbm, normed_ref),
+                (dup_hbm, left_ref.at[1]),
+            )
+        )
+    ]
+    for c in loads:
+        c.start()
+    next(scatter)
+    width = grad_ref.shape[2]
+    blocks = normed_ref.shape[1] // width
+
+    def gradients(which, out_hbm):
+        def stored(i):
+            column = pl.ds(pl.multiple_of(i * width, width), width)
+            slot = parity(i)
+            return pltpu.make_async_copy(
+                grad_ref.at[slot], out_hbm.at[:, column], store_sems.at[slot]
+            )
+
+        def body(i, carry):
+            column = pl.ds(pl.multiple_of(i * width, width), width)
+
+            @pl.when(i >= 2)
+            def _():
+                stored(i - 2).wait()
+
+            grad_ref[lax.rem(i, 2)] = nn_dot(left_ref[which], normed_ref[:, column]).astype(
+                jnp.bfloat16
+            )
+            stored(i).start()
+            return carry
+
+        lax.fori_loop(0, blocks, body, 0)
+        for i in (blocks - 2, blocks - 1):
+            stored(i).wait()
+
+    loads[0].wait()
+    loads[1].wait()
+    gradients(0, gate_hbm)
+    next(scatter)
+    loads[2].wait()
+    gradients(1, up_hbm)
+    run(scatter)
+
+
+def middle(part, normed, dgate, dup, cid):
+    _, _, m, width = part.shape
+    units, tokens = dgate.shape
+    low = jnp.bfloat16
+    return kernel_call(
+        middle_kernel,
+        "middle",
+        cid,
+        [
+            ((m, width), jnp.float32, pltpu.VMEM),
+            ((units, width), low, pl.ANY),
+            ((units, width), low, pl.ANY),
+        ],
+        [(a, pl.ANY) for a in (part, normed, dgate, dup)],
+        [pltpu.VMEM((4, m, width), low)]
+        + scatter_scratch(m, width)
+        + [
+            pltpu.VMEM((tokens, width), low),
+            pltpu.VMEM((2, units, tokens), low),
+            pltpu.VMEM((2, units, 256), low),
+            copies(SCATTER_COPIES),
+            pltpu.SemaphoreType.DMA((4,)),
+            pltpu.SemaphoreType.DMA((3,)),
+            pltpu.SemaphoreType.DMA((2,)),
+        ],
+        flops=4 * units * tokens * width,
+        moved=m * width * 80,
+    )
+
+
+def turn_kernel(
+    total_ref,
     residual_ref,
     cot_ref,
     small_ref,
     dresid_ref,
     gain_ref,
     all_ref,
-    pair_ref,
-    sum_ref,
-    got_ref,
     low_ref,
-    sems,
     gather_sems,
     local_sem,
 ):
     greet_plane()
     m, width = residual_ref.shape
-    run(scatter_steps(part_ref, dresid_ref, pair_ref, sum_ref, got_ref, Sender(sems)))
     gain_ref[...] = jnp.zeros_like(gain_ref)
 
     def finish(r, k, v):
@@ -980,7 +1259,7 @@
         norm_gradient(
             r,
             lambda r, k: residual_ref[r, lanes(k)],
-            dresid_ref,
+            total_ref,
             lambda k: small_ref[k, 1:2, :],
             gain_ref,
             finish,
@@ -992,73 +1271,62 @@
     run(gather_steps(low_ref, all_ref, Sender(gather_sems), local_sem))
 
 
-def middle(part, residual, cot_own, small, cid):
+def turn(total, residual, cot_own, small, cid):
     m, width = residual.shape
     whole = pltpu.VMEM
     dresid, gain, gathered = kernel_call(
-        middle_kernel,
-        "middle",
+        turn_kernel,
+        "turn",
         cid,
         [
             ((m, width), jnp.float32, whole),
             ((8, width), jnp.float32, whole),
             ((4, 2, m, width), jnp.bfloat16, pl.ANY),
         ],
+        [(a, whole) for a in (total, residual, cot_own, small)],
         [
-            (part.reshape(4, 2, m, width), whole),
-            (residual, whole),
-            (cot_own, whole),
-            (small, whole),
-        ],
-        scatter_scratch(m, width)
-        + [
             pltpu.VMEM((m, width), jnp.bfloat16),
-            copies(SCATTER_COPIES),
             copies(GATHER_COPIES),
             pltpu.SemaphoreType.DMA,
         ],
-        moved=residual.size * 120,
+        moved=residual.size * 80,
     )
     return dresid, gain, gathered.reshape(-1, width)
 
 
-def unmix_kernel(
-    heads,
+def back_kernel(
     dresid_ref,
     pack_ref,
-    col_ref,
-    row_ref,
-    qkv_ref,
-    exact_ref,
-    den_ref,
     part_ref,
     residual_ref,
-    dqkv_ref,
+    dmixed_ref,
     block_ref,
     out_dmixed,
-    dmixed_ref,
-    out_dqkv,
-    keys_ref,
-    dtile_ref,
-    dkey_ref,
-    dvalue_ref,
     total_ref,
+    held_ref,
     pair_ref,
     sum_ref,
     got_ref,
     sems,
     scatter_sems,
+    held_sems,
 ):
     span, z = lax.axis_size("seq"), lax.axis_index("seq")
     parts, _, depth = pack_ref.shape
-    tokens = qkv_ref.shape[1]
-    rows, length = col_ref.shape[0], col_ref.shape[2]
-    vcols, qcols = heads * VHEAD, heads * FDIM
+    tokens, vcols = dmixed_ref.shape[1:]
     first = pack_ref.shape[1] - vcols
     at, x_at, y_at, _, core = plane_places()
     peers = [lax.rem(z + k, span) for k in range(1, span)]
     greet([{"dp": x_at}, {"dp": y_at}, {"tensor": 1 - core}] + [{"seq": p} for p in peers])
-    scatter = scatter_steps(part_ref, total_ref, pair_ref, sum_ref, got_ref, Sender(scatter_sems))
+    scatter = scatter_steps(
+        part_ref,
+        total_ref,
+        pair_ref,
+        sum_ref,
+        got_ref,
+        Sender(scatter_sems),
+        (held_ref, held_sems),
+    )
     next(scatter)
     copy = Sender(sems)
 
@@ -1077,18 +1345,66 @@
         there.append(copy(out_dmixed.at[k], dmixed_ref.at[z], {"seq": p}))
         there[-1].start()
     project(z, dmixed_ref.at[z])
+    run(scatter)
+
+    def finish(r, carry):
+        block_ref[r] = (residual_ref[r] + total_ref[r]).astype(jnp.bfloat16)
+        return carry
+
+    row_blocks(block_ref.shape[0], ROW_STEP, finish)(0)
+    for c in there:
+        c.wait()
+
+
+def back(dresid_low, pack, part, residual, vcols, cid):
+    span = lax.axis_size("seq")
+    tokens = dresid_low.shape[0] // span
+    m, width = residual.shape
+    whole = pltpu.VMEM
+    return kernel_call(
+        back_kernel,
+        "back",
+        cid,
+        [((span, tokens, vcols), jnp.bfloat16, whole), ((m, width), jnp.bfloat16, whole)],
+        [(dresid_low, whole), (pack, whole), (part, pl.ANY), (residual, whole)],
+        [
+            pltpu.VMEM((span - 1, tokens, vcols), jnp.bfloat16),
+            pltpu.VMEM((m, width), jnp.float32),
+            pltpu.VMEM((4, m, width), jnp.bfloat16),
+        ]
+        + scatter_scratch(m, width)
+        + [copies(span - 1), copies(SCATTER_COPIES), pltpu.SemaphoreType.DMA((4,))],
+        moved=residual.size * 120,
+    )
+
+
+def unmix_kernel(
+    heads,
+    count,
+    col_ref,
+    row_ref,
+    qkv_ref,
+    exact_ref,
+    den_ref,
+    dmixed_ref,
+    *refs,
+):
+    ins, dqkv_ref, outs = refs[:count], refs[count], refs[count + 1 : 2 * count + 1]
+    out_dqkv, keys_ref, dtile_ref, dkey_ref, dvalue_ref, sems, shard_sems, local_sems = refs[
+        2 * count + 1 :
+    ]
+    span, z = lax.axis_size("seq"), lax.axis_index("seq")
+    rows, length = col_ref.shape[0], col_ref.shape[2]
+    vcols, qcols = heads * VHEAD, heads * FDIM
+    plane, at = lax.axis_size("dp"), lax.axis_index("dp")
+    peers = [lax.rem(z + k, span) for k in range(1, span)]
+    chips = [lax.rem(at + k, plane) for k in range(1, plane)]
+    greet([{"dp": p} for p in chips] + [{"seq": p} for p in peers])
+    copy = Sender(sems)
+    shards = swap_shards(ins, outs, chips, at, columns_of, block_of, Sender(shard_sems), local_sems)
     keys_in_place(qkv_ref, keys_ref, vcols, qcols)
     dkey_ref[...] = jnp.zeros_like(dkey_ref)
     dvalue_ref[...] = jnp.zeros_like(dvalue_ref)
-    run(scatter)
-
-    def finish(r, carry):
-        block_ref[r] = (residual_ref[r] + total_ref[r]).astype(jnp.bfloat16)
-        return carry
-
-    row_blocks(block_ref.shape[0], ROW_STEP, finish)(0)
-    for c in there:
-        c.wait()
 
     def one_block(step, carry):
         r, i = step // span, lax.rem(step, span)
@@ -1125,43 +1441,95 @@
             dtile_ref[i] + pltpu.roll(dkey_ref[i], qcols, axis=1)
         ).astype(jnp.bfloat16)
 
-    back = []
+    home = []
     for k, p in enumerate(peers):
         pack(p, out_dqkv.at[k])
-        back.append(copy(out_dqkv.at[k], dqkv_ref.at[z], {"seq": p}))
-        back[-1].start()
+        home.append(copy(out_dqkv.at[k], dqkv_ref.at[z], {"seq": p}))
+        home[-1].start()
     pack(z, dqkv_ref.at[z])
-    for c in back:
+    for c in home + shards:
         c.wait()
 
 
-def unmix(dresid_low, pack, seg_col, seg_row, qkv, exact, den, part, residual, heads, cid):
+def unmix(seg_col, seg_row, qkv, exact, den, dmixed, shards, heads, cid):
     span, tokens, wide = qkv.shape
+    plane = lax.axis_size("dp")
     vcols = heads * VHEAD
-    m, width = residual.shape
+    count = len(shards)
     whole = pltpu.VMEM
-    ins = (dresid_low, pack, seg_col, seg_row, qkv, exact, den, part.reshape(4, 2, m, width), residual)
-    dqkv, block = kernel_call(
-        partial(unmix_kernel, heads),
+    dqkv, *swapped = kernel_call(
+        partial(unmix_kernel, heads, count),
         "unmix",
         cid,
-        [((span, tokens, wide), jnp.bfloat16, whole), ((m, width), jnp.bfloat16, whole)],
-        [(a, whole) for a in ins],
+        [((span, tokens, wide), jnp.bfloat16, whole)]
+        + [((plane, p.shape[0], p.shape[1] // plane), p.dtype, pl.ANY) for p in shards],
+        [(a, whole) for a in (seg_col, seg_row, qkv, exact, den, dmixed)]
+        + [(p, pl.ANY) for p in shards],
         [
-            pltpu.VMEM((span - 1, tokens, vcols), jnp.bfloat16),
-            pltpu.VMEM((span, tokens, vcols), jnp.bfloat16),
             pltpu.VMEM((span - 1, tokens, wide), jnp.bfloat16),
             pltpu.VMEM((span, tokens, LANES), jnp.bfloat16),
             pltpu.VMEM((span, tokens, LANES), jnp.float32),
             pltpu.VMEM((span, tokens, LANES), jnp.float32),
             pltpu.VMEM((span, tokens, vcols), jnp.float32),
-            pltpu.VMEM((m, width), jnp.float32),
-        ]
-        + scatter_scratch(m, width)
-        + [copies(2 * (span - 1)), copies(SCATTER_COPIES)],
-        moved=residual.size * 160,
-    )
-    return dqkv.reshape(-1, wide), block
+            copies(span - 1),
+            copies(count * (plane - 1)),
+            pltpu.SemaphoreType.DMA((count,)),
+        ],
+        moved=qkv.size * 120,
+    )
+    return dqkv.reshape(-1, wide), swapped
+
+
+def last_kernel(count, *refs):
+    ins, gain_ref, outs, sum_ref = (
+        refs[:count],
+        refs[count],
+        refs[count + 1 : 2 * count + 1],
+        refs[2 * count + 1],
+    )
+    got_gain, sems, gain_sems, local_sems = refs[2 * count + 2 :]
+    plane, at = lax.axis_size("dp"), lax.axis_index("dp")
+    others, me = everyone()
+    greet(others)
+    copy_gain = Sender(gain_sems)
+    gains = [
+        copy_gain(gain_ref.at[p["seq"] * plane + p["dp"]], got_gain.at[me], p) for p in others
+    ]
+    for c in gains:
+        c.start()
+    chips = [lax.rem(at + k, plane) for k in range(1, plane)]
+    shards = swap_shards(ins, outs, chips, at, columns_of, block_of, Sender(sems), local_sems)
+    got_gain[me] = gain_ref[lax.axis_index("seq") * plane + at]
+    for c in gains:
+        c.wait()
+    total = got_gain[0]
+    for k in range(1, len(others) + 1):
+        total += got_gain[k]
+    sum_ref[...] = total
+    for c in shards:
+        c.wait()
+
+
+def last(shards, gains, cid):
+    plane = lax.axis_size("dp")
+    count = len(shards)
+    devices = lax.axis_size(("dp", "seq", "tensor"))
+    *swapped, total = kernel_call(
+        partial(last_kernel, count),
+        "last",
+        cid,
+        [((plane, p.shape[0], p.shape[1] // plane), p.dtype, pl.ANY) for p in shards]
+        + [(gains.shape[1:], jnp.float32, pltpu.VMEM)],
+        [(p, pl.ANY) for p in shards] + [(gains, pltpu.VMEM)],
+        [
+            pltpu.VMEM((devices,) + gains.shape[1:], jnp.float32),
+            copies(count * (plane - 1)),
+            copies(devices - 1),
+            pltpu.SemaphoreType.DMA((count,)),
+        ],
+        moved=1 << 26,
+    )
+    return swapped, total
 
 
 def everyone():
@@ -1193,8 +1561,6 @@
     out_ref,
     gains_ref,
     gain_ref,
-    out_gain,
-    got_gain,
     part_ref,
     total_ref,
     ordered_ref,
@@ -1204,13 +1570,10 @@
     got_ref,
     sems,
     pair_sems,
-    gain_sems,
     local_sems,
 ):
-    others, me = everyone()
-    greet(others)
+    greet_plane()
     core = lax.axis_index("tensor")
-    plane, span = lax.axis_size("dp"), lax.axis_size("seq")
     parts, _, depth = pack_ref.shape
     m, width = x_ref.shape
     wide = dqkv_ref.shape[1] - LANES + 2 * FDIM * ((dqkv_ref.shape[1] - LANES) // VHEAD)
@@ -1262,28 +1625,16 @@
     local.append(pltpu.make_async_copy(ordered_ref, grad_ref.at[core], local_sems.at[1]))
     to_pair[1].start()
     local[1].start()
-    out_gain[...] = jnp.zeros_like(out_gain)
+    gains_ref[...] = jnp.zeros_like(gains_ref)
     for k in range(blocks):
         for row, ref in enumerate((gain_ref, gain_two_ref)):
-            out_gain[k, row : row + 1] = jnp.sum(ref[:, lanes(k)], axis=0, keepdims=True)
-    copy_gain = Sender(gain_sems)
-    for p in others:
-        block = out_gain.at[p["seq"] * plane + p["dp"], pl.ds(0, 8)]
-        to_pair.append(copy_gain(block, got_gain.at[me], p))
-        to_pair[-1].start()
-    mine = lax.axis_index("seq") * plane + lax.axis_index("dp")
-    got_gain[me] = out_gain[mine]
+            gains_ref[k, row : row + 1] = jnp.sum(ref[:, lanes(k)], axis=0, keepdims=True)
     for c in to_pair + local:
         c.wait()
-    total = got_gain[0]
-    for k in range(1, len(others) + 1):
-        total += got_gain[k]
-    gains_ref[...] = total
 
 
 def leave(dqkv, pack, x, dresid, block, small, gain_two, cid):
     m, width = x.shape
-    devices = lax.axis_size(("dp", "seq", "tensor"))
     whole = pltpu.VMEM
     return kernel_call(
         exit_kernel,
@@ -1292,13 +1643,11 @@
         [
             ((2, m, width), jnp.float32, pl.ANY),
             ((2, m, width), jnp.bfloat16, pl.ANY),
-            ((8, LANES), jnp.float32, whole),
+            ((width // LANES, 8, LANES), jnp.float32, whole),
         ],
         [(a, whole) for a in (dqkv, pack, x, dresid, block, small, gain_two)],
         [
             pltpu.VMEM((8, width), jnp.float32),
-            pltpu.VMEM((width // LANES, 8, LANES), jnp.float32),
-            pltpu.VMEM((devices, 8, LANES), jnp.float32),
             pltpu.VMEM((4, 2, m, width), jnp.bfloat16),
             pltpu.VMEM((m, width), jnp.float32),
             pltpu.VMEM((m, width), jnp.float32),
@@ -1308,7 +1657,6 @@
         + [
             copies(SCATTER_COPIES),
             copies(2),
-            copies(devices - 1),
             pltpu.SemaphoreType.DMA((2,)),
         ],
         moved=x.size * 120,
@@ -1346,11 +1694,6 @@
             grads.astype(jnp.bfloat16), "seq", scatter_dimension=1, tiled=True
         )
 
-    def collect(parts, cid):
-        return exchange(
-            parts, "dp", cid, [(plane, p.shape[0], chunk) for p in parts], take=columns_of
-        )
-
     def split(w):
         return w.reshape(plane, -1, chunk)
 
@@ -1370,7 +1713,7 @@
     ffn_pack = jnp.concatenate([split(gate_weight.T), split(up_weight.T), split(down_weight)], axis=1)
     ffn_pack, _ = lax.optimization_barrier((ffn_pack, attn_pack))
     [ffn_pack] = exchange(
-        [ffn_pack], "dp", 2, [(ffn_pack.shape[1], plane * chunk)], put=columns_of
+        [ffn_pack], 2, [(ffn_pack.shape[1], plane * chunk)], put=columns_of
     )
     attn_pack, ffn_pack = over_seq(attn_pack), over_seq(ffn_pack)
     starts = small[:, 2:-2].reshape(span, plane * rows, length)
@@ -1384,34 +1727,31 @@
         tokens.reshape(cores, own, width), cotangent.reshape(cores, own, width), small, 3
     )
     qkv, mixed, exact, den, cot = mix(normed_one, attn_pack, seg_col, seg_row, cot_own, heads, 4)
-    residual, normed_two = branch(mixed, attn_pack, x, small, 5)
-    out_part, dnormed_part, dgate, dup, hidden = ffn(normed_two, cot, ffn_pack)
-    down_grad = tn_dot(hidden, cot).astype(jnp.bfloat16)
-    gate_grad = tn_dot(dgate, normed_two).astype(jnp.bfloat16)
-    up_grad = tn_dot(dup, normed_two).astype(jnp.bfloat16)
-    dnormed_part, gate_grad, up_grad, down_grad = lax.optimization_barrier(
-        (dnormed_part, gate_grad, up_grad, down_grad)
-    )
-    down_grad, gate_grad, up_grad = summed(down_grad), summed(gate_grad), summed(up_grad)
-    dresid, gain_two_grad, dresid_low = middle(dnormed_part, residual, cot_own, small, 6)
+    residual, normed_own = branch(mixed, attn_pack, x, small, 5)
+    normed_two, out_part, dnormed_part, dgate, dup, hidden = expand(
+        normed_own, cot, ffn_pack, 11
+    )
+    down_grad = nn_dot(hidden, cot).astype(jnp.bfloat16)
+    dnormed_part, down_grad = lax.optimization_barrier((dnormed_part, down_grad))
+    down_grad = summed(down_grad)
+    dnormed_two, gate_grad, up_grad = middle(dnormed_part, normed_two, dgate, dup, 6)
+    gate_grad, up_grad = summed(gate_grad), summed(up_grad)
+    dresid, gain_two_grad, dresid_low = turn(dnormed_two, residual, cot_own, small, 12)
     dresid_low, down_grad = lax.optimization_barrier((dresid_low, down_grad))
-    dqkv, block_own = unmix(
-        dresid_low, attn_pack, seg_col, seg_row, qkv, exact, den, out_part, residual, heads, 7
-    )
+    dmixed, block_own = back(dresid_low, attn_pack, out_part, residual, vcols, 7)
     out_grad = tn_dot(mixed, dresid_low).astype(jnp.bfloat16)
-    qkv_grad = tn_dot(dqkv, normed_one)[:qkv_rows].astype(jnp.bfloat16)
-    dqkv, out_grad, qkv_grad, gate_grad, up_grad = lax.optimization_barrier(
-        (dqkv, out_grad, qkv_grad, gate_grad, up_grad)
-    )
-    out_grad, qkv_grad = summed(out_grad), summed(qkv_grad)
-    dtokens, block_out, gain_grads = leave(
-        dqkv, attn_pack, x, dresid, block_own, small, gain_two_grad, 8
-    )
-    down_grad, gate_grad, up_grad, dtokens = lax.optimization_barrier(
-        (down_grad, gate_grad, up_grad, dtokens)
-    )
-    down_grad, gate_grad, up_grad = collect([down_grad, gate_grad, up_grad], 9)
-    out_grad, qkv_grad = collect([out_grad, qkv_grad], 10)
+    dmixed, gate_grad, out_grad = lax.optimization_barrier((dmixed, gate_grad, out_grad))
+    dqkv, (down_grad, gate_grad) = unmix(
+        seg_col, seg_row, qkv, exact, den, dmixed, [down_grad, gate_grad], heads, 8
+    )
+    qkv_grad = tn_dot(dqkv, normed_one).astype(jnp.bfloat16)[:qkv_rows]
+    out_grad = summed(out_grad)
+    dqkv, qkv_grad, up_grad = lax.optimization_barrier((dqkv, qkv_grad, up_grad))
+    qkv_grad = summed(qkv_grad)
+    dtokens, block_out, gains = leave(
+        dqkv, attn_pack, x, dresid, block_own, small, gain_two_grad, 9
+    )
+    (up_grad, out_grad, qkv_grad), gain_grads = last([up_grad, out_grad, qkv_grad], gains, 10)
 
     def stacked(a, start, size):
         return a[:, start : start + size].reshape(plane * size, chunk).astype(jnp.float32)

time: 782 us -> 699 us (0.89)
  Pallas kernels: 683 us -> 628 us
  matrix products: 45 us -> 24.6 us
    pallas_call x4 -> x1, Pallas kernels: 113 us -> 26.6 us  [exchange(): pl.pallas_call(partial(exchange_kernel, take, put, count), name='exchange...]
    pallas_call x6 -> x10, Pallas kernels: 553 us -> 585 us  [kernel_call(): pl.pallas_call(body, name=name, out_shape=[jax.ShapeDtypeStruct(s, d) for...]
    dot_general x5 -> x2, matrix products: 45 us -> 14.2 us  [tn_dot(): lax.dot_general(a, b, (((0,), (0,)), ((), ())), preferred_element_type=jn...]
    dot_general x0 -> x1, matrix products: none -> 10.3 us  [nn_dot(): lax.dot_general(a, b, (((1,), (0,)), ((), ())), preferred_element_type=jn...]
  transfers between devices with their start and end apart: 7 -> 7, of which waited for: 0 -> 1; matrix products, arithmetic and copies ran while one was open for 3% -> 3% of each run, Pallas kernels for 78% -> 74%
where the time goes in v4:
time: 699 us
  Pallas kernels  628 us (90%)
  matrix products  24.6 us (4%)
  local copies, waits for them, and re-layouts  17.5 us (3%)
  between operations  14.5 us (2%)
  other arithmetic  11.8 us (2%)
    pallas_call x10, Pallas kernels, kernel_call(): pl.pallas_call(body, name=name, out_shape=[jax.ShapeDtypeStruct(s, d) for...  585 us
    pallas_call x1, Pallas kernels, exchange(): pl.pallas_call(partial(exchange_kernel, take, put, count), name='exchange...  26.6 us
    pallas_call x1, Pallas kernels, first_exchange(): pl.pallas_call(first_kernel, name='first_exchange', out_shape=[jax.ShapeD...  16.7 us
    dot_general x2, matrix products, tn_dot(): lax.dot_general(a, b, (((0,), (0,)), ((), ())), preferred_element_type=jn...  14.2 us
  transfers between devices with their start and end apart: 7, of which 1 were waited for; matrix products, arithmetic and copies ran while one was open for 3% of the time, Pallas kernels for 74%

profile of v4, /device:TPU:0, one launch (start us, length us, event | category | flops | bytes accessed | tf_op | source)
XLA Modules:
  0.0 698.8 jit_solution(3287214987333312755)
XLA Ops:
  7.2 0.0 all-gather.5.cloned.1.call-start
  7.3 0.8 convert_element_type.46
  8.1 0.9 copy.31
  9.0 0.9 copy.32
  9.8 1.1 copy.30
  11.0 0.1 pad.6.clone
  11.1 0.7 bitcast_convert_fusion.5
  11.8 0.7 maximum_maximum_fusion.small_ref
  12.4 1.8 pad_maximum_fusion.1.pack_ref
  14.2 16.7 %first_exchange.1 = (bf16[576,512]{1,0:T(8,128)(2,1)}, f32[16,8,128]{2,1,0:T(8,128)}) custom-call(bf16[4,576,128]{2,1,0:T(8,128)(2,1)} %pad_maximum_fusion.1.pack_ref, f32[8,128]{1,0:T(8,128)} %maximum_maximum_fusion.small_ref), custom_call_target="tpu_custom_call" | custom-call | bytes 17694720 | tf_op jit(solution)/shard_map/first_exchange/pallas_call | solution.py:570
  30.9 0.0 all-gather.5.cloned.1.call-update
  31.0 0.0 all-gather.7.cloned.1.call-start
  31.0 0.0 copy-done.7
  31.0 0.0 copy-done.8
  31.0 1.5 pad_maximum_fusion.refs_0_
  32.5 26.6 %exchange.1 = bf16[2064,512]{1,0:T(8,128)(2,1)} custom-call(bf16[4,2064,128]{2,1,0:T(8,128)(2,1)} %pad_maximum_fusion.refs_0_), custom_call_target="tpu_custom_call" | custom-call | bytes 63406080 | tf_op jit(solution)/shard_map/exchange/pallas_call | solution.py:522
  59.1 0.0 all-gather.7.cloned.1.call-update
  59.1 0.0 reduce-scatter.6.cloned.1.call-start
  59.2 0.8 copy-done.3
  60.0 0.6 reduce-window.6
  60.6 0.2 slice_reduce_fusion
  60.8 0.2 reduce-window.9
  60.9 0.1 broadcast_add_fusion
  61.0 1.9 reduce_window_sum.34.col_ref
  62.9 43.4 %entry.1 = (bf16[4,2,256,2048]{3,2,1,0:T(8,128)(2,1)}, bf16[256,2048]{1,0:T(8,128)(2,1)}, bf16[256,2048]{1,0:T(8,128)(2,1)}) custom-call(bf16[2,256,2048]{2,1,0:T(8,128)(2,1)} %tokens_ref.1, bf16[2,256,2048]{2,1,0:T(8,128)(2,1)} %cot_ref.1, f32[16,8,128]{2,1,0:T(8,128)} %get-tuple-element.58.small_ref), custom_call_target="tpu_custom_call" | custom-call | bytes 41943040 | tf_op jit(solution)/shard_map/entry/pallas_call | solution.py:620
  106.3 0.0 all-gather.5.cloned.1.call-done
  106.3 129.4 %mix.1 = (bf16[4,512,384]{2,1,0:T(8,128)(2,1)}, bf16[4,512,256]{2,1,0:T(8,128)(2,1)}, f32[4,512,256]{2,1,0:T(8,128)}, f32[4,512,128]{2,1,0:T(8,128)}, bf16[4,2,256,2048]{3,2,1,0:T(8,128)(2,1)}) custom-call(bf16[2048,2048]{1,0:T(8,128)(2,1)} %bitcast.76, bf16[4,576,512]{2,1,0:T(8,128)(2,1)} %bitcast.72, f32[2,4,256,1]{3,2,1,0:T(8,128)} %reduce_window_sum.34.col_ref, ...), custom_call_target="tpu_custom_call" | custom-call | bytes 167772160 | tf_op jit(solution)/shard_map/mix/pallas_call | solution.py:620
  235.7 49.5 %branch.1 = (f32[256,2048]{1,0:T(8,128)}, bf16[256,2048]{1,0:T(8,128)(2,1)}) custom-call(bf16[2048,256]{1,0:T(8,128)(2,1)} %bitcast.78, bf16[4,576,512]{2,1,0:T(8,128)(2,1)} %bitcast.73, bf16[256,2048]{1,0:T(8,128)(2,1)} %get-tuple-element.66.x_ref, f32[16,8,128]{2,1,0:T(8,128)} %get-tuple-element.58.small_ref), custom_call_target="tpu_custom_call" | custom-call | bytes 41943040 | tf_op jit(solution)/shard_map/branch/pallas_call | solution.py:620
  285.3 1.5 all-gather.7.cloned.1.call-done
  286.8 55.6 %expand.1 = (bf16[4,2,256,2048]{3,2,1,0:T(8,128)(2,1)}, bf16[4,2,256,2048]{3,2,1,0:T(8,128)(2,1)}, bf16[4,2,256,2048]{3,2,1,0:T(8,128)(2,1)}, bf16[688,2048]{1,0...) custom-call(bf16[256,2048]{1,0:T(8,128)(2,1)} %get-tuple-element.67.own_ref, ...), custom_call_target="tpu_custom_call" | custom-call | flops 34628173824 | bytes 268435456 | tf_op jit(solution)/shard_map/expand/pallas_call | solution.py:620
  342.4 10.3 %convolution_convert_fusion = bf16[688,2048]{1,0:T(8,128)(2,1)} fusion(bf16[688,2048]{1,0:T(8,128)(2,1)} %get-tuple-element.71, bf16[2048,2048]{1,0:T(8,128)(2,1)} %bitcast.99), kind=kOutput, calls=%fused_computation | convolution fusion | flops 5772771328 | bytes 14024704 | tf_op jit(solution)/shard_map/dot_general | solution.py:303
  352.7 0.0 reduce-scatter.6.cloned.1.call-update
  352.8 0.0 reduce-scatter.8.cloned.1.call-start
  352.8 41.8 %middle.1 = (f32[256,2048]{1,0:T(8,128)}, bf16[688,2048]{1,0:T(8,128)(2,1)}, bf16[688,2048]{1,0:T(8,128)(2,1)}) custom-call(bf16[4,2,256,2048]{3,2,1,0:T(8,128)(2,1)} %get-tuple-element.72.part_hbm, bf16[2048,2048]{1,0:T(8,128)(2,1)} %bitcast.100, bf16[688,2048]{1,0:T(8,128)(2,1)} %get-tuple-element.74.dgate_hbm, bf16[688,2048]{1,0:T(8,128)(2,1)} %get-tuple-element.75.dup_hbm), custom_call_target="tpu_custom_call" | custom-call | flops 11542724608 | bytes 41943040 | tf_op jit(solution)/shard_map/middle/pallas_call | solution.py:620
  394.6 0.0 reduce-scatter.8.cloned.1.call-update
  394.6 0.0 reduce-scatter.10.cloned.1.call-start
  394.7 0.5 reduce-scatter.10.cloned.1.call-update
  395.2 0.0 reduce-scatter.12.cloned.1.call-start
  395.3 44.7 %turn.1 = (f32[256,2048]{1,0:T(8,128)}, f32[8,2048]{1,0:T(8,128)}, bf16[4,2,256,2048]{3,2,1,0:T(8,128)(2,1)}) custom-call(f32[256,2048]{1,0:T(8,128)} %get-tuple-element.76.total_ref, f32[256,2048]{1,0:T(8,128)} %get-tuple-element.77.residual_ref, bf16[256,2048]{1,0:T(8,128)(2,1)} %get-tuple-element.61.cot_ref, f32[16,8,128]{2,1,0:T(8,128)} %get-tuple-element.58.small_ref), custom_call_target="tpu_custom_call" | custom-call | bytes 41943040 | tf_op jit(solution)/shard_map/turn/pallas_call | solution.py:620
  440.0 0.0 reduce-scatter.6.cloned.1.call-done.refs_0_
  440.0 63.6 %back.1 = (bf16[4,512,256]{2,1,0:T(8,128)(2,1)}, bf16[256,2048]{1,0:T(8,128)(2,1)}) custom-call(bf16[2048,2048]{1,0:T(8,128)(2,1)} %bitcast.70, bf16[4,576,512]{2,1,0:T(8,128)(2,1)} %bitcast.74, bf16[4,2,256,2048]{3,2,1,0:T(8,128)(2,1)} %get-tuple-element.81.part_ref, f32[256,2048]{1,0:T(8,128)} %get-tuple-element.77.residual_ref), custom_call_target="tpu_custom_call" | custom-call | bytes 62914560 | tf_op jit(solution)/shard_map/back/pallas_call | solution.py:620
  503.7 6.7 convolution_convert_fusion.1
  510.4 0.0 reduce-scatter.12.cloned.1.call-update
  510.4 0.0 reduce-scatter.14.cloned.1.call-start
  510.5 65.8 %unmix.1 = (bf16[4,512,384]{2,1,0:T(8,128)(2,1)}, bf16[4,688,128]{2,1,0:T(8,128)(2,1)}, bf16[4,688,128]{2,1,0:T(8,128)(2,1)}) custom-call(f32[2,4,256,1]{3,2,1,0:T(8,128)} %reduce_window_sum.34.col_ref, f32[2,4,1,256]{3,2,1,0:T(1,128)} %bitcast.92, bf16[4,512,384]{2,1,0:T(8,128)(2,1)} %get-tuple-element.62.qkv_ref, ...), custom_call_target="tpu_custom_call" | custom-call | bytes 94371840 | tf_op jit(solution)/shard_map/unmix/pallas_call | solution.py:620
  576.3 7.5 %fusion.1 = bf16[384,2048]{1,0:T(8,128)(2,1)S(1)} fusion(bf16[2048,384]{1,0:T(8,128)(2,1)} %bitcast.80, bf16[2048,2048]{1,0:T(8,128)(2,1)} %bitcast.77), kind=kOutput, calls=%fused_computation.21 | convolution fusion | flops 3221225472 | bytes 11534336 | tf_op jit(solution)/shard_map/dot_general | solution.py:299
  583.9 1.1 slice.42
  585.0 0.0 reduce-scatter.14.cloned.1.call-update
  585.0 55.4 %leave.1 = (f32[2,256,2048]{2,1,0:T(8,128)}, bf16[2,256,2048]{2,1,0:T(8,128)(2,1)}, f32[16,8,128]{2,1,0:T(8,128)}) custom-call(bf16[2048,384]{1,0:T(8,128)(2,1)} %bitcast.81, bf16[4,576,512]{2,1,0:T(8,128)(2,1)} %bitcast.75, bf16[256,2048]{1,0:T(8,128)(2,1)} %get-tuple-element.66.x_ref, f32[256,2048]{1,0:T(8,128)} %get-tuple-element.90.dresid_ref, ...), custom_call_target="tpu_custom_call" | custom-call | bytes 62914560 | tf_op jit(solution)/shard_map/leave/pallas_call | solution.py:620
  640.5 1.2 convert_bitcast_fusion.1
  641.7 1.2 bitcast_convert_fusion
  642.9 35.4 %last.1 = (bf16[4,688,128]{2,1,0:T(8,128)(2,1)}, bf16[4,256,128]{2,1,0:T(8,128)(2,1)}, bf16[4,320,128]{2,1,0:T(8,128)(2,1)}, f32[8,128]{1,0:T(8,128)}) custom-call(bf16[688,512]{1,0:T(8,128)(2,1)} %reduce-scatter.10.cloned.1.call-done.refs_0_, bf16[256,512]{1,0:T(8,128)(2,1)} %reduce-scatter.12.cloned.1.call-done.refs_1_, ...), custom_call_target="tpu_custom_call" | custom-call | bytes 67108864 | tf_op jit(solution)/shard_map/last/pallas_call | solution.py:620
  678.4 0.9 fusion
  679.2 1.0 slice.35
  680.2 1.3 slice_bitcast_fusion
  681.5 0.7 copy.37
  682.2 0.7 copy.36
  683.0 0.1 bitcast_convert_fusion.2
  683.0 1.0 copy.38
  684.0 1.8 bitcast_convert_fusion.1
  685.8 1.2 convert_bitcast_fusion
  687.0 1.3 copy.41
  688.3 1.6 copy-done.1
  690.0 2.0 copy.42
  (31 shorter events, 0.1 us)
Async XLA Ops:
  7.2 23.8 %copy-start.7 = (bf16[2752,128]{1,0:T(8,128)(2,1)S(1)}, bf16[2752,128]{1,0:T(8,128)(2,1)}, u32[]{:S(2)}) copy-start(bf16[2752,128]{1,0:T(8,128)(2,1)} %param.22) | copy-start | bytes 2113540
  7.2 23.8 %copy-start.8 = (bf16[128,2752]{0,1:T(8,128)(2,1)S(1)}, bf16[128,2752]{0,1:T(8,128)(2,1)}, u32[]{:S(2)}) copy-start(bf16[128,2752]{0,1:T(8,128)(2,1)} %param.21) | copy-start | bytes 2113540
  7.2 23.8 %copy-start.9 = (bf16[128,2752]{0,1:T(8,128)(2,1)S(1)}, bf16[128,2752]{0,1:T(8,128)(2,1)}, u32[]{:S(2)}) copy-start(bf16[128,2752]{0,1:T(8,128)(2,1)} %param.20) | copy-start | bytes 2113540
  7.2 99.1 %all-gather.5.cloned.1.call-start = ((), (), s32[]{:S(2)}) async-start(), calls=%async_computation.10 | async-start | bytes 2949120 | tf_op jit(solution)/shard_map/all_gather | solution.py:1690
  31.0 255.8 %all-gather.7.cloned.1.call-start = ((), (), s32[]{:S(2)}) async-start(), calls=%async_computation.11 | async-start | bytes 10567680 | tf_op jit(solution)/shard_map/all_gather | solution.py:1690
  59.1 0.8 copy-start.3
  59.1 380.9 %reduce-scatter.6.cloned.1.call-start = ((), (), s32[]{:S(2)}) async-start(), calls=%async_computation.5 | async-start | bytes 3522560 | tf_op jit(solution)/shard_map/reduce_scatter | solution.py:1693
  61.0 45.3 %copy-start.10 = (f32[2,8,128]{2,1,0:T(8,128)}, f32[2,8,128]{2,1,0:T(8,128)S(1)}, u32[]{:S(2)}) copy-start(f32[2,8,128]{2,1,0:T(8,128)S(1)} %broadcast_add_fusion) | copy-start | bytes 24580
  352.8 157.6 %reduce-scatter.8.cloned.1.call-start = ((), (), s32[]{:S(2)}) async-start(), calls=%async_computation.6 | async-start | bytes 3522560 | tf_op jit(solution)/shard_map/reduce_scatter | solution.py:1693
  394.6 190.4 %reduce-scatter.10.cloned.1.call-start = ((), (), s32[]{:S(2)}) async-start(), calls=%async_computation.7 | async-start | bytes 3522560 | tf_op jit(solution)/shard_map/reduce_scatter | solution.py:1693
  395.2 247.7 %reduce-scatter.12.cloned.1.call-start = ((), (), s32[]{:S(2)}) async-start(), calls=%async_computation.8 | async-start | bytes 1310720 | tf_op jit(solution)/shard_map/reduce_scatter | solution.py:1693
  440.0 63.6 %copy-start = (bf16[4,512,256]{2,1,0:T(8,128)(2,1)S(1)}, bf16[4,512,256]{2,1,0:T(8,128)(2,1)}, u32[]{:S(2)}) copy-start(bf16[4,512,256]{2,1,0:T(8,128)(2,1)} %get-tuple-element.65) | copy-start | bytes 3145732
  510.4 132.5 %reduce-scatter.14.cloned.1.call-start = ((), (), s32[]{:S(2)}) async-start(), calls=%async_computation.9 | async-start | bytes 1638400 | tf_op jit(solution)/shard_map/reduce_scatter | solution.py:1693
  585.0 55.4 %copy-start.5 = (bf16[4,688,128]{2,1,0:T(8,128)(2,1)S(1)}, bf16[4,688,128]{2,1,0:T(8,128)(2,1)}, u32[]{:S(2)}) copy-start(bf16[4,688,128]{2,1,0:T(8,128)(2,1)} %get-tuple-element.102) | copy-start | bytes 2113540
  640.4 1.2 copy-start.4
  678.4 7.4 %copy-start.6 = (bf16[4,688,128]{2,1,0:T(8,128)(2,1)S(1)}, bf16[4,688,128]{2,1,0:T(8,128)(2,1)}, u32[]{:S(2)}) copy-start(bf16[4,688,128]{2,1,0:T(8,128)(2,1)} %get-tuple-element.103) | copy-start | bytes 2113540
  683.0 4.0 copy-start.2
  687.0 2.9 copy-start.1
Sparse Core Ops, SparseCore 0:
  31.1 48.6 all-gather.4
  81.4 205.3 all-gather.6
  352.9 66.8 reduce-scatter.5
  422.1 67.3 reduce-scatter.7
  491.6 71.0 reduce-scatter.9
  565.6 34.9 reduce-scatter.11
  603.5 30.4 reduce-scatter.13

commit v5 on v4

--- a/solution.py
+++ b/solution.py
@@ -2,6 +2,7 @@
 
 import jax
 import jax.numpy as jnp
+import numpy as np
 from jax import lax
 from jax.experimental import pallas as pl
 from jax.experimental.pallas import tpu as pltpu
@@ -679,23 +680,121 @@
     return gathered.reshape(-1, width), x, cot_own
 
 
+FEATURES = 256
+STATE_ROWS = 160
+CHUNKS = 4
+
+
+def feature_pairs():
+    first = np.full(FEATURES, -4096, np.int32)
+    second = np.full(FEATURES, -4096, np.int32)
+    pairs = [(i, j) for i in range(FDIM + 1) for j in range(i, FDIM + 1)]
+    for f, (i, j) in enumerate(pairs):
+        first[f], second[f] = i, j
+    return jnp.asarray(np.stack([first, second] + [first] * 6))
+
+
+def feature_scale(pairs_ref):
+    i, j = pairs_ref[0:1, :], pairs_ref[1:2, :]
+    square = jnp.where(i == j, 1.0 / 32.0, 1.0 / 16.0)
+    return jnp.where(j == FDIM, jnp.where(i == FDIM, 1.0, 0.25), square)
+
+
+def fill_selectors(pairs_ref, pick_ref, qcols):
+    kinds, heads = pick_ref.shape[:2]
+    lane = lax.broadcasted_iota(jnp.int32, (LANES, FEATURES), 0)
+    for kind in range(kinds):
+        for h in range(heads):
+            for side in range(2):
+                index = pairs_ref[side : side + 1, :]
+                source = jnp.where(
+                    index == FDIM, 2 * qcols, index + (kind * qcols + h * FDIM)
+                )
+                pick_ref[kind, h, side] = jnp.where(lane == source, 1.0, 0.0).astype(jnp.bfloat16)
+
+
+def factors(tile, pick_ref, kind, h):
+    return nn_dot(tile, pick_ref[kind, h, 0]), nn_dot(tile, pick_ref[kind, h, 1])
+
+
+def keys_in_place(tile, qcols):
+    return pltpu.roll(tile.astype(jnp.float32), LANES - qcols, axis=1).astype(jnp.bfloat16)
+
+
 def head_mask(rows, head):
     lane = lax.broadcasted_iota(jnp.int32, (rows, LANES), 1)
     return (lane >= head * FDIM) & (lane < (head + 1) * FDIM)
 
 
-def keys_in_place(qkv_ref, keys_ref, vcols, qcols):
-    for j in range(qkv_ref.shape[0]):
-        tile = qkv_ref[j, :, pl.ds(vcols, LANES)].astype(jnp.float32)
-        keys_ref[j] = pltpu.roll(tile, LANES - qcols, axis=1).astype(jnp.bfloat16)
-
-
-def masked_weights(query, key, col_ref, row_ref, r, i, j, length):
+def masked_weights(query, key, column, row):
+    length = query.shape[0]
     a = nt_dot(query, key) * 0.25
-    t = lax.broadcasted_iota(jnp.int32, (length, length), 0) + i * length
-    s = lax.broadcasted_iota(jnp.int32, (length, length), 1) + j * length
-    keep = (s <= t) & (col_ref[r, i] == row_ref[r, j])
+    t = lax.broadcasted_iota(jnp.int32, (length, length), 0)
+    s = lax.broadcasted_iota(jnp.int32, (length, length), 1)
+    keep = (s <= t) & (column == row)
     return a, jnp.where(keep, 1.0 + a + 0.5 * a * a, 0.0), keep
+
+
+class Segments:
+    def __init__(self, col_ref, row_ref, b):
+        self.column, self.row = col_ref[b], row_ref[b]
+        last = self.row[:, -1:]
+        self.head = self.column == 0.0
+        self.tail = self.column == last
+        self.keep = jnp.where(last == 0.0, 1.0, 0.0)
+
+
+def pass_states(state_ref, sums_ref, own_ref, own_sums_ref, out_ref, out_sums_ref, col_row, chunk):
+    col_ref, row_ref = col_row
+    rows, heads = state_ref.shape[0] // CHUNKS, state_ref.shape[1]
+    for n in range(rows):
+        b = chunk * rows + n
+        keep = Segments(col_ref, row_ref, b).keep
+        for h in range(heads):
+            out_ref[b, h] = (own_ref[b, h] + keep * state_ref[b, h].astype(jnp.float32)).astype(
+                jnp.bfloat16
+            )
+        out_sums_ref[b] = own_sums_ref[b] + keep * sums_ref[b]
+
+
+class Chain:
+    def __init__(self, forward, state_ref, sums_ref, out_ref, out_sums_ref, copy):
+        span, z = lax.axis_size("seq"), lax.axis_index("seq")
+        to = lax.rem(z + (1 if forward else span - 1), span)
+        self.gets = z > 0 if forward else z < span - 1
+        self.gives = z < span - 1 if forward else z > 0
+        rows = state_ref.shape[0] // CHUNKS
+        self.moves = []
+        for g in range(CHUNKS):
+            part = pl.ds(g * rows, rows)
+            used = pl.ds(0, STATE_ROWS)
+            self.moves.append(
+                (
+                    copy(
+                        out_ref.at[part, :, used], state_ref.at[part, :, used], {"seq": to}
+                    ),
+                    copy(out_sums_ref.at[part], sums_ref.at[part], {"seq": to}),
+                )
+            )
+
+    def get(self, g):
+        @pl.when(self.gets)
+        def _():
+            for c in self.moves[g]:
+                c.wait_recv()
+
+    def give(self, g):
+        @pl.when(self.gives)
+        def _():
+            for c in self.moves[g]:
+                c.start()
+
+    def close(self):
+        @pl.when(self.gives)
+        def _():
+            for move in self.moves:
+                for c in move:
+                    c.wait_send()
 
 
 def mix_kernel(
@@ -704,134 +803,176 @@
     pack_ref,
     col_ref,
     row_ref,
+    pairs_ref,
     cot_ref,
+    up_ref,
+    down_ref,
     qkv_ref,
     mixed_ref,
     exact_ref,
     den_ref,
+    state_ref,
+    sums_ref,
     cot_all_ref,
-    out_qkv,
-    out_mixed,
-    keys_ref,
+    up_all_ref,
+    down_all_ref,
+    pick_ref,
+    own_ref,
+    own_sums_ref,
+    out_ref,
+    out_sums_ref,
     sems,
     cot_sems,
     local_sem,
+    shard_sems,
+    shard_local_sems,
 ):
-    span, z = lax.axis_size("seq"), lax.axis_index("seq")
     parts, _, depth = pack_ref.shape
-    tokens = qkv_ref.shape[1]
-    rows, length = col_ref.shape[0], col_ref.shape[2]
+    rows, length = col_ref.shape[0], col_ref.shape[1]
     vcols, qcols = heads * VHEAD, heads * FDIM
     at, x_at, y_at, _, core = plane_places()
-    peers = [lax.rem(z + k, span) for k in range(1, span)]
-    greet([{"dp": x_at}, {"dp": y_at}, {"tensor": 1 - core}] + [{"seq": p} for p in peers])
+    plane, span, z = lax.axis_size("dp"), lax.axis_size("seq"), lax.axis_index("seq")
+    chips = [lax.rem(at + k, plane) for k in range(1, plane)]
+    state_ref[...] = jnp.zeros_like(state_ref)
+    sums_ref[...] = jnp.zeros_like(sums_ref)
+    greet(
+        [{"dp": p} for p in chips]
+        + [{"tensor": 1 - core}]
+        + [{"seq": lax.rem(z + k, span)} for k in (1, span - 1)]
+    )
     gather = gather_steps(cot_ref, cot_all_ref, Sender(cot_sems), local_sem)
     next(gather)
-    copy = Sender(sems)
-
-    def project(dest, out):
-        x = pl.ds(pl.multiple_of(dest * tokens, tokens), tokens)
-        value = jnp.zeros((tokens, vcols), jnp.float32)
-        tile = jnp.zeros((tokens, LANES), jnp.float32)
+    shards = swap_shards(
+        (up_ref, down_ref),
+        (up_all_ref, down_all_ref),
+        chips,
+        at,
+        block_of,
+        columns_of,
+        Sender(shard_sems),
+        shard_local_sems,
+    )
+    chain = Chain(True, state_ref, sums_ref, out_ref, out_sums_ref, Sender(sems))
+    fill_selectors(pairs_ref, pick_ref, qcols)
+    scale = feature_scale(pairs_ref)
+
+    def tokens_of(b):
+        return pl.ds(pl.multiple_of(b * length, length), length)
+
+    def first(b, carry):
+        t = tokens_of(b)
+        value = jnp.zeros((length, vcols), jnp.float32)
+        tile = jnp.zeros((length, LANES), jnp.float32)
         for s in range(parts):
-            piece = normed_ref[x, pl.ds(s * depth, depth)]
+            piece = normed_ref[t, pl.ds(s * depth, depth)]
             value += nt_dot(piece, pack_ref[s, pl.ds(0, vcols)])
             tile += nt_dot(piece, pack_ref[s, pl.ds(vcols, LANES)])
-        lane = lax.broadcasted_iota(jnp.int32, (tokens, LANES), 1)
-        out[:, pl.ds(0, vcols)] = value.astype(jnp.bfloat16)
-        out[:, pl.ds(vcols, LANES)] = jnp.where(lane < 2 * qcols, tile, 0.0).astype(jnp.bfloat16)
-
-    there = []
-    for k, p in enumerate(peers):
-        project(p, out_qkv.at[k])
-        there.append(copy(out_qkv.at[k], qkv_ref.at[z], {"seq": p}))
-        there[-1].start()
-    project(z, qkv_ref.at[z])
+        lane = lax.broadcasted_iota(jnp.int32, (length, LANES), 1)
+        tile = jnp.where(lane < 2 * qcols, tile, jnp.where(lane == 2 * qcols, 1.0, 0.0))
+        value, tile = value.astype(jnp.bfloat16), tile.astype(jnp.bfloat16)
+        qkv_ref[t, pl.ds(0, vcols)] = value
+        qkv_ref[t, pl.ds(vcols, LANES)] = tile
+        tail = Segments(col_ref, row_ref, b).tail
+        for h in range(heads):
+            one, two = factors(tile, pick_ref, 1, h)
+            lifted = jnp.where(tail, one * two * scale, 0.0)
+            own_ref[b, h] = tn_dot(
+                lifted.astype(jnp.bfloat16), value[:, h * VHEAD : (h + 1) * VHEAD]
+            )
+            own_sums_ref[b, h : h + 1] = jnp.sum(lifted, axis=0, keepdims=True)
+        return carry
+
+    own_sums_ref[...] = jnp.zeros_like(own_sums_ref)
+    lax.fori_loop(0, rows, first, 0)
+
+    def mixer(b, carry):
+        t = tokens_of(b)
+        seg = Segments(col_ref, row_ref, b)
+        tile = qkv_ref[t, pl.ds(vcols, LANES)]
+        key = keys_in_place(tile, qcols)
+        lane = lax.broadcasted_iota(jnp.int32, (length, LANES), 1)
+        dens = jnp.zeros((length, LANES), jnp.float32)
+        for h in range(heads):
+            v = pl.ds(h * VHEAD, VHEAD)
+            query = jnp.where(head_mask(length, h), tile, jnp.zeros_like(tile))
+            _, w, _ = masked_weights(query, key, seg.column, seg.row)
+            one, two = factors(tile, pick_ref, 0, h)
+            lifted = jnp.where(seg.head, one * two, 0.0)
+            num = nn_dot(w.astype(jnp.bfloat16), qkv_ref[t, v])
+            num += nn_dot(lifted.astype(jnp.bfloat16), state_ref[b, h])
+            den = jnp.sum(w, axis=1, keepdims=True)
+            den += jnp.sum(lifted * sums_ref[b, h : h + 1], axis=1, keepdims=True)
+            value = num / den
+            exact_ref[t, v] = value
+            mixed_ref[t, v] = value.astype(jnp.bfloat16)
+            dens = jnp.where(lane == h, den, dens)
+        den_ref[t] = dens
+        return carry
+
+    each = rows // CHUNKS
+    for g in range(CHUNKS):
+        chain.get(g)
+        pass_states(
+            state_ref, sums_ref, own_ref, own_sums_ref, out_ref, out_sums_ref, (col_ref, row_ref), g
+        )
+        chain.give(g)
+        if g == 0:
+            next(gather)
+            next(gather)
+            next(gather)
+        lax.fori_loop(g * each, (g + 1) * each, mixer, 0)
     run(gather)
-    for c in there:
+    for c in shards:
         c.wait()
-    keys_in_place(qkv_ref, keys_ref, vcols, qcols)
-
-    def mixer(i, out):
-        def one_row(r, carry):
-            t = pl.ds(pl.multiple_of(r * length, length), length)
-            tile = qkv_ref[i, t, pl.ds(vcols, LANES)]
-            queries = [
-                jnp.where(head_mask(length, h), tile, jnp.zeros_like(tile)) for h in range(heads)
-            ]
-
-            def block(j, carry):
-                new = []
-                for h in range(heads):
-                    num, den = carry[h]
-                    _, w, _ = masked_weights(
-                        queries[h], keys_ref[j, t], col_ref, row_ref, r, i, j, length
-                    )
-                    value = qkv_ref[j, t, pl.ds(h * VHEAD, VHEAD)]
-                    new.append(
-                        (
-                            num + nn_dot(w.astype(jnp.bfloat16), value),
-                            den + jnp.sum(w, axis=1, keepdims=True),
-                        )
-                    )
-                return tuple(new)
-
-            zero = (
-                jnp.zeros((length, VHEAD), jnp.float32),
-                jnp.zeros((length, 1), jnp.float32),
-            )
-            done = lax.fori_loop(0, i + 1, block, (zero,) * heads)
-            lane = lax.broadcasted_iota(jnp.int32, (length, LANES), 1)
-            dens = jnp.zeros((length, LANES), jnp.float32)
-            for h, (num, den) in enumerate(done):
-                v = num / den
-                exact_ref[i, t, pl.ds(h * VHEAD, VHEAD)] = v
-                out[t, pl.ds(h * VHEAD, VHEAD)] = v.astype(jnp.bfloat16)
-                dens = jnp.where(lane == h, den, dens)
-            den_ref[i, t] = dens
-            return carry
-
-        lax.fori_loop(0, rows, one_row, 0)
-
-    back = []
-    for k, p in enumerate(peers):
-        mixer(p, out_mixed.at[k])
-        back.append(copy(out_mixed.at[k], mixed_ref.at[z], {"seq": p}))
-        back[-1].start()
-    mixer(z, mixed_ref.at[z])
-    for c in back:
-        c.wait()
-
-
-def mix(normed, pack, seg_col, seg_row, cot_own, heads, cid):
-    span = lax.axis_size("seq")
-    tokens = normed.shape[0] // span
+    chain.close()
+
+
+def state_scratch(rows, heads):
+    return [
+        pltpu.VMEM((2, heads, 2, LANES, FEATURES), jnp.bfloat16),
+        pltpu.VMEM((rows, heads, FEATURES, VHEAD), jnp.float32),
+        pltpu.VMEM((rows, 8, FEATURES), jnp.float32),
+        pltpu.VMEM((rows, heads, FEATURES, VHEAD), jnp.bfloat16),
+        pltpu.VMEM((rows, 8, FEATURES), jnp.float32),
+    ]
+
+
+def mix(normed, pack, seg_col, seg_row, pairs, cot_own, up, down, heads, cid):
+    tokens = normed.shape[0]
+    rows = seg_col.shape[0]
     vcols = heads * VHEAD
     m, width = cot_own.shape
+    plane, size, chunk = up.shape
     whole = pltpu.VMEM
-    qkv, mixed, exact, den, cot = kernel_call(
+    out = kernel_call(
         partial(mix_kernel, heads),
         "mix",
         cid,
         [
-            ((span, tokens, vcols + LANES), jnp.bfloat16, whole),
-            ((span, tokens, vcols), jnp.bfloat16, whole),
-            ((span, tokens, vcols), jnp.float32, whole),
-            ((span, tokens, LANES), jnp.float32, whole),
+            ((tokens, vcols + LANES), jnp.bfloat16, whole),
+            ((tokens, vcols), jnp.bfloat16, whole),
+            ((tokens, vcols), jnp.float32, whole),
+            ((tokens, LANES), jnp.float32, whole),
+            ((rows, heads, FEATURES, VHEAD), jnp.bfloat16, whole),
+            ((rows, 8, FEATURES), jnp.float32, whole),
             ((4, 2, m, width), jnp.bfloat16, pl.ANY),
+            ((size, plane * chunk), jnp.bfloat16, pl.ANY),
+            ((size, plane * chunk), jnp.bfloat16, pl.ANY),
         ],
-        [(normed, whole), (pack, whole), (seg_col, whole), (seg_row, whole), (cot_own, whole)],
-        [
-            pltpu.VMEM((span - 1, tokens, vcols + LANES), jnp.bfloat16),
-            pltpu.VMEM((span - 1, tokens, vcols), jnp.bfloat16),
-            pltpu.VMEM((span, tokens, LANES), jnp.bfloat16),
-            copies(2 * (span - 1)),
+        [(a, whole) for a in (normed, pack, seg_col, seg_row, pairs, cot_own)]
+        + [(up, pl.ANY), (down, pl.ANY)],
+        state_scratch(rows, heads)
+        + [
+            copies(2 * CHUNKS),
             copies(GATHER_COPIES),
             pltpu.SemaphoreType.DMA,
+            copies(2 * (plane - 1)),
+            pltpu.SemaphoreType.DMA((2,)),
         ],
-        moved=normed.size * 40,
-    )
-    return qkv, mixed.reshape(-1, vcols), exact, den, cot.reshape(-1, width)
+        moved=normed.size * 30,
+    )
+    qkv, mixed, exact, den, state, sums, cot, up, down = out
+    return (qkv, mixed, exact, den, state, sums), cot.reshape(-1, width), up, down
 
 
 def branch_kernel(
@@ -914,69 +1055,43 @@
     return jnp.where(test, a, b)
 
 
-def ffn_block(x_at, cot_at, w_ref, out_ref, dnormed_ref, dgate_ref, dup_ref, hidden_ref):
-    parts, units, depth = w_ref.shape
-    units //= 3
-
-    def rows(k):
-        return pl.ds(k * units, units)
-
-    def cols(s):
-        return pl.ds(s * depth, depth)
-
-    def project(at, k):
-        total = nt_dot(at(cols(0)), w_ref[0, rows(k)])
-        for s in range(1, parts):
-            total += nt_dot(at(cols(s)), w_ref[s, rows(k)])
-        return total
-
-    gate, up, dhidden = project(x_at, 0), project(x_at, 1), project(cot_at, 2)
-    sig = jax.nn.sigmoid(gate)
-    silu = gate * sig
-    hidden = (silu * up).astype(jnp.bfloat16)
-    dgate = (dhidden * up * sig * (1.0 + gate * (1.0 - sig))).astype(jnp.bfloat16)
-    dup = (dhidden * silu).astype(jnp.bfloat16)
-    for s in range(parts):
-        dnormed_ref[:, cols(s)] = (
-            nn_dot(dgate, w_ref[s, rows(0)]) + nn_dot(dup, w_ref[s, rows(1)])
-        ).astype(jnp.bfloat16)
-        out_ref[:, cols(s)] = nn_dot(hidden, w_ref[s, rows(2)]).astype(jnp.bfloat16)
-    hidden_ref[...], dgate_ref[...], dup_ref[...] = hidden.T, dgate.T, dup.T
+def project(at, w_ref):
+    parts, _, depth = w_ref.shape
+    total = nt_dot(at(pl.ds(0, depth)), w_ref[0])
+    for s in range(1, parts):
+        total += nt_dot(at(pl.ds(s * depth, depth)), w_ref[s])
+    return total
 
 
 def expand_kernel(
     own_ref,
-    cot_hbm,
-    w_hbm,
+    gate_w_hbm,
+    up_w_hbm,
     normed_hbm,
-    out_hbm,
-    dnormed_hbm,
-    dgate_hbm,
-    dup_hbm,
-    hidden_hbm,
+    gate_hbm,
+    up_hbm,
     normed_ref,
-    w_ref,
-    cot_ref,
-    out_ref,
-    dnormed_ref,
-    dgate_ref,
-    dup_ref,
-    hidden_ref,
+    gate_w_ref,
+    up_w_ref,
+    gate_ref,
+    up_ref,
     sems,
     local_sem,
-    w_sem,
-    cot_sems,
+    w_sems,
     store_sems,
-    keep_sems,
+    keep_sem,
 ):
     greet_plane()
     at, x_at, y_at, d_at, core = plane_places()
-    m = own_ref.shape[0]
-    half = m // 2
+    half = own_ref.shape[0] // 2
     gather = gather_steps(own_ref, normed_ref, Sender(sems), local_sem)
     next(gather)
-    weights = pltpu.make_async_copy(w_hbm, w_ref, w_sem)
-    weights.start()
+    weights = [
+        pltpu.make_async_copy(gate_w_hbm, gate_w_ref, w_sems.at[0]),
+        pltpu.make_async_copy(up_w_hbm, up_w_ref, w_sems.at[1]),
+    ]
+    for c in weights:
+        c.start()
 
     def halves(i):
         k = choose(parity(i) == 0, core, 1 - core)
@@ -989,40 +1104,22 @@
             first, second = pl.multiple_of(first, half), pl.multiple_of(second, half)
         return (one, k, first), (two, k, second)
 
-    def cot_copies(i):
-        slot = parity(i)
-        return [
-            pltpu.make_async_copy(
-                cot_hbm.at[c, k, pl.ds(r, half)],
-                cot_ref.at[slot, pl.ds(n * half, half)],
-                cot_sems.at[slot, n],
-            )
-            for n, (c, k, r) in enumerate(halves(i))
-        ]
-
     def store_copies(i):
         slot = parity(i)
         found = []
         for n, (c, k, r) in enumerate(halves(i)):
             rows = pl.ds(n * half, half)
-            column = pl.ds(pl.multiple_of((c * 2 + k) * m + r, half), half)
-            pairs = [
-                (out_ref.at[slot, rows], out_hbm.at[c, k, pl.ds(r, half)]),
-                (dnormed_ref.at[slot, rows], dnormed_hbm.at[c, k, pl.ds(r, half)]),
-                (dgate_ref.at[slot, :, rows], dgate_hbm.at[:, column]),
-                (dup_ref.at[slot, :, rows], dup_hbm.at[:, column]),
-                (hidden_ref.at[slot, :, rows], hidden_hbm.at[:, column]),
-            ]
-            found += [
-                pltpu.make_async_copy(a, b, store_sems.at[slot, n * len(pairs) + q])
-                for q, (a, b) in enumerate(pairs)
-            ]
+            for q, (a, b) in enumerate(((gate_ref, gate_hbm), (up_ref, up_hbm))):
+                found.append(
+                    pltpu.make_async_copy(
+                        a.at[slot, rows], b.at[c, k, pl.ds(r, half)], store_sems.at[slot, 2 * n + q]
+                    )
+                )
         return found
 
-    for c in cot_copies(0):
-        c.start()
     next(gather)
-    weights.wait()
+    for c in weights:
+        c.wait()
 
     def body(i, carry):
         for step in range(1, 8):
@@ -1030,45 +1127,26 @@
             @pl.when(i == step)
             def _():
                 next(gather)
-
-        @pl.when(i < 7)
-        def _():
-            for c in cot_copies(i + 1):
-                c.start()
-
-        for c in cot_copies(i):
-            c.wait()
 
         @pl.when(i >= 2)
         def _():
             for c in store_copies(i - 2):
                 c.wait()
 
-        slot = lax.rem(i, 2)
+        slot = parity(i)
         pieces = halves(i)
 
-        def x_cols(cols):
+        def columns(cols):
             return jnp.concatenate([normed_ref[c, k, pl.ds(r, half), cols] for c, k, r in pieces])
 
-        def cot_cols(cols):
-            return cot_ref[slot, :, cols]
-
-        ffn_block(
-            x_cols,
-            cot_cols,
-            w_ref,
-            out_ref.at[slot],
-            dnormed_ref.at[slot],
-            dgate_ref.at[slot],
-            dup_ref.at[slot],
-            hidden_ref.at[slot],
-        )
+        gate_ref[slot] = project(columns, gate_w_ref)
+        up_ref[slot] = project(columns, up_w_ref)
         for c in store_copies(i):
             c.start()
         return carry
 
     lax.fori_loop(0, 8, body, 0)
-    keep = pltpu.make_async_copy(normed_ref, normed_hbm, keep_sems.at[0])
+    keep = pltpu.make_async_copy(normed_ref, normed_hbm, keep_sem)
     keep.start()
     for i in (6, 7):
         for c in store_copies(i):
@@ -1077,39 +1155,88 @@
     run(gather)
 
 
-def expand(own, cot, weights, cid):
+def expand(own, gate_w, up_w, cid):
     m, width = own.shape
-    units = weights.shape[1] // 3
-    tokens = 8 * m
-    whole, low = pltpu.VMEM, jnp.bfloat16
-    blocks = ((4, 2, m, width), low, pl.ANY)
-    thin = ((units, tokens), low, pl.ANY)
-    normed, out, dnormed, dgate, dup, hidden = kernel_call(
+    units = gate_w.shape[1]
+    low = jnp.bfloat16
+    thin = ((4, 2, m, units), jnp.float32, pl.ANY)
+    normed, gate, up = kernel_call(
         expand_kernel,
         "expand",
         cid,
-        [blocks, blocks, blocks, thin, thin, thin],
-        [(own, whole), (cot.reshape(4, 2, m, width), pl.ANY), (weights, pl.ANY)],
+        [((4, 2, m, width), low, pl.ANY), thin, thin],
+        [(own, pltpu.VMEM), (gate_w, pl.ANY), (up_w, pl.ANY)],
         [
             pltpu.VMEM((4, 2, m, width), low),
-            pltpu.VMEM(weights.shape, low),
-            pltpu.VMEM((2, m, width), low),
-            pltpu.VMEM((2, m, width), low),
-            pltpu.VMEM((2, m, width), low),
-            pltpu.VMEM((2, units, m), low),
-            pltpu.VMEM((2, units, m), low),
-            pltpu.VMEM((2, units, m), low),
+            pltpu.VMEM(gate_w.shape, low),
+            pltpu.VMEM(up_w.shape, low),
+            pltpu.VMEM((2, m, units), jnp.float32),
+            pltpu.VMEM((2, m, units), jnp.float32),
             copies(GATHER_COPIES),
             pltpu.SemaphoreType.DMA,
+            pltpu.SemaphoreType.DMA((2,)),
+            pltpu.SemaphoreType.DMA((2, 4)),
             pltpu.SemaphoreType.DMA,
-            pltpu.SemaphoreType.DMA((2, 2)),
-            pltpu.SemaphoreType.DMA((2, 10)),
-            pltpu.SemaphoreType.DMA((1,)),
         ],
-        flops=12 * tokens * width * units,
-        moved=1 << 28,
-    )
-    return normed.reshape(tokens, width), out, dnormed, dgate, dup, hidden
+        flops=32 * m * width * units,
+        moved=1 << 27,
+    )
+    return normed.reshape(8 * m, width), gate.reshape(8 * m, units), up.reshape(8 * m, units)
+
+
+def hidden_kernel(
+    gate_ref,
+    up_ref,
+    cot_ref,
+    gate_w_ref,
+    up_w_ref,
+    down_w_ref,
+    out_ref,
+    dnormed_ref,
+    dgate_ref,
+    dup_ref,
+    hidden_ref,
+):
+    parts, _, depth = down_w_ref.shape
+    gate, up = gate_ref[...], up_ref[...]
+    dhidden = project(lambda cols: cot_ref[:, cols], down_w_ref)
+    sig = jax.nn.sigmoid(gate)
+    silu = gate * sig
+    hidden = (silu * up).astype(jnp.bfloat16)
+    dgate = (dhidden * up * sig * (1.0 + gate * (1.0 - sig))).astype(jnp.bfloat16)
+    dup = (dhidden * silu).astype(jnp.bfloat16)
+    for s in range(parts):
+        cols = pl.ds(s * depth, depth)
+        dnormed_ref[:, cols] = (nn_dot(dgate, gate_w_ref[s]) + nn_dot(dup, up_w_ref[s])).astype(
+            jnp.bfloat16
+        )
+        out_ref[:, cols] = nn_dot(hidden, down_w_ref[s]).astype(jnp.bfloat16)
+    hidden_ref[...], dgate_ref[...], dup_ref[...] = hidden.T, dgate.T, dup.T
+
+
+def hidden_units(gate, up, cot, gate_w, up_w, down_w, block=256):
+    tokens, units = gate.shape
+    width = cot.shape[1]
+    low = jnp.bfloat16
+    wide = pl.BlockSpec((block, width), lambda i: (i, 0))
+    thin = pl.BlockSpec((block, units), lambda i: (i, 0))
+    turned = pl.BlockSpec((units, block), lambda i: (0, i))
+    weights = pl.BlockSpec(gate_w.shape, lambda i: (0, 0, 0), pipeline_mode=pl.Buffered(1))
+    return pl.pallas_call(
+        hidden_kernel,
+        name="hidden_units",
+        grid=(tokens // block,),
+        out_shape=[jax.ShapeDtypeStruct((tokens, width), low)] * 2
+        + [jax.ShapeDtypeStruct((units, tokens), low)] * 3,
+        in_specs=[thin, thin, wide, weights, weights, weights],
+        out_specs=[wide, wide, turned, turned, turned],
+        compiler_params=pltpu.CompilerParams(vmem_limit_bytes=VMEM_LIMIT),
+        cost_estimate=pl.CostEstimate(
+            flops=8 * tokens * width * units,
+            bytes_accessed=1 << 27,
+            transcendentals=tokens * units,
+        ),
+    )(gate, up, cot, gate_w, up_w, down_w)
 
 
 def norm_gradient(r, value_at, grad_ref, gain_at, gain_grad, finish, width):
@@ -1205,7 +1332,8 @@
 
 
 def middle(part, normed, dgate, dup, cid):
-    _, _, m, width = part.shape
+    m, width = part.shape[0] // 8, part.shape[1]
+    part = part.reshape(4, 2, m, width)
     units, tokens = dgate.shape
     low = jnp.bfloat16
     return kernel_call(
@@ -1294,30 +1422,59 @@
     return dresid, gain, gathered.reshape(-1, width)
 
 
-def back_kernel(
+def unmix_kernel(
+    heads,
+    count,
     dresid_ref,
     pack_ref,
     part_ref,
     residual_ref,
-    dmixed_ref,
-    block_ref,
-    out_dmixed,
-    total_ref,
-    held_ref,
-    pair_ref,
-    sum_ref,
-    got_ref,
-    sems,
-    scatter_sems,
-    held_sems,
+    col_ref,
+    row_ref,
+    pairs_ref,
+    qkv_ref,
+    exact_ref,
+    den_ref,
+    state_ref,
+    sums_ref,
+    *refs,
 ):
-    span, z = lax.axis_size("seq"), lax.axis_index("seq")
+    ins, dqkv_ref, block_ref = refs[:count], refs[count], refs[count + 1]
+    outs = refs[count + 2 : 2 * count + 2]
+    (
+        dmixed_ref,
+        back_ref,
+        back_sums_ref,
+        pick_ref,
+        own_ref,
+        own_sums_ref,
+        out_ref,
+        out_sums_ref,
+        total_ref,
+        held_ref,
+        pair_ref,
+        sum_ref,
+        got_ref,
+        sems,
+        shard_sems,
+        local_sems,
+        scatter_sems,
+        held_sems,
+    ) = refs[2 * count + 2 :]
     parts, _, depth = pack_ref.shape
-    tokens, vcols = dmixed_ref.shape[1:]
-    first = pack_ref.shape[1] - vcols
+    rows, length = col_ref.shape[0], col_ref.shape[1]
+    vcols, qcols = heads * VHEAD, heads * FDIM
+    first_row = pack_ref.shape[1] - vcols
     at, x_at, y_at, _, core = plane_places()
-    peers = [lax.rem(z + k, span) for k in range(1, span)]
-    greet([{"dp": x_at}, {"dp": y_at}, {"tensor": 1 - core}] + [{"seq": p} for p in peers])
+    plane, span, z = lax.axis_size("dp"), lax.axis_size("seq"), lax.axis_index("seq")
+    chips = [lax.rem(at + k, plane) for k in range(1, plane)]
+    back_ref[...] = jnp.zeros_like(back_ref)
+    back_sums_ref[...] = jnp.zeros_like(back_sums_ref)
+    greet(
+        [{"dp": p} for p in chips]
+        + [{"tensor": 1 - core}]
+        + [{"seq": lax.rem(z + k, span)} for k in (1, span - 1)]
+    )
     scatter = scatter_steps(
         part_ref,
         total_ref,
@@ -1328,23 +1485,99 @@
         (held_ref, held_sems),
     )
     next(scatter)
-    copy = Sender(sems)
-
-    def project(dest, out):
-        x = pl.ds(pl.multiple_of(dest * tokens, tokens), tokens)
-        total = jnp.zeros((tokens, vcols), jnp.float32)
+    chain = Chain(False, back_ref, back_sums_ref, out_ref, out_sums_ref, Sender(sems))
+    fill_selectors(pairs_ref, pick_ref, qcols)
+    scale = feature_scale(pairs_ref)
+
+    def tokens_of(b):
+        return pl.ds(pl.multiple_of(b * length, length), length)
+
+    def cotangents(t, h):
+        v = pl.ds(h * VHEAD, VHEAD)
+        dn = dmixed_ref[t, v].astype(jnp.float32) / den_ref[t, pl.ds(h, 1)]
+        dd = -jnp.sum(dn * exact_ref[t, v], axis=1, keepdims=True)
+        return dn.astype(jnp.bfloat16), dd
+
+    def first(b, carry):
+        t = tokens_of(b)
+        total = jnp.zeros((length, vcols), jnp.float32)
         for s in range(parts):
             total += nt_dot(
-                dresid_ref[x, pl.ds(s * depth, depth)], pack_ref[s, pl.ds(first, vcols)]
+                dresid_ref[t, pl.ds(s * depth, depth)], pack_ref[s, pl.ds(first_row, vcols)]
             )
-        out[...] = total.astype(jnp.bfloat16)
-
-    there = []
-    for k, p in enumerate(peers):
-        project(p, out_dmixed.at[k])
-        there.append(copy(out_dmixed.at[k], dmixed_ref.at[z], {"seq": p}))
-        there[-1].start()
-    project(z, dmixed_ref.at[z])
+        dmixed_ref[t] = total.astype(jnp.bfloat16)
+        head = Segments(col_ref, row_ref, b).head
+        tile = qkv_ref[t, pl.ds(vcols, LANES)]
+        for h in range(heads):
+            dn, dd = cotangents(t, h)
+            one, two = factors(tile, pick_ref, 0, h)
+            lifted = jnp.where(head, one * two, 0.0)
+            own_ref[b, h] = tn_dot(lifted.astype(jnp.bfloat16), dn)
+            own_sums_ref[b, h : h + 1] = jnp.sum(lifted * dd, axis=0, keepdims=True)
+        return carry
+
+    own_sums_ref[...] = jnp.zeros_like(own_sums_ref)
+    lax.fori_loop(0, rows, first, 0)
+    next(scatter)
+    shards = swap_shards(ins, outs, chips, at, columns_of, block_of, Sender(shard_sems), local_sems)
+
+    def lowered(dlifted, kind, h, one, two):
+        return nt_dot((dlifted * two).astype(jnp.bfloat16), pick_ref[kind, h, 0]) + nt_dot(
+            (dlifted * one).astype(jnp.bfloat16), pick_ref[kind, h, 1]
+        )
+
+    def mixer(b, carry):
+        t = tokens_of(b)
+        seg = Segments(col_ref, row_ref, b)
+        tile = qkv_ref[t, pl.ds(vcols, LANES)]
+        key = keys_in_place(tile, qcols)
+        dtile = jnp.zeros((length, LANES), jnp.float32)
+        dkey = jnp.zeros((length, LANES), jnp.float32)
+        for h in range(heads):
+            inside = head_mask(length, h)
+            v = pl.ds(h * VHEAD, VHEAD)
+            value = qkv_ref[t, v]
+            query = jnp.where(inside, tile, jnp.zeros_like(tile))
+            dn, dd = cotangents(t, h)
+            a, w, keep = masked_weights(query, key, seg.column, seg.row)
+            dw = jnp.where(keep, nt_dot(dn, value) + dd, 0.0)
+            da = (dw * (1.0 + a) * 0.25).astype(jnp.bfloat16)
+            dvalue = tn_dot(w.astype(jnp.bfloat16), dn)
+            dtile += jnp.where(inside, nn_dot(da, key), 0.0)
+            dkey += jnp.where(inside, tn_dot(da, query), 0.0)
+            one, two = factors(tile, pick_ref, 0, h)
+            dlifted = nt_dot(dn, state_ref[b, h]) + dd * sums_ref[b, h : h + 1]
+            dtile += lowered(jnp.where(seg.head, dlifted, 0.0), 0, h, one, two)
+            one, two = factors(tile, pick_ref, 1, h)
+            lifted = jnp.where(seg.tail, one * two * scale, 0.0)
+            dlifted = (nt_dot(value, back_ref[b, h]) + back_sums_ref[b, h : h + 1]) * scale
+            dtile += lowered(jnp.where(seg.tail, dlifted, 0.0), 1, h, one, two)
+            dvalue += nn_dot(lifted.astype(jnp.bfloat16), back_ref[b, h])
+            dqkv_ref[t, v] = dvalue.astype(jnp.bfloat16)
+        dtile += pltpu.roll(dkey, qcols, axis=1)
+        lane = lax.broadcasted_iota(jnp.int32, (length, LANES), 1)
+        dqkv_ref[t, pl.ds(vcols, LANES)] = jnp.where(lane < 2 * qcols, dtile, 0.0).astype(
+            jnp.bfloat16
+        )
+        return carry
+
+    each = rows // CHUNKS
+    for g in range(CHUNKS):
+        chain.get(g)
+        pass_states(
+            back_ref,
+            back_sums_ref,
+            own_ref,
+            own_sums_ref,
+            out_ref,
+            out_sums_ref,
+            (col_ref, row_ref),
+            g,
+        )
+        chain.give(g)
+        if g == 1:
+            next(scatter)
+        lax.fori_loop(g * each, (g + 1) * each, mixer, 0)
     run(scatter)
 
     def finish(r, carry):
@@ -1352,132 +1585,53 @@
         return carry
 
     row_blocks(block_ref.shape[0], ROW_STEP, finish)(0)
-    for c in there:
+    for c in shards:
         c.wait()
-
-
-def back(dresid_low, pack, part, residual, vcols, cid):
-    span = lax.axis_size("seq")
-    tokens = dresid_low.shape[0] // span
+    chain.close()
+
+
+def unmix(dresid_low, pack, part, residual, seg_col, seg_row, pairs, kept, shards, heads, cid):
+    tokens = dresid_low.shape[0]
+    plane, rows = lax.axis_size("dp"), seg_col.shape[0]
+    vcols = heads * VHEAD
     m, width = residual.shape
-    whole = pltpu.VMEM
-    return kernel_call(
-        back_kernel,
-        "back",
-        cid,
-        [((span, tokens, vcols), jnp.bfloat16, whole), ((m, width), jnp.bfloat16, whole)],
-        [(dresid_low, whole), (pack, whole), (part, pl.ANY), (residual, whole)],
-        [
-            pltpu.VMEM((span - 1, tokens, vcols), jnp.bfloat16),
-            pltpu.VMEM((m, width), jnp.float32),
-            pltpu.VMEM((4, m, width), jnp.bfloat16),
-        ]
-        + scatter_scratch(m, width)
-        + [copies(span - 1), copies(SCATTER_COPIES), pltpu.SemaphoreType.DMA((4,))],
-        moved=residual.size * 120,
-    )
-
-
-def unmix_kernel(
-    heads,
-    count,
-    col_ref,
-    row_ref,
-    qkv_ref,
-    exact_ref,
-    den_ref,
-    dmixed_ref,
-    *refs,
-):
-    ins, dqkv_ref, outs = refs[:count], refs[count], refs[count + 1 : 2 * count + 1]
-    out_dqkv, keys_ref, dtile_ref, dkey_ref, dvalue_ref, sems, shard_sems, local_sems = refs[
-        2 * count + 1 :
-    ]
-    span, z = lax.axis_size("seq"), lax.axis_index("seq")
-    rows, length = col_ref.shape[0], col_ref.shape[2]
-    vcols, qcols = heads * VHEAD, heads * FDIM
-    plane, at = lax.axis_size("dp"), lax.axis_index("dp")
-    peers = [lax.rem(z + k, span) for k in range(1, span)]
-    chips = [lax.rem(at + k, plane) for k in range(1, plane)]
-    greet([{"dp": p} for p in chips] + [{"seq": p} for p in peers])
-    copy = Sender(sems)
-    shards = swap_shards(ins, outs, chips, at, columns_of, block_of, Sender(shard_sems), local_sems)
-    keys_in_place(qkv_ref, keys_ref, vcols, qcols)
-    dkey_ref[...] = jnp.zeros_like(dkey_ref)
-    dvalue_ref[...] = jnp.zeros_like(dvalue_ref)
-
-    def one_block(step, carry):
-        r, i = step // span, lax.rem(step, span)
-        t = pl.ds(pl.multiple_of(r * length, length), length)
-        tile = qkv_ref[i, t, pl.ds(vcols, LANES)]
-        dtile = jnp.zeros((length, LANES), jnp.float32)
-        for h in range(heads):
-            inside = head_mask(length, h)
-            v = pl.ds(h * VHEAD, VHEAD)
-            query = jnp.where(inside, tile, jnp.zeros_like(tile))
-            dn = dmixed_ref[i, t, v].astype(jnp.float32) / den_ref[i, t, pl.ds(h, 1)]
-            dd = -jnp.sum(dn * exact_ref[i, t, v], axis=1, keepdims=True)
-            dn_low = dn.astype(jnp.bfloat16)
-
-            def block(j, dquery, query=query, v=v, dn_low=dn_low, dd=dd, inside=inside):
-                key = keys_ref[j, t]
-                a, w, keep = masked_weights(query, key, col_ref, row_ref, r, i, j, length)
-                dw = jnp.where(keep, nt_dot(dn_low, qkv_ref[j, t, v]) + dd, 0.0)
-                da = (dw * (1.0 + a) * 0.25).astype(jnp.bfloat16)
-                dvalue_ref[j, t, v] += tn_dot(w.astype(jnp.bfloat16), dn_low)
-                dkey_ref[j, t] += jnp.where(inside, tn_dot(da, query), 0.0)
-                return dquery + nn_dot(da, key)
-
-            dquery = lax.fori_loop(0, i + 1, block, jnp.zeros((length, LANES), jnp.float32))
-            dtile += jnp.where(inside, dquery, 0.0)
-        dtile_ref[i, t] = dtile
-        return carry
-
-    lax.fori_loop(0, rows * span, one_block, 0)
-
-    def pack(i, out):
-        out[:, pl.ds(0, vcols)] = dvalue_ref[i].astype(jnp.bfloat16)
-        out[:, pl.ds(vcols, LANES)] = (
-            dtile_ref[i] + pltpu.roll(dkey_ref[i], qcols, axis=1)
-        ).astype(jnp.bfloat16)
-
-    home = []
-    for k, p in enumerate(peers):
-        pack(p, out_dqkv.at[k])
-        home.append(copy(out_dqkv.at[k], dqkv_ref.at[z], {"seq": p}))
-        home[-1].start()
-    pack(z, dqkv_ref.at[z])
-    for c in home + shards:
-        c.wait()
-
-
-def unmix(seg_col, seg_row, qkv, exact, den, dmixed, shards, heads, cid):
-    span, tokens, wide = qkv.shape
-    plane = lax.axis_size("dp")
-    vcols = heads * VHEAD
     count = len(shards)
-    whole = pltpu.VMEM
-    dqkv, *swapped = kernel_call(
+    whole, low = pltpu.VMEM, jnp.bfloat16
+    dqkv, block, *swapped = kernel_call(
         partial(unmix_kernel, heads, count),
         "unmix",
         cid,
-        [((span, tokens, wide), jnp.bfloat16, whole)]
+        [((tokens, vcols + LANES), low, whole), ((m, width), low, whole)]
         + [((plane, p.shape[0], p.shape[1] // plane), p.dtype, pl.ANY) for p in shards],
-        [(a, whole) for a in (seg_col, seg_row, qkv, exact, den, dmixed)]
+        [
+            (dresid_low, whole),
+            (pack, whole),
+            (part.reshape(4, 2, m, width), pl.ANY),
+            (residual, whole),
+            (seg_col, whole),
+            (seg_row, whole),
+            (pairs, whole),
+        ]
+        + [(kept[n], whole) for n in (0, 2, 3, 4, 5)]
         + [(p, pl.ANY) for p in shards],
         [
-            pltpu.VMEM((span - 1, tokens, wide), jnp.bfloat16),
-            pltpu.VMEM((span, tokens, LANES), jnp.bfloat16),
-            pltpu.VMEM((span, tokens, LANES), jnp.float32),
-            pltpu.VMEM((span, tokens, LANES), jnp.float32),
-            pltpu.VMEM((span, tokens, vcols), jnp.float32),
-            copies(span - 1),
+            pltpu.VMEM((tokens, vcols), low),
+            pltpu.VMEM((rows, heads, FEATURES, VHEAD), low),
+            pltpu.VMEM((rows, 8, FEATURES), jnp.float32),
+        ]
+        + state_scratch(rows, heads)
+        + [pltpu.VMEM((m, width), jnp.float32), pltpu.VMEM((4, m, width), low)]
+        + scatter_scratch(m, width)
+        + [
+            copies(2 * CHUNKS),
             copies(count * (plane - 1)),
             pltpu.SemaphoreType.DMA((count,)),
+            copies(SCATTER_COPIES),
+            pltpu.SemaphoreType.DMA((4,)),
         ],
-        moved=qkv.size * 120,
-    )
-    return dqkv.reshape(-1, wide), swapped
+        moved=residual.size * 120,
+    )
+    return dqkv, block, swapped
 
 
 def last_kernel(count, *refs):
@@ -1684,7 +1838,6 @@
     heads = query_weight.shape[1] // FDIM // plane
     hidden_part = gate_weight.shape[1] // plane
     vcols, qcols = heads * VHEAD, heads * FDIM
-    all_rows = rows * plane // span
 
     def over_seq(pack):
         return lax.all_gather(pack, "seq", axis=0, tiled=False)
@@ -1709,27 +1862,42 @@
         [split(value_weight.T), split(query_weight.T), split(key_weight.T), split(output_weight)],
         axis=1,
     )
-    attn_pack, small = first_exchange(attn_pack, small, 1)
-    ffn_pack = jnp.concatenate([split(gate_weight.T), split(up_weight.T), split(down_weight)], axis=1)
-    ffn_pack, _ = lax.optimization_barrier((ffn_pack, attn_pack))
-    [ffn_pack] = exchange(
-        [ffn_pack], 2, [(ffn_pack.shape[1], plane * chunk)], put=columns_of
-    )
-    attn_pack, ffn_pack = over_seq(attn_pack), over_seq(ffn_pack)
+    [attn_pack] = exchange(
+        [attn_pack], 1, [(attn_pack.shape[1], plane * chunk)], put=columns_of
+    )
+    gate_w, small = lax.optimization_barrier((split(gate_weight.T), small, attn_pack))[:2]
+    gate_w, small = first_exchange(gate_w, small, 2)
+    attn_pack, gate_w = over_seq(attn_pack), over_seq(gate_w)
     starts = small[:, 2:-2].reshape(span, plane * rows, length)
-    starts = lax.dynamic_slice_in_dim(starts, lax.axis_index("seq") * all_rows, all_rows, 1)
-    segments = jnp.cumsum(starts.transpose(1, 0, 2).reshape(all_rows, span * length), axis=1)
+    segments = jnp.cumsum(
+        lax.dynamic_index_in_dim(starts, lax.axis_index("seq"), 0, keepdims=False), axis=1
+    )
 
     qkv_rows = vcols + 2 * qcols
-    seg_col = segments.reshape(all_rows, span, length, 1)
-    seg_row = segments.reshape(all_rows, span, 1, length)
+    seg_col = segments[:, :, None]
+    seg_row = segments[:, None, :]
+    pairs = feature_pairs()
     normed_one, x, cot_own = entry(
         tokens.reshape(cores, own, width), cotangent.reshape(cores, own, width), small, 3
     )
-    qkv, mixed, exact, den, cot = mix(normed_one, attn_pack, seg_col, seg_row, cot_own, heads, 4)
+    kept, cot, up_w, down_w = mix(
+        normed_one,
+        attn_pack,
+        seg_col,
+        seg_row,
+        pairs,
+        cot_own,
+        split(up_weight.T),
+        split(down_weight),
+        heads,
+        4,
+    )
+    mixed = kept[1]
+    up_w, down_w = over_seq(up_w), over_seq(down_w)
     residual, normed_own = branch(mixed, attn_pack, x, small, 5)
-    normed_two, out_part, dnormed_part, dgate, dup, hidden = expand(
-        normed_own, cot, ffn_pack, 11
+    normed_two, gate, up = expand(normed_own, gate_w, up_w, 11)
+    out_part, dnormed_part, dgate, dup, hidden = hidden_units(
+        gate, up, cot, gate_w, up_w, down_w
     )
     down_grad = nn_dot(hidden, cot).astype(jnp.bfloat16)
     dnormed_part, down_grad = lax.optimization_barrier((dnormed_part, down_grad))
@@ -1737,21 +1905,31 @@
     dnormed_two, gate_grad, up_grad = middle(dnormed_part, normed_two, dgate, dup, 6)
     gate_grad, up_grad = summed(gate_grad), summed(up_grad)
     dresid, gain_two_grad, dresid_low = turn(dnormed_two, residual, cot_own, small, 12)
-    dresid_low, down_grad = lax.optimization_barrier((dresid_low, down_grad))
-    dmixed, block_own = back(dresid_low, attn_pack, out_part, residual, vcols, 7)
     out_grad = tn_dot(mixed, dresid_low).astype(jnp.bfloat16)
-    dmixed, gate_grad, out_grad = lax.optimization_barrier((dmixed, gate_grad, out_grad))
-    dqkv, (down_grad, gate_grad) = unmix(
-        seg_col, seg_row, qkv, exact, den, dmixed, [down_grad, gate_grad], heads, 8
+    dresid_low, down_grad, out_grad = lax.optimization_barrier((dresid_low, down_grad, out_grad))
+    dqkv, block_own, (down_grad,) = unmix(
+        dresid_low,
+        attn_pack,
+        out_part,
+        residual,
+        seg_col,
+        seg_row,
+        pairs,
+        kept,
+        [down_grad],
+        heads,
+        8,
     )
     qkv_grad = tn_dot(dqkv, normed_one).astype(jnp.bfloat16)[:qkv_rows]
     out_grad = summed(out_grad)
-    dqkv, qkv_grad, up_grad = lax.optimization_barrier((dqkv, qkv_grad, up_grad))
+    dqkv, qkv_grad, gate_grad = lax.optimization_barrier((dqkv, qkv_grad, gate_grad))
     qkv_grad = summed(qkv_grad)
     dtokens, block_out, gains = leave(
         dqkv, attn_pack, x, dresid, block_own, small, gain_two_grad, 9
     )
-    (up_grad, out_grad, qkv_grad), gain_grads = last([up_grad, out_grad, qkv_grad], gains, 10)
+    (gate_grad, up_grad, out_grad, qkv_grad), gain_grads = last(
+        [gate_grad, up_grad, out_grad, qkv_grad], gains, 10
+    )
 
     def stacked(a, start, size):
         return a[:, start : start + size].reshape(plane * size, chunk).astype(jnp.float32)
@@ -1780,7 +1958,7 @@
         and cores == 2
         and heads % plane == 0
         and (gate_weight.shape[1] // cores) % (16 * plane) == 0
-        and tokens.shape[0] % span == 0
+        and tokens.shape[0] % CHUNKS == 0
     )
 
 

time: 699 us -> 633 us (0.906)
  Pallas kernels: 628 us -> 532 us
  waiting for transfers between devices: 2.19 us -> 34.1 us
    pallas_call x10 -> x9, Pallas kernels: 585 us -> 467 us  [kernel_call(): pl.pallas_call(body, name=name, out_shape=[jax.ShapeDtypeStruct(s, d) for...]
    pallas_call x0 -> x1, Pallas kernels: none -> 37.2 us  [hidden_units(): pl.pallas_call(hidden_kernel, name='hidden_units', grid=(tokens // block,...]
    all_gather x2 -> x4, waiting for transfers between devices: 1.53 us -> 32.8 us  [over_seq(): return lax.all_gather(pack, 'seq', axis=0, tiled=False)]
    pallas_call x1, Pallas kernels: 26.6 us -> 11.6 us  [exchange(): pl.pallas_call(partial(exchange_kernel, take, put, count), name='exchange...]
  transfers between devices with their start and end apart: 7 -> 9, of which waited for: 1 -> 2; matrix products, arithmetic and copies ran while one was open for 3% -> 3% of each run, Pallas kernels for 74% -> 72%
where the time goes in v5:
time: 633 us
  Pallas kernels  532 us (84%)
  waiting for transfers between devices  34.1 us (5%)
  matrix products  24.7 us (4%)
  local copies, waits for them, and re-layouts  16.9 us (3%)
  between operations  14.1 us (2%)
  other arithmetic  9.84 us (2%)
    pallas_call x9, Pallas kernels, kernel_call(): pl.pallas_call(body, name=name, out_shape=[jax.ShapeDtypeStruct(s, d) for...  467 us
    pallas_call x1, Pallas kernels, hidden_units(): pl.pallas_call(hidden_kernel, name='hidden_units', grid=(tokens // block,...  37.2 us
    all_gather x4, waiting for transfers between devices, over_seq(): return lax.all_gather(pack, 'seq', axis=0, tiled=False)  32.8 us
    pallas_call x1, Pallas kernels, first_exchange(): pl.pallas_call(first_kernel, name='first_exchange', out_shape=[jax.ShapeD...  16.6 us
    dot_general x2, matrix products, tn_dot(): lax.dot_general(a, b, (((0,), (0,)), ((), ())), preferred_element_type=jn...  14.3 us
  transfers between devices with their start and end apart: 9, of which 2 were waited for; matrix products, arithmetic and copies ran while one was open for 3% of the time, Pallas kernels for 72%

profile of v5, /device:TPU:0, one launch (start us, length us, event | category | flops | bytes accessed | tf_op | source)
XLA Modules:
  0.0 632.5 jit_solution(7581225105793664032)
XLA Ops:
  7.2 0.0 all-gather.9.cloned.1.call-start
  7.3 0.9 copy.33
  8.1 0.9 copy.34
  9.0 1.1 copy.32
  10.1 1.8 pad_maximum_fusion.refs_0_
  11.9 11.6 %exchange.1 = bf16[576,512]{1,0:T(8,128)(2,1)} custom-call(bf16[4,576,128]{2,1,0:T(8,128)(2,1)} %pad_maximum_fusion.refs_0_), custom_call_target="tpu_custom_call" | custom-call | bytes 17694720 | tf_op jit(solution)/shard_map/exchange/pallas_call | solution.py:523
  23.6 0.0 all-gather.9.cloned.1.call-update
  23.6 0.0 all-gather.11.cloned.1.call-start
  23.7 0.1 pad.7.clone
  23.8 0.7 maximum_maximum_fusion.small_ref
  24.4 16.6 %first_exchange.1 = (bf16[688,512]{1,0:T(8,128)(2,1)}, f32[16,8,128]{2,1,0:T(8,128)}) custom-call(bf16[4,688,128]{2,1,0:T(8,128)(2,1)} %bitcast.85, f32[8,128]{1,0:T(8,128)} %maximum_maximum_fusion.small_ref), custom_call_target="tpu_custom_call" | custom-call | bytes 21135360 | tf_op jit(solution)/shard_map/first_exchange/pallas_call | solution.py:571
  41.0 0.0 all-gather.11.cloned.1.call-update
  41.0 0.0 all-gather.13.cloned.1.call-start
  41.1 0.8 slice.27
  42.0 0.6 reduce-window.6
  42.6 0.2 slice_reduce_fusion
  42.8 0.1 broadcast_add_fusion
  42.8 0.6 copy.35
  43.4 0.1 fusion.8
  43.5 1.4 copy.36.col_ref
  44.9 43.5 %entry.1 = (bf16[4,2,256,2048]{3,2,1,0:T(8,128)(2,1)}, bf16[256,2048]{1,0:T(8,128)(2,1)}, bf16[256,2048]{1,0:T(8,128)(2,1)}) custom-call(bf16[2,256,2048]{2,1,0:T(8,128)(2,1)} %tokens_ref.1, bf16[2,256,2048]{2,1,0:T(8,128)(2,1)} %cot_ref.1, f32[16,8,128]{2,1,0:T(8,128)} %get-tuple-element.64.small_ref), custom_call_target="tpu_custom_call" | custom-call | bytes 41943040 | tf_op jit(solution)/shard_map/entry/pallas_call | solution.py:621
  88.3 0.0 all-gather.9.cloned.1.call-done
  88.4 63.5 %mix.1 = (bf16[2048,384]{1,0:T(8,128)(2,1)}, bf16[2048,256]{1,0:T(8,128)(2,1)}, f32[2048,256]{1,0:T(8,128)}, f32[2048,128]{1,0:T(8,128)}, bf16[8,2,256,128]{3,2,...) custom-call(bf16[2048,2048]{1,0:T(8,128)(2,1)} %bitcast.82, ...), custom_call_target="tpu_custom_call" | custom-call | bytes 125829120 | tf_op jit(solution)/shard_map/mix/pallas_call | solution.py:621
  151.9 0.0 all-gather.13.cloned.1.call-update
  151.9 0.0 all-gather.15.cloned.1.call-start
  152.0 0.5 all-gather.15.cloned.1.call-update
  152.5 0.2 reduce-scatter.6.cloned.1.call-start
  152.7 48.6 %branch.1 = (f32[256,2048]{1,0:T(8,128)}, bf16[256,2048]{1,0:T(8,128)(2,1)}) custom-call(bf16[2048,256]{1,0:T(8,128)(2,1)} %get-tuple-element.67.mixed_ref, bf16[4,576,512]{2,1,0:T(8,128)(2,1)} %bitcast.78, bf16[256,2048]{1,0:T(8,128)(2,1)} %get-tuple-element.68.x_ref, f32[16,8,128]{2,1,0:T(8,128)} %get-tuple-element.64.small_ref), custom_call_target="tpu_custom_call" | custom-call | bytes 41943040 | tf_op jit(solution)/shard_map/branch/pallas_call | solution.py:621
  201.4 0.0 all-gather.11.cloned.1.call-done
  201.4 20.1 %all-gather.13.cloned.1.call-done = bf16[2752,512]{1,0:T(8,128)(2,1)} async-done(((bf16[688,512]{1,0:T(8,128)(2,1)}), bf16[2752,512]{1,0:T(8,128)(2,1)}) %all-gather.13.cloned.1.call-update) | async-done | bytes 2818064 | tf_op jit(solution)/shard_map/all_gather | solution.py:1843
  221.5 45.6 %expand.1 = (bf16[4,2,256,2048]{3,2,1,0:T(8,128)(2,1)}, f32[4,2,256,688]{3,2,1,0:T(8,128)}, f32[4,2,256,688]{3,2,1,0:T(8,128)}) custom-call(bf16[256,2048]{1,0:T(8,128)(2,1)} %get-tuple-element.69.own_ref, bf16[4,688,512]{2,1,0:T(8,128)(2,1)} %bitcast.101, bf16[4,688,512]{2,1,0:T(8,128)(2,1)} %bitcast.103), custom_call_target="tpu_custom_call" | custom-call | flops 11542724608 | bytes 134217728 | tf_op jit(solution)/shard_map/expand/pallas_call | solution.py:621
  267.2 12.6 %all-gather.15.cloned.1.call-done = bf16[2752,512]{1,0:T(8,128)(2,1)} async-done(((bf16[688,512]{1,0:T(8,128)(2,1)}), bf16[2752,512]{1,0:T(8,128)(2,1)}) %all-gather.15.cloned.1.call-update) | async-done | bytes 2818064 | tf_op jit(solution)/shard_map/all_gather | solution.py:1843
  279.8 37.2 %hidden_units.1 = (bf16[2048,2048]{1,0:T(8,128)(2,1)}, bf16[2048,2048]{1,0:T(8,128)(2,1)}, bf16[688,2048]{1,0:T(8,128)(2,1)}, bf16[688,2048]{1,0:T(8,128)(2,1)}, bf16[688,2048]{1,0:T(8,128)(2,1)}) custom-call(f32[2048,688]{1,0:T(8,128)} %bitcast.108, f32[2048,688]{1,0:T(8,128)} %bitcast.109, bf16[2048,2048]{1,0:T(8,128)(2,1)} %bitcast.99, ...), custom_call_target="tpu_custom_call" | custom-call | flops 23085449216 | bytes 134217728 | tf_op jit(solution)/shard_map/hidden_units/pallas_call | solution.py:1225
  317.0 10.4 %convolution_convert_fusion = bf16[688,2048]{1,0:T(8,128)(2,1)} fusion(bf16[688,2048]{1,0:T(8,128)(2,1)} %get-tuple-element.77, bf16[2048,2048]{1,0:T(8,128)(2,1)} %bitcast.100), kind=kOutput, calls=%fused_computation | convolution fusion | flops 5772771328 | bytes 14024704 | tf_op jit(solution)/shard_map/dot_general | solution.py:304
  327.4 0.0 reduce-scatter.8.cloned.1.call-start
  327.5 42.1 %middle.1 = (f32[256,2048]{1,0:T(8,128)}, bf16[688,2048]{1,0:T(8,128)(2,1)}, bf16[688,2048]{1,0:T(8,128)(2,1)}) custom-call(bf16[4,2,256,2048]{3,2,1,0:T(8,128)(2,1)} %bitcast.107, bf16[2048,2048]{1,0:T(8,128)(2,1)} %bitcast.106, bf16[688,2048]{1,0:T(8,128)(2,1)} %get-tuple-element.80.dgate_hbm, bf16[688,2048]{1,0:T(8,128)(2,1)} %get-tuple-element.81.dup_hbm), custom_call_target="tpu_custom_call" | custom-call | flops 11542724608 | bytes 41943040 | tf_op jit(solution)/shard_map/middle/pallas_call | solution.py:621
  369.6 0.0 reduce-scatter.8.cloned.1.call-update
  369.6 0.0 reduce-scatter.10.cloned.1.call-start
  369.7 0.7 reduce-scatter.10.cloned.1.call-update
  370.4 0.0 reduce-scatter.12.cloned.1.call-start
  370.4 45.3 %turn.1 = (f32[256,2048]{1,0:T(8,128)}, f32[8,2048]{1,0:T(8,128)}, bf16[4,2,256,2048]{3,2,1,0:T(8,128)(2,1)}) custom-call(f32[256,2048]{1,0:T(8,128)} %get-tuple-element.82.total_ref, f32[256,2048]{1,0:T(8,128)} %get-tuple-element.83.residual_ref, bf16[256,2048]{1,0:T(8,128)(2,1)} %get-tuple-element.66.cot_ref, f32[16,8,128]{2,1,0:T(8,128)} %get-tuple-element.64.small_ref), custom_call_target="tpu_custom_call" | custom-call | bytes 41943040 | tf_op jit(solution)/shard_map/turn/pallas_call | solution.py:621
  415.8 6.8 %convolution_convert_fusion.1 = bf16[256,2048]{1,0:T(8,128)(2,1)} fusion(bf16[2048,256]{1,0:T(8,128)(2,1)S(1)} %copy-done, bf16[2048,2048]{1,0:T(8,128)(2,1)} %bitcast.75), kind=kOutput, calls=%fused_computation.2 | convolution fusion | flops 2148007936 | bytes 10485760 | tf_op jit(solution)/shard_map/dot_general | solution.py:300
  422.5 0.0 reduce-scatter.12.cloned.1.call-update
  422.6 0.0 reduce-scatter.14.cloned.1.call-start
  422.6 93.8 %unmix.1 = (bf16[2048,384]{1,0:T(8,128)(2,1)}, bf16[256,2048]{1,0:T(8,128)(2,1)}, bf16[4,688,128]{2,1,0:T(8,128)(2,1)}) custom-call(bf16[2048,2048]{1,0:T(8,128)(2,1)} %bitcast.76, bf16[4,576,512]{2,1,0:T(8,128)(2,1)} %bitcast.79, bf16[4,2,256,2048]{3,2,1,0:T(8,128)(2,1)} %bitcast.81, f32[256,2048]{1,0:T(8,128)} %get-tuple-element.83.residual_ref, ...), custom_call_target="tpu_custom_call" | custom-call | bytes 62914560 | tf_op jit(solution)/shard_map/unmix/pallas_call | solution.py:621
  516.4 7.5 %fusion.1 = bf16[384,2048]{1,0:T(8,128)(2,1)S(1)} fusion(bf16[2048,384]{1,0:T(8,128)(2,1)} %get-tuple-element.96.dqkv_ref, bf16[2048,2048]{1,0:T(8,128)(2,1)} %bitcast.83), kind=kOutput, calls=%fused_computation.20 | convolution fusion | flops 3221225472 | bytes 11534336 | tf_op jit(solution)/shard_map/dot_general | solution.py:300
  523.9 1.1 slice.42
  525.1 0.0 reduce-scatter.14.cloned.1.call-update
  525.1 55.1 %leave.1 = (f32[2,256,2048]{2,1,0:T(8,128)}, bf16[2,256,2048]{2,1,0:T(8,128)(2,1)}, f32[16,8,128]{2,1,0:T(8,128)}) custom-call(bf16[2048,384]{1,0:T(8,128)(2,1)} %get-tuple-element.96.dqkv_ref, bf16[4,576,512]{2,1,0:T(8,128)(2,1)} %bitcast.80, bf16[256,2048]{1,0:T(8,128)(2,1)} %get-tuple-element.68.x_ref, f32[256,2048]{1,0:T(8,128)} %get-tuple-element.97.dresid_ref, ...), custom_call_target="tpu_custom_call" | custom-call | bytes 62914560 | tf_op jit(solution)/shard_map/leave/pallas_call | solution.py:621
  580.3 1.2 bitcast_convert_fusion
  581.5 29.3 %last.1 = (bf16[4,688,128]{2,1,0:T(8,128)(2,1)}, bf16[4,688,128]{2,1,0:T(8,128)(2,1)}, bf16[4,256,128]{2,1,0:T(8,128)(2,1)}, bf16[4,320,128]{2,1,0:T(8,128)(2,1)}, f32[8,128]{1,0:T(8,128)}) custom-call(bf16[688,512]{1,0:T(8,128)(2,1)} %reduce-scatter.8.cloned.1.call-done.refs_0_, bf16[688,512]{1,0:T(8,128)(2,1)} %reduce-scatter.10.cloned.1.call-done.refs_1_, ...), custom_call_target="tpu_custom_call" | custom-call | bytes 67108864 | tf_op jit(solution)/shard_map/last/pallas_call | solution.py:621
  610.8 0.8 fusion
  611.6 1.0 slice.35
  612.6 1.3 slice_bitcast_fusion
  613.9 0.7 copy.39
  614.6 0.7 copy.38
  615.4 0.1 bitcast_convert_fusion.2
  615.4 1.0 copy.40
  616.4 1.8 bitcast_convert_fusion.1
  618.2 2.3 convert_bitcast_fusion.1
  620.5 1.2 convert_bitcast_fusion
  621.7 1.3 copy.43
  623.1 0.9 copy-done.1
  624.0 2.0 copy.44
  (31 shorter events, 0.2 us)
Async XLA Ops:
  7.2 16.5 %copy-start.5 = (s32[2,256]{1,0:T(2,128)S(1)}, s32[2,256]{1,0:T(2,128)}, u32[]{:S(2)}) copy-start(s32[2,256]{1,0:T(2,128)} %param.14) | copy-start | bytes 6148
  7.2 16.6 %copy-start.6 = (bf16[128]{0:T(256)(128)(2,1)S(1)}, bf16[128]{0:T(256)(128)(2,1)}, u32[]{:S(2)}) copy-start(bf16[128]{0:T(256)(128)(2,1)} %param.16) | copy-start | bytes 772
  7.2 16.6 %copy-start.7 = (bf16[128]{0:T(256)(128)(2,1)S(1)}, bf16[128]{0:T(256)(128)(2,1)}, u32[]{:S(2)}) copy-start(bf16[128]{0:T(256)(128)(2,1)} %param.15) | copy-start | bytes 772
  7.2 81.2 %all-gather.9.cloned.1.call-start = ((), (), s32[]{:S(2)}) async-start(), calls=%async_computation.10 | async-start | bytes 2949120 | tf_op jit(solution)/shard_map/all_gather | solution.py:1843
  23.6 177.8 %all-gather.11.cloned.1.call-start = ((), (), s32[]{:S(2)}) async-start(), calls=%async_computation.11 | async-start | bytes 3522560 | tf_op jit(solution)/shard_map/all_gather | solution.py:1843
  41.0 180.5 %all-gather.13.cloned.1.call-start = ((), (), s32[]{:S(2)}) async-start(), calls=%async_computation.12 | async-start | bytes 3522560 | tf_op jit(solution)/shard_map/all_gather | solution.py:1843
  151.9 127.8 %all-gather.15.cloned.1.call-start = ((), (), s32[]{:S(2)}) async-start(), calls=%async_computation.13 | async-start | bytes 3522560 | tf_op jit(solution)/shard_map/all_gather | solution.py:1843
  152.5 270.0 %reduce-scatter.6.cloned.1.call-start = ((), (), s32[]{:S(2)}) async-start(), calls=%async_computation.5 | async-start | bytes 3522560 | tf_op jit(solution)/shard_map/reduce_scatter | solution.py:1846
  327.4 197.7 %reduce-scatter.8.cloned.1.call-start = ((), (), s32[]{:S(2)}) async-start(), calls=%async_computation.6 | async-start | bytes 3522560 | tf_op jit(solution)/shard_map/reduce_scatter | solution.py:1846
  369.6 211.9 %reduce-scatter.10.cloned.1.call-start = ((), (), s32[]{:S(2)}) async-start(), calls=%async_computation.7 | async-start | bytes 3522560 | tf_op jit(solution)/shard_map/reduce_scatter | solution.py:1846
  370.4 45.4 %copy-start = (bf16[2048,256]{1,0:T(8,128)(2,1)S(1)}, bf16[2048,256]{1,0:T(8,128)(2,1)}, u32[]{:S(2)}) copy-start(bf16[2048,256]{1,0:T(8,128)(2,1)} %get-tuple-element.67.mixed_ref) | copy-start | bytes 3145732
  370.4 211.1 %reduce-scatter.12.cloned.1.call-start = ((), (), s32[]{:S(2)}) async-start(), calls=%async_computation.8 | async-start | bytes 1310720 | tf_op jit(solution)/shard_map/reduce_scatter | solution.py:1846
  422.6 158.9 %reduce-scatter.14.cloned.1.call-start = ((), (), s32[]{:S(2)}) async-start(), calls=%async_computation.9 | async-start | bytes 1638400 | tf_op jit(solution)/shard_map/reduce_scatter | solution.py:1846
  525.1 55.1 %copy-start.3 = (bf16[4,688,128]{2,1,0:T(8,128)(2,1)S(1)}, bf16[4,688,128]{2,1,0:T(8,128)(2,1)}, u32[]{:S(2)}) copy-start(bf16[4,688,128]{2,1,0:T(8,128)(2,1)} %get-tuple-element.112) | copy-start | bytes 2113540
  611.6 8.9 %copy-start.4 = (bf16[4,688,128]{2,1,0:T(8,128)(2,1)S(1)}, bf16[4,688,128]{2,1,0:T(8,128)(2,1)}, u32[]{:S(2)}) copy-start(bf16[4,688,128]{2,1,0:T(8,128)(2,1)} %get-tuple-element.111) | copy-start | bytes 2113540
  615.4 6.3 copy-start.2
  620.5 3.5 copy-start.1
Sparse Core Ops, SparseCore 0:
  23.7 51.5 all-gather.8
  76.9 68.3 all-gather.10
  152.0 69.4 all-gather.12
  222.9 56.7 all-gather.14
  327.5 53.8 reduce-scatter.5
  383.7 54.9 reduce-scatter.7
  441.0 67.3 reduce-scatter.9
  511.4 28.1 reduce-scatter.11
  542.5 29.8 reduce-scatter.13

commit v6 on v5

--- a/solution.py
+++ b/solution.py
@@ -432,8 +432,6 @@
     lo, hi = pl.ds(0, half), pl.ds(half, half)
     order = (d_at, x_at, y_at, at)
     pairs = [copy(part_ref.at[to, 1 - core], pair_ref.at[j], sp) for j, to in enumerate(order)]
-    for c in pairs:
-        c.start()
     own = [part_ref.at[to, core] for to in order]
     fetched = []
     if held is not None:
@@ -442,8 +440,14 @@
             pltpu.make_async_copy(o, buffer.at[j], held_sems.at[j]) for j, o in enumerate(own)
         ]
         own = [buffer.at[j] for j in range(4)]
-        for c in fetched:
-            c.start()
+
+    def sent(j, rows, place):
+        return copy(sum_ref.at[j, rows], got_ref.at[j, rows], place)
+
+    d_lo, d_hi = sent(0, lo, xp), sent(0, hi, yp)
+    x_lo, y_hi, x_hi, y_lo = sent(1, lo, xp), sent(2, hi, yp), sent(1, hi, xp), sent(2, lo, yp)
+    for c in pairs + fetched:
+        c.start()
     yield
 
     def ready(j):
@@ -454,11 +458,6 @@
     def total(j, rows, *more):
         add_rows(sum_ref.at[j, rows], own[j].at[rows], pair_ref.at[j, rows], *more)
 
-    def sent(j, rows, place):
-        return copy(sum_ref.at[j, rows], got_ref.at[j, rows], place)
-
-    d_lo, d_hi = sent(0, lo, xp), sent(0, hi, yp)
-    x_lo, y_hi, x_hi, y_lo = sent(1, lo, xp), sent(2, hi, yp), sent(1, hi, xp), sent(2, lo, yp)
     ready(0)
     total(0, lo)
     d_lo.start()
@@ -512,9 +511,9 @@
     return ref.at[index]
 
 
-def columns_of(ref, index):
+def columns_of(ref, index, rows=slice(None)):
     width = ref.shape[1] // lax.axis_size("dp")
-    return ref.at[:, pl.ds(pl.multiple_of(index * width, width), width)]
+    return ref.at[rows, pl.ds(pl.multiple_of(index * width, width), width)]
 
 
 def exchange(arrays, cid, shapes, take=block_of, put=block_of):
@@ -537,7 +536,14 @@
     )(*arrays)
 
 
-def first_kernel(pack_ref, small_ref, out_ref, all_ref, sems, small_sems, local_sems):
+def first_kernel(count, *refs):
+    ins, small_ref, outs, all_ref = (
+        refs[:count],
+        refs[count],
+        refs[count + 1 : 2 * count + 1],
+        refs[2 * count + 1],
+    )
+    sems, small_sems, local_sems, small_local_sem = refs[2 * count + 2 :]
     plane, span = lax.axis_size("dp"), lax.axis_size("seq")
     at, z = lax.axis_index("dp"), lax.axis_index("seq")
     places = [
@@ -547,46 +553,36 @@
         if i or k
     ]
     greet(places)
-    copy, copy_small = Sender(sems), Sender(small_sems)
+    copy_small = Sender(small_sems)
     block = all_ref.at[z * plane + at]
-    copies = [copy_small(small_ref, block, p) for p in places]
-    for i in range(1, plane):
-        to = lax.rem(at + i, plane)
-        copies.append(copy(pack_ref.at[to], columns_of(out_ref, at), {"dp": to}))
-    copies.append(pltpu.make_async_copy(small_ref, block, local_sems.at[0]))
-    copies.append(
-        pltpu.make_async_copy(pack_ref.at[at], columns_of(out_ref, at), local_sems.at[1])
-    )
-    for c in copies:
+    started = [copy_small(small_ref, block, p) for p in places]
+    started.append(pltpu.make_async_copy(small_ref, block, small_local_sem))
+    for c in started:
         c.start()
-    for c in copies:
+    chips = [lax.rem(at + k, plane) for k in range(1, plane)]
+    started += swap_shards(ins, outs, chips, at, block_of, columns_of, Sender(sems), local_sems)
+    for c in started:
         c.wait()
 
 
-def first_exchange(pack, small, cid):
+def first_exchange(packs, small, cid):
     plane, span = lax.axis_size("dp"), lax.axis_size("seq")
-    _, size, chunk = pack.shape
-    anywhere = pl.BlockSpec(memory_space=pl.ANY)
-    whole = pl.BlockSpec(memory_space=pltpu.VMEM)
-    return pl.pallas_call(
-        first_kernel,
-        name="first_exchange",
-        out_shape=[
-            jax.ShapeDtypeStruct((size, plane * chunk), pack.dtype),
-            jax.ShapeDtypeStruct((span * plane,) + small.shape, small.dtype),
+    count = len(packs)
+    return kernel_call(
+        partial(first_kernel, count),
+        "first_exchange",
+        cid,
+        [((p.shape[1], plane * p.shape[2]), p.dtype, pl.ANY) for p in packs]
+        + [((span * plane,) + small.shape, small.dtype, pltpu.VMEM)],
+        [(p, pl.ANY) for p in packs] + [(small, pltpu.VMEM)],
+        [
+            copies(count * (plane - 1)),
+            copies(plane * span - 1),
+            pltpu.SemaphoreType.DMA((count,)),
+            pltpu.SemaphoreType.DMA,
         ],
-        in_specs=[anywhere, whole],
-        out_specs=[anywhere, whole],
-        scratch_shapes=[
-            pltpu.SemaphoreType.DMA((2, plane - 1)),
-            pltpu.SemaphoreType.DMA((2, plane * span - 1)),
-            pltpu.SemaphoreType.DMA((2,)),
-        ],
-        compiler_params=pltpu.CompilerParams(collective_id=cid, has_side_effects=True),
-        cost_estimate=pl.CostEstimate(
-            flops=0, bytes_accessed=60 * pack.size, transcendentals=0
-        ),
-    )(pack, small)
+        moved=1 << 26,
+    )
 
 
 def run(*steps):
@@ -683,6 +679,7 @@
 FEATURES = 256
 STATE_ROWS = 160
 CHUNKS = 4
+EARLY = 320
 
 
 def feature_pairs():
@@ -744,77 +741,93 @@
         self.keep = jnp.where(last == 0.0, 1.0, 0.0)
 
 
-def pass_states(state_ref, sums_ref, own_ref, own_sums_ref, out_ref, out_sums_ref, col_row, chunk):
-    col_ref, row_ref = col_row
-    rows, heads = state_ref.shape[0] // CHUNKS, state_ref.shape[1]
-    for n in range(rows):
-        b = chunk * rows + n
-        keep = Segments(col_ref, row_ref, b).keep
-        for h in range(heads):
-            out_ref[b, h] = (own_ref[b, h] + keep * state_ref[b, h].astype(jnp.float32)).astype(
-                jnp.bfloat16
+class Chain:
+    def __init__(self, forward, col_ref, row_ref, state_ref, sums_ref, scratch, copy_sems):
+        span, z = lax.axis_size("seq"), lax.axis_index("seq")
+        self.span = span
+        self.to = {"seq": lax.rem(z + (1 if forward else span - 1), span)}
+        self.distance = z if forward else span - 1 - z
+        self.gets, self.gives = self.distance > 0, self.distance < span - 1
+        self.segments = (col_ref, row_ref)
+        self.state_ref, self.sums_ref = state_ref, sums_ref
+        self.own_ref, self.own_sums_ref, self.out_ref, self.out_sums_ref = scratch
+        self.sems = copy_sems
+        self.rows = state_ref.shape[0] // CHUNKS
+
+    def moves(self, g):
+        part = pl.ds(g * self.rows, self.rows)
+        used = pl.ds(0, STATE_ROWS)
+        pairs = (
+            (self.out_ref.at[part, :, used], self.state_ref.at[part, :, used]),
+            (self.out_sums_ref.at[part], self.sums_ref.at[part]),
+        )
+        return [
+            pltpu.make_async_remote_copy(
+                src_ref=a,
+                dst_ref=b,
+                send_sem=self.sems.at[0, 2 * g + n],
+                recv_sem=self.sems.at[1, 2 * g + n],
+                device_id=self.to,
+                device_id_type=MESH_ID,
             )
-        out_sums_ref[b] = own_sums_ref[b] + keep * sums_ref[b]
-
-
-class Chain:
-    def __init__(self, forward, state_ref, sums_ref, out_ref, out_sums_ref, copy):
-        span, z = lax.axis_size("seq"), lax.axis_index("seq")
-        to = lax.rem(z + (1 if forward else span - 1), span)
-        self.gets = z > 0 if forward else z < span - 1
-        self.gives = z < span - 1 if forward else z > 0
-        rows = state_ref.shape[0] // CHUNKS
-        self.moves = []
-        for g in range(CHUNKS):
-            part = pl.ds(g * rows, rows)
-            used = pl.ds(0, STATE_ROWS)
-            self.moves.append(
-                (
-                    copy(
-                        out_ref.at[part, :, used], state_ref.at[part, :, used], {"seq": to}
-                    ),
-                    copy(out_sums_ref.at[part], sums_ref.at[part], {"seq": to}),
-                )
-            )
-
-    def get(self, g):
-        @pl.when(self.gets)
+            for n, (a, b) in enumerate(pairs)
+        ]
+
+    def step(self, n):
+        g = n - self.distance
+
+        @pl.when((g >= 0) & (g < CHUNKS))
         def _():
-            for c in self.moves[g]:
-                c.wait_recv()
-
-    def give(self, g):
-        @pl.when(self.gives)
-        def _():
-            for c in self.moves[g]:
-                c.start()
+            @pl.when(self.gets)
+            def _():
+                for c in self.moves(g):
+                    c.wait_recv()
+
+            for i in range(self.rows):
+                b = g * self.rows + i
+                keep = Segments(*self.segments, b).keep
+                for h in range(self.state_ref.shape[1]):
+                    before = self.state_ref[b, h].astype(jnp.float32)
+                    self.out_ref[b, h] = (self.own_ref[b, h] + keep * before).astype(jnp.bfloat16)
+                self.out_sums_ref[b] = self.own_sums_ref[b] + keep * self.sums_ref[b]
+
+            @pl.when(self.gives)
+            def _():
+                for c in self.moves(g):
+                    c.start()
+
+    def run(self, work, between=()):
+        def body(n, carry):
+            for at, piece in enumerate(between):
+
+                @pl.when(n == at)
+                def _():
+                    piece()
+
+            work(n, self.step)
+            return carry
+
+        lax.fori_loop(0, CHUNKS + self.span - 1, body, 0)
 
     def close(self):
         @pl.when(self.gives)
         def _():
-            for move in self.moves:
-                for c in move:
+            for g in range(CHUNKS):
+                for c in self.moves(g):
                     c.wait_send()
 
 
-def mix_kernel(
+def states_kernel(
     heads,
     normed_ref,
     pack_ref,
     col_ref,
     row_ref,
     pairs_ref,
-    cot_ref,
-    up_ref,
     down_ref,
     qkv_ref,
-    mixed_ref,
-    exact_ref,
-    den_ref,
     state_ref,
     sums_ref,
-    cot_all_ref,
-    up_all_ref,
     down_all_ref,
     pick_ref,
     own_ref,
@@ -822,29 +835,23 @@
     out_ref,
     out_sums_ref,
     sems,
-    cot_sems,
-    local_sem,
     shard_sems,
     shard_local_sems,
 ):
     parts, _, depth = pack_ref.shape
     rows, length = col_ref.shape[0], col_ref.shape[1]
     vcols, qcols = heads * VHEAD, heads * FDIM
-    at, x_at, y_at, _, core = plane_places()
-    plane, span, z = lax.axis_size("dp"), lax.axis_size("seq"), lax.axis_index("seq")
+    plane, span = lax.axis_size("dp"), lax.axis_size("seq")
+    at, z = lax.axis_index("dp"), lax.axis_index("seq")
     chips = [lax.rem(at + k, plane) for k in range(1, plane)]
     state_ref[...] = jnp.zeros_like(state_ref)
     sums_ref[...] = jnp.zeros_like(sums_ref)
     greet(
-        [{"dp": p} for p in chips]
-        + [{"tensor": 1 - core}]
-        + [{"seq": lax.rem(z + k, span)} for k in (1, span - 1)]
-    )
-    gather = gather_steps(cot_ref, cot_all_ref, Sender(cot_sems), local_sem)
-    next(gather)
+        [{"dp": p} for p in chips] + [{"seq": lax.rem(z + k, span)} for k in (1, span - 1)]
+    )
     shards = swap_shards(
-        (up_ref, down_ref),
-        (up_all_ref, down_all_ref),
+        (down_ref,),
+        (down_all_ref,),
         chips,
         at,
         block_of,
@@ -852,7 +859,15 @@
         Sender(shard_sems),
         shard_local_sems,
     )
-    chain = Chain(True, state_ref, sums_ref, out_ref, out_sums_ref, Sender(sems))
+    chain = Chain(
+        True,
+        col_ref,
+        row_ref,
+        state_ref,
+        sums_ref,
+        (own_ref, own_sums_ref, out_ref, out_sums_ref),
+        sems,
+    )
     fill_selectors(pairs_ref, pick_ref, qcols)
     scale = feature_scale(pairs_ref)
 
@@ -883,24 +898,76 @@
         return carry
 
     own_sums_ref[...] = jnp.zeros_like(own_sums_ref)
-    lax.fori_loop(0, rows, first, 0)
-
-    def mixer(b, carry):
+    each = rows // CHUNKS
+
+    def work(n, step):
+        @pl.when(n < CHUNKS)
+        def _():
+            lax.fori_loop(n * each, (n + 1) * each, first, 0)
+
+        step(n)
+
+    chain.run(work)
+    for c in shards:
+        c.wait()
+    chain.close()
+
+
+def mix_kernel(
+    heads,
+    qkv_ref,
+    col_ref,
+    row_ref,
+    pairs_ref,
+    state_ref,
+    sums_ref,
+    cot_ref,
+    mixed_ref,
+    exact_ref,
+    den_ref,
+    cot_all_ref,
+    pick_ref,
+    cot_sems,
+    local_sem,
+):
+    rows, length = col_ref.shape[0], col_ref.shape[1]
+    vcols, qcols = heads * VHEAD, heads * FDIM
+    greet_plane()
+    gather = gather_steps(cot_ref, cot_all_ref, Sender(cot_sems), local_sem)
+    next(gather)
+    fill_selectors(pairs_ref, pick_ref, qcols)
+
+    def tokens_of(b):
+        return pl.ds(pl.multiple_of(b * length, length), length)
+
+    lane = lax.broadcasted_iota(jnp.int32, (length, LANES), 1)
+
+    def here(b, carry):
         t = tokens_of(b)
         seg = Segments(col_ref, row_ref, b)
         tile = qkv_ref[t, pl.ds(vcols, LANES)]
         key = keys_in_place(tile, qcols)
-        lane = lax.broadcasted_iota(jnp.int32, (length, LANES), 1)
         dens = jnp.zeros((length, LANES), jnp.float32)
         for h in range(heads):
             v = pl.ds(h * VHEAD, VHEAD)
             query = jnp.where(head_mask(length, h), tile, jnp.zeros_like(tile))
             _, w, _ = masked_weights(query, key, seg.column, seg.row)
+            exact_ref[t, v] = nn_dot(w.astype(jnp.bfloat16), qkv_ref[t, v])
+            dens = jnp.where(lane == h, jnp.sum(w, axis=1, keepdims=True), dens)
+        den_ref[t] = dens
+        return carry
+
+    def before(b, carry):
+        t = tokens_of(b)
+        head = Segments(col_ref, row_ref, b).head
+        tile = qkv_ref[t, pl.ds(vcols, LANES)]
+        dens = den_ref[t]
+        for h in range(heads):
+            v = pl.ds(h * VHEAD, VHEAD)
             one, two = factors(tile, pick_ref, 0, h)
-            lifted = jnp.where(seg.head, one * two, 0.0)
-            num = nn_dot(w.astype(jnp.bfloat16), qkv_ref[t, v])
-            num += nn_dot(lifted.astype(jnp.bfloat16), state_ref[b, h])
-            den = jnp.sum(w, axis=1, keepdims=True)
+            lifted = jnp.where(head, one * two, 0.0)
+            num = exact_ref[t, v] + nn_dot(lifted.astype(jnp.bfloat16), state_ref[b, h])
+            den = dens[:, h : h + 1]
             den += jnp.sum(lifted * sums_ref[b, h : h + 1], axis=1, keepdims=True)
             value = num / den
             exact_ref[t, v] = value
@@ -909,22 +976,19 @@
         den_ref[t] = dens
         return carry
 
-    each = rows // CHUNKS
-    for g in range(CHUNKS):
-        chain.get(g)
-        pass_states(
-            state_ref, sums_ref, own_ref, own_sums_ref, out_ref, out_sums_ref, (col_ref, row_ref), g
-        )
-        chain.give(g)
-        if g == 0:
-            next(gather)
-            next(gather)
-            next(gather)
-        lax.fori_loop(g * each, (g + 1) * each, mixer, 0)
+    def row(b, carry):
+        for at in range(1, 6):
+
+            @pl.when(b == at)
+            def _():
+                next(gather)
+
+        here(b, 0)
+        before(b, 0)
+        return carry
+
+    lax.fori_loop(0, rows, row, 0)
     run(gather)
-    for c in shards:
-        c.wait()
-    chain.close()
 
 
 def state_scratch(rows, heads):
@@ -937,42 +1001,53 @@
     ]
 
 
-def mix(normed, pack, seg_col, seg_row, pairs, cot_own, up, down, heads, cid):
+def states(normed, pack, seg_col, seg_row, pairs, down, heads, cid):
     tokens = normed.shape[0]
     rows = seg_col.shape[0]
     vcols = heads * VHEAD
+    plane, size, chunk = down.shape
+    whole = pltpu.VMEM
+    return kernel_call(
+        partial(states_kernel, heads),
+        "states",
+        cid,
+        [
+            ((tokens, vcols + LANES), jnp.bfloat16, whole),
+            ((rows, heads, FEATURES, VHEAD), jnp.bfloat16, whole),
+            ((rows, 8, FEATURES), jnp.float32, whole),
+            ((size, plane * chunk), jnp.bfloat16, pl.ANY),
+        ],
+        [(a, whole) for a in (normed, pack, seg_col, seg_row, pairs)] + [(down, pl.ANY)],
+        state_scratch(rows, heads)
+        + [copies(2 * CHUNKS), copies(plane - 1), pltpu.SemaphoreType.DMA((1,))],
+        moved=normed.size * 20,
+    )
+
+
+def mix(qkv, seg_col, seg_row, pairs, state, sums, cot_own, heads, cid):
+    tokens = qkv.shape[0]
+    vcols = heads * VHEAD
     m, width = cot_own.shape
-    plane, size, chunk = up.shape
     whole = pltpu.VMEM
-    out = kernel_call(
+    mixed, exact, den, cot = kernel_call(
         partial(mix_kernel, heads),
         "mix",
         cid,
         [
-            ((tokens, vcols + LANES), jnp.bfloat16, whole),
             ((tokens, vcols), jnp.bfloat16, whole),
             ((tokens, vcols), jnp.float32, whole),
             ((tokens, LANES), jnp.float32, whole),
-            ((rows, heads, FEATURES, VHEAD), jnp.bfloat16, whole),
-            ((rows, 8, FEATURES), jnp.float32, whole),
             ((4, 2, m, width), jnp.bfloat16, pl.ANY),
-            ((size, plane * chunk), jnp.bfloat16, pl.ANY),
-            ((size, plane * chunk), jnp.bfloat16, pl.ANY),
         ],
-        [(a, whole) for a in (normed, pack, seg_col, seg_row, pairs, cot_own)]
-        + [(up, pl.ANY), (down, pl.ANY)],
-        state_scratch(rows, heads)
-        + [
-            copies(2 * CHUNKS),
+        [(a, whole) for a in (qkv, seg_col, seg_row, pairs, state, sums, cot_own)],
+        [
+            pltpu.VMEM((2, heads, 2, LANES, FEATURES), jnp.bfloat16),
             copies(GATHER_COPIES),
             pltpu.SemaphoreType.DMA,
-            copies(2 * (plane - 1)),
-            pltpu.SemaphoreType.DMA((2,)),
         ],
-        moved=normed.size * 30,
-    )
-    qkv, mixed, exact, den, state, sums, cot, up, down = out
-    return (qkv, mixed, exact, den, state, sums), cot.reshape(-1, width), up, down
+        moved=cot_own.size * 80,
+    )
+    return mixed, exact, den, cot.reshape(-1, width)
 
 
 def branch_kernel(
@@ -1055,26 +1130,48 @@
     return jnp.where(test, a, b)
 
 
-def project(at, w_ref):
+def project(at, w_ref, rows):
     parts, _, depth = w_ref.shape
-    total = nt_dot(at(pl.ds(0, depth)), w_ref[0])
+    total = nt_dot(at(pl.ds(0, depth)), w_ref[0, rows])
     for s in range(1, parts):
-        total += nt_dot(at(pl.ds(s * depth, depth)), w_ref[s])
+        total += nt_dot(at(pl.ds(s * depth, depth)), w_ref[s, rows])
     return total
+
+
+def arrivals(i, half):
+    at, x_at, y_at, d_at, core = plane_places()
+    k = choose(parity(i) == 0, core, 1 - core)
+    one = choose(i < 2, at, choose(i < 6, x_at, d_at))
+    two = choose(i < 2, at, choose(i < 6, y_at, d_at))
+    late = (i >= 4) & (i < 6)
+    late = int(late) if isinstance(late, bool) else late.astype(jnp.int32)
+    first, second = late * half, (1 - late) * half
+    if not isinstance(i, int):
+        first, second = pl.multiple_of(first, half), pl.multiple_of(second, half)
+    return (one, k, first), (two, k, second)
+
+
+def stacked_copies(early, late, out, sems):
+    rows = early.shape[1]
+    return [
+        pltpu.make_async_copy(early, out.at[:, pl.ds(0, rows)], sems.at[0]),
+        pltpu.make_async_copy(late, out.at[:, pl.ds(rows, late.shape[1])], sems.at[1]),
+    ]
 
 
 def expand_kernel(
     own_ref,
-    gate_w_hbm,
-    up_w_hbm,
+    early_hbm,
+    late_hbm,
     normed_hbm,
     gate_hbm,
     up_hbm,
+    hidden_hbm,
     normed_ref,
-    gate_w_ref,
-    up_w_ref,
+    w_ref,
     gate_ref,
     up_ref,
+    hidden_ref,
     sems,
     local_sem,
     w_sems,
@@ -1082,39 +1179,30 @@
     keep_sem,
 ):
     greet_plane()
-    at, x_at, y_at, d_at, core = plane_places()
     half = own_ref.shape[0] // 2
+    units = gate_ref.shape[2]
     gather = gather_steps(own_ref, normed_ref, Sender(sems), local_sem)
     next(gather)
-    weights = [
-        pltpu.make_async_copy(gate_w_hbm, gate_w_ref, w_sems.at[0]),
-        pltpu.make_async_copy(up_w_hbm, up_w_ref, w_sems.at[1]),
-    ]
+    weights = stacked_copies(early_hbm, late_hbm, w_ref, w_sems)
     for c in weights:
         c.start()
-
-    def halves(i):
-        k = choose(parity(i) == 0, core, 1 - core)
-        one = choose(i < 2, at, choose(i < 6, x_at, d_at))
-        two = choose(i < 2, at, choose(i < 6, y_at, d_at))
-        late = (i >= 4) & (i < 6)
-        late = int(late) if isinstance(late, bool) else late.astype(jnp.int32)
-        first, second = late * half, (1 - late) * half
-        if not isinstance(i, int):
-            first, second = pl.multiple_of(first, half), pl.multiple_of(second, half)
-        return (one, k, first), (two, k, second)
 
     def store_copies(i):
         slot = parity(i)
         found = []
-        for n, (c, k, r) in enumerate(halves(i)):
+        for n, (c, k, r) in enumerate(arrivals(i, half)):
             rows = pl.ds(n * half, half)
-            for q, (a, b) in enumerate(((gate_ref, gate_hbm), (up_ref, up_hbm))):
-                found.append(
-                    pltpu.make_async_copy(
-                        a.at[slot, rows], b.at[c, k, pl.ds(r, half)], store_sems.at[slot, 2 * n + q]
-                    )
-                )
+            column = (c * 2 + k) * (2 * half) + r
+            pairs = (
+                (gate_ref.at[slot, rows], gate_hbm.at[c, k, pl.ds(r, half)]),
+                (up_ref.at[slot, rows], up_hbm.at[c, k, pl.ds(r, half)]),
+                (
+                    hidden_ref.at[slot, :, rows],
+                    hidden_hbm.at[:, pl.ds(pl.multiple_of(column, half), half)],
+                ),
+            )
+            for q, (a, b) in enumerate(pairs):
+                found.append(pltpu.make_async_copy(a, b, store_sems.at[slot, 3 * n + q]))
         return found
 
     next(gather)
@@ -1134,13 +1222,15 @@
                 c.wait()
 
         slot = parity(i)
-        pieces = halves(i)
+        pieces = arrivals(i, half)
 
         def columns(cols):
             return jnp.concatenate([normed_ref[c, k, pl.ds(r, half), cols] for c, k, r in pieces])
 
-        gate_ref[slot] = project(columns, gate_w_ref)
-        up_ref[slot] = project(columns, up_w_ref)
+        gate = project(columns, w_ref, pl.ds(0, units))
+        up = project(columns, w_ref, pl.ds(units, units))
+        gate_ref[slot], up_ref[slot] = gate, up
+        hidden_ref[slot] = (gate * jax.nn.sigmoid(gate) * up).astype(jnp.bfloat16).T
         for c in store_copies(i):
             c.start()
         return carry
@@ -1155,51 +1245,65 @@
     run(gather)
 
 
-def expand(own, gate_w, up_w, cid):
+def expand(own, early, late, cid):
     m, width = own.shape
-    units = gate_w.shape[1]
+    weights = (early.shape[0], early.shape[1] + late.shape[1], early.shape[2])
+    units = weights[1] // 2
     low = jnp.bfloat16
     thin = ((4, 2, m, units), jnp.float32, pl.ANY)
-    normed, gate, up = kernel_call(
+    normed, gate, up, hidden = kernel_call(
         expand_kernel,
         "expand",
         cid,
-        [((4, 2, m, width), low, pl.ANY), thin, thin],
-        [(own, pltpu.VMEM), (gate_w, pl.ANY), (up_w, pl.ANY)],
+        [((4, 2, m, width), low, pl.ANY), thin, thin, ((units, 8 * m), low, pl.ANY)],
+        [(own, pltpu.VMEM), (early, pl.ANY), (late, pl.ANY)],
         [
             pltpu.VMEM((4, 2, m, width), low),
-            pltpu.VMEM(gate_w.shape, low),
-            pltpu.VMEM(up_w.shape, low),
+            pltpu.VMEM(weights, low),
             pltpu.VMEM((2, m, units), jnp.float32),
             pltpu.VMEM((2, m, units), jnp.float32),
+            pltpu.VMEM((2, units, m), low),
             copies(GATHER_COPIES),
             pltpu.SemaphoreType.DMA,
             pltpu.SemaphoreType.DMA((2,)),
-            pltpu.SemaphoreType.DMA((2, 4)),
+            pltpu.SemaphoreType.DMA((2, 6)),
             pltpu.SemaphoreType.DMA,
         ],
         flops=32 * m * width * units,
         moved=1 << 27,
     )
-    return normed.reshape(8 * m, width), gate.reshape(8 * m, units), up.reshape(8 * m, units)
+    flat = (8 * m, units)
+    return normed.reshape(8 * m, width), gate.reshape(flat), up.reshape(flat), hidden
 
 
 def hidden_kernel(
     gate_ref,
     up_ref,
     cot_ref,
-    gate_w_ref,
-    up_w_ref,
-    down_w_ref,
+    early_hbm,
+    late_hbm,
+    down_hbm,
     out_ref,
     dnormed_ref,
     dgate_ref,
     dup_ref,
-    hidden_ref,
+    w_ref,
+    down_w_ref,
+    w_sems,
 ):
-    parts, _, depth = down_w_ref.shape
+    parts, units, depth = down_w_ref.shape
+
+    @pl.when(pl.program_id(0) == 0)
+    def _():
+        weights = stacked_copies(early_hbm, late_hbm, w_ref, w_sems)
+        weights.append(pltpu.make_async_copy(down_hbm, down_w_ref, w_sems.at[2]))
+        for c in weights:
+            c.start()
+        for c in weights:
+            c.wait()
+
     gate, up = gate_ref[...], up_ref[...]
-    dhidden = project(lambda cols: cot_ref[:, cols], down_w_ref)
+    dhidden = project(lambda cols: cot_ref[:, cols], down_w_ref, pl.ds(0, units))
     sig = jax.nn.sigmoid(gate)
     silu = gate * sig
     hidden = (silu * up).astype(jnp.bfloat16)
@@ -1207,36 +1311,42 @@
     dup = (dhidden * silu).astype(jnp.bfloat16)
     for s in range(parts):
         cols = pl.ds(s * depth, depth)
-        dnormed_ref[:, cols] = (nn_dot(dgate, gate_w_ref[s]) + nn_dot(dup, up_w_ref[s])).astype(
-            jnp.bfloat16
-        )
+        dnormed_ref[:, cols] = (
+            nn_dot(dgate, w_ref[s, pl.ds(0, units)]) + nn_dot(dup, w_ref[s, pl.ds(units, units)])
+        ).astype(jnp.bfloat16)
         out_ref[:, cols] = nn_dot(hidden, down_w_ref[s]).astype(jnp.bfloat16)
-    hidden_ref[...], dgate_ref[...], dup_ref[...] = hidden.T, dgate.T, dup.T
-
-
-def hidden_units(gate, up, cot, gate_w, up_w, down_w, block=256):
+    dgate_ref[...], dup_ref[...] = dgate.T, dup.T
+
+
+def hidden_units(gate, up, cot, early, late, down_w, block=256):
     tokens, units = gate.shape
     width = cot.shape[1]
     low = jnp.bfloat16
     wide = pl.BlockSpec((block, width), lambda i: (i, 0))
     thin = pl.BlockSpec((block, units), lambda i: (i, 0))
     turned = pl.BlockSpec((units, block), lambda i: (0, i))
-    weights = pl.BlockSpec(gate_w.shape, lambda i: (0, 0, 0), pipeline_mode=pl.Buffered(1))
+    anywhere = pl.BlockSpec(memory_space=pl.ANY)
+    stacked = (early.shape[0], early.shape[1] + late.shape[1], early.shape[2])
     return pl.pallas_call(
         hidden_kernel,
         name="hidden_units",
         grid=(tokens // block,),
         out_shape=[jax.ShapeDtypeStruct((tokens, width), low)] * 2
-        + [jax.ShapeDtypeStruct((units, tokens), low)] * 3,
-        in_specs=[thin, thin, wide, weights, weights, weights],
-        out_specs=[wide, wide, turned, turned, turned],
+        + [jax.ShapeDtypeStruct((units, tokens), low)] * 2,
+        in_specs=[thin, thin, wide, anywhere, anywhere, anywhere],
+        out_specs=[wide, wide, turned, turned],
+        scratch_shapes=[
+            pltpu.VMEM(stacked, low),
+            pltpu.VMEM(down_w.shape, low),
+            pltpu.SemaphoreType.DMA((3,)),
+        ],
         compiler_params=pltpu.CompilerParams(vmem_limit_bytes=VMEM_LIMIT),
         cost_estimate=pl.CostEstimate(
             flops=8 * tokens * width * units,
             bytes_accessed=1 << 27,
             transcendentals=tokens * units,
         ),
-    )(gate, up, cot, gate_w, up_w, down_w)
+    )(gate, up, cot, early, late, down_w)
 
 
 def norm_gradient(r, value_at, grad_ref, gain_at, gain_grad, finish, width):
@@ -1262,8 +1372,7 @@
     dgate_hbm,
     dup_hbm,
     total_ref,
-    gate_hbm,
-    up_hbm,
+    grads_hbm,
     held_ref,
     pair_ref,
     sum_ref,
@@ -1297,12 +1406,14 @@
     width = grad_ref.shape[2]
     blocks = normed_ref.shape[1] // width
 
-    def gradients(which, out_hbm):
+    def gradients(which):
+        rows = pl.ds(which * grad_ref.shape[1], grad_ref.shape[1])
+
         def stored(i):
             column = pl.ds(pl.multiple_of(i * width, width), width)
             slot = parity(i)
             return pltpu.make_async_copy(
-                grad_ref.at[slot], out_hbm.at[:, column], store_sems.at[slot]
+                grad_ref.at[slot], grads_hbm.at[rows, column], store_sems.at[slot]
             )
 
         def body(i, carry):
@@ -1324,10 +1435,10 @@
 
     loads[0].wait()
     loads[1].wait()
-    gradients(0, gate_hbm)
+    gradients(0)
     next(scatter)
     loads[2].wait()
-    gradients(1, up_hbm)
+    gradients(1)
     run(scatter)
 
 
@@ -1342,8 +1453,7 @@
         cid,
         [
             ((m, width), jnp.float32, pltpu.VMEM),
-            ((units, width), low, pl.ANY),
-            ((units, width), low, pl.ANY),
+            ((2 * units, width), low, pl.ANY),
         ],
         [(a, pl.ANY) for a in (part, normed, dgate, dup)],
         [pltpu.VMEM((4, m, width), low)]
@@ -1367,15 +1477,24 @@
     residual_ref,
     cot_ref,
     small_ref,
+    pack_ref,
+    mixed_ref,
     dresid_ref,
     gain_ref,
+    dmixed_ref,
+    grad_ref,
     all_ref,
     low_ref,
+    sum_ref,
     gather_sems,
     local_sem,
 ):
     greet_plane()
     m, width = residual_ref.shape
+    half = m // 2
+    parts, _, depth = pack_ref.shape
+    vcols = mixed_ref.shape[3]
+    first_row = pack_ref.shape[1] - vcols
     gain_ref[...] = jnp.zeros_like(gain_ref)
 
     def finish(r, k, v):
@@ -1396,37 +1515,71 @@
         return carry
 
     row_blocks(m, ROW_STEP, body)(0)
-    run(gather_steps(low_ref, all_ref, Sender(gather_sems), local_sem))
-
-
-def turn(total, residual, cot_own, small, cid):
+    gather = gather_steps(low_ref, all_ref, Sender(gather_sems), local_sem)
+    next(gather)
+    sum_ref[...] = jnp.zeros_like(sum_ref)
+    next(gather)
+
+    def block(i, carry):
+        for step in range(1, 8):
+
+            @pl.when(i == step)
+            def _():
+                next(gather)
+
+        pieces = arrivals(i, half)
+
+        def columns(cols):
+            return jnp.concatenate([all_ref[c, k, pl.ds(r, half), cols] for c, k, r in pieces])
+
+        left = jnp.concatenate([mixed_ref[c, k, pl.ds(r, half)] for c, k, r in pieces])
+        dmixed = project(columns, pack_ref, pl.ds(first_row, vcols)).astype(jnp.bfloat16)
+        for n, (c, k, r) in enumerate(pieces):
+            dmixed_ref[c, k, pl.ds(r, half)] = dmixed[n * half : (n + 1) * half]
+        for s in range(parts):
+            cols = pl.ds(s * depth, depth)
+            sum_ref[:, cols] += tn_dot(left, columns(cols))
+        return carry
+
+    lax.fori_loop(0, 8, block, 0)
+    grad_ref[...] = sum_ref[...].astype(jnp.bfloat16)
+    run(gather)
+
+
+def turn(total, residual, cot_own, small, pack, mixed, cid):
     m, width = residual.shape
-    whole = pltpu.VMEM
-    dresid, gain, gathered = kernel_call(
+    vcols = mixed.shape[1]
+    whole, low = pltpu.VMEM, jnp.bfloat16
+    dresid, gain, dmixed, grad = kernel_call(
         turn_kernel,
         "turn",
         cid,
         [
             ((m, width), jnp.float32, whole),
             ((8, width), jnp.float32, whole),
-            ((4, 2, m, width), jnp.bfloat16, pl.ANY),
+            ((4, 2, m, vcols), low, whole),
+            ((vcols, width), low, whole),
         ],
-        [(a, whole) for a in (total, residual, cot_own, small)],
+        [(a, whole) for a in (total, residual, cot_own, small, pack)]
+        + [(mixed.reshape(4, 2, m, vcols), whole)],
         [
-            pltpu.VMEM((m, width), jnp.bfloat16),
+            pltpu.VMEM((4, 2, m, width), low),
+            pltpu.VMEM((m, width), low),
+            pltpu.VMEM((vcols, width), jnp.float32),
             copies(GATHER_COPIES),
             pltpu.SemaphoreType.DMA,
         ],
         moved=residual.size * 80,
     )
-    return dresid, gain, gathered.reshape(-1, width)
+    return dresid, gain, dmixed.reshape(8 * m, vcols), grad
 
 
 def unmix_kernel(
     heads,
     count,
-    dresid_ref,
-    pack_ref,
+    dmixed_ref,
+    normed_hbm,
+    output_grad_ref,
     part_ref,
     residual_ref,
     col_ref,
@@ -1439,10 +1592,13 @@
     sums_ref,
     *refs,
 ):
-    ins, dqkv_ref, block_ref = refs[:count], refs[count], refs[count + 1]
-    outs = refs[count + 2 : 2 * count + 2]
+    ins, dqkv_ref, block_ref, grad_ref = refs[:count], *refs[count : count + 3]
+    outs = refs[count + 3 : 2 * count + 3]
     (
-        dmixed_ref,
+        normed_ref,
+        turned_ref,
+        dvalue_ref,
+        dtile_ref,
         back_ref,
         back_sums_ref,
         pick_ref,
@@ -1460,14 +1616,15 @@
         local_sems,
         scatter_sems,
         held_sems,
-    ) = refs[2 * count + 2 :]
-    parts, _, depth = pack_ref.shape
+        normed_sem,
+    ) = refs[2 * count + 3 :]
     rows, length = col_ref.shape[0], col_ref.shape[1]
     vcols, qcols = heads * VHEAD, heads * FDIM
-    first_row = pack_ref.shape[1] - vcols
     at, x_at, y_at, _, core = plane_places()
     plane, span, z = lax.axis_size("dp"), lax.axis_size("seq"), lax.axis_index("seq")
     chips = [lax.rem(at + k, plane) for k in range(1, plane)]
+    normed_copy = pltpu.make_async_copy(normed_hbm, normed_ref, normed_sem)
+    normed_copy.start()
     back_ref[...] = jnp.zeros_like(back_ref)
     back_sums_ref[...] = jnp.zeros_like(back_sums_ref)
     greet(
@@ -1485,7 +1642,15 @@
         (held_ref, held_sems),
     )
     next(scatter)
-    chain = Chain(False, back_ref, back_sums_ref, out_ref, out_sums_ref, Sender(sems))
+    chain = Chain(
+        False,
+        col_ref,
+        row_ref,
+        back_ref,
+        back_sums_ref,
+        (own_ref, own_sums_ref, out_ref, out_sums_ref),
+        sems,
+    )
     fill_selectors(pairs_ref, pick_ref, qcols)
     scale = feature_scale(pairs_ref)
 
@@ -1500,12 +1665,6 @@
 
     def first(b, carry):
         t = tokens_of(b)
-        total = jnp.zeros((length, vcols), jnp.float32)
-        for s in range(parts):
-            total += nt_dot(
-                dresid_ref[t, pl.ds(s * depth, depth)], pack_ref[s, pl.ds(first_row, vcols)]
-            )
-        dmixed_ref[t] = total.astype(jnp.bfloat16)
         head = Segments(col_ref, row_ref, b).head
         tile = qkv_ref[t, pl.ds(vcols, LANES)]
         for h in range(heads):
@@ -1517,8 +1676,6 @@
         return carry
 
     own_sums_ref[...] = jnp.zeros_like(own_sums_ref)
-    lax.fori_loop(0, rows, first, 0)
-    next(scatter)
     shards = swap_shards(ins, outs, chips, at, columns_of, block_of, Sender(shard_sems), local_sems)
 
     def lowered(dlifted, kind, h, one, two):
@@ -1526,7 +1683,7 @@
             (dlifted * one).astype(jnp.bfloat16), pick_ref[kind, h, 1]
         )
 
-    def mixer(b, carry):
+    def here(b, carry):
         t = tokens_of(b)
         seg = Segments(col_ref, row_ref, b)
         tile = qkv_ref[t, pl.ds(vcols, LANES)]
@@ -1536,48 +1693,58 @@
         for h in range(heads):
             inside = head_mask(length, h)
             v = pl.ds(h * VHEAD, VHEAD)
-            value = qkv_ref[t, v]
             query = jnp.where(inside, tile, jnp.zeros_like(tile))
             dn, dd = cotangents(t, h)
             a, w, keep = masked_weights(query, key, seg.column, seg.row)
-            dw = jnp.where(keep, nt_dot(dn, value) + dd, 0.0)
+            dw = jnp.where(keep, nt_dot(dn, qkv_ref[t, v]) + dd, 0.0)
             da = (dw * (1.0 + a) * 0.25).astype(jnp.bfloat16)
-            dvalue = tn_dot(w.astype(jnp.bfloat16), dn)
+            dvalue_ref[t, v] = tn_dot(w.astype(jnp.bfloat16), dn)
             dtile += jnp.where(inside, nn_dot(da, key), 0.0)
             dkey += jnp.where(inside, tn_dot(da, query), 0.0)
             one, two = factors(tile, pick_ref, 0, h)
             dlifted = nt_dot(dn, state_ref[b, h]) + dd * sums_ref[b, h : h + 1]
             dtile += lowered(jnp.where(seg.head, dlifted, 0.0), 0, h, one, two)
+        dtile_ref[t] = dtile + pltpu.roll(dkey, qcols, axis=1)
+        return carry
+
+    def after(b, carry):
+        t = tokens_of(b)
+        tail = Segments(col_ref, row_ref, b).tail
+        tile = qkv_ref[t, pl.ds(vcols, LANES)]
+        dtile = dtile_ref[t]
+        for h in range(heads):
+            v = pl.ds(h * VHEAD, VHEAD)
             one, two = factors(tile, pick_ref, 1, h)
-            lifted = jnp.where(seg.tail, one * two * scale, 0.0)
-            dlifted = (nt_dot(value, back_ref[b, h]) + back_sums_ref[b, h : h + 1]) * scale
-            dtile += lowered(jnp.where(seg.tail, dlifted, 0.0), 1, h, one, two)
-            dvalue += nn_dot(lifted.astype(jnp.bfloat16), back_ref[b, h])
+            lifted = jnp.where(tail, one * two * scale, 0.0)
+            dlifted = nt_dot(qkv_ref[t, v], back_ref[b, h]) + back_sums_ref[b, h : h + 1]
+            dtile += lowered(jnp.where(tail, dlifted * scale, 0.0), 1, h, one, two)
+            dvalue = dvalue_ref[t, v] + nn_dot(lifted.astype(jnp.bfloat16), back_ref[b, h])
             dqkv_ref[t, v] = dvalue.astype(jnp.bfloat16)
-        dtile += pltpu.roll(dkey, qcols, axis=1)
         lane = lax.broadcasted_iota(jnp.int32, (length, LANES), 1)
         dqkv_ref[t, pl.ds(vcols, LANES)] = jnp.where(lane < 2 * qcols, dtile, 0.0).astype(
             jnp.bfloat16
         )
+        turned_ref[:, t] = dqkv_ref[t].T
         return carry
 
     each = rows // CHUNKS
-    for g in range(CHUNKS):
-        chain.get(g)
-        pass_states(
-            back_ref,
-            back_sums_ref,
-            own_ref,
-            own_sums_ref,
-            out_ref,
-            out_sums_ref,
-            (col_ref, row_ref),
-            g,
-        )
-        chain.give(g)
-        if g == 1:
-            next(scatter)
-        lax.fori_loop(g * each, (g + 1) * each, mixer, 0)
+
+    def work(n, step):
+        @pl.when(n < CHUNKS)
+        def _():
+            lax.fori_loop(n * each, (n + 1) * each, first, 0)
+
+        step(n)
+
+        @pl.when(n < CHUNKS)
+        def _():
+            lax.fori_loop(n * each, (n + 1) * each, here, 0)
+
+    def advance():
+        next(scatter)
+
+    chain.run(work, [lambda: None, advance, lambda: None, lambda: None, advance])
+    lax.fori_loop(0, rows, after, 0)
     run(scatter)
 
     def finish(r, carry):
@@ -1585,37 +1752,59 @@
         return carry
 
     row_blocks(block_ref.shape[0], ROW_STEP, finish)(0)
+    normed_copy.wait()
+    wide = 4 * LANES
+    qkv_rows = grad_ref.shape[0] - vcols
+    grad_ref[pl.ds(qkv_rows, vcols)] = output_grad_ref[...]
+
+    def gradient(i, carry):
+        cols = pl.ds(pl.multiple_of(i * wide, wide), wide)
+        grad_ref[pl.ds(0, qkv_rows), cols] = nn_dot(
+            turned_ref[pl.ds(0, qkv_rows)], normed_ref[:, cols]
+        ).astype(jnp.bfloat16)
+        return carry
+
+    lax.fori_loop(0, normed_ref.shape[1] // wide, gradient, 0)
     for c in shards:
         c.wait()
     chain.close()
 
 
-def unmix(dresid_low, pack, part, residual, seg_col, seg_row, pairs, kept, shards, heads, cid):
-    tokens = dresid_low.shape[0]
+def unmix(dmixed, normed, output_grad, part, residual, segments, pairs, kept, shards, heads, cid):
+    seg_col, seg_row = segments
+    tokens, vcols = dmixed.shape
     plane, rows = lax.axis_size("dp"), seg_col.shape[0]
-    vcols = heads * VHEAD
+    grad_rows = 2 * vcols + 2 * heads * FDIM
     m, width = residual.shape
     count = len(shards)
     whole, low = pltpu.VMEM, jnp.bfloat16
-    dqkv, block, *swapped = kernel_call(
+    dqkv, block, grad, *swapped = kernel_call(
         partial(unmix_kernel, heads, count),
         "unmix",
         cid,
-        [((tokens, vcols + LANES), low, whole), ((m, width), low, whole)]
+        [
+            ((tokens, vcols + LANES), low, whole),
+            ((m, width), low, whole),
+            ((grad_rows, width), low, whole),
+        ]
         + [((plane, p.shape[0], p.shape[1] // plane), p.dtype, pl.ANY) for p in shards],
         [
-            (dresid_low, whole),
-            (pack, whole),
+            (dmixed, whole),
+            (normed, pl.ANY),
+            (output_grad, whole),
             (part.reshape(4, 2, m, width), pl.ANY),
             (residual, whole),
             (seg_col, whole),
             (seg_row, whole),
             (pairs, whole),
         ]
-        + [(kept[n], whole) for n in (0, 2, 3, 4, 5)]
+        + [(a, whole) for a in kept]
         + [(p, pl.ANY) for p in shards],
         [
-            pltpu.VMEM((tokens, vcols), low),
+            pltpu.VMEM((tokens, width), low),
+            pltpu.VMEM((vcols + LANES, tokens), low),
+            pltpu.VMEM((tokens, vcols), jnp.float32),
+            pltpu.VMEM((tokens, LANES), jnp.float32),
             pltpu.VMEM((rows, heads, FEATURES, VHEAD), low),
             pltpu.VMEM((rows, 8, FEATURES), jnp.float32),
         ]
@@ -1628,10 +1817,11 @@
             pltpu.SemaphoreType.DMA((count,)),
             copies(SCATTER_COPIES),
             pltpu.SemaphoreType.DMA((4,)),
+            pltpu.SemaphoreType.DMA,
         ],
         moved=residual.size * 120,
     )
-    return dqkv, block, swapped
+    return dqkv, block, grad, swapped
 
 
 def last_kernel(count, *refs):
@@ -1711,9 +1901,11 @@
     block_ref,
     small_ref,
     gain_two_ref,
+    shards_ref,
     grad_ref,
     out_ref,
     gains_ref,
+    shards_all_ref,
     gain_ref,
     part_ref,
     total_ref,
@@ -1725,9 +1917,31 @@
     sems,
     pair_sems,
     local_sems,
+    shard_sems,
+    shard_local_sems,
 ):
-    greet_plane()
+    plane, at = lax.axis_size("dp"), lax.axis_index("dp")
     core = lax.axis_index("tensor")
+    chips = [lax.rem(at + k, plane) for k in range(1, plane)]
+    greet([{"dp": p} for p in chips] + [{"tensor": 1 - core}])
+    shard_copy = Sender(shard_sems)
+
+    half = shards_ref.shape[0] // 2
+
+    def swap(n):
+        rows = pl.ds(n * half, half)
+        return swap_shards(
+            (shards_ref,),
+            (shards_all_ref,),
+            chips,
+            at,
+            lambda ref, p: columns_of(ref, p, rows),
+            lambda ref, p: ref.at[p, rows],
+            shard_copy,
+            shard_local_sems.at[pl.ds(n, 1)],
+        )
+
+    shards = swap(0)
     parts, _, depth = pack_ref.shape
     m, width = x_ref.shape
     wide = dqkv_ref.shape[1] - LANES + 2 * FDIM * ((dqkv_ref.shape[1] - LANES) // VHEAD)
@@ -1756,6 +1970,9 @@
     local = [pltpu.make_async_copy(low_ref, out_ref.at[core], local_sems.at[0])]
     to_pair[0].start()
     local[0].start()
+    next(scatter)
+    next(scatter)
+    shards += swap(1)
     run(scatter)
     gain_ref[...] = jnp.zeros_like(gain_ref)
 
@@ -1783,12 +2000,13 @@
     for k in range(blocks):
         for row, ref in enumerate((gain_ref, gain_two_ref)):
             gains_ref[k, row : row + 1] = jnp.sum(ref[:, lanes(k)], axis=0, keepdims=True)
-    for c in to_pair + local:
+    for c in to_pair + local + shards:
         c.wait()
 
 
-def leave(dqkv, pack, x, dresid, block, small, gain_two, cid):
+def leave(dqkv, pack, x, dresid, block, small, gain_two, shards, cid):
     m, width = x.shape
+    plane = lax.axis_size("dp")
     whole = pltpu.VMEM
     return kernel_call(
         exit_kernel,
@@ -1798,8 +2016,10 @@
             ((2, m, width), jnp.float32, pl.ANY),
             ((2, m, width), jnp.bfloat16, pl.ANY),
             ((width // LANES, 8, LANES), jnp.float32, whole),
-        ],
-        [(a, whole) for a in (dqkv, pack, x, dresid, block, small, gain_two)],
+        ]
+        + [((plane, p.shape[0], p.shape[1] // plane), p.dtype, pl.ANY) for p in shards],
+        [(a, whole) for a in (dqkv, pack, x, dresid, block, small, gain_two)]
+        + [(p, pl.ANY) for p in shards],
         [
             pltpu.VMEM((8, width), jnp.float32),
             pltpu.VMEM((4, 2, m, width), jnp.bfloat16),
@@ -1811,6 +2031,8 @@
         + [
             copies(SCATTER_COPIES),
             copies(2),
+            pltpu.SemaphoreType.DMA((2,)),
+            copies(2 * (plane - 1)),
             pltpu.SemaphoreType.DMA((2,)),
         ],
         moved=x.size * 120,
@@ -1865,9 +2087,12 @@
     [attn_pack] = exchange(
         [attn_pack], 1, [(attn_pack.shape[1], plane * chunk)], put=columns_of
     )
-    gate_w, small = lax.optimization_barrier((split(gate_weight.T), small, attn_pack))[:2]
-    gate_w, small = first_exchange(gate_w, small, 2)
-    attn_pack, gate_w = over_seq(attn_pack), over_seq(gate_w)
+    gate_w = split(gate_weight.T)
+    early_w = gate_w[:, :EARLY]
+    late_w = jnp.concatenate([gate_w[:, EARLY:], split(up_weight.T)], axis=1)
+    early_w, late_w, small = lax.optimization_barrier((early_w, late_w, small, attn_pack))[:3]
+    early_w, late_w, small = first_exchange([early_w, late_w], small, 2)
+    attn_pack, early_w = over_seq(attn_pack), over_seq(early_w)
     starts = small[:, 2:-2].reshape(span, plane * rows, length)
     segments = jnp.cumsum(
         lax.dynamic_index_in_dim(starts, lax.axis_index("seq"), 0, keepdims=False), axis=1
@@ -1880,56 +2105,46 @@
     normed_one, x, cot_own = entry(
         tokens.reshape(cores, own, width), cotangent.reshape(cores, own, width), small, 3
     )
-    kept, cot, up_w, down_w = mix(
+    qkv, state, sums, down_w = states(
+        normed_one, attn_pack, seg_col, seg_row, pairs, split(down_weight), heads, 4
+    )
+    late_w, down_w = lax.optimization_barrier((late_w, down_w))
+    late_w, down_w = over_seq(late_w), over_seq(down_w)
+    mixed, exact, den, cot = mix(
+        qkv, seg_col, seg_row, pairs, state, sums, cot_own, heads, 13
+    )
+    residual, normed_own = branch(mixed, attn_pack, x, small, 5)
+    normed_two, gate, up, hidden = expand(normed_own, early_w, late_w, 11)
+    down_grad = nn_dot(hidden, cot).astype(jnp.bfloat16)
+    gate, down_grad = lax.optimization_barrier((gate, down_grad))
+    down_grad = summed(down_grad)
+    out_part, dnormed_part, dgate, dup = hidden_units(
+        gate, up, cot, early_w, late_w, down_w
+    )
+    dnormed_two, gate_up_grad = middle(dnormed_part, normed_two, dgate, dup, 6)
+    gate_up_grad = summed(gate_up_grad)
+    dresid, gain_two_grad, dmixed, out_grad = turn(
+        dnormed_two, residual, cot_own, small, attn_pack, mixed, 12
+    )
+    dmixed, down_grad = lax.optimization_barrier((dmixed, down_grad))
+    dqkv, block_own, attn_grad, (down_grad,) = unmix(
+        dmixed,
         normed_one,
-        attn_pack,
-        seg_col,
-        seg_row,
-        pairs,
-        cot_own,
-        split(up_weight.T),
-        split(down_weight),
-        heads,
-        4,
-    )
-    mixed = kept[1]
-    up_w, down_w = over_seq(up_w), over_seq(down_w)
-    residual, normed_own = branch(mixed, attn_pack, x, small, 5)
-    normed_two, gate, up = expand(normed_own, gate_w, up_w, 11)
-    out_part, dnormed_part, dgate, dup, hidden = hidden_units(
-        gate, up, cot, gate_w, up_w, down_w
-    )
-    down_grad = nn_dot(hidden, cot).astype(jnp.bfloat16)
-    dnormed_part, down_grad = lax.optimization_barrier((dnormed_part, down_grad))
-    down_grad = summed(down_grad)
-    dnormed_two, gate_grad, up_grad = middle(dnormed_part, normed_two, dgate, dup, 6)
-    gate_grad, up_grad = summed(gate_grad), summed(up_grad)
-    dresid, gain_two_grad, dresid_low = turn(dnormed_two, residual, cot_own, small, 12)
-    out_grad = tn_dot(mixed, dresid_low).astype(jnp.bfloat16)
-    dresid_low, down_grad, out_grad = lax.optimization_barrier((dresid_low, down_grad, out_grad))
-    dqkv, block_own, (down_grad,) = unmix(
-        dresid_low,
-        attn_pack,
+        out_grad,
         out_part,
         residual,
-        seg_col,
-        seg_row,
+        (seg_col, seg_row),
         pairs,
-        kept,
+        (qkv, exact, den, state, sums),
         [down_grad],
         heads,
         8,
     )
-    qkv_grad = tn_dot(dqkv, normed_one).astype(jnp.bfloat16)[:qkv_rows]
-    out_grad = summed(out_grad)
-    dqkv, qkv_grad, gate_grad = lax.optimization_barrier((dqkv, qkv_grad, gate_grad))
-    qkv_grad = summed(qkv_grad)
-    dtokens, block_out, gains = leave(
-        dqkv, attn_pack, x, dresid, block_own, small, gain_two_grad, 9
-    )
-    (gate_grad, up_grad, out_grad, qkv_grad), gain_grads = last(
-        [gate_grad, up_grad, out_grad, qkv_grad], gains, 10
-    )
+    attn_grad = summed(attn_grad)
+    dtokens, block_out, gains, gate_up_grad = leave(
+        dqkv, attn_pack, x, dresid, block_own, small, gain_two_grad, [gate_up_grad], 9
+    )
+    (attn_grad,), gain_grads = last([attn_grad], gains, 10)
 
     def stacked(a, start, size):
         return a[:, start : start + size].reshape(plane * size, chunk).astype(jnp.float32)
@@ -1940,12 +2155,12 @@
         dtokens.reshape(rows, length, width),
         gain_grads[0],
         gain_grads[1],
-        stacked(qkv_grad, vcols, qcols).T,
-        stacked(qkv_grad, vcols + qcols, qcols).T,
-        stacked(qkv_grad, 0, vcols).T,
-        stacked(out_grad, 0, vcols),
-        stacked(gate_grad, 0, h).T,
-        stacked(up_grad, 0, h).T,
+        stacked(attn_grad, vcols, qcols).T,
+        stacked(attn_grad, vcols + qcols, qcols).T,
+        stacked(attn_grad, 0, vcols).T,
+        stacked(attn_grad, qkv_rows, vcols),
+        stacked(gate_up_grad, 0, h).T,
+        stacked(gate_up_grad, h, h).T,
         stacked(down_grad, 0, h),
     )
 
@@ -1958,6 +2173,7 @@
         and cores == 2
         and heads % plane == 0
         and (gate_weight.shape[1] // cores) % (16 * plane) == 0
+        and gate_weight.shape[1] // cores // plane > EARLY
         and tokens.shape[0] % CHUNKS == 0
     )
 

time: 633 us -> 597 us (0.943)
  waiting for transfers between devices: 34.1 us -> 2.73 us
  matrix products: 24.7 us -> 10.4 us
  Pallas kernels: 532 us -> 541 us
    all_gather x4, waiting for transfers between devices: 32.8 us -> 2.06 us  [over_seq(): return lax.all_gather(pack, 'seq', axis=0, tiled=False)]
    pallas_call x9 -> x11, Pallas kernels: 467 us -> 491 us  [kernel_call(): pl.pallas_call(body, name=name, out_shape=[jax.ShapeDtypeStruct(s, d) for...]
    pallas_call x1 -> x0, Pallas kernels: 16.6 us -> none  [first_exchange(): pl.pallas_call(first_kernel, name='first_exchange', out_shape=[jax.ShapeD...]
    dot_general x2 -> x0, matrix products: 14.3 us -> none  [tn_dot(): lax.dot_general(a, b, (((0,), (0,)), ((), ())), preferred_element_type=jn...]
  transfers between devices with their start and end apart: 9 -> 7, of which waited for: 2 -> 2; matrix products, arithmetic and copies ran while one was open for 3% -> 3% of each run, Pallas kernels for 72% -> 86%
where the time goes in v6:
time: 597 us
  Pallas kernels  541 us (91%)
  local copies, waits for them, and re-layouts  18.6 us (3%)
  between operations  14.4 us (2%)
  matrix products  10.4 us (2%)
  other arithmetic  8.96 us (2%)
    pallas_call x11, Pallas kernels, kernel_call(): pl.pallas_call(body, name=name, out_shape=[jax.ShapeDtypeStruct(s, d) for...  491 us
    pallas_call x1, Pallas kernels, hidden_units(): pl.pallas_call(hidden_kernel, name='hidden_units', grid=(tokens // block,...  37.9 us
  transfers between devices with their start and end apart: 7, of which 2 were waited for; matrix products, arithmetic and copies ran while one was open for 3% of the time, Pallas kernels for 86%

profile of v6, /device:TPU:0, one launch (start us, length us, event | category | flops | bytes accessed | tf_op | source)
XLA Modules:
  0.0 596.6 jit_solution(2254028991992612773)
XLA Ops:
  7.2 0.0 all-gather.9.cloned.1.call-start
  7.2 0.9 copy.33
  8.2 0.9 copy.34
  9.0 1.1 copy.32
  10.2 1.9 pad_maximum_fusion.1.refs_0_
  12.1 11.6 %exchange.1 = bf16[576,512]{1,0:T(8,128)(2,1)} custom-call(bf16[4,576,128]{2,1,0:T(8,128)(2,1)} %pad_maximum_fusion.1.refs_0_), custom_call_target="tpu_custom_call" | custom-call | bytes 17694720 | tf_op jit(solution)/shard_map/exchange/pallas_call | solution.py:522
  23.7 0.0 all-gather.9.cloned.1.call-update
  23.7 0.0 all-gather.11.cloned.1.call-start
  23.8 0.7 slice.52.refs_0_
  24.6 0.1 pad.7.clone
  24.7 0.7 maximum_maximum_fusion.refs_2_
  25.4 1.1 pad_maximum_fusion.refs_1_
  26.4 24.2 %first_exchange.1 = (bf16[320,512]{1,0:T(8,128)(2,1)}, bf16[1056,512]{1,0:T(8,128)(2,1)}, f32[16,8,128]{2,1,0:T(8,128)}) custom-call(bf16[4,320,128]{2,1,0:T(8,128)(2,1)} %slice.52.refs_0_, bf16[4,1056,128]{2,1,0:T(8,128)(2,1)} %pad_maximum_fusion.refs_1_, f32[8,128]{1,0:T(8,128)} %maximum_maximum_fusion.refs_2_), custom_call_target="tpu_custom_call" | custom-call | bytes 67108864 | tf_op jit(solution)/shard_map/first_exchange/pallas_call | solution.py:617
  50.7 0.0 all-gather.11.cloned.1.call-update
  50.7 0.0 all-gather.13.cloned.1.call-start
  50.7 0.8 slice.41
  51.6 0.6 reduce-window.6
  52.2 0.2 slice_reduce_fusion
  52.4 0.1 broadcast_add_fusion
  52.5 0.6 copy.35
  53.1 0.1 fusion.5
  53.2 1.4 copy.36.col_ref
  54.5 43.5 %entry.1 = (bf16[4,2,256,2048]{3,2,1,0:T(8,128)(2,1)}, bf16[256,2048]{1,0:T(8,128)(2,1)}, bf16[256,2048]{1,0:T(8,128)(2,1)}) custom-call(bf16[2,256,2048]{2,1,0:T(8,128)(2,1)} %tokens_ref.1, bf16[2,256,2048]{2,1,0:T(8,128)(2,1)} %cot_ref.1, f32[16,8,128]{2,1,0:T(8,128)} %get-tuple-element.63.small_ref), custom_call_target="tpu_custom_call" | custom-call | bytes 41943040 | tf_op jit(solution)/shard_map/entry/pallas_call | solution.py:617
  98.0 0.0 all-gather.9.cloned.1.call-done
  98.1 26.7 %states.1 = (bf16[2048,384]{1,0:T(8,128)(2,1)}, bf16[8,2,256,128]{3,2,1,0:T(8,128)(2,1)}, f32[8,8,256]{2,1,0:T(8,128)}, bf16[688,512]{1,0:T(8,128)(2,1)}) custom-call(bf16[2048,2048]{1,0:T(8,128)(2,1)} %bitcast.76, bf16[4,576,512]{2,1,0:T(8,128)(2,1)} %bitcast.72, f32[8,256,1]{2,1,0:T(8,128)} %copy.36.col_ref, f32[8,1,256]{2,1,0:T(1,128)} %bitcast.89, ...), custom_call_target="tpu_custom_call" | custom-call | bytes 83886080 | tf_op jit(solution)/shard_map/states/pallas_call | solution.py:617
  124.8 0.0 all-gather.13.cloned.1.call-update
  124.9 0.0 all-gather.15.cloned.1.call-start
  124.9 0.5 all-gather.15.cloned.1.call-update
  125.4 0.0 reduce-scatter.4.cloned.1.call-start
  125.5 43.7 %mix.1 = (bf16[2048,256]{1,0:T(8,128)(2,1)}, f32[2048,256]{1,0:T(8,128)}, f32[2048,128]{1,0:T(8,128)}, bf16[4,2,256,2048]{3,2,1,0:T(8,128)(2,1)}) custom-call(bf16[2048,384]{1,0:T(8,128)(2,1)} %get-tuple-element.65.qkv_ref, f32[8,256,1]{2,1,0:T(8,128)} %copy.36.col_ref, f32[8,1,256]{2,1,0:T(1,128)} %bitcast.90, s32[8,256]{1,0:T(8,128)} %constant.19.clone.pairs_ref, ...), custom_call_target="tpu_custom_call" | custom-call | bytes 41943040 | tf_op jit(solution)/shard_map/mix/pallas_call | solution.py:617
  169.2 48.7 %branch.1 = (f32[256,2048]{1,0:T(8,128)}, bf16[256,2048]{1,0:T(8,128)(2,1)}) custom-call(bf16[2048,256]{1,0:T(8,128)(2,1)} %get-tuple-element.69.mixed_ref, bf16[4,576,512]{2,1,0:T(8,128)(2,1)} %bitcast.73, bf16[256,2048]{1,0:T(8,128)(2,1)} %get-tuple-element.70.x_ref, f32[16,8,128]{2,1,0:T(8,128)} %get-tuple-element.63.small_ref), custom_call_target="tpu_custom_call" | custom-call | bytes 41943040 | tf_op jit(solution)/shard_map/branch/pallas_call | solution.py:617
  217.9 0.0 all-gather.11.cloned.1.call-done
  218.0 0.9 all-gather.13.cloned.1.call-done
  218.9 46.2 %expand.1 = (bf16[4,2,256,2048]{3,2,1,0:T(8,128)(2,1)}, f32[4,2,256,688]{3,2,1,0:T(8,128)}, f32[4,2,256,688]{3,2,1,0:T(8,128)}, bf16[688,2048]{1,0:T(8,128)(2,1)}) custom-call(bf16[256,2048]{1,0:T(8,128)(2,1)} %get-tuple-element.71.own_ref, bf16[4,320,512]{2,1,0:T(8,128)(2,1)} %bitcast.103, bf16[4,1056,512]{2,1,0:T(8,128)(2,1)} %bitcast.100), custom_call_target="tpu_custom_call" | custom-call | flops 11542724608 | bytes 134217728 | tf_op jit(solution)/shard_map/expand/pallas_call | solution.py:617
  265.1 10.4 %convolution_convert_fusion = bf16[688,2048]{1,0:T(8,128)(2,1)} fusion(bf16[688,2048]{1,0:T(8,128)(2,1)} %get-tuple-element.77, bf16[2048,2048]{1,0:T(8,128)(2,1)} %bitcast.98), kind=kOutput, calls=%fused_computation | convolution fusion | flops 5772771328 | bytes 14024704 | tf_op jit(solution)/shard_map/dot_general | solution.py:304
  275.5 0.2 reduce-scatter.6.cloned.1.call-start
  275.7 1.1 all-gather.15.cloned.1.call-done
  276.8 37.9 %hidden_units.1 = (bf16[2048,2048]{1,0:T(8,128)(2,1)}, bf16[2048,2048]{1,0:T(8,128)(2,1)}, bf16[688,2048]{1,0:T(8,128)(2,1)}, bf16[688,2048]{1,0:T(8,128)(2,1)}) custom-call(f32[2048,688]{1,0:T(8,128)} %bitcast.107, f32[2048,688]{1,0:T(8,128)} %bitcast.108, bf16[2048,2048]{1,0:T(8,128)(2,1)} %bitcast.99, bf16[4,320,512]{2,1,0:T(8,128)(2,1)} %bitcast.104, ...), custom_call_target="tpu_custom_call" | custom-call | flops 23085449216 | bytes 134217728 | tf_op jit(solution)/shard_map/hidden_units/pallas_call | solution.py:1330
  314.8 42.1 %middle.1 = (f32[256,2048]{1,0:T(8,128)}, bf16[1376,2048]{1,0:T(8,128)(2,1)}) custom-call(bf16[4,2,256,2048]{3,2,1,0:T(8,128)(2,1)} %bitcast.106, bf16[2048,2048]{1,0:T(8,128)(2,1)} %bitcast.105, bf16[688,2048]{1,0:T(8,128)(2,1)} %get-tuple-element.84.dgate_hbm, bf16[688,2048]{1,0:T(8,128)(2,1)} %get-tuple-element.85.dup_hbm), custom_call_target="tpu_custom_call" | custom-call | flops 11542724608 | bytes 41943040 | tf_op jit(solution)/shard_map/middle/pallas_call | solution.py:617
  356.9 0.0 reduce-scatter.6.cloned.1.call-update
  356.9 0.0 reduce-scatter.8.cloned.1.call-start
  357.0 46.2 %turn.1 = (f32[256,2048]{1,0:T(8,128)}, f32[8,2048]{1,0:T(8,128)}, bf16[4,2,256,256]{3,2,1,0:T(8,128)(2,1)}, bf16[256,2048]{1,0:T(8,128)(2,1)}) custom-call(f32[256,2048]{1,0:T(8,128)} %get-tuple-element.86.total_ref, f32[256,2048]{1,0:T(8,128)} %get-tuple-element.87.residual_ref, bf16[256,2048]{1,0:T(8,128)(2,1)} %get-tuple-element.68.cot_ref, ...), custom_call_target="tpu_custom_call" | custom-call | bytes 41943040 | tf_op jit(solution)/shard_map/turn/pallas_call | solution.py:617
  403.2 0.0 reduce-scatter.4.cloned.1.call-done.refs_0_
  403.2 95.6 %unmix.1 = (bf16[2048,384]{1,0:T(8,128)(2,1)}, bf16[256,2048]{1,0:T(8,128)(2,1)}, bf16[576,2048]{1,0:T(8,128)(2,1)}, bf16[4,688,128]{2,1,0:T(8,128)(2,1)}) custom-call(bf16[2048,256]{1,0:T(8,128)(2,1)} %bitcast.80, bf16[2048,2048]{1,0:T(8,128)(2,1)} %bitcast.77, bf16[256,2048]{1,0:T(8,128)(2,1)} %get-tuple-element.91.output_grad_ref, ...), custom_call_target="tpu_custom_call" | custom-call | bytes 62914560 | tf_op jit(solution)/shard_map/unmix/pallas_call | solution.py:617
  498.8 0.0 reduce-scatter.8.cloned.1.call-update
  498.8 1.1 copy-done.5
  499.9 1.2 bitcast_convert_fusion
  501.1 58.4 %leave.1 = (f32[2,256,2048]{2,1,0:T(8,128)}, bf16[2,256,2048]{2,1,0:T(8,128)(2,1)}, f32[16,8,128]{2,1,0:T(8,128)}, bf16[4,1376,128]{2,1,0:T(8,128)(2,1)}) custom-call(bf16[2048,384]{1,0:T(8,128)(2,1)} %get-tuple-element.96.dqkv_ref, bf16[4,576,512]{2,1,0:T(8,128)(2,1)} %bitcast.75, bf16[256,2048]{1,0:T(8,128)(2,1)} %get-tuple-element.70.x_ref, ...), custom_call_target="tpu_custom_call" | custom-call | bytes 62914560 | tf_op jit(solution)/shard_map/leave/pallas_call | solution.py:617
  559.5 0.0 reduce-scatter.8.cloned.1.call-done.refs_0_
  559.6 16.0 %last.1 = (bf16[4,576,128]{2,1,0:T(8,128)(2,1)}, f32[8,128]{1,0:T(8,128)}) custom-call(bf16[576,512]{1,0:T(8,128)(2,1)} %reduce-scatter.8.cloned.1.call-done.refs_0_, f32[16,8,128]{2,1,0:T(8,128)} %get-tuple-element.104.refs_1_), custom_call_target="tpu_custom_call" | custom-call | bytes 67108864 | tf_op jit(solution)/shard_map/last/pallas_call | solution.py:617
  575.6 0.8 fusion.2
  576.4 1.2 fusion.1
  577.6 1.3 slice_bitcast_fusion
  578.9 0.7 copy.40
  579.6 0.7 copy.39
  580.3 0.8 bitcast_convert_fusion.1
  581.2 0.1 bitcast_convert_fusion.2
  581.2 1.0 copy.41
  582.2 0.1 fusion
  582.3 1.2 convert_bitcast_fusion
  583.6 1.2 convert_bitcast_fusion.1
  584.8 1.3 copy.44
  586.1 1.6 copy-done
  587.7 2.0 copy.45
  (29 shorter events, 0.2 us)
Async XLA Ops:
  7.2 16.6 %copy-start.3 = (bf16[128,2752]{0,1:T(8,128)(2,1)S(1)}, bf16[128,2752]{0,1:T(8,128)(2,1)}, u32[]{:S(2)}) copy-start(bf16[128,2752]{0,1:T(8,128)(2,1)} %param.21) | copy-start | bytes 2113540
  7.2 90.9 %all-gather.9.cloned.1.call-start = ((), (), s32[]{:S(2)}) async-start(), calls=%async_computation.6 | async-start | bytes 2949120 | tf_op jit(solution)/shard_map/all_gather | solution.py:2065
  10.2 14.4 %copy-start.6 = (s32[2,256]{1,0:T(2,128)S(1)}, s32[2,256]{1,0:T(2,128)}, u32[]{:S(2)}) copy-start(s32[2,256]{1,0:T(2,128)} %param.14) | copy-start | bytes 6148
  10.2 14.5 %copy-start.7 = (bf16[128]{0:T(256)(128)(2,1)S(1)}, bf16[128]{0:T(256)(128)(2,1)}, u32[]{:S(2)}) copy-start(bf16[128]{0:T(256)(128)(2,1)} %param.16) | copy-start | bytes 772
  10.2 14.5 %copy-start.8 = (bf16[128]{0:T(256)(128)(2,1)S(1)}, bf16[128]{0:T(256)(128)(2,1)}, u32[]{:S(2)}) copy-start(bf16[128]{0:T(256)(128)(2,1)} %param.15) | copy-start | bytes 772
  10.2 15.2 %copy-start.4 = (bf16[128,2752]{0,1:T(8,128)(2,1)S(1)}, bf16[128,2752]{0,1:T(8,128)(2,1)}, u32[]{:S(2)}) copy-start(bf16[128,2752]{0,1:T(8,128)(2,1)} %param.22) | copy-start | bytes 2113540
  23.7 194.2 %all-gather.11.cloned.1.call-start = ((), (), s32[]{:S(2)}) async-start(), calls=%async_computation.7 | async-start | bytes 1638400 | tf_op jit(solution)/shard_map/all_gather | solution.py:2065
  50.7 168.2 %all-gather.13.cloned.1.call-start = ((), (), s32[]{:S(2)}) async-start(), calls=%async_computation.8 | async-start | bytes 5406720 | tf_op jit(solution)/shard_map/all_gather | solution.py:2065
  124.9 152.0 %all-gather.15.cloned.1.call-start = ((), (), s32[]{:S(2)}) async-start(), calls=%async_computation.9 | async-start | bytes 3522560 | tf_op jit(solution)/shard_map/all_gather | solution.py:2065
  125.4 277.8 %reduce-scatter.4.cloned.1.call-start = ((), (), s32[]{:S(2)}) async-start(), calls=%async_computation.3 | async-start | bytes 3522560 | tf_op jit(solution)/shard_map/reduce_scatter | solution.py:2068
  275.5 225.6 %reduce-scatter.6.cloned.1.call-start = ((), (), s32[]{:S(2)}) async-start(), calls=%async_computation.4 | async-start | bytes 7045120 | tf_op jit(solution)/shard_map/reduce_scatter | solution.py:2068
  356.9 202.7 %reduce-scatter.8.cloned.1.call-start = ((), (), s32[]{:S(2)}) async-start(), calls=%async_computation.5 | async-start | bytes 2949120 | tf_op jit(solution)/shard_map/reduce_scatter | solution.py:2068
  498.8 1.1 copy-start.5
  576.4 5.8 copy-start.2
  582.3 2.5 copy-start.1
  584.8 2.9 copy-start
Sparse Core Ops, SparseCore 0:
  23.9 51.5 all-gather.8
  77.1 31.5 all-gather.10
  125.0 93.8 all-gather.12
  220.3 56.5 all-gather.14
  279.0 61.3 reduce-scatter.3
  357.0 122.1 reduce-scatter.5
  499.0 46.1 reduce-scatter.7

commit v7 on v6

--- a/solution.py
+++ b/solution.py
@@ -425,7 +425,7 @@
         c.wait_send()
 
 
-def scatter_steps(part_ref, out_ref, pair_ref, sum_ref, got_ref, copy, held=None):
+def scatter_steps(part_ref, out_ref, pair_ref, sum_ref, got_ref, copy, held=None, start=True):
     at, x_at, y_at, d_at, core = plane_places()
     half = part_ref.shape[2] // 2
     xp, yp, sp = {"dp": x_at}, {"dp": y_at}, {"tensor": 1 - core}
@@ -446,9 +446,9 @@
 
     d_lo, d_hi = sent(0, lo, xp), sent(0, hi, yp)
     x_lo, y_hi, x_hi, y_lo = sent(1, lo, xp), sent(2, hi, yp), sent(1, hi, xp), sent(2, lo, yp)
-    for c in pairs + fetched:
+    for c in (pairs if start else []) + fetched:
         c.start()
-    yield
+    yield pairs
 
     def ready(j):
         if fetched:
@@ -463,9 +463,11 @@
     d_lo.start()
     total(0, hi)
     d_hi.start()
+    yield
     ready(1)
     total(1, lo)
     x_lo.start()
+    yield
     ready(2)
     total(2, hi)
     y_hi.start()
@@ -585,6 +587,11 @@
     )
 
 
+def advance(steps, count=1):
+    for _ in range(count):
+        next(steps)
+
+
 def run(*steps):
     for g in steps:
         for _ in g:
@@ -678,8 +685,8 @@
 
 FEATURES = 256
 STATE_ROWS = 160
-CHUNKS = 4
-EARLY = 320
+CHUNKS = 8
+EARLY = 272
 
 
 def feature_pairs():
@@ -1272,81 +1279,200 @@
         flops=32 * m * width * units,
         moved=1 << 27,
     )
-    flat = (8 * m, units)
-    return normed.reshape(8 * m, width), gate.reshape(flat), up.reshape(flat), hidden
+    return normed.reshape(8 * m, width), gate, up, hidden
 
 
 def hidden_kernel(
+    gate_hbm,
+    up_hbm,
+    cot_hbm,
+    early_hbm,
+    late_hbm,
+    down_hbm,
+    normed_hbm,
+    out_hbm,
+    total_ref,
+    grads_hbm,
     gate_ref,
     up_ref,
     cot_ref,
-    early_hbm,
-    late_hbm,
-    down_hbm,
     out_ref,
-    dnormed_ref,
-    dgate_ref,
-    dup_ref,
     w_ref,
     down_w_ref,
+    part_ref,
+    pair_ref,
+    sum_ref,
+    got_ref,
+    turned_ref,
+    normed_ref,
+    grad_ref,
+    sems,
     w_sems,
+    load_sems,
+    store_sems,
+    normed_sem,
+    grad_sems,
 ):
+    greet_plane()
+    at, x_at, y_at, d_at, core = plane_places()
     parts, units, depth = down_w_ref.shape
-
-    @pl.when(pl.program_id(0) == 0)
-    def _():
-        weights = stacked_copies(early_hbm, late_hbm, w_ref, w_sems)
-        weights.append(pltpu.make_async_copy(down_hbm, down_w_ref, w_sems.at[2]))
-        for c in weights:
-            c.start()
-        for c in weights:
+    m = cot_ref.shape[1]
+    scatter = scatter_steps(
+        part_ref, total_ref, pair_ref, sum_ref, got_ref, Sender(sems), start=False
+    )
+    pairs = next(scatter)
+    weights = stacked_copies(early_hbm, late_hbm, w_ref, w_sems)
+    weights.append(pltpu.make_async_copy(down_hbm, down_w_ref, w_sems.at[2]))
+    normed_copy = pltpu.make_async_copy(normed_hbm, normed_ref, normed_sem)
+
+    def place(i):
+        chip = choose(i < 2, d_at, choose(i < 4, x_at, choose(i < 6, y_at, at)))
+        return chip, choose(parity(i) == 0, 1 - core, core)
+
+    def loads(i):
+        slot, (c, k) = parity(i), place(i)
+        return [
+            pltpu.make_async_copy(a.at[c, k], b.at[slot], load_sems.at[slot, n])
+            for n, (a, b) in enumerate(
+                ((gate_hbm, gate_ref), (up_hbm, up_ref), (cot_hbm, cot_ref))
+            )
+        ]
+
+    def store(i):
+        slot, (c, k) = parity(i), place(i)
+        return pltpu.make_async_copy(out_ref.at[slot], out_hbm.at[c, k], store_sems.at[slot])
+
+    for c in weights + loads(0):
+        c.start()
+    normed_copy.start()
+    for c in weights:
+        c.wait()
+
+    def body(i, carry):
+        for step in (2, 4, 6):
+
+            @pl.when(i == step)
+            def _():
+                next(scatter)
+
+        @pl.when(i < 7)
+        def _():
+            for c in loads(i + 1):
+                c.start()
+
+        for c in loads(i):
             c.wait()
 
-    gate, up = gate_ref[...], up_ref[...]
-    dhidden = project(lambda cols: cot_ref[:, cols], down_w_ref, pl.ds(0, units))
-    sig = jax.nn.sigmoid(gate)
-    silu = gate * sig
-    hidden = (silu * up).astype(jnp.bfloat16)
-    dgate = (dhidden * up * sig * (1.0 + gate * (1.0 - sig))).astype(jnp.bfloat16)
-    dup = (dhidden * silu).astype(jnp.bfloat16)
-    for s in range(parts):
-        cols = pl.ds(s * depth, depth)
-        dnormed_ref[:, cols] = (
-            nn_dot(dgate, w_ref[s, pl.ds(0, units)]) + nn_dot(dup, w_ref[s, pl.ds(units, units)])
-        ).astype(jnp.bfloat16)
-        out_ref[:, cols] = nn_dot(hidden, down_w_ref[s]).astype(jnp.bfloat16)
-    dgate_ref[...], dup_ref[...] = dgate.T, dup.T
-
-
-def hidden_units(gate, up, cot, early, late, down_w, block=256):
-    tokens, units = gate.shape
-    width = cot.shape[1]
+        @pl.when(i >= 2)
+        def _():
+            store(i - 2).wait()
+
+        slot, (chip, k) = parity(i), place(i)
+        gate, up = gate_ref[slot], up_ref[slot]
+        dhidden = project(lambda cols: cot_ref[slot, :, cols], down_w_ref, pl.ds(0, units))
+        sig = jax.nn.sigmoid(gate)
+        silu = gate * sig
+        hidden = (silu * up).astype(jnp.bfloat16)
+        dgate = (dhidden * up * sig * (1.0 + gate * (1.0 - sig))).astype(jnp.bfloat16)
+        dup = (dhidden * silu).astype(jnp.bfloat16)
+        for s in range(parts):
+            cols = pl.ds(s * depth, depth)
+            part_ref[chip, k, :, cols] = (
+                nn_dot(dgate, w_ref[s, pl.ds(0, units)])
+                + nn_dot(dup, w_ref[s, pl.ds(units, units)])
+            ).astype(jnp.bfloat16)
+            out_ref[slot, :, cols] = nn_dot(hidden, down_w_ref[s]).astype(jnp.bfloat16)
+        store(i).start()
+        for j in range(4):
+
+            @pl.when(i == 2 * j)
+            def _():
+                pairs[j].start()
+
+        column = pl.ds(pl.multiple_of((chip * 2 + k) * m, m), m)
+        turned_ref[0, :, column], turned_ref[1, :, column] = dgate.T, dup.T
+        return carry
+
+    lax.fori_loop(0, 8, body, 0)
+    next(scatter)
+    store(6).wait()
+    store(7).wait()
+    normed_copy.wait()
+    width = grad_ref.shape[2]
+    blocks = normed_ref.shape[1] // width
+
+    def gradients(which):
+        rows = pl.ds(which * units, units)
+
+        def stored(i):
+            column = pl.ds(pl.multiple_of(i * width, width), width)
+            slot = parity(i)
+            return pltpu.make_async_copy(
+                grad_ref.at[slot], grads_hbm.at[rows, column], grad_sems.at[slot]
+            )
+
+        def body(i, carry):
+            column = pl.ds(pl.multiple_of(i * width, width), width)
+
+            @pl.when(i >= 2)
+            def _():
+                stored(i - 2).wait()
+
+            grad_ref[parity(i)] = nn_dot(turned_ref[which], normed_ref[:, column]).astype(
+                jnp.bfloat16
+            )
+            stored(i).start()
+            return carry
+
+        lax.fori_loop(0, blocks, body, 0)
+        for i in (blocks - 2, blocks - 1):
+            stored(i).wait()
+
+    gradients(0)
+    gradients(1)
+    run(scatter)
+
+
+def hidden_units(gate, up, cot, early, late, down_w, normed, cid):
+    _, _, m, units = gate.shape
+    tokens, width = normed.shape
     low = jnp.bfloat16
-    wide = pl.BlockSpec((block, width), lambda i: (i, 0))
-    thin = pl.BlockSpec((block, units), lambda i: (i, 0))
-    turned = pl.BlockSpec((units, block), lambda i: (0, i))
-    anywhere = pl.BlockSpec(memory_space=pl.ANY)
     stacked = (early.shape[0], early.shape[1] + late.shape[1], early.shape[2])
-    return pl.pallas_call(
+    ins = (gate, up, cot.reshape(4, 2, m, width), early, late, down_w, normed)
+    return kernel_call(
         hidden_kernel,
-        name="hidden_units",
-        grid=(tokens // block,),
-        out_shape=[jax.ShapeDtypeStruct((tokens, width), low)] * 2
-        + [jax.ShapeDtypeStruct((units, tokens), low)] * 2,
-        in_specs=[thin, thin, wide, anywhere, anywhere, anywhere],
-        out_specs=[wide, wide, turned, turned],
-        scratch_shapes=[
+        "hidden_units",
+        cid,
+        [
+            ((4, 2, m, width), low, pl.ANY),
+            ((m, width), jnp.float32, pltpu.VMEM),
+            ((2 * units, width), low, pl.ANY),
+        ],
+        [(a, pl.ANY) for a in ins],
+        [
+            pltpu.VMEM((2, m, units), jnp.float32),
+            pltpu.VMEM((2, m, units), jnp.float32),
+            pltpu.VMEM((2, m, width), low),
+            pltpu.VMEM((2, m, width), low),
             pltpu.VMEM(stacked, low),
             pltpu.VMEM(down_w.shape, low),
+            pltpu.VMEM((4, 2, m, width), low),
+        ]
+        + scatter_scratch(m, width)
+        + [
+            pltpu.VMEM((2, units, tokens), low),
+            pltpu.VMEM((tokens, width), low),
+            pltpu.VMEM((2, units, 2 * LANES), low),
+            copies(SCATTER_COPIES),
             pltpu.SemaphoreType.DMA((3,)),
+            pltpu.SemaphoreType.DMA((2, 3)),
+            pltpu.SemaphoreType.DMA((2,)),
+            pltpu.SemaphoreType.DMA,
+            pltpu.SemaphoreType.DMA((2,)),
         ],
-        compiler_params=pltpu.CompilerParams(vmem_limit_bytes=VMEM_LIMIT),
-        cost_estimate=pl.CostEstimate(
-            flops=8 * tokens * width * units,
-            bytes_accessed=1 << 27,
-            transcendentals=tokens * units,
-        ),
-    )(gate, up, cot, early, late, down_w)
+        flops=12 * tokens * width * units,
+        moved=1 << 27,
+    )
 
 
 def norm_gradient(r, value_at, grad_ref, gain_at, gain_grad, finish, width):
@@ -1364,112 +1490,6 @@
             (g * v * scale).reshape(ROW_STEP // 8, 8, LANES), axis=0
         )
         finish(r, k, scale * g * gain_at(k) - v * pull)
-
-
-def middle_kernel(
-    part_hbm,
-    normed_hbm,
-    dgate_hbm,
-    dup_hbm,
-    total_ref,
-    grads_hbm,
-    held_ref,
-    pair_ref,
-    sum_ref,
-    got_ref,
-    normed_ref,
-    left_ref,
-    grad_ref,
-    sems,
-    held_sems,
-    load_sems,
-    store_sems,
-):
-    greet_plane()
-    scatter = scatter_steps(
-        part_hbm, total_ref, pair_ref, sum_ref, got_ref, Sender(sems), (held_ref, held_sems)
-    )
-    next(scatter)
-    loads = [
-        pltpu.make_async_copy(a, b, load_sems.at[n])
-        for n, (a, b) in enumerate(
-            (
-                (dgate_hbm, left_ref.at[0]),
-                (normed_hbm, normed_ref),
-                (dup_hbm, left_ref.at[1]),
-            )
-        )
-    ]
-    for c in loads:
-        c.start()
-    next(scatter)
-    width = grad_ref.shape[2]
-    blocks = normed_ref.shape[1] // width
-
-    def gradients(which):
-        rows = pl.ds(which * grad_ref.shape[1], grad_ref.shape[1])
-
-        def stored(i):
-            column = pl.ds(pl.multiple_of(i * width, width), width)
-            slot = parity(i)
-            return pltpu.make_async_copy(
-                grad_ref.at[slot], grads_hbm.at[rows, column], store_sems.at[slot]
-            )
-
-        def body(i, carry):
-            column = pl.ds(pl.multiple_of(i * width, width), width)
-
-            @pl.when(i >= 2)
-            def _():
-                stored(i - 2).wait()
-
-            grad_ref[lax.rem(i, 2)] = nn_dot(left_ref[which], normed_ref[:, column]).astype(
-                jnp.bfloat16
-            )
-            stored(i).start()
-            return carry
-
-        lax.fori_loop(0, blocks, body, 0)
-        for i in (blocks - 2, blocks - 1):
-            stored(i).wait()
-
-    loads[0].wait()
-    loads[1].wait()
-    gradients(0)
-    next(scatter)
-    loads[2].wait()
-    gradients(1)
-    run(scatter)
-
-
-def middle(part, normed, dgate, dup, cid):
-    m, width = part.shape[0] // 8, part.shape[1]
-    part = part.reshape(4, 2, m, width)
-    units, tokens = dgate.shape
-    low = jnp.bfloat16
-    return kernel_call(
-        middle_kernel,
-        "middle",
-        cid,
-        [
-            ((m, width), jnp.float32, pltpu.VMEM),
-            ((2 * units, width), low, pl.ANY),
-        ],
-        [(a, pl.ANY) for a in (part, normed, dgate, dup)],
-        [pltpu.VMEM((4, m, width), low)]
-        + scatter_scratch(m, width)
-        + [
-            pltpu.VMEM((tokens, width), low),
-            pltpu.VMEM((2, units, tokens), low),
-            pltpu.VMEM((2, units, 256), low),
-            copies(SCATTER_COPIES),
-            pltpu.SemaphoreType.DMA((4,)),
-            pltpu.SemaphoreType.DMA((3,)),
-            pltpu.SemaphoreType.DMA((2,)),
-        ],
-        flops=4 * units * tokens * width,
-        moved=m * width * 80,
-    )
 
 
 def turn_kernel(
@@ -1740,11 +1760,17 @@
         def _():
             lax.fori_loop(n * each, (n + 1) * each, here, 0)
 
-    def advance():
-        next(scatter)
-
-    chain.run(work, [lambda: None, advance, lambda: None, lambda: None, advance])
-    lax.fori_loop(0, rows, after, 0)
+        done = n - chain.distance
+
+        @pl.when((done >= 0) & (done < CHUNKS))
+        def _():
+            lax.fori_loop(done * each, (done + 1) * each, after, 0)
+
+    nothing = lambda: None
+    chain.run(
+        work,
+        [nothing] * 2 + [lambda: advance(scatter, 3)] + [nothing] * 3 + [lambda: advance(scatter)],
+    )
     run(scatter)
 
     def finish(r, carry):
@@ -1792,7 +1818,7 @@
             (dmixed, whole),
             (normed, pl.ANY),
             (output_grad, whole),
-            (part.reshape(4, 2, m, width), pl.ANY),
+            (part, pl.ANY),
             (residual, whole),
             (seg_col, whole),
             (seg_row, whole),
@@ -1970,8 +1996,7 @@
     local = [pltpu.make_async_copy(low_ref, out_ref.at[core], local_sems.at[0])]
     to_pair[0].start()
     local[0].start()
-    next(scatter)
-    next(scatter)
+    advance(scatter, 4)
     shards += swap(1)
     run(scatter)
     gain_ref[...] = jnp.zeros_like(gain_ref)
@@ -2118,10 +2143,9 @@
     down_grad = nn_dot(hidden, cot).astype(jnp.bfloat16)
     gate, down_grad = lax.optimization_barrier((gate, down_grad))
     down_grad = summed(down_grad)
-    out_part, dnormed_part, dgate, dup = hidden_units(
-        gate, up, cot, early_w, late_w, down_w
-    )
-    dnormed_two, gate_up_grad = middle(dnormed_part, normed_two, dgate, dup, 6)
+    out_part, dnormed_two, gate_up_grad = hidden_units(
+        gate, up, cot, early_w, late_w, down_w, normed_two, 6
+    )
     gate_up_grad = summed(gate_up_grad)
     dresid, gain_two_grad, dmixed, out_grad = turn(
         dnormed_two, residual, cot_own, small, attn_pack, mixed, 12

time: 597 us -> 561 us (0.940)
  Pallas kernels: 541 us -> 504 us
    pallas_call x1 -> x0, Pallas kernels: 37.9 us -> none  [hidden_units(): pl.pallas_call(hidden_kernel, name='hidden_units', grid=(tokens // block,...]
  transfers between devices with their start and end apart: 7 -> 7, of which waited for: 2 -> 2; matrix products, arithmetic and copies ran while one was open for 3% -> 3% of each run, Pallas kernels for 86% -> 85%
where the time goes in v7:
time: 561 us; the launch traced here: 560 us
  Pallas kernels  504 us (90%)
  local copies, waits for them, and re-layouts  18.6 us (3%)
  between operations  14.4 us (3%)
  matrix products  10.3 us (2%)
  other arithmetic  8.98 us (2%)
    pallas_call x11, Pallas kernels, kernel_call(): pl.pallas_call(body, name=name, out_shape=[jax.ShapeDtypeStruct(s, d) for...  492 us
    pallas_call x1, Pallas kernels, exchange(): pl.pallas_call(partial(exchange_kernel, take, put, count), name='exchange...  11.6 us
  transfers between devices with their start and end apart: 7, of which 2 were waited for; matrix products, arithmetic and copies ran while one was open for 3% of the time, Pallas kernels for 85%

profile of v7, /device:TPU:0, one launch (start us, length us, event | category | flops | bytes accessed | tf_op | source)
XLA Modules:
  0.0 560.3 jit_solution(12592316099443149358)
XLA Ops:
  7.2 0.0 all-gather.9.cloned.1.call-start
  7.2 0.9 copy.33
  8.2 0.9 copy.34
  9.0 1.1 copy.32
  10.2 1.9 pad_maximum_fusion.1.refs_0_
  12.1 11.6 %exchange.1 = bf16[576,512]{1,0:T(8,128)(2,1)} custom-call(bf16[4,576,128]{2,1,0:T(8,128)(2,1)} %pad_maximum_fusion.1.refs_0_), custom_call_target="tpu_custom_call" | custom-call | bytes 17694720 | tf_op jit(solution)/shard_map/exchange/pallas_call | solution.py:524
  23.7 0.0 all-gather.9.cloned.1.call-update
  23.7 0.0 all-gather.11.cloned.1.call-start
  23.8 0.7 slice.52.refs_0_
  24.6 0.1 pad.7.clone
  24.7 0.7 maximum_maximum_fusion.refs_2_
  25.3 1.1 pad_maximum_fusion.refs_1_
  26.4 24.2 %first_exchange.1 = (bf16[272,512]{1,0:T(8,128)(2,1)}, bf16[1104,512]{1,0:T(8,128)(2,1)}, f32[16,8,128]{2,1,0:T(8,128)}) custom-call(bf16[4,272,128]{2,1,0:T(8,128)(2,1)} %slice.52.refs_0_, bf16[4,1104,128]{2,1,0:T(8,128)(2,1)} %pad_maximum_fusion.refs_1_, f32[8,128]{1,0:T(8,128)} %maximum_maximum_fusion.refs_2_), custom_call_target="tpu_custom_call" | custom-call | bytes 67108864 | tf_op jit(solution)/shard_map/first_exchange/pallas_call | solution.py:624
  50.6 0.0 all-gather.11.cloned.1.call-update
  50.6 0.0 all-gather.13.cloned.1.call-start
  50.7 0.8 slice.41
  51.6 0.6 reduce-window.6
  52.1 0.2 slice_reduce_fusion
  52.4 0.1 broadcast_add_fusion
  52.4 0.6 copy.35
  53.0 0.1 fusion.5
  53.1 1.4 copy.36.col_ref
  54.5 43.5 %entry.1 = (bf16[4,2,256,2048]{3,2,1,0:T(8,128)(2,1)}, bf16[256,2048]{1,0:T(8,128)(2,1)}, bf16[256,2048]{1,0:T(8,128)(2,1)}) custom-call(bf16[2,256,2048]{2,1,0:T(8,128)(2,1)} %tokens_ref.1, bf16[2,256,2048]{2,1,0:T(8,128)(2,1)} %cot_ref.1, f32[16,8,128]{2,1,0:T(8,128)} %get-tuple-element.60.small_ref), custom_call_target="tpu_custom_call" | custom-call | bytes 41943040 | tf_op jit(solution)/shard_map/entry/pallas_call | solution.py:624
  97.9 0.0 all-gather.9.cloned.1.call-done
  98.0 25.4 %states.1 = (bf16[2048,384]{1,0:T(8,128)(2,1)}, bf16[8,2,256,128]{3,2,1,0:T(8,128)(2,1)}, f32[8,8,256]{2,1,0:T(8,128)}, bf16[688,512]{1,0:T(8,128)(2,1)}) custom-call(bf16[2048,2048]{1,0:T(8,128)(2,1)} %bitcast.72, bf16[4,576,512]{2,1,0:T(8,128)(2,1)} %bitcast.68, f32[8,256,1]{2,1,0:T(8,128)} %copy.36.col_ref, f32[8,1,256]{2,1,0:T(1,128)} %bitcast.84, ...), custom_call_target="tpu_custom_call" | custom-call | bytes 83886080 | tf_op jit(solution)/shard_map/states/pallas_call | solution.py:624
  123.4 0.0 all-gather.13.cloned.1.call-update
  123.4 0.0 all-gather.15.cloned.1.call-start
  123.5 0.5 all-gather.15.cloned.1.call-update
  124.0 0.0 reduce-scatter.4.cloned.1.call-start
  124.1 43.8 %mix.1 = (bf16[2048,256]{1,0:T(8,128)(2,1)}, f32[2048,256]{1,0:T(8,128)}, f32[2048,128]{1,0:T(8,128)}, bf16[4,2,256,2048]{3,2,1,0:T(8,128)(2,1)}) custom-call(bf16[2048,384]{1,0:T(8,128)(2,1)} %get-tuple-element.62.qkv_ref, f32[8,256,1]{2,1,0:T(8,128)} %copy.36.col_ref, f32[8,1,256]{2,1,0:T(1,128)} %bitcast.85, s32[8,256]{1,0:T(8,128)} %constant.19.clone.pairs_ref, ...), custom_call_target="tpu_custom_call" | custom-call | bytes 41943040 | tf_op jit(solution)/shard_map/mix/pallas_call | solution.py:624
  167.8 48.6 %branch.1 = (f32[256,2048]{1,0:T(8,128)}, bf16[256,2048]{1,0:T(8,128)(2,1)}) custom-call(bf16[2048,256]{1,0:T(8,128)(2,1)} %get-tuple-element.66.mixed_ref, bf16[4,576,512]{2,1,0:T(8,128)(2,1)} %bitcast.69, bf16[256,2048]{1,0:T(8,128)(2,1)} %get-tuple-element.67.x_ref, f32[16,8,128]{2,1,0:T(8,128)} %get-tuple-element.60.small_ref), custom_call_target="tpu_custom_call" | custom-call | bytes 41943040 | tf_op jit(solution)/shard_map/branch/pallas_call | solution.py:624
  216.4 0.0 all-gather.11.cloned.1.call-done
  216.4 1.7 all-gather.13.cloned.1.call-done
  218.2 46.4 %expand.1 = (bf16[4,2,256,2048]{3,2,1,0:T(8,128)(2,1)}, f32[4,2,256,688]{3,2,1,0:T(8,128)}, f32[4,2,256,688]{3,2,1,0:T(8,128)}, bf16[688,2048]{1,0:T(8,128)(2,1)}) custom-call(bf16[256,2048]{1,0:T(8,128)(2,1)} %get-tuple-element.68.own_ref, bf16[4,272,512]{2,1,0:T(8,128)(2,1)} %bitcast.97, bf16[4,1104,512]{2,1,0:T(8,128)(2,1)} %bitcast.94), custom_call_target="tpu_custom_call" | custom-call | flops 11542724608 | bytes 134217728 | tf_op jit(solution)/shard_map/expand/pallas_call | solution.py:624
  264.5 10.3 %convolution_convert_fusion = bf16[688,2048]{1,0:T(8,128)(2,1)} fusion(bf16[688,2048]{1,0:T(8,128)(2,1)} %get-tuple-element.74, bf16[2048,2048]{1,0:T(8,128)(2,1)} %bitcast.93), kind=kOutput, calls=%fused_computation | convolution fusion | flops 5772771328 | bytes 14024704 | tf_op jit(solution)/shard_map/dot_general | solution.py:304
  274.9 0.0 reduce-scatter.4.cloned.1.call-update
  274.9 0.2 reduce-scatter.6.cloned.1.call-start
  275.1 1.1 all-gather.15.cloned.1.call-done
  276.2 57.7 %hidden_units.1 = (bf16[4,2,256,2048]{3,2,1,0:T(8,128)(2,1)}, f32[256,2048]{1,0:T(8,128)}, bf16[1376,2048]{1,0:T(8,128)(2,1)}) custom-call(f32[4,2,256,688]{3,2,1,0:T(8,128)} %get-tuple-element.76.gate_hbm, f32[4,2,256,688]{3,2,1,0:T(8,128)} %get-tuple-element.77.up_hbm, bf16[4,2,256,2048]{3,2,1,0:T(8,128)(2,1)} %get-tuple-element.75.cot_hbm, ...), custom_call_target="tpu_custom_call" | custom-call | flops 34628173824 | bytes 134217728 | tf_op jit(solution)/shard_map/hidden_units/pallas_call | solution.py:624
  333.9 0.0 reduce-scatter.6.cloned.1.call-update
  333.9 0.0 reduce-scatter.8.cloned.1.call-start
  334.0 46.2 %turn.1 = (f32[256,2048]{1,0:T(8,128)}, f32[8,2048]{1,0:T(8,128)}, bf16[4,2,256,256]{3,2,1,0:T(8,128)(2,1)}, bf16[256,2048]{1,0:T(8,128)(2,1)}) custom-call(f32[256,2048]{1,0:T(8,128)} %get-tuple-element.80.total_ref, f32[256,2048]{1,0:T(8,128)} %get-tuple-element.81.residual_ref, bf16[256,2048]{1,0:T(8,128)(2,1)} %get-tuple-element.65.cot_ref, ...), custom_call_target="tpu_custom_call" | custom-call | bytes 41943040 | tf_op jit(solution)/shard_map/turn/pallas_call | solution.py:624
  380.2 0.0 reduce-scatter.4.cloned.1.call-done.refs_0_
  380.2 83.8 %unmix.1 = (bf16[2048,384]{1,0:T(8,128)(2,1)}, bf16[256,2048]{1,0:T(8,128)(2,1)}, bf16[576,2048]{1,0:T(8,128)(2,1)}, bf16[4,688,128]{2,1,0:T(8,128)(2,1)}) custom-call(bf16[2048,256]{1,0:T(8,128)(2,1)} %bitcast.75, bf16[2048,2048]{1,0:T(8,128)(2,1)} %bitcast.73, bf16[256,2048]{1,0:T(8,128)(2,1)} %get-tuple-element.85.output_grad_ref, ...), custom_call_target="tpu_custom_call" | custom-call | bytes 62914560 | tf_op jit(solution)/shard_map/unmix/pallas_call | solution.py:624
  464.0 0.0 reduce-scatter.8.cloned.1.call-update
  464.0 1.1 copy-done.5
  465.1 1.2 bitcast_convert_fusion
  466.3 59.6 %leave.1 = (f32[2,256,2048]{2,1,0:T(8,128)}, bf16[2,256,2048]{2,1,0:T(8,128)(2,1)}, f32[16,8,128]{2,1,0:T(8,128)}, bf16[4,1376,128]{2,1,0:T(8,128)(2,1)}) custom-call(bf16[2048,384]{1,0:T(8,128)(2,1)} %get-tuple-element.90.dqkv_ref, bf16[4,576,512]{2,1,0:T(8,128)(2,1)} %bitcast.71, bf16[256,2048]{1,0:T(8,128)(2,1)} %get-tuple-element.67.x_ref, ...), custom_call_target="tpu_custom_call" | custom-call | bytes 62914560 | tf_op jit(solution)/shard_map/leave/pallas_call | solution.py:624
  525.9 0.0 reduce-scatter.8.cloned.1.call-done.refs_0_
  526.0 13.4 %last.1 = (bf16[4,576,128]{2,1,0:T(8,128)(2,1)}, f32[8,128]{1,0:T(8,128)}) custom-call(bf16[576,512]{1,0:T(8,128)(2,1)} %reduce-scatter.8.cloned.1.call-done.refs_0_, f32[16,8,128]{2,1,0:T(8,128)} %get-tuple-element.98.refs_1_), custom_call_target="tpu_custom_call" | custom-call | bytes 67108864 | tf_op jit(solution)/shard_map/last/pallas_call | solution.py:624
  539.3 0.8 fusion.2
  540.1 1.2 fusion.1
  541.3 1.3 slice_bitcast_fusion
  542.6 0.7 copy.40
  543.3 0.7 copy.39
  544.1 0.8 bitcast_convert_fusion.1
  544.9 0.1 bitcast_convert_fusion.2
  545.0 1.0 copy.41
  546.0 0.1 fusion
  546.1 1.2 convert_bitcast_fusion
  547.3 1.2 convert_bitcast_fusion.1
  548.5 1.3 copy.44
  549.8 1.6 copy-done
  551.5 2.0 copy.45
  (28 shorter events, 0.2 us)
Async XLA Ops:
  7.2 16.6 %copy-start.4 = (bf16[128,2752]{0,1:T(8,128)(2,1)S(1)}, bf16[128,2752]{0,1:T(8,128)(2,1)}, u32[]{:S(2)}) copy-start(bf16[128,2752]{0,1:T(8,128)(2,1)} %param.21) | copy-start | bytes 2113540
  7.2 90.8 %all-gather.9.cloned.1.call-start = ((), (), s32[]{:S(2)}) async-start(), calls=%async_computation.6 | async-start | bytes 2949120 | tf_op jit(solution)/shard_map/all_gather | solution.py:2090
  10.2 14.4 %copy-start.6 = (s32[2,256]{1,0:T(2,128)S(1)}, s32[2,256]{1,0:T(2,128)}, u32[]{:S(2)}) copy-start(s32[2,256]{1,0:T(2,128)} %param.14) | copy-start | bytes 6148
  10.2 14.5 %copy-start.7 = (bf16[128]{0:T(256)(128)(2,1)S(1)}, bf16[128]{0:T(256)(128)(2,1)}, u32[]{:S(2)}) copy-start(bf16[128]{0:T(256)(128)(2,1)} %param.16) | copy-start | bytes 772
  10.2 14.5 %copy-start.8 = (bf16[128]{0:T(256)(128)(2,1)S(1)}, bf16[128]{0:T(256)(128)(2,1)}, u32[]{:S(2)}) copy-start(bf16[128]{0:T(256)(128)(2,1)} %param.15) | copy-start | bytes 772
  10.2 15.1 %copy-start.3 = (bf16[128,2752]{0,1:T(8,128)(2,1)S(1)}, bf16[128,2752]{0,1:T(8,128)(2,1)}, u32[]{:S(2)}) copy-start(bf16[128,2752]{0,1:T(8,128)(2,1)} %param.22) | copy-start | bytes 2113540
  23.7 192.7 %all-gather.11.cloned.1.call-start = ((), (), s32[]{:S(2)}) async-start(), calls=%async_computation.7 | async-start | bytes 1392640 | tf_op jit(solution)/shard_map/all_gather | solution.py:2090
  50.6 167.6 %all-gather.13.cloned.1.call-start = ((), (), s32[]{:S(2)}) async-start(), calls=%async_computation.8 | async-start | bytes 5652480 | tf_op jit(solution)/shard_map/all_gather | solution.py:2090
  123.4 152.8 %all-gather.15.cloned.1.call-start = ((), (), s32[]{:S(2)}) async-start(), calls=%async_computation.9 | async-start | bytes 3522560 | tf_op jit(solution)/shard_map/all_gather | solution.py:2090
  124.0 256.2 %reduce-scatter.4.cloned.1.call-start = ((), (), s32[]{:S(2)}) async-start(), calls=%async_computation.3 | async-start | bytes 3522560 | tf_op jit(solution)/shard_map/reduce_scatter | solution.py:2093
  274.9 191.4 %reduce-scatter.6.cloned.1.call-start = ((), (), s32[]{:S(2)}) async-start(), calls=%async_computation.4 | async-start | bytes 7045120 | tf_op jit(solution)/shard_map/reduce_scatter | solution.py:2093
  333.9 192.0 %reduce-scatter.8.cloned.1.call-start = ((), (), s32[]{:S(2)}) async-start(), calls=%async_computation.5 | async-start | bytes 2949120 | tf_op jit(solution)/shard_map/reduce_scatter | solution.py:2093
  464.0 1.1 copy-start.5
  540.1 5.8 %copy-start.2 = (bf16[4,1376,128]{2,1,0:T(8,128)(2,1)S(1)}, bf16[4,1376,128]{2,1,0:T(8,128)(2,1)}, u32[]{:S(2)}) copy-start(bf16[4,1376,128]{2,1,0:T(8,128)(2,1)} %get-tuple-element.101) | copy-start | bytes 4227076
  546.1 2.5 copy-start.1
  548.5 2.9 copy-start
Sparse Core Ops, SparseCore 0:
  23.9 51.5 all-gather.8
  77.1 27.8 all-gather.10
  123.6 94.5 all-gather.12
  219.6 56.5 all-gather.14
  279.0 57.3 reduce-scatter.3
  338.6 114.1 reduce-scatter.5
  464.2 45.1 reduce-scatter.7

commit v8 on v7

--- a/solution.py
+++ b/solution.py
@@ -345,6 +345,26 @@
     greet([{"dp": x_at}, {"dp": y_at}, {"tensor": 1 - core}])
 
 
+def leaving(i):
+    at, x_at, y_at, d_at, core = plane_places()
+    chip = choose(i < 2, d_at, choose(i < 4, x_at, choose(i < 6, y_at, at)))
+    return chip, choose(parity(i) == 0, 1 - core, core)
+
+
+def produce_parts(block, pairs):
+    def body(i, carry):
+        block(*leaving(i))
+        for j, pair in enumerate(pairs):
+
+            @pl.when(i == 2 * j)
+            def _():
+                pair.start()
+
+        return carry
+
+    lax.fori_loop(0, 8, body, 0)
+
+
 def add_rows(dst, *srcs, step=64):
     def body(i, carry):
         r = pl.ds(pl.multiple_of(i * step, step), step)
@@ -538,14 +558,9 @@
     )(*arrays)
 
 
-def first_kernel(count, *refs):
-    ins, small_ref, outs, all_ref = (
-        refs[:count],
-        refs[count],
-        refs[count + 1 : 2 * count + 1],
-        refs[2 * count + 1],
-    )
-    sems, small_sems, local_sems, small_local_sem = refs[2 * count + 2 :]
+def small_kernel(
+    small_ref, pack_ref, all_ref, out_ref, small_sems, small_local_sem, sems, local_sems
+):
     plane, span = lax.axis_size("dp"), lax.axis_size("seq")
     at, z = lax.axis_index("dp"), lax.axis_index("seq")
     places = [
@@ -562,28 +577,32 @@
     for c in started:
         c.start()
     chips = [lax.rem(at + k, plane) for k in range(1, plane)]
-    started += swap_shards(ins, outs, chips, at, block_of, columns_of, Sender(sems), local_sems)
+    started += swap_shards(
+        (pack_ref,), (out_ref,), chips, at, block_of, columns_of, Sender(sems), local_sems
+    )
     for c in started:
         c.wait()
 
 
-def first_exchange(packs, small, cid):
+def small_exchange(small, pack, cid):
     plane, span = lax.axis_size("dp"), lax.axis_size("seq")
-    count = len(packs)
+    _, size, chunk = pack.shape
     return kernel_call(
-        partial(first_kernel, count),
-        "first_exchange",
+        small_kernel,
+        "small_exchange",
         cid,
-        [((p.shape[1], plane * p.shape[2]), p.dtype, pl.ANY) for p in packs]
-        + [((span * plane,) + small.shape, small.dtype, pltpu.VMEM)],
-        [(p, pl.ANY) for p in packs] + [(small, pltpu.VMEM)],
         [
-            copies(count * (plane - 1)),
+            ((span * plane,) + small.shape, small.dtype, pltpu.VMEM),
+            ((size, plane * chunk), pack.dtype, pl.ANY),
+        ],
+        [(small, pltpu.VMEM), (pack, pl.ANY)],
+        [
             copies(plane * span - 1),
-            pltpu.SemaphoreType.DMA((count,)),
             pltpu.SemaphoreType.DMA,
+            copies(plane - 1),
+            pltpu.SemaphoreType.DMA((1,)),
         ],
-        moved=1 << 26,
+        moved=1 << 24,
     )
 
 
@@ -638,7 +657,17 @@
 
 
 def entry_kernel(
-    tokens_ref, cot_ref, small_ref, all_ref, x_ref, cot_own_ref, normed_ref, sems, local_sem
+    tokens_ref,
+    cot_ref,
+    small_ref,
+    all_ref,
+    x_ref,
+    cot_own_ref,
+    column_ref,
+    row_ref,
+    normed_ref,
+    sems,
+    local_sem,
 ):
     greet_plane()
     core = lax.axis_index("tensor")
@@ -661,13 +690,35 @@
         return carry
 
     row_blocks(m, ROW_STEP, body)(0)
-    run(gather_steps(normed_ref, all_ref, Sender(sems), local_sem))
-
-
-def entry(tokens, cot, small, cid):
+    gather = gather_steps(normed_ref, all_ref, Sender(sems), local_sem)
+    next(gather)
+    plane, z = lax.axis_size("dp"), lax.axis_index("seq")
+    rows, _, length = row_ref.shape
+    pieces = length // LANES
+    starts = []
+    for chip in range(plane):
+        block = small_ref[z * plane + chip]
+        for r in range(rows // plane):
+            first = 2 + r * pieces
+            starts.append(
+                jnp.concatenate([block[first + p : first + p + 1] for p in range(pieces)], axis=1)
+            )
+    starts = jnp.concatenate(starts).astype(jnp.bfloat16)
+    down = lax.broadcasted_iota(jnp.int32, (length, length), 0)
+    across = lax.broadcasted_iota(jnp.int32, (length, length), 1)
+    counts = nn_dot(starts, jnp.where(down <= across, 1.0, 0.0).astype(jnp.bfloat16))
+    turned = nt_dot(jnp.where(across <= down, 1.0, 0.0).astype(jnp.bfloat16), starts)
+    for b in range(rows):
+        row_ref[b] = counts[b : b + 1]
+        column_ref[b] = turned[:, b : b + 1]
+    run(gather)
+
+
+def entry(tokens, cot, small, length, cid):
     cores, m, width = tokens.shape
+    rows = 4 * cores * m // length
     whole = pltpu.VMEM
-    gathered, x, cot_own = kernel_call(
+    gathered, x, cot_own, seg_col, seg_row = kernel_call(
         entry_kernel,
         "entry",
         cid,
@@ -675,18 +726,21 @@
             ((4, cores, m, width), jnp.bfloat16, pl.ANY),
             ((m, width), jnp.bfloat16, whole),
             ((m, width), jnp.bfloat16, whole),
+            ((rows, length, 1), jnp.float32, whole),
+            ((rows, 1, length), jnp.float32, whole),
         ],
         [(tokens, whole), (cot, whole), (small, whole)],
         [pltpu.VMEM((m, width), jnp.bfloat16), copies(GATHER_COPIES), pltpu.SemaphoreType.DMA],
         moved=tokens.size * 40,
     )
-    return gathered.reshape(-1, width), x, cot_own
+    return gathered.reshape(-1, width), x, cot_own, seg_col, seg_row
 
 
 FEATURES = 256
 STATE_ROWS = 160
+PIECES = 1
 CHUNKS = 8
-EARLY = 272
+EARLY = 192
 
 
 def feature_pairs():
@@ -761,47 +815,68 @@
         self.sems = copy_sems
         self.rows = state_ref.shape[0] // CHUNKS
 
+    def pieces(self, g):
+        some = STATE_ROWS // PIECES
+        return [
+            (g * self.rows + i, h, k * some)
+            for i in range(self.rows)
+            for h in range(self.state_ref.shape[1])
+            for k in range(PIECES)
+        ]
+
+    def move(self, g, n, source, target):
+        count = self.rows * self.state_ref.shape[1] * PIECES + 1
+        return pltpu.make_async_remote_copy(
+            src_ref=source,
+            dst_ref=target,
+            send_sem=self.sems.at[0, count * g + n],
+            recv_sem=self.sems.at[1, count * g + n],
+            device_id=self.to,
+            device_id_type=MESH_ID,
+        )
+
     def moves(self, g):
         part = pl.ds(g * self.rows, self.rows)
-        used = pl.ds(0, STATE_ROWS)
-        pairs = (
-            (self.out_ref.at[part, :, used], self.state_ref.at[part, :, used]),
-            (self.out_sums_ref.at[part], self.sums_ref.at[part]),
-        )
-        return [
-            pltpu.make_async_remote_copy(
-                src_ref=a,
-                dst_ref=b,
-                send_sem=self.sems.at[0, 2 * g + n],
-                recv_sem=self.sems.at[1, 2 * g + n],
-                device_id=self.to,
-                device_id_type=MESH_ID,
+        found = [self.move(g, 0, self.out_sums_ref.at[part], self.sums_ref.at[part])]
+        for n, (b, h, first) in enumerate(self.pieces(g)):
+            used = pl.ds(first, STATE_ROWS // PIECES)
+            found.append(
+                self.move(g, n + 1, self.out_ref.at[b, h, used], self.state_ref.at[b, h, used])
             )
-            for n, (a, b) in enumerate(pairs)
-        ]
+        return found
 
     def step(self, n):
         g = n - self.distance
 
         @pl.when((g >= 0) & (g < CHUNKS))
         def _():
-            @pl.when(self.gets)
-            def _():
-                for c in self.moves(g):
-                    c.wait_recv()
-
+            moves = self.moves(g)
+
+            def take(move):
+                @pl.when(self.gets)
+                def _():
+                    move.wait_recv()
+
+            def give(move):
+                @pl.when(self.gives)
+                def _():
+                    move.start()
+
+            for (b, h, first), move in zip(self.pieces(g), moves[1:]):
+                take(move)
+                used = pl.ds(first, STATE_ROWS // PIECES)
+                keep = Segments(*self.segments, b).keep
+                before = self.state_ref[b, h, used].astype(jnp.float32)
+                self.out_ref[b, h, used] = (self.own_ref[b, h, used] + keep * before).astype(
+                    jnp.bfloat16
+                )
+                give(move)
+            take(moves[0])
             for i in range(self.rows):
                 b = g * self.rows + i
                 keep = Segments(*self.segments, b).keep
-                for h in range(self.state_ref.shape[1]):
-                    before = self.state_ref[b, h].astype(jnp.float32)
-                    self.out_ref[b, h] = (self.own_ref[b, h] + keep * before).astype(jnp.bfloat16)
                 self.out_sums_ref[b] = self.own_sums_ref[b] + keep * self.sums_ref[b]
-
-            @pl.when(self.gives)
-            def _():
-                for c in self.moves(g):
-                    c.start()
+            give(moves[0])
 
     def run(self, work, between=()):
         def body(n, carry):
@@ -831,11 +906,11 @@
     col_ref,
     row_ref,
     pairs_ref,
-    down_ref,
+    late_ref,
     qkv_ref,
     state_ref,
     sums_ref,
-    down_all_ref,
+    late_all_ref,
     pick_ref,
     own_ref,
     own_sums_ref,
@@ -857,8 +932,8 @@
         [{"dp": p} for p in chips] + [{"seq": lax.rem(z + k, span)} for k in (1, span - 1)]
     )
     shards = swap_shards(
-        (down_ref,),
-        (down_all_ref,),
+        (late_ref,),
+        (late_all_ref,),
         chips,
         at,
         block_of,
@@ -1008,11 +1083,11 @@
     ]
 
 
-def states(normed, pack, seg_col, seg_row, pairs, down, heads, cid):
+def states(normed, pack, seg_col, seg_row, pairs, shards, heads, cid):
     tokens = normed.shape[0]
     rows = seg_col.shape[0]
     vcols = heads * VHEAD
-    plane, size, chunk = down.shape
+    plane = lax.axis_size("dp")
     whole = pltpu.VMEM
     return kernel_call(
         partial(states_kernel, heads),
@@ -1022,11 +1097,16 @@
             ((tokens, vcols + LANES), jnp.bfloat16, whole),
             ((rows, heads, FEATURES, VHEAD), jnp.bfloat16, whole),
             ((rows, 8, FEATURES), jnp.float32, whole),
-            ((size, plane * chunk), jnp.bfloat16, pl.ANY),
+        ]
+        + [((p.shape[1], plane * p.shape[2]), p.dtype, pl.ANY) for p in shards],
+        [(a, whole) for a in (normed, pack, seg_col, seg_row, pairs)]
+        + [(p, pl.ANY) for p in shards],
+        state_scratch(rows, heads)
+        + [
+            copies(rows * heads * PIECES + CHUNKS),
+            copies(len(shards) * (plane - 1)),
+            pltpu.SemaphoreType.DMA((len(shards),)),
         ],
-        [(a, whole) for a in (normed, pack, seg_col, seg_row, pairs)] + [(down, pl.ANY)],
-        state_scratch(rows, heads)
-        + [copies(2 * CHUNKS), copies(plane - 1), pltpu.SemaphoreType.DMA((1,))],
         moved=normed.size * 20,
     )
 
@@ -1074,18 +1154,20 @@
     parts, _, depth = pack_ref.shape
     m, width = x_ref.shape
     vcols = mixed_ref.shape[1]
-    first = pack_ref.shape[1] - vcols
-
-    def project(b, carry):
-        left = mixed_ref[pl.ds(pl.multiple_of(b * m, m), m)]
+    first = pack_ref.shape[1] - EARLY - vcols
+
+    def block(chip, core):
+        left = mixed_ref[pl.ds(pl.multiple_of((chip * 2 + core) * m, m), m)]
         for s in range(parts):
-            part_ref[b // 2, lax.rem(b, 2), :, pl.ds(s * depth, depth)] = nn_dot(
+            part_ref[chip, core, :, pl.ds(s * depth, depth)] = nn_dot(
                 left, pack_ref[s, pl.ds(first, vcols)]
             ).astype(jnp.bfloat16)
-        return carry
-
-    lax.fori_loop(0, 8, project, 0)
-    run(scatter_steps(part_ref, residual_ref, pair_ref, sum_ref, got_ref, Sender(sems)))
+
+    scatter = scatter_steps(
+        part_ref, residual_ref, pair_ref, sum_ref, got_ref, Sender(sems), start=False
+    )
+    produce_parts(block, next(scatter))
+    run(scatter)
 
     def body(r, carry):
         acc = jnp.zeros((ROW_STEP, LANES), jnp.float32)
@@ -1159,10 +1241,10 @@
 
 
 def stacked_copies(early, late, out, sems):
-    rows = early.shape[1]
+    rows = pl.ds(early.shape[1] - EARLY, EARLY)
     return [
-        pltpu.make_async_copy(early, out.at[:, pl.ds(0, rows)], sems.at[0]),
-        pltpu.make_async_copy(late, out.at[:, pl.ds(rows, late.shape[1])], sems.at[1]),
+        pltpu.make_async_copy(early.at[:, rows], out.at[:, pl.ds(0, EARLY)], sems.at[0]),
+        pltpu.make_async_copy(late, out.at[:, pl.ds(EARLY, late.shape[1])], sems.at[1]),
     ]
 
 
@@ -1254,7 +1336,7 @@
 
 def expand(own, early, late, cid):
     m, width = own.shape
-    weights = (early.shape[0], early.shape[1] + late.shape[1], early.shape[2])
+    weights = (early.shape[0], EARLY + late.shape[1], early.shape[2])
     units = weights[1] // 2
     low = jnp.bfloat16
     thin = ((4, 2, m, units), jnp.float32, pl.ANY)
@@ -1325,12 +1407,8 @@
     weights.append(pltpu.make_async_copy(down_hbm, down_w_ref, w_sems.at[2]))
     normed_copy = pltpu.make_async_copy(normed_hbm, normed_ref, normed_sem)
 
-    def place(i):
-        chip = choose(i < 2, d_at, choose(i < 4, x_at, choose(i < 6, y_at, at)))
-        return chip, choose(parity(i) == 0, 1 - core, core)
-
     def loads(i):
-        slot, (c, k) = parity(i), place(i)
+        slot, (c, k) = parity(i), leaving(i)
         return [
             pltpu.make_async_copy(a.at[c, k], b.at[slot], load_sems.at[slot, n])
             for n, (a, b) in enumerate(
@@ -1339,7 +1417,7 @@
         ]
 
     def store(i):
-        slot, (c, k) = parity(i), place(i)
+        slot, (c, k) = parity(i), leaving(i)
         return pltpu.make_async_copy(out_ref.at[slot], out_hbm.at[c, k], store_sems.at[slot])
 
     for c in weights + loads(0):
@@ -1367,7 +1445,7 @@
         def _():
             store(i - 2).wait()
 
-        slot, (chip, k) = parity(i), place(i)
+        slot, (chip, k) = parity(i), leaving(i)
         gate, up = gate_ref[slot], up_ref[slot]
         dhidden = project(lambda cols: cot_ref[slot, :, cols], down_w_ref, pl.ds(0, units))
         sig = jax.nn.sigmoid(gate)
@@ -1437,7 +1515,7 @@
     _, _, m, units = gate.shape
     tokens, width = normed.shape
     low = jnp.bfloat16
-    stacked = (early.shape[0], early.shape[1] + late.shape[1], early.shape[2])
+    stacked = (early.shape[0], EARLY + late.shape[1], early.shape[2])
     ins = (gate, up, cot.reshape(4, 2, m, width), early, late, down_w, normed)
     return kernel_call(
         hidden_kernel,
@@ -1514,7 +1592,7 @@
     half = m // 2
     parts, _, depth = pack_ref.shape
     vcols = mixed_ref.shape[3]
-    first_row = pack_ref.shape[1] - vcols
+    first_row = pack_ref.shape[1] - EARLY - vcols
     gain_ref[...] = jnp.zeros_like(gain_ref)
 
     def finish(r, k, v):
@@ -1838,7 +1916,7 @@
         + [pltpu.VMEM((m, width), jnp.float32), pltpu.VMEM((4, m, width), low)]
         + scatter_scratch(m, width)
         + [
-            copies(2 * CHUNKS),
+            copies(rows * heads * PIECES + CHUNKS),
             copies(count * (plane - 1)),
             pltpu.SemaphoreType.DMA((count,)),
             copies(SCATTER_COPIES),
@@ -1974,17 +2052,17 @@
     blocks = width // LANES
     copy = Sender(pair_sems)
 
-    def project(b, carry):
-        left = dqkv_ref[pl.ds(pl.multiple_of(b * m, m), m), pl.ds(0, wide)]
+    def block(chip, core):
+        left = dqkv_ref[pl.ds(pl.multiple_of((chip * 2 + core) * m, m), m), pl.ds(0, wide)]
         for s in range(parts):
-            part_ref[b // 2, lax.rem(b, 2), :, pl.ds(s * depth, depth)] = nn_dot(
+            part_ref[chip, core, :, pl.ds(s * depth, depth)] = nn_dot(
                 left, pack_ref[s, pl.ds(0, wide)]
             ).astype(jnp.bfloat16)
-        return carry
-
-    lax.fori_loop(0, 8, project, 0)
-    scatter = scatter_steps(part_ref, total_ref, pair_ref, sum_ref, got_ref, Sender(sems))
-    next(scatter)
+
+    scatter = scatter_steps(
+        part_ref, total_ref, pair_ref, sum_ref, got_ref, Sender(sems), start=False
+    )
+    produce_parts(block, next(scatter))
 
     def order(r, carry):
         for k in range(blocks):
@@ -2105,50 +2183,53 @@
             jnp.zeros((2, chunk), jnp.float32),
         ]
     )
-    attn_pack = jnp.concatenate(
-        [split(value_weight.T), split(query_weight.T), split(key_weight.T), split(output_weight)],
+    gate_w = split(gate_weight.T)
+    pack = jnp.concatenate(
+        [
+            split(value_weight.T),
+            split(query_weight.T),
+            split(key_weight.T),
+            split(output_weight),
+            gate_w[:, :EARLY],
+        ],
         axis=1,
     )
-    [attn_pack] = exchange(
-        [attn_pack], 1, [(attn_pack.shape[1], plane * chunk)], put=columns_of
-    )
-    gate_w = split(gate_weight.T)
-    early_w = gate_w[:, :EARLY]
+    [pack] = exchange([pack], 1, [(pack.shape[1], plane * chunk)], put=columns_of)
+    small, pack = lax.optimization_barrier((small, pack))
+    small, down_w = small_exchange(small, split(down_weight), 2)
+    pack = over_seq(pack)
     late_w = jnp.concatenate([gate_w[:, EARLY:], split(up_weight.T)], axis=1)
-    early_w, late_w, small = lax.optimization_barrier((early_w, late_w, small, attn_pack))[:3]
-    early_w, late_w, small = first_exchange([early_w, late_w], small, 2)
-    attn_pack, early_w = over_seq(attn_pack), over_seq(early_w)
-    starts = small[:, 2:-2].reshape(span, plane * rows, length)
-    segments = jnp.cumsum(
-        lax.dynamic_index_in_dim(starts, lax.axis_index("seq"), 0, keepdims=False), axis=1
-    )
-
     qkv_rows = vcols + 2 * qcols
-    seg_col = segments[:, :, None]
-    seg_row = segments[:, None, :]
     pairs = feature_pairs()
-    normed_one, x, cot_own = entry(
-        tokens.reshape(cores, own, width), cotangent.reshape(cores, own, width), small, 3
-    )
-    qkv, state, sums, down_w = states(
-        normed_one, attn_pack, seg_col, seg_row, pairs, split(down_weight), heads, 4
+    normed_one, x, cot_own, seg_col, seg_row = entry(
+        tokens.reshape(cores, own, width), cotangent.reshape(cores, own, width), small, length, 3
+    )
+    qkv, state, sums, late_w = states(
+        normed_one,
+        pack,
+        seg_col,
+        seg_row,
+        pairs,
+        [late_w],
+        heads,
+        4,
     )
     late_w, down_w = lax.optimization_barrier((late_w, down_w))
     late_w, down_w = over_seq(late_w), over_seq(down_w)
     mixed, exact, den, cot = mix(
         qkv, seg_col, seg_row, pairs, state, sums, cot_own, heads, 13
     )
-    residual, normed_own = branch(mixed, attn_pack, x, small, 5)
-    normed_two, gate, up, hidden = expand(normed_own, early_w, late_w, 11)
+    residual, normed_own = branch(mixed, pack, x, small, 5)
+    normed_two, gate, up, hidden = expand(normed_own, pack, late_w, 11)
     down_grad = nn_dot(hidden, cot).astype(jnp.bfloat16)
     gate, down_grad = lax.optimization_barrier((gate, down_grad))
     down_grad = summed(down_grad)
     out_part, dnormed_two, gate_up_grad = hidden_units(
-        gate, up, cot, early_w, late_w, down_w, normed_two, 6
+        gate, up, cot, pack, late_w, down_w, normed_two, 6
     )
     gate_up_grad = summed(gate_up_grad)
     dresid, gain_two_grad, dmixed, out_grad = turn(
-        dnormed_two, residual, cot_own, small, attn_pack, mixed, 12
+        dnormed_two, residual, cot_own, small, pack, mixed, 12
     )
     dmixed, down_grad = lax.optimization_barrier((dmixed, down_grad))
     dqkv, block_own, attn_grad, (down_grad,) = unmix(
@@ -2166,7 +2247,7 @@
     )
     attn_grad = summed(attn_grad)
     dtokens, block_out, gains, gate_up_grad = leave(
-        dqkv, attn_pack, x, dresid, block_own, small, gain_two_grad, [gate_up_grad], 9
+        dqkv, pack, x, dresid, block_own, small, gain_two_grad, [gate_up_grad], 9
     )
     (attn_grad,), gain_grads = last([attn_grad], gains, 10)
 

time: 561 us -> 553 us (0.986)
  Pallas kernels: 504 us -> 489 us
  waiting for transfers between devices: 3.52 us -> 13.2 us
    pallas_call x11, Pallas kernels: 492 us -> 475 us  [kernel_call(): pl.pallas_call(body, name=name, out_shape=[jax.ShapeDtypeStruct(s, d) for...]
    all_gather x4 -> x3, waiting for transfers between devices: 2.86 us -> 12.4 us  [over_seq(): return lax.all_gather(pack, 'seq', axis=0, tiled=False)]
  transfers between devices with their start and end apart: 7 -> 6, of which waited for: 2 -> 3; matrix products, arithmetic and copies ran while one was open for 3% -> 2% of each run, Pallas kernels for 85% -> 79%
where the time goes in v8:
time: 553 us; the launch traced here: 552 us
  Pallas kernels  489 us (88%)
  local copies, waits for them, and re-layouts  17.6 us (3%)
  between operations  14.4 us (3%)
  waiting for transfers between devices  13.2 us (2%)
  matrix products  10.3 us (2%)
  other arithmetic  7.11 us (1%)
    pallas_call x11, Pallas kernels, kernel_call(): pl.pallas_call(body, name=name, out_shape=[jax.ShapeDtypeStruct(s, d) for...  475 us
    pallas_call x1, Pallas kernels, exchange(): pl.pallas_call(partial(exchange_kernel, take, put, count), name='exchange...  13.7 us
    all_gather x3, waiting for transfers between devices, over_seq(): return lax.all_gather(pack, 'seq', axis=0, tiled=False)  12.4 us
  transfers between devices with their start and end apart: 6, of which 3 were waited for; matrix products, arithmetic and copies ran while one was open for 2% of the time, Pallas kernels for 79%

profile of v8, /device:TPU:0, one launch (start us, length us, event | category | flops | bytes accessed | tf_op | source)
XLA Modules:
  0.0 552.1 jit_solution(1870118330426331142)
XLA Ops:
  7.2 0.0 copy-start.5
  7.2 0.0 copy-start.7
  7.2 0.0 copy-start.8
  7.2 0.0 all-gather.7.cloned.1.call-start
  7.3 0.7 convert_element_type.40
  8.0 0.9 copy.25
  8.9 0.9 copy.26
  9.8 1.1 copy.24
  10.9 1.0 constant_dynamic-update-slice_fusion
  11.9 1.0 slice_dynamic-update-slice_fusion.refs_0_
  12.9 0.0 copy-start.3
  12.9 0.9 copy-done.3
  13.8 13.7 %exchange.1 = bf16[768,512]{1,0:T(8,128)(2,1)} custom-call(bf16[4,768,128]{2,1,0:T(8,128)(2,1)} %copy-done.3), custom_call_target="tpu_custom_call" | custom-call | bytes 23592960 | tf_op jit(solution)/shard_map/exchange/pallas_call | solution.py:544
  27.5 0.1 pad.5.clone
  27.6 0.0 copy-done.7
  27.6 0.0 copy-done.8
  27.6 0.7 maximum_maximum_fusion.small_ref
  28.3 0.0 all-gather.7.cloned.1.call-update
  28.3 0.0 all-gather.9.cloned.1.call-start
  28.3 0.0 copy-done.5
  28.4 0.0 copy-start.4
  28.4 16.6 %small_exchange.1 = (f32[16,8,128]{2,1,0:T(8,128)}, bf16[688,512]{1,0:T(8,128)(2,1)}) custom-call(f32[8,128]{1,0:T(8,128)} %maximum_maximum_fusion.small_ref, bf16[4,688,128]{2,1,0:T(8,128)(2,1)} %bitcast.76), custom_call_target="tpu_custom_call" | custom-call | bytes 16777216 | tf_op jit(solution)/shard_map/small_exchange/pallas_call | solution.py:643
  45.1 43.9 %entry.1 = (bf16[4,2,256,2048]{3,2,1,0:T(8,128)(2,1)}, bf16[256,2048]{1,0:T(8,128)(2,1)}, bf16[256,2048]{1,0:T(8,128)(2,1)}, f32[8,256,1]{2,1,0:T(8,128)}, f32[8,1,256]{2,1,0:T(1,128)}) custom-call(bf16[2,256,2048]{2,1,0:T(8,128)(2,1)} %tokens_ref.1, bf16[2,256,2048]{2,1,0:T(8,128)(2,1)} %cot_ref.1, f32[16,8,128]{2,1,0:T(8,128)} %get-tuple-element.58.small_ref), custom_call_target="tpu_custom_call" | custom-call | bytes 41943040 | tf_op jit(solution)/shard_map/entry/pallas_call | solution.py:643
  88.9 1.1 pad_maximum_fusion.late_ref
  90.1 3.0 all-gather.7.cloned.1.call-done
  93.1 26.2 %states.1 = (bf16[2048,384]{1,0:T(8,128)(2,1)}, bf16[8,2,256,128]{3,2,1,0:T(8,128)(2,1)}, f32[8,8,256]{2,1,0:T(8,128)}, bf16[1184,512]{1,0:T(8,128)(2,1)}) custom-call(bf16[2048,2048]{1,0:T(8,128)(2,1)} %bitcast.68, bf16[4,768,512]{2,1,0:T(8,128)(2,1)} %bitcast.62, f32[8,256,1]{2,1,0:T(8,128)} %get-tuple-element.61.col_ref, ...), custom_call_target="tpu_custom_call" | custom-call | bytes 83886080 | tf_op jit(solution)/shard_map/states/pallas_call | solution.py:643
  119.3 0.0 all-gather.9.cloned.1.call-update
  119.3 0.0 all-gather.11.cloned.1.call-start
  119.4 0.7 all-gather.11.cloned.1.call-update
  120.1 0.0 reduce-scatter.4.cloned.1.call-start
  120.1 43.2 %mix.1 = (bf16[2048,256]{1,0:T(8,128)(2,1)}, f32[2048,256]{1,0:T(8,128)}, f32[2048,128]{1,0:T(8,128)}, bf16[4,2,256,2048]{3,2,1,0:T(8,128)(2,1)}) custom-call(bf16[2048,384]{1,0:T(8,128)(2,1)} %get-tuple-element.63.qkv_ref, f32[8,256,1]{2,1,0:T(8,128)} %get-tuple-element.61.col_ref, f32[8,1,256]{2,1,0:T(1,128)} %get-tuple-element.62.row_ref, ...), custom_call_target="tpu_custom_call" | custom-call | bytes 41943040 | tf_op jit(solution)/shard_map/mix/pallas_call | solution.py:643
  163.4 46.5 %branch.1 = (f32[256,2048]{1,0:T(8,128)}, bf16[256,2048]{1,0:T(8,128)(2,1)}) custom-call(bf16[2048,256]{1,0:T(8,128)(2,1)} %get-tuple-element.67.mixed_ref, bf16[4,768,512]{2,1,0:T(8,128)(2,1)} %bitcast.63, bf16[256,2048]{1,0:T(8,128)(2,1)} %get-tuple-element.68.x_ref, f32[16,8,128]{2,1,0:T(8,128)} %get-tuple-element.58.small_ref), custom_call_target="tpu_custom_call" | custom-call | bytes 41943040 | tf_op jit(solution)/shard_map/branch/pallas_call | solution.py:643
  209.8 8.3 %all-gather.9.cloned.1.call-done = bf16[4736,512]{1,0:T(8,128)(2,1)} async-done(((bf16[1184,512]{1,0:T(8,128)(2,1)}), bf16[4736,512]{1,0:T(8,128)(2,1)}) %all-gather.9.cloned.1.call-update) | async-done | bytes 4849680 | tf_op jit(solution)/shard_map/all_gather | solution.py:2168
  218.1 46.4 %expand.1 = (bf16[4,2,256,2048]{3,2,1,0:T(8,128)(2,1)}, f32[4,2,256,688]{3,2,1,0:T(8,128)}, f32[4,2,256,688]{3,2,1,0:T(8,128)}, bf16[688,2048]{1,0:T(8,128)(2,1)}) custom-call(bf16[256,2048]{1,0:T(8,128)(2,1)} %get-tuple-element.69.own_ref, bf16[4,768,512]{2,1,0:T(8,128)(2,1)} %bitcast.64, bf16[4,1184,512]{2,1,0:T(8,128)(2,1)} %bitcast.87), custom_call_target="tpu_custom_call" | custom-call | flops 11542724608 | bytes 134217728 | tf_op jit(solution)/shard_map/expand/pallas_call | solution.py:643
  264.5 10.3 %convolution_convert_fusion = bf16[688,2048]{1,0:T(8,128)(2,1)} fusion(bf16[688,2048]{1,0:T(8,128)(2,1)} %get-tuple-element.74, bf16[2048,2048]{1,0:T(8,128)(2,1)} %bitcast.86), kind=kOutput, calls=%fused_computation | convolution fusion | flops 5772771328 | bytes 14024704 | tf_op jit(solution)/shard_map/dot_general | solution.py:304
  274.9 0.0 reduce-scatter.4.cloned.1.call-update
  274.9 0.2 reduce-scatter.6.cloned.1.call-start
  275.1 1.1 all-gather.11.cloned.1.call-done
  276.2 57.7 %hidden_units.1 = (bf16[4,2,256,2048]{3,2,1,0:T(8,128)(2,1)}, f32[256,2048]{1,0:T(8,128)}, bf16[1376,2048]{1,0:T(8,128)(2,1)}) custom-call(f32[4,2,256,688]{3,2,1,0:T(8,128)} %get-tuple-element.76.gate_hbm, f32[4,2,256,688]{3,2,1,0:T(8,128)} %get-tuple-element.77.up_hbm, bf16[4,2,256,2048]{3,2,1,0:T(8,128)(2,1)} %get-tuple-element.75.cot_hbm, ...), custom_call_target="tpu_custom_call" | custom-call | flops 34628173824 | bytes 134217728 | tf_op jit(solution)/shard_map/hidden_units/pallas_call | solution.py:643
  333.9 0.0 reduce-scatter.6.cloned.1.call-update
  333.9 0.0 reduce-scatter.8.cloned.1.call-start
  334.0 46.5 %turn.1 = (f32[256,2048]{1,0:T(8,128)}, f32[8,2048]{1,0:T(8,128)}, bf16[4,2,256,256]{3,2,1,0:T(8,128)(2,1)}, bf16[256,2048]{1,0:T(8,128)(2,1)}) custom-call(f32[256,2048]{1,0:T(8,128)} %get-tuple-element.80.total_ref, f32[256,2048]{1,0:T(8,128)} %get-tuple-element.81.residual_ref, bf16[256,2048]{1,0:T(8,128)(2,1)} %get-tuple-element.66.cot_ref, ...), custom_call_target="tpu_custom_call" | custom-call | bytes 41943040 | tf_op jit(solution)/shard_map/turn/pallas_call | solution.py:643
  380.5 0.0 reduce-scatter.4.cloned.1.call-done.refs_0_
  380.5 76.8 %unmix.1 = (bf16[2048,384]{1,0:T(8,128)(2,1)}, bf16[256,2048]{1,0:T(8,128)(2,1)}, bf16[576,2048]{1,0:T(8,128)(2,1)}, bf16[4,688,128]{2,1,0:T(8,128)(2,1)}) custom-call(bf16[2048,256]{1,0:T(8,128)(2,1)} %bitcast.71, bf16[2048,2048]{1,0:T(8,128)(2,1)} %bitcast.69, bf16[256,2048]{1,0:T(8,128)(2,1)} %get-tuple-element.85.output_grad_ref, ...), custom_call_target="tpu_custom_call" | custom-call | bytes 62914560 | tf_op jit(solution)/shard_map/unmix/pallas_call | solution.py:643
  457.3 0.0 reduce-scatter.8.cloned.1.call-update
  457.3 1.1 copy-done.6
  458.4 1.2 bitcast_convert_fusion
  459.6 57.6 %leave.1 = (f32[2,256,2048]{2,1,0:T(8,128)}, bf16[2,256,2048]{2,1,0:T(8,128)(2,1)}, f32[16,8,128]{2,1,0:T(8,128)}, bf16[4,1376,128]{2,1,0:T(8,128)(2,1)}) custom-call(bf16[2048,384]{1,0:T(8,128)(2,1)} %get-tuple-element.90.dqkv_ref, bf16[4,768,512]{2,1,0:T(8,128)(2,1)} %bitcast.67, bf16[256,2048]{1,0:T(8,128)(2,1)} %get-tuple-element.68.x_ref, ...), custom_call_target="tpu_custom_call" | custom-call | bytes 62914560 | tf_op jit(solution)/shard_map/leave/pallas_call | solution.py:643
  517.2 0.0 reduce-scatter.8.cloned.1.call-done.refs_0_
  517.2 14.0 %last.1 = (bf16[4,576,128]{2,1,0:T(8,128)(2,1)}, f32[8,128]{1,0:T(8,128)}) custom-call(bf16[576,512]{1,0:T(8,128)(2,1)} %reduce-scatter.8.cloned.1.call-done.refs_0_, f32[16,8,128]{2,1,0:T(8,128)} %get-tuple-element.98.refs_1_), custom_call_target="tpu_custom_call" | custom-call | bytes 67108864 | tf_op jit(solution)/shard_map/last/pallas_call | solution.py:643
  531.2 0.8 fusion.2
  532.0 1.1 fusion.1
  533.1 1.3 slice_bitcast_fusion
  534.4 0.7 copy.28
  535.1 0.7 copy.27
  535.9 0.8 bitcast_convert_fusion.1
  536.7 0.1 bitcast_convert_fusion.2
  536.8 1.0 copy.29
  537.8 0.1 fusion
  537.9 1.2 convert_bitcast_fusion
  539.1 1.2 convert_bitcast_fusion.1
  540.3 1.3 copy.36
  541.6 1.6 copy-done
  543.3 2.0 copy.37
  (17 shorter events, 0.1 us)
Async XLA Ops:
  7.2 21.2 %copy-start.5 = (bf16[128,2752]{0,1:T(8,128)(2,1)S(1)}, bf16[128,2752]{0,1:T(8,128)(2,1)}, u32[]{:S(2)}) copy-start(bf16[128,2752]{0,1:T(8,128)(2,1)} %param.21) | copy-start | bytes 2113540
  7.2 20.4 %copy-start.7 = (bf16[128]{0:T(256)(128)(2,1)S(1)}, bf16[128]{0:T(256)(128)(2,1)}, u32[]{:S(2)}) copy-start(bf16[128]{0:T(256)(128)(2,1)} %param.16) | copy-start | bytes 772
  7.2 20.4 %copy-start.8 = (bf16[128]{0:T(256)(128)(2,1)S(1)}, bf16[128]{0:T(256)(128)(2,1)}, u32[]{:S(2)}) copy-start(bf16[128]{0:T(256)(128)(2,1)} %param.15) | copy-start | bytes 772
  7.2 85.9 %all-gather.7.cloned.1.call-start = ((), (), s32[]{:S(2)}) async-start(), calls=%async_computation.6 | async-start | bytes 3932160 | tf_op jit(solution)/shard_map/all_gather | solution.py:2168
  12.9 0.9 copy-start.3
  28.3 189.8 %all-gather.9.cloned.1.call-start = ((), (), s32[]{:S(2)}) async-start(), calls=%async_computation.7 | async-start | bytes 6062080 | tf_op jit(solution)/shard_map/all_gather | solution.py:2168
  28.4 60.6 %copy-start.4 = (bf16[128,2752]{0,1:T(8,128)(2,1)S(1)}, bf16[128,2752]{0,1:T(8,128)(2,1)}, u32[]{:S(2)}) copy-start(bf16[128,2752]{0,1:T(8,128)(2,1)} %param.22) | copy-start | bytes 2113540
  119.3 156.9 %all-gather.11.cloned.1.call-start = ((), (), s32[]{:S(2)}) async-start(), calls=%async_computation.8 | async-start | bytes 3522560 | tf_op jit(solution)/shard_map/all_gather | solution.py:2168
  120.1 260.4 %reduce-scatter.4.cloned.1.call-start = ((), (), s32[]{:S(2)}) async-start(), calls=%async_computation.3 | async-start | bytes 3522560 | tf_op jit(solution)/shard_map/reduce_scatter | solution.py:2171
  274.9 184.7 %reduce-scatter.6.cloned.1.call-start = ((), (), s32[]{:S(2)}) async-start(), calls=%async_computation.4 | async-start | bytes 7045120 | tf_op jit(solution)/shard_map/reduce_scatter | solution.py:2171
  333.9 183.3 %reduce-scatter.8.cloned.1.call-start = ((), (), s32[]{:S(2)}) async-start(), calls=%async_computation.5 | async-start | bytes 2949120 | tf_op jit(solution)/shard_map/reduce_scatter | solution.py:2171
  457.3 1.1 copy-start.6
  517.2 20.5 %copy-start.2 = (bf16[4,1376,128]{2,1,0:T(8,128)(2,1)S(1)}, bf16[4,1376,128]{2,1,0:T(8,128)(2,1)}, u32[]{:S(2)}) copy-start(bf16[4,1376,128]{2,1,0:T(8,128)(2,1)} %get-tuple-element.101) | copy-start | bytes 4227076
  537.9 2.5 copy-start.1
  540.3 2.9 copy-start
Sparse Core Ops, SparseCore 0:
  28.4 64.6 all-gather.6
  119.5 98.5 all-gather.8
  219.7 56.5 all-gather.10
  279.0 53.8 reduce-scatter.3
  335.2 114.0 reduce-scatter.5
  457.4 46.1 reduce-scatter.7

commit v9 on v8

--- a/solution.py
+++ b/solution.py
@@ -316,11 +316,16 @@
     )
 
 
+loading = []
+
+
 def greet(places):
     barrier = pltpu.get_barrier_semaphore()
     for place in places:
         pl.semaphore_signal(barrier, inc=1, device_id=place, device_id_type=MESH_ID)
     pl.semaphore_wait(barrier, len(places))
+    while loading:
+        loading.pop().wait()
 
 
 class Sender:
@@ -638,18 +643,42 @@
     return jnp.sum(acc, axis=1, keepdims=True) * (1.0 / width)
 
 
+class Rows:
+    def __init__(self, pack, first, count):
+        self.array, self.rows = pack, pl.ds(first, count)
+        self.shape, self.dtype = (pack.shape[0], count, pack.shape[2]), pack.dtype
+        self.size = pack.shape[0] * count * pack.shape[2]
+
+
 def kernel_call(body, name, cid, outs, ins, scratch, flops=0, moved=0):
-    params = dict(has_side_effects=True, vmem_limit_bytes=VMEM_LIMIT)
+    big = [n for n, (a, m) in enumerate(ins) if m == pltpu.VMEM and a.size >= 1 << 16]
+    count, params = len(ins), dict(has_side_effects=True, vmem_limit_bytes=VMEM_LIMIT)
+
+    def loaded(*refs):
+        refs, buffers, sems = list(refs[: -len(big) - 1]), refs[-len(big) - 1 : -1], refs[-1]
+        for k, n in enumerate(big):
+            source = refs[n]
+            if isinstance(ins[n][0], Rows):
+                source = source.at[:, ins[n][0].rows]
+            loading.append(pltpu.make_async_copy(source, buffers[k], sems.at[k]))
+            loading[-1].start()
+            refs[n] = buffers[k]
+        body(*refs)
+
     return pl.pallas_call(
-        body,
+        loaded if big else body,
         name=name,
         out_shape=[jax.ShapeDtypeStruct(s, d) for s, d, _ in outs],
-        in_specs=[pl.BlockSpec(memory_space=m) for _, m in ins],
+        in_specs=[
+            pl.BlockSpec(memory_space=pl.ANY if n in big else ins[n][1]) for n in range(count)
+        ],
         out_specs=[pl.BlockSpec(memory_space=m) for _, _, m in outs],
-        scratch_shapes=scratch,
+        scratch_shapes=list(scratch)
+        + [pltpu.VMEM(ins[n][0].shape, ins[n][0].dtype) for n in big]
+        + ([pltpu.SemaphoreType.DMA((len(big),))] if big else []),
         compiler_params=pltpu.CompilerParams(collective_id=cid, **params),
         cost_estimate=pl.CostEstimate(flops=flops, bytes_accessed=moved, transcendentals=0),
-    )(*[a for a, _ in ins])
+    )(*[a.array if isinstance(a, Rows) else a for a, _ in ins])
 
 
 def copies(count):
@@ -881,6 +910,8 @@
     def run(self, work, between=()):
         def body(n, carry):
             for at, piece in enumerate(between):
+                if piece is None:
+                    continue
 
                 @pl.when(n == at)
                 def _():
@@ -1154,7 +1185,7 @@
     parts, _, depth = pack_ref.shape
     m, width = x_ref.shape
     vcols = mixed_ref.shape[1]
-    first = pack_ref.shape[1] - EARLY - vcols
+    first = pack_ref.shape[1] - vcols
 
     def block(chip, core):
         left = mixed_ref[pl.ds(pl.multiple_of((chip * 2 + core) * m, m), m)]
@@ -1592,7 +1623,7 @@
     half = m // 2
     parts, _, depth = pack_ref.shape
     vcols = mixed_ref.shape[3]
-    first_row = pack_ref.shape[1] - EARLY - vcols
+    first_row = pack_ref.shape[1] - vcols
     gain_ref[...] = jnp.zeros_like(gain_ref)
 
     def finish(r, k, v):
@@ -1694,6 +1725,7 @@
     outs = refs[count + 3 : 2 * count + 3]
     (
         normed_ref,
+        early_ref,
         turned_ref,
         dvalue_ref,
         dtile_ref,
@@ -1844,31 +1876,43 @@
         def _():
             lax.fori_loop(done * each, (done + 1) * each, after, 0)
 
-    nothing = lambda: None
-    chain.run(
-        work,
-        [nothing] * 2 + [lambda: advance(scatter, 3)] + [nothing] * 3 + [lambda: advance(scatter)],
-    )
-    run(scatter)
-
     def finish(r, carry):
         block_ref[r] = (residual_ref[r] + total_ref[r]).astype(jnp.bfloat16)
         return carry
 
-    row_blocks(block_ref.shape[0], ROW_STEP, finish)(0)
-    normed_copy.wait()
+    def output():
+        run(scatter)
+        row_blocks(block_ref.shape[0], ROW_STEP, finish)(0)
+
     wide = 4 * LANES
     qkv_rows = grad_ref.shape[0] - vcols
+    early = (rows - each) * length
+
+    def gradient(t, put):
+        def body(i, carry):
+            cols = pl.ds(pl.multiple_of(i * wide, wide), wide)
+            put(cols, nn_dot(turned_ref[pl.ds(0, qkv_rows), t], normed_ref[t, cols]))
+            return carry
+
+        lax.fori_loop(0, normed_ref.shape[1] // wide, body, 0)
+
+    def keep(cols, value):
+        early_ref[:, cols] = value
+
+    def close(cols, value):
+        grad_ref[pl.ds(0, qkv_rows), cols] = (early_ref[:, cols] + value).astype(jnp.bfloat16)
+
+    def most():
+        normed_copy.wait()
+        gradient(pl.ds(0, early), keep)
+
+    steps = [None] * (CHUNKS + span - 1)
+    steps[2] = lambda: advance(scatter, 3)
+    steps[6] = lambda: advance(scatter)
+    steps[-2], steps[-1] = output, most
+    chain.run(work, steps)
+    gradient(pl.ds(early, each * length), close)
     grad_ref[pl.ds(qkv_rows, vcols)] = output_grad_ref[...]
-
-    def gradient(i, carry):
-        cols = pl.ds(pl.multiple_of(i * wide, wide), wide)
-        grad_ref[pl.ds(0, qkv_rows), cols] = nn_dot(
-            turned_ref[pl.ds(0, qkv_rows)], normed_ref[:, cols]
-        ).astype(jnp.bfloat16)
-        return carry
-
-    lax.fori_loop(0, normed_ref.shape[1] // wide, gradient, 0)
     for c in shards:
         c.wait()
     chain.close()
@@ -1906,6 +1950,7 @@
         + [(p, pl.ANY) for p in shards],
         [
             pltpu.VMEM((tokens, width), low),
+            pltpu.VMEM((grad_rows - vcols, width), jnp.float32),
             pltpu.VMEM((vcols + LANES, tokens), low),
             pltpu.VMEM((tokens, vcols), jnp.float32),
             pltpu.VMEM((tokens, LANES), jnp.float32),
@@ -2204,9 +2249,10 @@
     normed_one, x, cot_own, seg_col, seg_row = entry(
         tokens.reshape(cores, own, width), cotangent.reshape(cores, own, width), small, length, 3
     )
+    into, out_of = Rows(pack, 0, vcols + LANES), Rows(pack, qkv_rows, vcols)
     qkv, state, sums, late_w = states(
         normed_one,
-        pack,
+        into,
         seg_col,
         seg_row,
         pairs,
@@ -2219,7 +2265,7 @@
     mixed, exact, den, cot = mix(
         qkv, seg_col, seg_row, pairs, state, sums, cot_own, heads, 13
     )
-    residual, normed_own = branch(mixed, pack, x, small, 5)
+    residual, normed_own = branch(mixed, out_of, x, small, 5)
     normed_two, gate, up, hidden = expand(normed_own, pack, late_w, 11)
     down_grad = nn_dot(hidden, cot).astype(jnp.bfloat16)
     gate, down_grad = lax.optimization_barrier((gate, down_grad))
@@ -2229,7 +2275,7 @@
     )
     gate_up_grad = summed(gate_up_grad)
     dresid, gain_two_grad, dmixed, out_grad = turn(
-        dnormed_two, residual, cot_own, small, pack, mixed, 12
+        dnormed_two, residual, cot_own, small, out_of, mixed, 12
     )
     dmixed, down_grad = lax.optimization_barrier((dmixed, down_grad))
     dqkv, block_own, attn_grad, (down_grad,) = unmix(
@@ -2247,7 +2293,7 @@
     )
     attn_grad = summed(attn_grad)
     dtokens, block_out, gains, gate_up_grad = leave(
-        dqkv, pack, x, dresid, block_own, small, gain_two_grad, [gate_up_grad], 9
+        dqkv, into, x, dresid, block_own, small, gain_two_grad, [gate_up_grad], 9
     )
     (attn_grad,), gain_grads = last([attn_grad], gains, 10)
 

time: 553 us -> 549 us (level)
  Pallas kernels: 489 us -> 482 us
    pallas_call x11, Pallas kernels: 475 us -> 469 us  [kernel_call(): pl.pallas_call(loaded if big else body, name=name, out_shape=[jax.ShapeDt...]
where the time goes in v9:
time: 549 us; the launch traced here: 548 us
  Pallas kernels  482 us (88%)
  local copies, waits for them, and re-layouts  17.6 us (3%)
  waiting for transfers between devices  15.6 us (3%)
  between operations  14.4 us (3%)
  matrix products  10.3 us (2%)
  other arithmetic  7.11 us (1%)
    pallas_call x11, Pallas kernels, kernel_call(): pl.pallas_call(loaded if big else body, name=name, out_shape=[jax.ShapeDt...  469 us
    all_gather x3, waiting for transfers between devices, over_seq(): return lax.all_gather(pack, 'seq', axis=0, tiled=False)  14.8 us
    pallas_call x1, Pallas kernels, exchange(): pl.pallas_call(partial(exchange_kernel, take, put, count), name='exchange...  13.7 us
  transfers between devices with their start and end apart: 6, of which 3 were waited for; matrix products, arithmetic and copies ran while one was open for 2% of the time, Pallas kernels for 79%

profile of v9, /device:TPU:0, one launch (start us, length us, event | category | flops | bytes accessed | tf_op | source)
XLA Modules:
  0.0 547.8 jit_solution(14697925089925348984)
XLA Ops:
  7.2 0.0 copy-start.5
  7.2 0.0 copy-start.7
  7.2 0.0 all-gather.7.cloned.1.call-start
  7.3 0.7 convert_element_type.40
  8.0 0.9 copy.25
  8.9 0.9 copy.26
  9.8 1.1 copy.24
  10.9 1.0 constant_dynamic-update-slice_fusion
  11.9 1.0 slice_dynamic-update-slice_fusion.refs_0_
  12.9 0.0 copy-start.3
  12.9 0.9 copy-done.3
  13.8 13.7 %exchange.1 = bf16[768,512]{1,0:T(8,128)(2,1)} custom-call(bf16[4,768,128]{2,1,0:T(8,128)(2,1)} %copy-done.3), custom_call_target="tpu_custom_call" | custom-call | bytes 23592960 | tf_op jit(solution)/shard_map/exchange/pallas_call | solution.py:549
  27.5 0.1 pad.5.clone
  27.6 0.0 copy-done.7
  27.6 0.7 maximum_maximum_fusion.small_ref
  28.3 0.0 all-gather.7.cloned.1.call-update
  28.3 0.0 all-gather.9.cloned.1.call-start
  28.3 0.0 copy-done.5
  28.4 0.0 copy-start.4
  28.4 16.6 %small_exchange.1 = (f32[16,8,128]{2,1,0:T(8,128)}, bf16[688,512]{1,0:T(8,128)(2,1)}) custom-call(f32[8,128]{1,0:T(8,128)} %maximum_maximum_fusion.small_ref, bf16[4,688,128]{2,1,0:T(8,128)(2,1)} %bitcast.76), custom_call_target="tpu_custom_call" | custom-call | bytes 16777216 | tf_op jit(solution)/shard_map/small_exchange/pallas_call | solution.py:668
  45.1 43.5 %entry.1 = (bf16[4,2,256,2048]{3,2,1,0:T(8,128)(2,1)}, bf16[256,2048]{1,0:T(8,128)(2,1)}, bf16[256,2048]{1,0:T(8,128)(2,1)}, f32[8,256,1]{2,1,0:T(8,128)}, f32[8,1,256]{2,1,0:T(1,128)}) custom-call(bf16[2,256,2048]{2,1,0:T(8,128)(2,1)} %refs_0_.1, bf16[2,256,2048]{2,1,0:T(8,128)(2,1)} %refs_1_.1, f32[16,8,128]{2,1,0:T(8,128)} %get-tuple-element.58.refs_2_.refs_3_.refs_5_), custom_call_target="tpu_custom_call" | custom-call | bytes 41943040 | tf_op jit(solution)/shard_map/entry/pallas_call | solution.py:668
  88.5 1.1 pad_maximum_fusion.refs_5_
  89.6 3.4 all-gather.7.cloned.1.call-done
  93.1 24.3 %states.1 = (bf16[2048,384]{1,0:T(8,128)(2,1)}, bf16[8,2,256,128]{3,2,1,0:T(8,128)(2,1)}, f32[8,8,256]{2,1,0:T(8,128)}, bf16[1184,512]{1,0:T(8,128)(2,1)}) custom-call(bf16[2048,2048]{1,0:T(8,128)(2,1)} %bitcast.68, bf16[4,768,512]{2,1,0:T(8,128)(2,1)} %bitcast.62, f32[8,256,1]{2,1,0:T(8,128)} %get-tuple-element.61.refs_2_.refs_1_.refs_5_, ...), custom_call_target="tpu_custom_call" | custom-call | bytes 83886080 | tf_op jit(solution)/shard_map/states/pallas_call | solution.py:668
  117.3 0.0 all-gather.9.cloned.1.call-update
  117.4 0.0 all-gather.11.cloned.1.call-start
  117.4 0.7 all-gather.11.cloned.1.call-update
  118.1 0.0 reduce-scatter.4.cloned.1.call-start
  118.2 44.0 %mix.1 = (bf16[2048,256]{1,0:T(8,128)(2,1)}, f32[2048,256]{1,0:T(8,128)}, f32[2048,128]{1,0:T(8,128)}, bf16[4,2,256,2048]{3,2,1,0:T(8,128)(2,1)}) custom-call(bf16[2048,384]{1,0:T(8,128)(2,1)} %get-tuple-element.63.refs_0_.refs_8_, f32[8,256,1]{2,1,0:T(8,128)} %get-tuple-element.61.refs_2_.refs_1_.refs_5_, ...), custom_call_target="tpu_custom_call" | custom-call | bytes 41943040 | tf_op jit(solution)/shard_map/mix/pallas_call | solution.py:668
  162.2 46.3 %branch.1 = (f32[256,2048]{1,0:T(8,128)}, bf16[256,2048]{1,0:T(8,128)(2,1)}) custom-call(bf16[2048,256]{1,0:T(8,128)(2,1)} %get-tuple-element.67.refs_0_, bf16[4,768,512]{2,1,0:T(8,128)(2,1)} %bitcast.63, bf16[256,2048]{1,0:T(8,128)(2,1)} %get-tuple-element.68.refs_2_, f32[16,8,128]{2,1,0:T(8,128)} %get-tuple-element.58.refs_2_.refs_3_.refs_5_), custom_call_target="tpu_custom_call" | custom-call | bytes 41943040 | tf_op jit(solution)/shard_map/branch/pallas_call | solution.py:668
  208.5 9.0 %all-gather.9.cloned.1.call-done = bf16[4736,512]{1,0:T(8,128)(2,1)} async-done(((bf16[1184,512]{1,0:T(8,128)(2,1)}), bf16[4736,512]{1,0:T(8,128)(2,1)}) %all-gather.9.cloned.1.call-update) | async-done | bytes 4849680 | tf_op jit(solution)/shard_map/all_gather | solution.py:2213
  217.5 45.2 %expand.1 = (bf16[4,2,256,2048]{3,2,1,0:T(8,128)(2,1)}, f32[4,2,256,688]{3,2,1,0:T(8,128)}, f32[4,2,256,688]{3,2,1,0:T(8,128)}, bf16[688,2048]{1,0:T(8,128)(2,1)}) custom-call(bf16[256,2048]{1,0:T(8,128)(2,1)} %get-tuple-element.69.refs_0_, bf16[4,768,512]{2,1,0:T(8,128)(2,1)} %bitcast.64, bf16[4,1184,512]{2,1,0:T(8,128)(2,1)} %bitcast.87), custom_call_target="tpu_custom_call" | custom-call | flops 11542724608 | bytes 134217728 | tf_op jit(solution)/shard_map/expand/pallas_call | solution.py:668
  262.7 10.3 %convolution_convert_fusion = bf16[688,2048]{1,0:T(8,128)(2,1)} fusion(bf16[688,2048]{1,0:T(8,128)(2,1)} %get-tuple-element.74, bf16[2048,2048]{1,0:T(8,128)(2,1)} %bitcast.86), kind=kOutput, calls=%fused_computation | convolution fusion | flops 5772771328 | bytes 14024704 | tf_op jit(solution)/shard_map/dot_general | solution.py:304
  273.1 0.0 reduce-scatter.4.cloned.1.call-update
  273.1 0.2 reduce-scatter.6.cloned.1.call-start
  273.3 2.3 all-gather.11.cloned.1.call-done
  275.6 57.7 %hidden_units.1 = (bf16[4,2,256,2048]{3,2,1,0:T(8,128)(2,1)}, f32[256,2048]{1,0:T(8,128)}, bf16[1376,2048]{1,0:T(8,128)(2,1)}) custom-call(f32[4,2,256,688]{3,2,1,0:T(8,128)} %get-tuple-element.76.gate_hbm, f32[4,2,256,688]{3,2,1,0:T(8,128)} %get-tuple-element.77.up_hbm, bf16[4,2,256,2048]{3,2,1,0:T(8,128)(2,1)} %get-tuple-element.75.cot_hbm, ...), custom_call_target="tpu_custom_call" | custom-call | flops 34628173824 | bytes 134217728 | tf_op jit(solution)/shard_map/hidden_units/pallas_call | solution.py:668
  333.3 0.0 reduce-scatter.6.cloned.1.call-update
  333.3 0.0 reduce-scatter.8.cloned.1.call-start
  333.4 45.5 %turn.1 = (f32[256,2048]{1,0:T(8,128)}, f32[8,2048]{1,0:T(8,128)}, bf16[4,2,256,256]{3,2,1,0:T(8,128)(2,1)}, bf16[256,2048]{1,0:T(8,128)(2,1)}) custom-call(f32[256,2048]{1,0:T(8,128)} %get-tuple-element.80.refs_0_, f32[256,2048]{1,0:T(8,128)} %get-tuple-element.81.refs_1_.refs_4_, bf16[256,2048]{1,0:T(8,128)(2,1)} %get-tuple-element.66.refs_6_.refs_2_, ...), custom_call_target="tpu_custom_call" | custom-call | bytes 41943040 | tf_op jit(solution)/shard_map/turn/pallas_call | solution.py:668
  378.9 0.0 reduce-scatter.4.cloned.1.call-done.refs_13_
  378.9 74.6 %unmix.1 = (bf16[2048,384]{1,0:T(8,128)(2,1)}, bf16[256,2048]{1,0:T(8,128)(2,1)}, bf16[576,2048]{1,0:T(8,128)(2,1)}, bf16[4,688,128]{2,1,0:T(8,128)(2,1)}) custom-call(bf16[2048,256]{1,0:T(8,128)(2,1)} %bitcast.71, bf16[2048,2048]{1,0:T(8,128)(2,1)} %bitcast.69, bf16[256,2048]{1,0:T(8,128)(2,1)} %get-tuple-element.85.refs_2_, ...), custom_call_target="tpu_custom_call" | custom-call | bytes 62914560 | tf_op jit(solution)/shard_map/unmix/pallas_call | solution.py:668
  453.5 0.0 reduce-scatter.8.cloned.1.call-update
  453.5 1.1 copy-done.6
  454.6 1.2 bitcast_convert_fusion
  455.8 56.9 %leave.1 = (f32[2,256,2048]{2,1,0:T(8,128)}, bf16[2,256,2048]{2,1,0:T(8,128)(2,1)}, f32[16,8,128]{2,1,0:T(8,128)}, bf16[4,1376,128]{2,1,0:T(8,128)(2,1)}) custom-call(bf16[2048,384]{1,0:T(8,128)(2,1)} %get-tuple-element.90.refs_0_, bf16[4,768,512]{2,1,0:T(8,128)(2,1)} %bitcast.67, bf16[256,2048]{1,0:T(8,128)(2,1)} %get-tuple-element.68.refs_2_, ...), custom_call_target="tpu_custom_call" | custom-call | bytes 62914560 | tf_op jit(solution)/shard_map/leave/pallas_call | solution.py:668
  512.7 0.0 reduce-scatter.8.cloned.1.call-done.refs_0_
  512.8 14.1 %last.1 = (bf16[4,576,128]{2,1,0:T(8,128)(2,1)}, f32[8,128]{1,0:T(8,128)}) custom-call(bf16[576,512]{1,0:T(8,128)(2,1)} %reduce-scatter.8.cloned.1.call-done.refs_0_, f32[16,8,128]{2,1,0:T(8,128)} %get-tuple-element.98.refs_1_), custom_call_target="tpu_custom_call" | custom-call | bytes 67108864 | tf_op jit(solution)/shard_map/last/pallas_call | solution.py:668
  526.9 0.8 fusion.2
  527.7 1.1 fusion.1
  528.7 1.3 slice_bitcast_fusion
  530.0 0.7 copy.28
  530.8 0.7 copy.27
  531.5 0.8 bitcast_convert_fusion.1
  532.4 0.1 bitcast_convert_fusion.2
  532.4 1.0 copy.29
  533.4 0.0 copy-done.2
  533.4 0.1 fusion
  533.5 1.2 convert_bitcast_fusion
  534.7 1.2 convert_bitcast_fusion.1
  536.0 0.0 copy-done.1
  536.0 1.3 copy.36
  537.3 1.6 copy-done
  538.9 2.0 copy.37
  (17 shorter events, 0.1 us)
Async XLA Ops:
  7.2 21.2 %copy-start.5 = (bf16[128,2752]{0,1:T(8,128)(2,1)S(1)}, bf16[128,2752]{0,1:T(8,128)(2,1)}, u32[]{:S(2)}) copy-start(bf16[128,2752]{0,1:T(8,128)(2,1)} %param.21) | copy-start | bytes 2113540
  7.2 20.4 %copy-start.7 = (bf16[128]{0:T(256)(128)(2,1)S(1)}, bf16[128]{0:T(256)(128)(2,1)}, u32[]{:S(2)}) copy-start(bf16[128]{0:T(256)(128)(2,1)} %param.16) | copy-start | bytes 772
  7.2 20.4 %copy-start.8 = (bf16[128]{0:T(256)(128)(2,1)S(1)}, bf16[128]{0:T(256)(128)(2,1)}, u32[]{:S(2)}) copy-start(bf16[128]{0:T(256)(128)(2,1)} %param.15) | copy-start | bytes 772
  7.2 85.9 %all-gather.7.cloned.1.call-start = ((), (), s32[]{:S(2)}) async-start(), calls=%async_computation.6 | async-start | bytes 3932160 | tf_op jit(solution)/shard_map/all_gather | solution.py:2213
  12.9 0.9 copy-start.3
  28.3 189.2 %all-gather.9.cloned.1.call-start = ((), (), s32[]{:S(2)}) async-start(), calls=%async_computation.7 | async-start | bytes 6062080 | tf_op jit(solution)/shard_map/all_gather | solution.py:2213
  28.4 60.1 %copy-start.4 = (bf16[128,2752]{0,1:T(8,128)(2,1)S(1)}, bf16[128,2752]{0,1:T(8,128)(2,1)}, u32[]{:S(2)}) copy-start(bf16[128,2752]{0,1:T(8,128)(2,1)} %param.22) | copy-start | bytes 2113540
  117.4 158.3 %all-gather.11.cloned.1.call-start = ((), (), s32[]{:S(2)}) async-start(), calls=%async_computation.8 | async-start | bytes 3522560 | tf_op jit(solution)/shard_map/all_gather | solution.py:2213
  118.1 260.8 %reduce-scatter.4.cloned.1.call-start = ((), (), s32[]{:S(2)}) async-start(), calls=%async_computation.3 | async-start | bytes 3522560 | tf_op jit(solution)/shard_map/reduce_scatter | solution.py:2216
  273.1 182.7 %reduce-scatter.6.cloned.1.call-start = ((), (), s32[]{:S(2)}) async-start(), calls=%async_computation.4 | async-start | bytes 7045120 | tf_op jit(solution)/shard_map/reduce_scatter | solution.py:2216
  333.3 179.4 %reduce-scatter.8.cloned.1.call-start = ((), (), s32[]{:S(2)}) async-start(), calls=%async_computation.5 | async-start | bytes 2949120 | tf_op jit(solution)/shard_map/reduce_scatter | solution.py:2216
  453.5 1.1 copy-start.6
  512.7 20.7 %copy-start.2 = (bf16[4,1376,128]{2,1,0:T(8,128)(2,1)S(1)}, bf16[4,1376,128]{2,1,0:T(8,128)(2,1)}, u32[]{:S(2)}) copy-start(bf16[4,1376,128]{2,1,0:T(8,128)(2,1)} %get-tuple-element.101) | copy-start | bytes 4227076
  533.5 2.5 copy-start.1
  536.0 2.9 copy-start
Sparse Core Ops, SparseCore 0:
  28.4 64.6 all-gather.6
  117.5 99.9 all-gather.8
  219.1 56.5 all-gather.10
  278.4 53.8 reduce-scatter.3
  334.5 114.1 reduce-scatter.5
  453.6 46.9 reduce-scatter.7

commit v10 on v9

--- a/solution.py
+++ b/solution.py
@@ -525,15 +525,6 @@
     return started
 
 
-def exchange_kernel(take, put, count, *refs):
-    ins, outs, sems, local_sems = refs[:count], refs[count : 2 * count], refs[-2], refs[-1]
-    size, me = lax.axis_size("dp"), lax.axis_index("dp")
-    peers = [lax.rem(me + k, size) for k in range(1, size)]
-    greet([{"dp": p} for p in peers])
-    for c in swap_shards(ins, outs, peers, me, take, put, Sender(sems), local_sems):
-        c.wait()
-
-
 def block_of(ref, index):
     return ref.at[index]
 
@@ -543,24 +534,57 @@
     return ref.at[rows, pl.ds(pl.multiple_of(index * width, width), width)]
 
 
-def exchange(arrays, cid, shapes, take=block_of, put=block_of):
-    count, peers = len(arrays), lax.axis_size("dp") - 1
-    anywhere = [pl.BlockSpec(memory_space=pl.ANY)] * count
-    return pl.pallas_call(
-        partial(exchange_kernel, take, put, count),
-        name="exchange",
-        out_shape=[jax.ShapeDtypeStruct(s, x.dtype) for s, x in zip(shapes, arrays)],
-        in_specs=anywhere,
-        out_specs=anywhere,
-        scratch_shapes=[
-            pltpu.SemaphoreType.DMA((2, count * peers)),
-            pltpu.SemaphoreType.DMA((count,)),
+def weights_kernel(
+    value_ref,
+    query_ref,
+    key_ref,
+    output_ref,
+    early_ref,
+    out_ref,
+    pack_ref,
+    sems,
+    local_sems,
+):
+    plane, at = lax.axis_size("dp"), lax.axis_index("dp")
+    chips = [lax.rem(at + k, plane) for k in range(1, plane)]
+    greet([{"dp": p} for p in chips])
+    vcols, qcols = value_ref.shape[1] // plane, query_ref.shape[1] // plane
+    queries, keys = query_ref[...].T, key_ref[...].T
+    for j in range(plane):
+        first = 0
+        for piece in (
+            value_ref[:, j * vcols : (j + 1) * vcols].T,
+            queries[j * qcols : (j + 1) * qcols],
+            keys[j * qcols : (j + 1) * qcols],
+            output_ref[j * vcols : (j + 1) * vcols],
+            early_ref[j],
+        ):
+            pack_ref[j, first : first + piece.shape[0]] = piece
+            first += piece.shape[0]
+    for c in swap_shards(
+        (pack_ref,), (out_ref,), chips, at, block_of, columns_of, Sender(sems), local_sems
+    ):
+        c.wait()
+
+
+def weights_exchange(value, query, key, output, early, cid):
+    plane, rows, chunk = early.shape
+    size = rows + (value.shape[1] + query.shape[1] + key.shape[1] + output.shape[0]) // plane
+    whole = pltpu.VMEM
+    [pack] = kernel_call(
+        weights_kernel,
+        "exchange",
+        cid,
+        [((size, plane * chunk), value.dtype, pl.ANY)],
+        [(a, whole) for a in (value, query, key, output, early)],
+        [
+            pltpu.VMEM((plane, size, chunk), value.dtype),
+            copies(plane - 1),
+            pltpu.SemaphoreType.DMA((1,)),
         ],
-        compiler_params=pltpu.CompilerParams(collective_id=cid, has_side_effects=True),
-        cost_estimate=pl.CostEstimate(
-            flops=0, bytes_accessed=60 * sum(x.size for x in arrays), transcendentals=0
-        ),
-    )(*arrays)
+        moved=1 << 24,
+    )
+    return pack
 
 
 def small_kernel(
@@ -1601,20 +1625,37 @@
         finish(r, k, scale * g * gain_at(k) - v * pull)
 
 
+def mixer_cotangents(dmixed, exact, den, h):
+    v = slice(h * VHEAD, (h + 1) * VHEAD)
+    dn = dmixed[:, v].astype(jnp.float32) / den[:, h : h + 1]
+    dd = -jnp.sum(dn * exact[:, v], axis=1, keepdims=True)
+    return dn.astype(jnp.bfloat16), dd
+
+
 def turn_kernel(
+    heads,
     total_ref,
     residual_ref,
     cot_ref,
     small_ref,
     pack_ref,
     mixed_ref,
+    col_ref,
+    row_ref,
+    pairs_ref,
+    qkv_ref,
+    exact_ref,
+    den_ref,
     dresid_ref,
     gain_ref,
     dmixed_ref,
     grad_ref,
+    own_ref,
+    own_sums_ref,
     all_ref,
     low_ref,
     sum_ref,
+    pick_ref,
     gather_sems,
     local_sem,
 ):
@@ -1647,7 +1688,21 @@
     gather = gather_steps(low_ref, all_ref, Sender(gather_sems), local_sem)
     next(gather)
     sum_ref[...] = jnp.zeros_like(sum_ref)
+    own_sums_ref[...] = jnp.zeros_like(own_sums_ref)
+    fill_selectors(pairs_ref, pick_ref, heads * FDIM)
     next(gather)
+
+    def first(chip, k):
+        b = chip * 2 + k
+        head = Segments(col_ref, row_ref, b).head
+        t = pl.ds(pl.multiple_of(b * m, m), m)
+        tile = qkv_ref[t, pl.ds(vcols, LANES)]
+        for h in range(heads):
+            dn, dd = mixer_cotangents(dmixed_ref[chip, k], exact_ref[t], den_ref[t], h)
+            one, two = factors(tile, pick_ref, 0, h)
+            lifted = jnp.where(head, one * two, 0.0)
+            own_ref[b, h] = tn_dot(lifted.astype(jnp.bfloat16), dn)
+            own_sums_ref[b, h : h + 1] = jnp.sum(lifted * dd, axis=0, keepdims=True)
 
     def block(i, carry):
         for step in range(1, 8):
@@ -1668,6 +1723,15 @@
         for s in range(parts):
             cols = pl.ds(s * depth, depth)
             sum_ref[:, cols] += tn_dot(left, columns(cols))
+        (one, k, _), (two, _, _) = pieces
+
+        def rows_done(n, carry):
+            first(jnp.where(n == 0, one, two), k)
+            return carry
+
+        both = ((i >= 4) & (i < 6)).astype(jnp.int32)
+        whole = ((i < 2) | (i >= 4)).astype(jnp.int32)
+        lax.fori_loop(0, whole + both, rows_done, 0)
         return carry
 
     lax.fori_loop(0, 8, block, 0)
@@ -1675,12 +1739,13 @@
     run(gather)
 
 
-def turn(total, residual, cot_own, small, pack, mixed, cid):
+def turn(total, residual, cot_own, small, pack, mixed, segments, pairs, kept, heads, cid):
     m, width = residual.shape
     vcols = mixed.shape[1]
+    rows = segments[0].shape[0]
     whole, low = pltpu.VMEM, jnp.bfloat16
-    dresid, gain, dmixed, grad = kernel_call(
-        turn_kernel,
+    dresid, gain, dmixed, grad, own, own_sums = kernel_call(
+        partial(turn_kernel, heads),
         "turn",
         cid,
         [
@@ -1688,19 +1753,23 @@
             ((8, width), jnp.float32, whole),
             ((4, 2, m, vcols), low, whole),
             ((vcols, width), low, whole),
+            ((rows, heads, FEATURES, VHEAD), jnp.float32, whole),
+            ((rows, 8, FEATURES), jnp.float32, whole),
         ],
         [(a, whole) for a in (total, residual, cot_own, small, pack)]
-        + [(mixed.reshape(4, 2, m, vcols), whole)],
+        + [(mixed.reshape(4, 2, m, vcols), whole)]
+        + [(a, whole) for a in (*segments, pairs, *kept)],
         [
             pltpu.VMEM((4, 2, m, width), low),
             pltpu.VMEM((m, width), low),
             pltpu.VMEM((vcols, width), jnp.float32),
+            pltpu.VMEM((2, heads, 2, LANES, FEATURES), low),
             copies(GATHER_COPIES),
             pltpu.SemaphoreType.DMA,
         ],
         moved=residual.size * 80,
     )
-    return dresid, gain, dmixed.reshape(8 * m, vcols), grad
+    return dresid, gain, dmixed.reshape(8 * m, vcols), grad, own, own_sums
 
 
 def unmix_kernel(
@@ -1719,6 +1788,8 @@
     den_ref,
     state_ref,
     sums_ref,
+    own_ref,
+    own_sums_ref,
     *refs,
 ):
     ins, dqkv_ref, block_ref, grad_ref = refs[:count], *refs[count : count + 3]
@@ -1732,8 +1803,6 @@
         back_ref,
         back_sums_ref,
         pick_ref,
-        own_ref,
-        own_sums_ref,
         out_ref,
         out_sums_ref,
         total_ref,
@@ -1788,24 +1857,8 @@
         return pl.ds(pl.multiple_of(b * length, length), length)
 
     def cotangents(t, h):
-        v = pl.ds(h * VHEAD, VHEAD)
-        dn = dmixed_ref[t, v].astype(jnp.float32) / den_ref[t, pl.ds(h, 1)]
-        dd = -jnp.sum(dn * exact_ref[t, v], axis=1, keepdims=True)
-        return dn.astype(jnp.bfloat16), dd
-
-    def first(b, carry):
-        t = tokens_of(b)
-        head = Segments(col_ref, row_ref, b).head
-        tile = qkv_ref[t, pl.ds(vcols, LANES)]
-        for h in range(heads):
-            dn, dd = cotangents(t, h)
-            one, two = factors(tile, pick_ref, 0, h)
-            lifted = jnp.where(head, one * two, 0.0)
-            own_ref[b, h] = tn_dot(lifted.astype(jnp.bfloat16), dn)
-            own_sums_ref[b, h : h + 1] = jnp.sum(lifted * dd, axis=0, keepdims=True)
-        return carry
-
-    own_sums_ref[...] = jnp.zeros_like(own_sums_ref)
+        return mixer_cotangents(dmixed_ref[t], exact_ref[t], den_ref[t], h)
+
     shards = swap_shards(ins, outs, chips, at, columns_of, block_of, Sender(shard_sems), local_sems)
 
     def lowered(dlifted, kind, h, one, two):
@@ -1860,10 +1913,6 @@
     each = rows // CHUNKS
 
     def work(n, step):
-        @pl.when(n < CHUNKS)
-        def _():
-            lax.fori_loop(n * each, (n + 1) * each, first, 0)
-
         step(n)
 
         @pl.when(n < CHUNKS)
@@ -1918,7 +1967,9 @@
     chain.close()
 
 
-def unmix(dmixed, normed, output_grad, part, residual, segments, pairs, kept, shards, heads, cid):
+def unmix(
+    dmixed, normed, output_grad, part, residual, segments, pairs, kept, own, shards, heads, cid
+):
     seg_col, seg_row = segments
     tokens, vcols = dmixed.shape
     plane, rows = lax.axis_size("dp"), seg_col.shape[0]
@@ -1946,7 +1997,7 @@
             (seg_row, whole),
             (pairs, whole),
         ]
-        + [(a, whole) for a in kept]
+        + [(a, whole) for a in (*kept, *own)]
         + [(p, pl.ANY) for p in shards],
         [
             pltpu.VMEM((tokens, width), low),
@@ -1957,7 +2008,11 @@
             pltpu.VMEM((rows, heads, FEATURES, VHEAD), low),
             pltpu.VMEM((rows, 8, FEATURES), jnp.float32),
         ]
-        + state_scratch(rows, heads)
+        + [
+            pltpu.VMEM((2, heads, 2, LANES, FEATURES), low),
+            pltpu.VMEM((rows, heads, FEATURES, VHEAD), low),
+            pltpu.VMEM((rows, 8, FEATURES), jnp.float32),
+        ]
         + [pltpu.VMEM((m, width), jnp.float32), pltpu.VMEM((4, m, width), low)]
         + scatter_scratch(m, width)
         + [
@@ -2220,6 +2275,13 @@
     def split(w):
         return w.reshape(plane, -1, chunk)
 
+    gate_w = split(gate_weight.T)
+    pack = weights_exchange(
+        value_weight, query_weight, key_weight, output_weight, gate_w[:, :EARLY], 1
+    )
+    attn_gain, mlp_gain, doc_starts, pack = lax.optimization_barrier(
+        (attn_gain, mlp_gain, doc_starts, pack)
+    )
     small = jnp.concatenate(
         [
             attn_gain.astype(jnp.float32)[None],
@@ -2228,19 +2290,6 @@
             jnp.zeros((2, chunk), jnp.float32),
         ]
     )
-    gate_w = split(gate_weight.T)
-    pack = jnp.concatenate(
-        [
-            split(value_weight.T),
-            split(query_weight.T),
-            split(key_weight.T),
-            split(output_weight),
-            gate_w[:, :EARLY],
-        ],
-        axis=1,
-    )
-    [pack] = exchange([pack], 1, [(pack.shape[1], plane * chunk)], put=columns_of)
-    small, pack = lax.optimization_barrier((small, pack))
     small, down_w = small_exchange(small, split(down_weight), 2)
     pack = over_seq(pack)
     late_w = jnp.concatenate([gate_w[:, EARLY:], split(up_weight.T)], axis=1)
@@ -2274,8 +2323,19 @@
         gate, up, cot, pack, late_w, down_w, normed_two, 6
     )
     gate_up_grad = summed(gate_up_grad)
-    dresid, gain_two_grad, dmixed, out_grad = turn(
-        dnormed_two, residual, cot_own, small, out_of, mixed, 12
+    segments = (seg_col, seg_row)
+    dresid, gain_two_grad, dmixed, out_grad, *sums_own = turn(
+        dnormed_two,
+        residual,
+        cot_own,
+        small,
+        out_of,
+        mixed,
+        segments,
+        pairs,
+        (qkv, exact, den),
+        heads,
+        12,
     )
     dmixed, down_grad = lax.optimization_barrier((dmixed, down_grad))
     dqkv, block_own, attn_grad, (down_grad,) = unmix(
@@ -2284,9 +2344,10 @@
         out_grad,
         out_part,
         residual,
-        (seg_col, seg_row),
+        segments,
         pairs,
         (qkv, exact, den, state, sums),
+        sums_own,
         [down_grad],
         heads,
         8,
@@ -2295,6 +2356,7 @@
     dtokens, block_out, gains, gate_up_grad = leave(
         dqkv, into, x, dresid, block_own, small, gain_two_grad, [gate_up_grad], 9
     )
+    down_grad, gains = lax.optimization_barrier((down_grad, gains))
     (attn_grad,), gain_grads = last([attn_grad], gains, 10)
 
     def stacked(a, start, size):

time: 549 us -> 542 us (0.987)
    pallas_call x11 -> x12, Pallas kernels: 469 us -> 483 us  [kernel_call(): pl.pallas_call(loaded if big else body, name=name, out_shape=[jax.ShapeDt...]
    pallas_call x1 -> x0, Pallas kernels: 13.7 us -> none  [exchange(): pl.pallas_call(partial(exchange_kernel, take, put, count), name='exchange...]
where the time goes in v10:
time: 542 us
  Pallas kernels  483 us (89%)
  waiting for transfers between devices  14.8 us (3%)
  between operations  14.4 us (3%)
  local copies, waits for them, and re-layouts  12.5 us (2%)
  matrix products  10.3 us (2%)
  other arithmetic  6.37 us (1%)
    pallas_call x12, Pallas kernels, kernel_call(): pl.pallas_call(loaded if big else body, name=name, out_shape=[jax.ShapeDt...  483 us
    all_gather x3, waiting for transfers between devices, over_seq(): return lax.all_gather(pack, 'seq', axis=0, tiled=False)  14 us
  transfers between devices with their start and end apart: 6, of which 3 were waited for; matrix products, arithmetic and copies ran while one was open for 2% of the time, Pallas kernels for 79%

profile of v10, /device:TPU:0, one launch (start us, length us, event | category | flops | bytes accessed | tf_op | source)
XLA Modules:
  0.0 541.5 jit_solution(15780568880390476810)
XLA Ops:
  7.2 0.0 copy-start.4
  7.2 0.0 copy-start.7
  7.2 0.0 copy-start.8
  7.2 0.0 copy-start.6
  7.2 0.0 all-gather.7.cloned.1.call-start
  7.3 1.7 slice.40.refs_4_
  8.9 14.5 %exchange.1 = bf16[768,512]{1,0:T(8,128)(2,1)} custom-call(bf16[128,1024]{1,0:T(8,128)(2,1)} %refs_0_.2, bf16[128,128]{1,0:T(8,128)(2,1)} %refs_1_.2, bf16[128,128]{1,0:T(8,128)(2,1)} %refs_2_.1, bf16[1024,128]{1,0:T(8,128)(2,1)} %refs_3_.2, bf16[4,192,128]{2,1,0:T(8,128)(2,1)} %slice.40.refs_4_), custom_call_target="tpu_custom_call" | custom-call | bytes 16777216 | tf_op jit(solution)/shard_map/exchange/pallas_call | solution.py:692
  23.5 0.0 all-gather.7.cloned.1.call-update
  23.5 0.0 all-gather.9.cloned.1.call-start
  23.5 0.0 copy-done.4
  23.6 0.0 copy-done.6
  23.6 0.1 pad.5.clone
  23.7 0.0 copy-done.7
  23.7 0.0 copy-done.8
  23.7 0.7 maximum_maximum_fusion.small_ref
  24.4 16.6 %small_exchange.1 = (f32[16,8,128]{2,1,0:T(8,128)}, bf16[688,512]{1,0:T(8,128)(2,1)}) custom-call(f32[8,128]{1,0:T(8,128)} %maximum_maximum_fusion.small_ref, bf16[4,688,128]{2,1,0:T(8,128)(2,1)} %bitcast.68), custom_call_target="tpu_custom_call" | custom-call | bytes 16777216 | tf_op jit(solution)/shard_map/small_exchange/pallas_call | solution.py:692
  41.0 43.5 %entry.1 = (bf16[4,2,256,2048]{3,2,1,0:T(8,128)(2,1)}, bf16[256,2048]{1,0:T(8,128)(2,1)}, bf16[256,2048]{1,0:T(8,128)(2,1)}, f32[8,256,1]{2,1,0:T(8,128)}, f32[8,1,256]{2,1,0:T(1,128)}) custom-call(bf16[2,256,2048]{2,1,0:T(8,128)(2,1)} %refs_0_.3, bf16[2,256,2048]{2,1,0:T(8,128)(2,1)} %refs_1_.3, f32[16,8,128]{2,1,0:T(8,128)} %get-tuple-element.66.refs_2_.refs_3_.refs_5_), custom_call_target="tpu_custom_call" | custom-call | bytes 41943040 | tf_op jit(solution)/shard_map/entry/pallas_call | solution.py:692
  84.5 0.0 copy-done.3
  84.5 1.1 pad_maximum_fusion.refs_5_
  85.6 2.6 all-gather.7.cloned.1.call-done
  88.3 24.3 %states.1 = (bf16[2048,384]{1,0:T(8,128)(2,1)}, bf16[8,2,256,128]{3,2,1,0:T(8,128)(2,1)}, f32[8,8,256]{2,1,0:T(8,128)}, bf16[1184,512]{1,0:T(8,128)(2,1)}) custom-call(bf16[2048,2048]{1,0:T(8,128)(2,1)} %bitcast.61, bf16[4,768,512]{2,1,0:T(8,128)(2,1)} %bitcast.55, f32[8,256,1]{2,1,0:T(8,128)} %get-tuple-element.69.refs_2_.refs_1_.refs_6_.refs_5_, ...), custom_call_target="tpu_custom_call" | custom-call | bytes 83886080 | tf_op jit(solution)/shard_map/states/pallas_call | solution.py:692
  112.6 0.0 all-gather.9.cloned.1.call-update
  112.6 0.0 all-gather.11.cloned.1.call-start
  112.6 0.7 all-gather.11.cloned.1.call-update
  113.3 0.0 reduce-scatter.4.cloned.1.call-start
  113.4 44.0 %mix.1 = (bf16[2048,256]{1,0:T(8,128)(2,1)}, f32[2048,256]{1,0:T(8,128)}, f32[2048,128]{1,0:T(8,128)}, bf16[4,2,256,2048]{3,2,1,0:T(8,128)(2,1)}) custom-call(bf16[2048,384]{1,0:T(8,128)(2,1)} %get-tuple-element.71.refs_0_.refs_9_.refs_8_, f32[8,256,1]{2,1,0:T(8,128)} %get-tuple-element.69.refs_2_.refs_1_.refs_6_.refs_5_, ...), custom_call_target="tpu_custom_call" | custom-call | bytes 41943040 | tf_op jit(solution)/shard_map/mix/pallas_call | solution.py:692
  157.4 46.3 %branch.1 = (f32[256,2048]{1,0:T(8,128)}, bf16[256,2048]{1,0:T(8,128)(2,1)}) custom-call(bf16[2048,256]{1,0:T(8,128)(2,1)} %get-tuple-element.75.refs_0_, bf16[4,768,512]{2,1,0:T(8,128)(2,1)} %bitcast.56, bf16[256,2048]{1,0:T(8,128)(2,1)} %get-tuple-element.76.refs_2_, f32[16,8,128]{2,1,0:T(8,128)} %get-tuple-element.66.refs_2_.refs_3_.refs_5_), custom_call_target="tpu_custom_call" | custom-call | bytes 41943040 | tf_op jit(solution)/shard_map/branch/pallas_call | solution.py:692
  203.7 9.0 %all-gather.9.cloned.1.call-done = bf16[4736,512]{1,0:T(8,128)(2,1)} async-done(((bf16[1184,512]{1,0:T(8,128)(2,1)}), bf16[4736,512]{1,0:T(8,128)(2,1)}) %all-gather.9.cloned.1.call-update) | async-done | bytes 4849680 | tf_op jit(solution)/shard_map/all_gather | solution.py:2268
  212.7 45.2 %expand.1 = (bf16[4,2,256,2048]{3,2,1,0:T(8,128)(2,1)}, f32[4,2,256,688]{3,2,1,0:T(8,128)}, f32[4,2,256,688]{3,2,1,0:T(8,128)}, bf16[688,2048]{1,0:T(8,128)(2,1)}) custom-call(bf16[256,2048]{1,0:T(8,128)(2,1)} %get-tuple-element.77.refs_0_, bf16[4,768,512]{2,1,0:T(8,128)(2,1)} %bitcast.57, bf16[4,1184,512]{2,1,0:T(8,128)(2,1)} %bitcast.73), custom_call_target="tpu_custom_call" | custom-call | flops 11542724608 | bytes 134217728 | tf_op jit(solution)/shard_map/expand/pallas_call | solution.py:692
  257.9 10.3 %convolution_convert_fusion = bf16[688,2048]{1,0:T(8,128)(2,1)} fusion(bf16[688,2048]{1,0:T(8,128)(2,1)} %get-tuple-element.82, bf16[2048,2048]{1,0:T(8,128)(2,1)} %bitcast.72), kind=kOutput, calls=%fused_computation | convolution fusion | flops 5772771328 | bytes 14024704 | tf_op jit(solution)/shard_map/dot_general | solution.py:304
  268.3 0.0 reduce-scatter.4.cloned.1.call-update
  268.3 0.2 reduce-scatter.6.cloned.1.call-start
  268.5 2.3 all-gather.11.cloned.1.call-done
  270.8 57.7 %hidden_units.1 = (bf16[4,2,256,2048]{3,2,1,0:T(8,128)(2,1)}, f32[256,2048]{1,0:T(8,128)}, bf16[1376,2048]{1,0:T(8,128)(2,1)}) custom-call(f32[4,2,256,688]{3,2,1,0:T(8,128)} %get-tuple-element.84.gate_hbm, f32[4,2,256,688]{3,2,1,0:T(8,128)} %get-tuple-element.85.up_hbm, bf16[4,2,256,2048]{3,2,1,0:T(8,128)(2,1)} %get-tuple-element.83.cot_hbm, ...), custom_call_target="tpu_custom_call" | custom-call | flops 34628173824 | bytes 134217728 | tf_op jit(solution)/shard_map/hidden_units/pallas_call | solution.py:692
  328.5 0.0 reduce-scatter.6.cloned.1.call-update
  328.5 0.0 reduce-scatter.8.cloned.1.call-start
  328.6 48.9 %turn.1 = (f32[256,2048]{1,0:T(8,128)}, f32[8,2048]{1,0:T(8,128)}, bf16[4,2,256,256]{3,2,1,0:T(8,128)(2,1)}, bf16[256,2048]{1,0:T(8,128)(2,1)}, f32[8,2,256,128]{3,2,1,0:T(8,128)}, /*index=5*/f32[8,8,256]{2,1,0:T(8,128)}) custom-call(f32[256,2048]{1,0:T(8,128)} %get-tuple-element.88.refs_0_, f32[256,2048]{1,0:T(8,128)} %get-tuple-element.89.refs_1_.refs_4_, ...), custom_call_target="tpu_custom_call" | custom-call | bytes 41943040 | tf_op jit(solution)/shard_map/turn/pallas_call | solution.py:692
  377.4 0.0 reduce-scatter.4.cloned.1.call-done.refs_15_
  377.5 71.3 %unmix.1 = (bf16[2048,384]{1,0:T(8,128)(2,1)}, bf16[256,2048]{1,0:T(8,128)(2,1)}, bf16[576,2048]{1,0:T(8,128)(2,1)}, bf16[4,688,128]{2,1,0:T(8,128)(2,1)}) custom-call(bf16[2048,256]{1,0:T(8,128)(2,1)} %bitcast.64, bf16[2048,2048]{1,0:T(8,128)(2,1)} %bitcast.62, bf16[256,2048]{1,0:T(8,128)(2,1)} %get-tuple-element.95.refs_2_, ...), custom_call_target="tpu_custom_call" | custom-call | bytes 62914560 | tf_op jit(solution)/shard_map/unmix/pallas_call | solution.py:692
  448.8 0.0 reduce-scatter.8.cloned.1.call-update
  448.8 0.0 reduce-scatter.6.cloned.1.call-done.refs_7_
  448.8 56.5 %leave.1 = (f32[2,256,2048]{2,1,0:T(8,128)}, bf16[2,256,2048]{2,1,0:T(8,128)(2,1)}, f32[16,8,128]{2,1,0:T(8,128)}, bf16[4,1376,128]{2,1,0:T(8,128)(2,1)}) custom-call(bf16[2048,384]{1,0:T(8,128)(2,1)} %get-tuple-element.100.refs_0_, bf16[4,768,512]{2,1,0:T(8,128)(2,1)} %bitcast.60, bf16[256,2048]{1,0:T(8,128)(2,1)} %get-tuple-element.76.refs_2_, ...), custom_call_target="tpu_custom_call" | custom-call | bytes 62914560 | tf_op jit(solution)/shard_map/leave/pallas_call | solution.py:692
  505.3 0.0 copy-start.5
  505.3 0.0 reduce-scatter.8.cloned.1.call-done.refs_0_
  505.3 14.1 %last.1 = (bf16[4,576,128]{2,1,0:T(8,128)(2,1)}, f32[8,128]{1,0:T(8,128)}) custom-call(bf16[576,512]{1,0:T(8,128)(2,1)} %reduce-scatter.8.cloned.1.call-done.refs_0_, f32[16,8,128]{2,1,0:T(8,128)} %get-tuple-element.110.refs_1_), custom_call_target="tpu_custom_call" | custom-call | bytes 67108864 | tf_op jit(solution)/shard_map/last/pallas_call | solution.py:692
  519.4 0.8 fusion.2
  520.2 1.1 fusion.1
  521.3 1.3 slice_bitcast_fusion
  522.6 0.7 copy.25
  523.3 0.7 copy.24
  524.1 0.8 bitcast_convert_fusion.1
  524.9 0.1 bitcast_convert_fusion.2
  525.0 1.0 copy.26
  525.9 0.0 copy-done.5
  526.0 1.2 bitcast_convert_fusion
  527.2 0.0 copy-done.2
  527.2 0.1 fusion
  527.3 0.0 copy-start.1
  527.3 1.2 convert_bitcast_fusion
  528.5 1.2 convert_bitcast_fusion.1
  529.7 0.0 copy-done.1
  529.7 1.3 copy.29
  531.1 1.6 copy-done
  532.7 2.0 copy.30
  (10 shorter events, 0.1 us)
Async XLA Ops:
  7.2 16.4 %copy-start.4 = (bf16[128,2752]{0,1:T(8,128)(2,1)S(1)}, bf16[128,2752]{0,1:T(8,128)(2,1)}, u32[]{:S(2)}) copy-start(bf16[128,2752]{0,1:T(8,128)(2,1)} %param.21) | copy-start | bytes 2113540
  7.2 16.5 %copy-start.7 = (bf16[128]{0:T(256)(128)(2,1)S(1)}, bf16[128]{0:T(256)(128)(2,1)}, u32[]{:S(2)}) copy-start(bf16[128]{0:T(256)(128)(2,1)} %param.16) | copy-start | bytes 772
  7.2 16.5 %copy-start.8 = (bf16[128]{0:T(256)(128)(2,1)S(1)}, bf16[128]{0:T(256)(128)(2,1)}, u32[]{:S(2)}) copy-start(bf16[128]{0:T(256)(128)(2,1)} %param.15) | copy-start | bytes 772
  7.2 16.4 %copy-start.6 = (s32[2,256]{1,0:T(2,128)S(1)}, s32[2,256]{1,0:T(2,128)}, u32[]{:S(2)}) copy-start(s32[2,256]{1,0:T(2,128)} %param.14) | copy-start | bytes 6148
  7.2 81.1 %all-gather.7.cloned.1.call-start = ((), (), s32[]{:S(2)}) async-start(), calls=%async_computation.6 | async-start | bytes 3932160 | tf_op jit(solution)/shard_map/all_gather | solution.py:2268
  23.5 189.2 %all-gather.9.cloned.1.call-start = ((), (), s32[]{:S(2)}) async-start(), calls=%async_computation.7 | async-start | bytes 6062080 | tf_op jit(solution)/shard_map/all_gather | solution.py:2268
  24.4 60.1 %copy-start.3 = (bf16[128,2752]{0,1:T(8,128)(2,1)S(1)}, bf16[128,2752]{0,1:T(8,128)(2,1)}, u32[]{:S(2)}) copy-start(bf16[128,2752]{0,1:T(8,128)(2,1)} %param.22) | copy-start | bytes 2113540
  112.6 158.2 %all-gather.11.cloned.1.call-start = ((), (), s32[]{:S(2)}) async-start(), calls=%async_computation.8 | async-start | bytes 3522560 | tf_op jit(solution)/shard_map/all_gather | solution.py:2268
  113.3 264.1 %reduce-scatter.4.cloned.1.call-start = ((), (), s32[]{:S(2)}) async-start(), calls=%async_computation.3 | async-start | bytes 3522560 | tf_op jit(solution)/shard_map/reduce_scatter | solution.py:2271
  268.3 180.5 %reduce-scatter.6.cloned.1.call-start = ((), (), s32[]{:S(2)}) async-start(), calls=%async_computation.4 | async-start | bytes 7045120 | tf_op jit(solution)/shard_map/reduce_scatter | solution.py:2271
  328.5 176.8 %reduce-scatter.8.cloned.1.call-start = ((), (), s32[]{:S(2)}) async-start(), calls=%async_computation.5 | async-start | bytes 2949120 | tf_op jit(solution)/shard_map/reduce_scatter | solution.py:2271
  505.3 20.6 %copy-start.5 = (bf16[4,688,128]{2,1,0:T(8,128)(2,1)S(1)}, bf16[4,688,128]{2,1,0:T(8,128)(2,1)}, u32[]{:S(2)}) copy-start(bf16[4,688,128]{2,1,0:T(8,128)(2,1)} %get-tuple-element.114) | copy-start | bytes 2113540
  524.1 3.1 copy-start.2
  527.3 2.5 copy-start.1
  529.7 2.9 copy-start
Sparse Core Ops, SparseCore 0:
  23.6 64.6 all-gather.6
  112.7 99.9 all-gather.8
  214.3 56.5 all-gather.10
  273.6 53.8 reduce-scatter.3
  329.7 114.1 reduce-scatter.5
  448.9 46.9 reduce-scatter.7
